TPU v7x, 32 devices: a whole 2x2x4 slice. The times are simulated.
32 devices in a mesh: expert: 4 (over x, core), context: 4 (over z), dp: 2 (over y).
Axes of the slice: x: 2, y: 2, z: 4, core: 2. Of those that a mesh axis runs over, the one named last changes fastest.
Arguments:
- tokens: bfloat16 [8, 1024, 1536], P(('expert', 'dp'), 'context'), may hold values from -6 to 6
- routes: int32 [8, 1024, 8], P(('expert', 'dp'), 'context'), may hold values from 0 to 19, all different within a row
- cotangent: bfloat16 [8, 1024, 1536], P(('expert', 'dp'), 'context'), may hold values from -6 to 6
- norm_attn: bfloat16 [1536], replicated, may hold values from 0.5 to 1.5
- w_query: bfloat16 [1536, 1536], replicated, may hold values from -0.15625 to 0.15625
- w_key: bfloat16 [1536, 512], replicated, may hold values from -0.15625 to 0.15625
- w_value: bfloat16 [1536, 512], replicated, may hold values from -0.15625 to 0.15625
- w_out: bfloat16 [1536, 1536], replicated, may hold values from -1.25 to 1.25
- norm_ffn: bfloat16 [1536], replicated, may hold values from 0.5 to 1.5
- w_router: bfloat16 [1536, 20], replicated, may hold values from -0.078125 to 0.078125
- w_gate: bfloat16 [20, 1536, 512], P('expert'), may hold values from -0.15625 to 0.15625
- w_up: bfloat16 [20, 1536, 512], P('expert'), may hold values from -0.15625 to 0.15625
- w_down: bfloat16 [20, 512, 1536], P('expert'), may hold values from -0.75 to 0.75
Outputs:
- layer_out: bfloat16 [8, 1024, 1536], P(('expert', 'dp'), 'context')
- grad_tokens: bfloat16 [8, 1024, 1536], P(('expert', 'dp'), 'context')
- grad_norm_attn: float32 [1536], P(('expert', 'context', 'dp'))
- grad_w_query: float32 [1536, 1536], P(('expert', 'context', 'dp'))
- grad_w_key: float32 [1536, 512], P(('expert', 'context', 'dp'))
- grad_w_value: float32 [1536, 512], P(('expert', 'context', 'dp'))
- grad_w_out: float32 [1536, 1536], P(('expert', 'context', 'dp'))
- grad_norm_ffn: float32 [1536], P(('expert', 'context', 'dp'))
- grad_w_router: float32 [1536, 20], P(('expert', 'context', 'dp'))
- grad_w_gate: float32 [20, 1536, 512], P('expert', ('context', 'dp'))
- grad_w_up: float32 [20, 1536, 512], P('expert', ('context', 'dp'))
- grad_w_down: float32 [20, 512, 1536], P('expert', ('context', 'dp'))
Inputs may be any that keep to these rules, and one draw needn't show every extreme that they name: `routes`: each token names 8 different experts; every expert is named by some token.
All inputs are finite; a program needn't handle non-finite values.
Results may differ from a plain program's by a relative error of at most 0.018.
Values may be sent and summed in bfloat16 or wider, within the bound.
No kernel may reach another device: no remote copies, remote signals or barrier semaphores. Data moves between devices by JAX's collectives and lax.ppermute only.
A program may use at most 256 MiB of HBM per device.

v0:
```python
import jax
import jax.numpy as jnp
from jax import lax
from jax.sharding import PartitionSpec as P

HEADS = 24
KV_HEADS = 8
HEAD_DIM = 64


EPS = 1e-05
ROPE_BASE = 10000.0
NEG_LARGE = -1e30


def rope_tables(positions):
    half_dim = HEAD_DIM // 2
    frequency = ROPE_BASE ** (-2.0 * jnp.arange(half_dim, dtype=jnp.float32) / HEAD_DIM)
    angles = positions.astype(jnp.float32)[:, None] * frequency[None, :]
    angles = jnp.concatenate([angles, angles], -1)
    return (jnp.cos(angles), jnp.sin(angles))


def rotate(values, cosine, sine_table):
    half_dim = values.shape[-1] // 2
    turned = jnp.concatenate([-values[..., half_dim:], values[..., :half_dim]], -1)
    return values * cosine[:, None, :] + turned * sine_table[:, None, :]


def rotate_back(grad_in, cosine, sine_table):
    half_dim = grad_in.shape[-1] // 2
    scaled = grad_in * sine_table[:, None, :]
    turned = jnp.concatenate([scaled[..., half_dim:], -scaled[..., :half_dim]], -1)
    return grad_in * cosine[:, None, :] + turned


def rms_scale(values):
    return lax.rsqrt(jnp.mean(values * values, -1, keepdims=True) + EPS)


def norm_back(grad_out, values, scale, gain):
    weighted = gain * grad_out
    return scale * weighted - values * scale**3 * jnp.mean(weighted * values, -1, keepdims=True)


def body(
    tokens,
    routes,
    cotangent,
    norm_attn,
    w_query,
    w_key,
    w_value,
    w_out,
    norm_ffn,
    w_router,
    w_gate,
    w_up,
    w_down,
):
    count = tokens.shape[1]
    width = tokens.shape[2]
    grouping = HEADS // KV_HEADS
    kv_width = KV_HEADS * HEAD_DIM
    top_k = routes.shape[2]
    local_experts = w_gate.shape[0]
    expert_count = lax.axis_size("expert")
    all_experts = local_experts * expert_count
    capacity = (9 * count * top_k + 8 * all_experts - 1) // (8 * all_experts)
    n_slots = all_experts * capacity
    context_count = lax.axis_size("context")
    context_index = lax.axis_index("context")
    first_pos = context_index * count
    scale_factor = HEAD_DIM ** (-0.5)
    hidden = tokens[0].astype(jnp.float32)
    upstream = cotangent[0].astype(jnp.float32)
    gain_attn = norm_attn.astype(jnp.float32)
    gain_ffn = norm_ffn.astype(jnp.float32)
    scale_attn = rms_scale(hidden)
    normed_attn = (hidden * scale_attn * gain_attn).astype(jnp.bfloat16)
    query_raw = jnp.dot(normed_attn, w_query, preferred_element_type=jnp.float32)
    key_raw = jnp.dot(normed_attn, w_key, preferred_element_type=jnp.float32)
    value_raw = jnp.dot(normed_attn, w_value, preferred_element_type=jnp.float32)
    query_pos = first_pos + jnp.arange(count, dtype=jnp.int32)
    cosine, sine_table = rope_tables(query_pos)
    queries = rotate(query_raw.reshape(count, HEADS, HEAD_DIM), cosine, sine_table).astype(
        jnp.bfloat16
    )
    queries = queries.reshape(count, KV_HEADS, grouping, HEAD_DIM)
    keys_own = (
        rotate(key_raw.reshape(count, KV_HEADS, HEAD_DIM), cosine, sine_table)
        .astype(jnp.bfloat16)
        .reshape(count, kv_width)
    )
    values_own = value_raw.astype(jnp.bfloat16)
    key_all, value_all = (
        lax.all_gather(keys_own, "context", axis=0, tiled=True),
        lax.all_gather(values_own, "context", axis=0, tiled=True),
    )

    def block_scores(block_index):
        key_block = key_all[block_index * count : (block_index + 1) * count].reshape(
            count, KV_HEADS, HEAD_DIM
        )
        value_block = value_all[block_index * count : (block_index + 1) * count].reshape(
            count, KV_HEADS, HEAD_DIM
        )
        visible = (
            query_pos[:, None]
            >= (block_index * count + jnp.arange(count, dtype=jnp.int32))[None, :]
        )
        scores = scale_factor * jnp.einsum(
            "qhgd,khd->hgqk", queries, key_block, preferred_element_type=jnp.float32
        )
        return (key_block, value_block, visible, jnp.where(visible, scores, NEG_LARGE))

    run_max = jnp.full((KV_HEADS, grouping, count), NEG_LARGE, jnp.float32)
    run_sum = jnp.zeros((KV_HEADS, grouping, count), jnp.float32)
    for block_index in range(context_count):

        def update(running, block_index=block_index):
            old_max, old_sum = running
            _, _, visible, scores = block_scores(block_index)
            new_max = jnp.maximum(old_max, jnp.max(scores, -1))
            exp_block = jnp.where(visible, jnp.exp(scores - new_max[..., None]), 0.0)
            return (new_max, jnp.exp(old_max - new_max) * old_sum + jnp.sum(exp_block, -1))

        run_max, run_sum = lax.cond(
            block_index <= context_index, update, lambda unchanged: unchanged, (run_max, run_sum)
        )
    log_total = run_max + jnp.log(run_sum)
    attn_f32 = jnp.zeros((count, KV_HEADS, grouping, HEAD_DIM), jnp.float32)
    for block_index in range(context_count):

        def accumulate(previous, block_index=block_index):
            _, value_block, visible, scores = block_scores(block_index)
            prob_block = jnp.where(visible, jnp.exp(scores - log_total[..., None]), 0.0).astype(
                jnp.bfloat16
            )
            return previous + jnp.einsum(
                "hgqk,khd->qhgd", prob_block, value_block, preferred_element_type=jnp.float32
            )

        attn_f32 = lax.cond(
            block_index <= context_index, accumulate, lambda unchanged: unchanged, attn_f32
        )
    attn_low = attn_f32.reshape(count, HEADS * HEAD_DIM).astype(jnp.bfloat16)
    middle = hidden + jnp.dot(attn_low, w_out, preferred_element_type=jnp.float32)
    scale_ffn = rms_scale(middle)
    normed_ffn = (middle * scale_ffn * gain_ffn).astype(jnp.bfloat16)
    logits = jnp.dot(normed_ffn, w_router, preferred_element_type=jnp.float32)
    flat_route = routes[0].reshape(count * top_k)
    one_hot = (flat_route[:, None] == jnp.arange(all_experts, dtype=jnp.int32)[None, :]).astype(
        jnp.int32
    )
    selector = one_hot.reshape(count, top_k, all_experts).astype(jnp.float32)
    chosen = jnp.sum(selector * logits[:, None, :], -1)
    gate_probs = jax.nn.softmax(chosen, -1)
    ranking = jnp.sum((jnp.cumsum(one_hot, 0) - one_hot) * one_hot, 1)
    dest_slot = jnp.where(ranking < capacity, flat_route * capacity + ranking + 1, 0)
    pair_of_slot = (
        jnp.zeros((n_slots + 1,), jnp.int32)
        .at[dest_slot]
        .set(jnp.arange(1, count * top_k + 1, dtype=jnp.int32))[1:]
    )
    token_of_slot = jnp.where(pair_of_slot > 0, (pair_of_slot - 1) // top_k + 1, 0)
    zero_row = jnp.zeros((1, width), jnp.bfloat16)
    padded_rows = jnp.concatenate([zero_row, normed_ffn], 0)
    send_rows = padded_rows[token_of_slot].reshape(expert_count, local_experts, capacity, width)
    received = lax.all_to_all(send_rows, "expert", split_axis=0, concat_axis=0, tiled=True)
    gate_act = jnp.einsum("secd,edf->secf", received, w_gate, preferred_element_type=jnp.float32)
    up_act = jnp.einsum("secd,edf->secf", received, w_up, preferred_element_type=jnp.float32)
    hidden_act = (jax.nn.silu(gate_act) * up_act).astype(jnp.bfloat16)
    expert_out = jnp.einsum(
        "secf,efd->secd", hidden_act, w_down, preferred_element_type=jnp.float32
    ).astype(jnp.bfloat16)
    returned = lax.all_to_all(expert_out, "expert", split_axis=0, concat_axis=0, tiled=True)
    padded_out = jnp.concatenate([zero_row, returned.reshape(n_slots, width)], 0)
    picked = padded_out[dest_slot].reshape(count, top_k, width).astype(jnp.float32)
    ffn_sum = jnp.sum(gate_probs[:, :, None] * picked, 1)
    result = (middle + ffn_sum).astype(jnp.bfloat16)
    grad_gates = jnp.sum(picked * upstream[:, None, :], -1)
    grad_pairs = (
        (gate_probs[:, :, None] * upstream[:, None, :])
        .astype(jnp.bfloat16)
        .reshape(count * top_k, width)
    )
    padded_grads = jnp.concatenate([zero_row, grad_pairs], 0)
    send_grads = padded_grads[pair_of_slot].reshape(expert_count, local_experts, capacity, width)
    grad_recv = lax.all_to_all(send_grads, "expert", split_axis=0, concat_axis=0, tiled=True)
    sigmoid_gate = jax.nn.sigmoid(gate_act)
    silu_gate = gate_act * sigmoid_gate
    hidden_back = (silu_gate * up_act).astype(jnp.bfloat16)
    grad_hidden_act = jnp.einsum(
        "secd,efd->secf", grad_recv, w_down, preferred_element_type=jnp.float32
    )
    grad_down = jnp.einsum(
        "secf,secd->efd", hidden_back, grad_recv, preferred_element_type=jnp.float32
    )
    grad_gate_act = (
        grad_hidden_act * up_act * sigmoid_gate * (1.0 + gate_act * (1.0 - sigmoid_gate))
    ).astype(jnp.bfloat16)
    grad_up_act = (grad_hidden_act * silu_gate).astype(jnp.bfloat16)
    grad_gate_w = jnp.einsum(
        "secd,secf->edf", received, grad_gate_act, preferred_element_type=jnp.float32
    )
    grad_up_w = jnp.einsum(
        "secd,secf->edf", received, grad_up_act, preferred_element_type=jnp.float32
    )
    grad_rows = (
        jnp.einsum("secf,edf->secd", grad_gate_act, w_gate, preferred_element_type=jnp.float32)
        + jnp.einsum("secf,edf->secd", grad_up_act, w_up, preferred_element_type=jnp.float32)
    ).astype(jnp.bfloat16)
    grad_back = lax.all_to_all(grad_rows, "expert", split_axis=0, concat_axis=0, tiled=True)
    padded_back = jnp.concatenate([zero_row, grad_back.reshape(n_slots, width)], 0)
    grad_normed_ffn = jnp.sum(
        padded_back[dest_slot].reshape(count, top_k, width).astype(jnp.float32), 1
    )
    grad_chosen = gate_probs * (grad_gates - jnp.sum(gate_probs * grad_gates, -1, keepdims=True))
    grad_logits = jnp.sum(selector * grad_chosen[:, :, None], 1).astype(jnp.bfloat16)
    grad_normed_ffn = grad_normed_ffn + jnp.dot(
        grad_logits, w_router.T, preferred_element_type=jnp.float32
    )
    grad_router = jnp.dot(normed_ffn.T, grad_logits, preferred_element_type=jnp.float32)
    grad_gain_ffn = jnp.sum(grad_normed_ffn * middle * scale_ffn, 0)
    grad_middle = upstream + norm_back(grad_normed_ffn, middle, scale_ffn, gain_ffn)
    grad_branch = grad_middle.astype(jnp.bfloat16)
    grad_w_out = jnp.dot(attn_low.T, grad_branch, preferred_element_type=jnp.float32)
    grad_attn = jnp.dot(grad_branch, w_out.T, preferred_element_type=jnp.float32).astype(
        jnp.bfloat16
    )
    grad_attn = grad_attn.reshape(count, KV_HEADS, grouping, HEAD_DIM)
    offsets = jnp.transpose(jnp.sum(grad_attn.astype(jnp.float32) * attn_f32, -1), (1, 2, 0))
    grad_query = jnp.zeros((count, KV_HEADS, grouping, HEAD_DIM), jnp.float32)
    key_terms = []
    value_terms = []
    for block_index in range(context_count):

        def backward_block(query_accum, block_index=block_index):
            key_block, value_block, visible, scores = block_scores(block_index)
            prob_block = jnp.where(visible, jnp.exp(scores - log_total[..., None]), 0.0)
            grad_probs = jnp.einsum(
                "qhgd,khd->hgqk", grad_attn, value_block, preferred_element_type=jnp.float32
            )
            grad_scores = (prob_block * (grad_probs - offsets[..., None])).astype(jnp.bfloat16)
            new_query = query_accum + scale_factor * jnp.einsum(
                "hgqk,khd->qhgd", grad_scores, key_block, preferred_element_type=jnp.float32
            )
            key_term = scale_factor * jnp.einsum(
                "hgqk,qhgd->khd", grad_scores, queries, preferred_element_type=jnp.float32
            )
            value_term = jnp.einsum(
                "hgqk,qhgd->khd",
                prob_block.astype(jnp.bfloat16),
                grad_attn,
                preferred_element_type=jnp.float32,
            )
            return (
                new_query,
                key_term.reshape(count, kv_width),
                value_term.reshape(count, kv_width),
            )

        def skip_block(query_accum):
            empty_rows = jnp.zeros((count, kv_width), jnp.float32)
            return (query_accum, empty_rows, empty_rows)

        grad_query, key_term, value_term = lax.cond(
            block_index <= context_index, backward_block, skip_block, grad_query
        )
        key_terms.append(key_term)
        value_terms.append(value_term)
    key_sum, value_sum = (
        lax.psum_scatter(
            jnp.concatenate(key_terms, 0).astype(jnp.bfloat16),
            "context",
            scatter_dimension=0,
            tiled=True,
        ).astype(jnp.float32),
        lax.psum_scatter(
            jnp.concatenate(value_terms, 0).astype(jnp.bfloat16),
            "context",
            scatter_dimension=0,
            tiled=True,
        ).astype(jnp.float32),
    )
    grad_query_raw = (
        rotate_back(grad_query.reshape(count, HEADS, HEAD_DIM), cosine, sine_table)
        .reshape(count, HEADS * HEAD_DIM)
        .astype(jnp.bfloat16)
    )
    grad_key_raw = (
        rotate_back(key_sum.reshape(count, KV_HEADS, HEAD_DIM), cosine, sine_table)
        .reshape(count, kv_width)
        .astype(jnp.bfloat16)
    )
    grad_value_raw = value_sum.astype(jnp.bfloat16)
    grad_w_query = jnp.dot(normed_attn.T, grad_query_raw, preferred_element_type=jnp.float32)
    grad_w_key = jnp.dot(normed_attn.T, grad_key_raw, preferred_element_type=jnp.float32)
    grad_w_value = jnp.dot(normed_attn.T, grad_value_raw, preferred_element_type=jnp.float32)
    grad_normed_attn = (
        jnp.dot(grad_query_raw, w_query.T, preferred_element_type=jnp.float32)
        + jnp.dot(grad_key_raw, w_key.T, preferred_element_type=jnp.float32)
        + jnp.dot(grad_value_raw, w_value.T, preferred_element_type=jnp.float32)
    )
    grad_gain_attn = jnp.sum(grad_normed_attn * hidden * scale_attn, 0)
    grad_hidden = grad_middle + norm_back(grad_normed_attn, hidden, scale_attn, gain_attn)
    dense_sums = (
        lax.psum_scatter(
            grad_gain_attn, ("expert", "context", "dp"), scatter_dimension=0, tiled=True
        ),
        lax.psum_scatter(
            grad_w_query, ("expert", "context", "dp"), scatter_dimension=0, tiled=True
        ),
        lax.psum_scatter(grad_w_key, ("expert", "context", "dp"), scatter_dimension=0, tiled=True),
        lax.psum_scatter(
            grad_w_value, ("expert", "context", "dp"), scatter_dimension=0, tiled=True
        ),
        lax.psum_scatter(grad_w_out, ("expert", "context", "dp"), scatter_dimension=0, tiled=True),
        lax.psum_scatter(
            grad_gain_ffn, ("expert", "context", "dp"), scatter_dimension=0, tiled=True
        ),
        lax.psum_scatter(grad_router, ("expert", "context", "dp"), scatter_dimension=0, tiled=True),
    )
    expert_sums = (
        lax.psum_scatter(
            grad_gate_w.astype(jnp.bfloat16), ("context", "dp"), scatter_dimension=1, tiled=True
        ).astype(jnp.float32),
        lax.psum_scatter(
            grad_up_w.astype(jnp.bfloat16), ("context", "dp"), scatter_dimension=1, tiled=True
        ).astype(jnp.float32),
        lax.psum_scatter(
            grad_down.astype(jnp.bfloat16), ("context", "dp"), scatter_dimension=1, tiled=True
        ).astype(jnp.float32),
    )
    return (
        result[None],
        grad_hidden.astype(jnp.bfloat16)[None],
        dense_sums[0],
        dense_sums[1],
        dense_sums[2],
        dense_sums[3],
        dense_sums[4],
        dense_sums[5],
        dense_sums[6],
        expert_sums[0],
        expert_sums[1],
        expert_sums[2],
    )


def solution(mesh):
    return jax.shard_map(
        body,
        mesh=mesh,
        in_specs=(
            P(("expert", "dp"), "context", None),
            P(("expert", "dp"), "context", None),
            P(("expert", "dp"), "context", None),
            P(),
            P(),
            P(),
            P(),
            P(),
            P(),
            P(),
            P("expert", None, None),
            P("expert", None, None),
            P("expert", None, None),
        ),
        out_specs=(
            P(("expert", "dp"), "context", None),
            P(("expert", "dp"), "context", None),
            P(("expert", "context", "dp")),
            P(("expert", "context", "dp"), None),
            P(("expert", "context", "dp"), None),
            P(("expert", "context", "dp"), None),
            P(("expert", "context", "dp"), None),
            P(("expert", "context", "dp")),
            P(("expert", "context", "dp"), None),
            P("expert", ("context", "dp"), None),
            P("expert", ("context", "dp"), None),
            P("expert", ("context", "dp"), None),
        ),
        check_vma=False,
    )
```

profile of v0, /device:TPU:0, one launch (start us, length us, event | category | flops | bytes accessed | tf_op | source)
XLA Modules:
  0.0 1717.6 jit_solution(11164186134340201541)
XLA Ops:
  55.9 21.3 %all-gather.5.cloned.1.call-done = bf16[1024,512]{1,0:T(8,128)(2,1)} async-done(((bf16[256,512]{1,0:T(8,128)(2,1)}), bf16[1024,512]{1,0:T(8,128)(2,1)}) %all-gather.5.cloned.1.call-update) | async-done | bytes 1048592 | tf_op jit(solution)/shard_map/all_gather | solution.py:98
  127.7 19.7 %gather_fusion.2 = bf16[2320,1536]{1,0:T(8,128)(2,1)} fusion(bf16[2049,1536]{1,0:T(8,128)(2,1)} %concatenate.52, s32[3072]{0:T(1024)S(1)} %get-tuple-element.640), kind=kCustom, calls=%fused_computation.2 | custom fusion | bytes 14263360 | tf_op jit(solution)/shard_map/gather | solution.py:189
  147.4 9.8 reshape.567
  157.2 43.4 %all-to-all-done = bf16[4,5,116,1536]{3,2,1,0:T(8,128)(2,1)} async-done(((bf16[4,5,116,1536]{3,2,1,0:T(8,128)(2,1)}), bf16[4,5,116,1536]{3,2,1,0:T(8,128)(2,1)}, u32[]{:S(2)}, u32[]{:S(2)}) %all-to-all-start) | async-done | bytes 7127072 | tf_op jit(solution)/shard_map/all_to_all | solution.py:170
  206.4 11.6 fusion.146
  218.0 11.5 fusion.150
  229.5 59.2 %all-to-all-done.2 = bf16[4,5,116,1536]{3,2,1,0:T(8,128)(2,1)} async-done(((bf16[4,5,116,1536]{3,2,1,0:T(8,128)(2,1)}), bf16[4,5,116,1536]{3,2,1,0:T(8,128)(2,1)}, u32[]{:S(2)}, u32[]{:S(2)}) %all-to-all-start.2) | async-done | bytes 7127072 | tf_op jit(solution)/shard_map/all_to_all | solution.py:190
  288.7 13.1 fusion.167
  318.9 13.3 fusion.144
  332.2 11.7 fusion.156
  350.5 50.7 %all-to-all-done.1 = bf16[4,5,116,1536]{3,2,1,0:T(8,128)(2,1)} async-done(((bf16[4,5,116,1536]{3,2,1,0:T(8,128)(2,1)}), bf16[4,5,116,1536]{3,2,1,0:T(8,128)(2,1)}, u32[]{:S(2)}, u32[]{:S(2)}) %all-to-all-start.1) | async-done | bytes 7127072 | tf_op jit(solution)/shard_map/all_to_all | solution.py:177
  406.7 9.7 reshape.566
  424.2 17.3 %gather_fusion.1 = bf16[2048,1536]{1,0:T(8,128)(2,1)} fusion(bf16[2321,1536]{1,0:T(8,128)(2,1)} %concatenate.51, s32[2048]{0:T(1024)S(1)} %broadcast_clamp_fusion), kind=kCustom, calls=%fused_computation.1 | custom fusion | bytes 12591104 | tf_op jit(solution)/shard_map/gather | solution.py:179
  441.5 9.7 fusion.142
  451.4 37.6 %all-to-all-done.3 = bf16[4,5,116,1536]{3,2,1,0:T(8,128)(2,1)} async-done(((bf16[4,5,116,1536]{3,2,1,0:T(8,128)(2,1)}), bf16[4,5,116,1536]{3,2,1,0:T(8,128)(2,1)}, u32[]{:S(2)}, u32[]{:S(2)}) %all-to-all-start.3) | async-done | bytes 7127072 | tf_op jit(solution)/shard_map/all_to_all | solution.py:214
  488.9 9.8 reshape.568
  506.4 17.6 %gather_fusion.3 = bf16[2048,1536]{1,0:T(8,128)(2,1)} fusion(bf16[2321,1536]{1,0:T(8,128)(2,1)} %concatenate.53, s32[2048]{0:T(1024)S(1)} %broadcast_clamp_fusion), kind=kCustom, calls=%fused_computation.3 | custom fusion | bytes 12591104 | tf_op jit(solution)/shard_map/gather | solution.py:217
  541.8 13.3 conditional.20
  566.1 11.2 bitcast_convert_fusion
  577.6 11.3 bitcast_convert_fusion.1
  589.0 11.3 bitcast_convert_fusion.2
  600.4 56.7 %reduce-scatter.15.cloned.1.call-done = bf16[256,512]{0,1:T(8,128)(2,1)} async-done(((bf16[1024,512]{0,1:T(8,128)(2,1)}), bf16[256,512]{0,1:T(8,128)(2,1)}) %reduce-scatter.15.cloned.1.call-update) | async-done | bytes 262160 | tf_op jit(solution)/shard_map/reduce_scatter | solution.py:280
  660.6 25.2 %reduce-scatter.13.cloned.1.call-done = bf16[256,512]{0,1:T(8,128)(2,1)} async-done(((bf16[1024,512]{0,1:T(8,128)(2,1)}), bf16[256,512]{0,1:T(8,128)(2,1)}) %reduce-scatter.13.cloned.1.call-update) | async-done | bytes 262160 | tf_op jit(solution)/shard_map/reduce_scatter | solution.py:274
  714.0 71.4 %reduce-scatter.31.cloned.1.call-done = f32[48,20]{1,0:T(8,128)} async-done(((f32[1536,20]{1,0:T(8,128)}), f32[48,20]{1,0:T(8,128)}) %reduce-scatter.31.cloned.1.call-update) | async-done | bytes 3856
  791.4 43.3 %all-reduce.6 = (f32[1536]{0:T(1024)S(1)}, f32[1536]{0:T(1024)S(1)}) all-reduce(f32[1536]{0:T(1024)S(1)} %get-tuple-element.601, f32[1536]{0:T(1024)S(1)} %copy-done.41), channel_id=4, replica_groups=mesh['expert'=4,'context'=4,'dp'=2] {'expert','context','dp'}, use_global_device_ids=true, to_apply=%region_52.53.clone | all-reduce | flops 3072 | bytes 24576
  839.2 89.9 %reduce-scatter.29.cloned.1.call-done = bf16[5,64,1536]{2,1,0:T(8,128)(2,1)} async-done(((bf16[5,512,1536]{2,1,0:T(8,128)(2,1)}), bf16[5,64,1536]{2,1,0:T(8,128)(2,1)}) %reduce-scatter.29.cloned.1.call-update) | async-done | bytes 983056 | tf_op jit(solution)/shard_map/reduce_scatter | solution.py:332
  931.8 140.1 %reduce-scatter.27.cloned.1.call-done = bf16[5,192,512]{2,1,0:T(8,128)(2,1)} async-done(((bf16[5,1536,512]{2,1,0:T(8,128)(2,1)}), bf16[5,192,512]{2,1,0:T(8,128)(2,1)}) %reduce-scatter.27.cloned.1.call-update) | async-done | bytes 983056 | tf_op jit(solution)/shard_map/reduce_scatter | solution.py:329
  1074.6 140.0 %reduce-scatter.25.cloned.1.call-done = bf16[5,192,512]{2,1,0:T(8,128)(2,1)} async-done(((bf16[5,1536,512]{2,1,0:T(8,128)(2,1)}), bf16[5,192,512]{2,1,0:T(8,128)(2,1)}) %reduce-scatter.25.cloned.1.call-update) | async-done | bytes 983056 | tf_op jit(solution)/shard_map/reduce_scatter | solution.py:326
  1217.4 103.8 %reduce-scatter.21.cloned.1.call-done = f32[48,512]{1,0:T(8,128)} async-done(((f32[1536,512]{1,0:T(8,128)}), f32[48,512]{1,0:T(8,128)}) %reduce-scatter.21.cloned.1.call-update) | async-done | bytes 98320 | tf_op jit(solution)/shard_map/reduce_scatter | solution.py:316
  1321.2 106.3 %reduce-scatter.19.cloned.1.call-done = f32[48,512]{1,0:T(8,128)} async-done(((f32[1536,512]{1,0:T(8,128)}), f32[48,512]{1,0:T(8,128)}) %reduce-scatter.19.cloned.1.call-update) | async-done | bytes 98320 | tf_op jit(solution)/shard_map/reduce_scatter | solution.py:315
  1427.5 141.1 %reduce-scatter.23.cloned.1.call-done = f32[48,1536]{1,0:T(8,128)} async-done(((f32[1536,1536]{1,0:T(8,128)}), f32[48,1536]{1,0:T(8,128)}) %reduce-scatter.23.cloned.1.call-update) | async-done | bytes 294928 | tf_op jit(solution)/shard_map/reduce_scatter | solution.py:319
  1568.6 142.0 %reduce-scatter.17.cloned.1.call-done = f32[48,1536]{1,0:T(8,128)} async-done(((f32[1536,1536]{1,0:T(8,128)}), f32[48,1536]{1,0:T(8,128)}) %reduce-scatter.17.cloned.1.call-update) | async-done | bytes 294928 | tf_op jit(solution)/shard_map/reduce_scatter | solution.py:312
  (261 shorter events, 260.0 us)
Async XLA Ops:
  7.2 42.6 %all-gather.3.cloned.1.call-start = ((), (), s32[]{:S(2)}) async-start(), calls=%async_computation.14 | async-start | bytes 1310720 | tf_op jit(solution)/shard_map/all_gather | solution.py:97
  9.3 30.3 %copy-start.39 = (f32[256]{0:T(256)}, f32[256]{0:T(256)S(1)}, u32[]{:S(2)}) copy-start(f32[256]{0:T(256)S(1)} %get-tuple-element.633) | copy-start | bytes 3076
  10.0 29.6 %copy-start.30 = (f32[1536]{0:T(1024)}, f32[1536]{0:T(1024)S(1)}, u32[]{:S(2)}) copy-start(f32[1536]{0:T(1024)S(1)} %convert_element_type.246) | copy-start | bytes 18436
  10.2 33.5 %copy-start.21 = (f32[256,64]{0,1:T(8,128)}, f32[256,64]{0,1:T(8,128)S(1)}, u32[]{:S(2)}) copy-start(f32[256,64]{0,1:T(8,128)S(1)} %get-tuple-element.628) | copy-start | bytes 196612
  10.2 33.5 %copy-start.27 = (f32[256,64]{0,1:T(8,128)}, f32[256,64]{0,1:T(8,128)S(1)}, u32[]{:S(2)}) copy-start(f32[256,64]{0,1:T(8,128)S(1)} %get-tuple-element.629) | copy-start | bytes 196612
  16.1 61.1 %all-gather.5.cloned.1.call-start = ((), (), s32[]{:S(2)}) async-start(), calls=%async_computation.15 | async-start | bytes 1310720 | tf_op jit(solution)/shard_map/all_gather | solution.py:98
  17.6 69.0 %copy-start.34 = (s32[256]{0:T(256)}, s32[256]{0:T(256)S(1)}, u32[]{:S(2)}) copy-start(s32[256]{0:T(256)S(1)} %iota_add_fusion.10) | copy-start | bytes 3076
  18.0 74.9 %copy-start.37 = (f32[1536]{0:T(1024)}, f32[1536]{0:T(1024)S(1)}, u32[]{:S(2)}) copy-start(f32[1536]{0:T(1024)S(1)} %convert_element_type.258) | copy-start | bytes 18436
  44.1 42.5 %copy-start.1 = (bf16[256,24,64]{0,2,1:T(8,128)(2,1)}, bf16[256,24,64]{0,2,1:T(8,128)(2,1)S(1)}, u32[]{:S(2)}) copy-start(bf16[256,24,64]{0,2,1:T(8,128)(2,1)S(1)} %fusion.194) | copy-start | bytes 2359300
  55.9 30.7 %copy-start.42 = (f32[8,3,256]{2,1,0:T(4,128)}, f32[8,3,256]{2,1,0:T(4,128)S(1)}, u32[]{:S(2)}) copy-start(f32[8,3,256]{2,1,0:T(4,128)S(1)} %log_add_fusion) | copy-start | bytes 73732
  112.7 87.8 %all-to-all-start = ((bf16[4,5,116,1536]{3,2,1,0:T(8,128)(2,1)}), bf16[4,5,116,1536]{3,2,1,0:T(8,128)(2,1)}, u32[]{:S(2)}, u32[]{:S(2)}) async-start(bf16[4,5,116,1536]{3,2,1,0:T(8,128)(2,1)} %reshape.565), calls=%async_computation | async-start | bytes 14745600 | tf_op jit(solution)/shard_map/all_to_all | solution.py:170
  200.5 88.2 %all-to-all-start.2 = ((bf16[4,5,116,1536]{3,2,1,0:T(8,128)(2,1)}), bf16[4,5,116,1536]{3,2,1,0:T(8,128)(2,1)}, u32[]{:S(2)}, u32[]{:S(2)}) async-start(bf16[4,5,116,1536]{3,2,1,0:T(8,128)(2,1)} %reshape.567), calls=%async_computation.2 | async-start | bytes 14745600 | tf_op jit(solution)/shard_map/all_to_all | solution.py:190
  313.3 87.9 %all-to-all-start.1 = ((bf16[4,5,116,1536]{3,2,1,0:T(8,128)(2,1)}), bf16[4,5,116,1536]{3,2,1,0:T(8,128)(2,1)}, u32[]{:S(2)}, u32[]{:S(2)}) async-start(bf16[4,5,116,1536]{3,2,1,0:T(8,128)(2,1)} %copy.214), calls=%async_computation.1 | async-start | bytes 14745600 | tf_op jit(solution)/shard_map/all_to_all | solution.py:177
  350.5 56.2 %copy-start.48 = (s32[2048,1]{0,1:T(1,128)S(1)}, s32[2048,1]{0,1:T(1,128)}, u32[]{:S(2)}) copy-start(s32[2048,1]{0,1:T(1,128)} %copy-done.47) | copy-start | bytes 24580
  401.2 87.7 %all-to-all-start.3 = ((bf16[4,5,116,1536]{3,2,1,0:T(8,128)(2,1)}), bf16[4,5,116,1536]{3,2,1,0:T(8,128)(2,1)}, u32[]{:S(2)}, u32[]{:S(2)}) async-start(bf16[4,5,116,1536]{3,2,1,0:T(8,128)(2,1)} %copy.217), calls=%async_computation.3 | async-start | bytes 14745600 | tf_op jit(solution)/shard_map/all_to_all | solution.py:214
  406.7 250.5 %reduce-scatter.15.cloned.1.call-start = ((), (), s32[]{:S(2)}) async-start(), calls=%async_computation.17 | async-start | bytes 1310720 | tf_op jit(solution)/shard_map/reduce_scatter | solution.py:280
  562.3 123.5 %reduce-scatter.13.cloned.1.call-start = ((), (), s32[]{:S(2)}) async-start(), calls=%async_computation.16 | async-start | bytes 1310720 | tf_op jit(solution)/shard_map/reduce_scatter | solution.py:274
  564.7 220.8 %reduce-scatter.31.cloned.1.call-start = ((), (), s32[]{:S(2)}) async-start(), calls=%async_computation.25 | async-start | bytes 811008
  566.1 363.0 %reduce-scatter.29.cloned.1.call-start = ((), (), s32[]{:S(2)}) async-start(), calls=%async_computation.24 | async-start | bytes 8847360 | tf_op jit(solution)/shard_map/reduce_scatter | solution.py:332
  577.4 494.5 %reduce-scatter.27.cloned.1.call-start = ((), (), s32[]{:S(2)}) async-start(), calls=%async_computation.23 | async-start | bytes 8847360 | tf_op jit(solution)/shard_map/reduce_scatter | solution.py:329
  588.9 625.7 %reduce-scatter.25.cloned.1.call-start = ((), (), s32[]{:S(2)}) async-start(), calls=%async_computation.22 | async-start | bytes 8847360 | tf_op jit(solution)/shard_map/reduce_scatter | solution.py:326
  600.3 56.9 %copy-start.5 = (bf16[1,256,1536]{2,1,0:T(8,128)(2,1)S(1)}, bf16[1,256,1536]{2,1,0:T(8,128)(2,1)}, u32[]{:S(2)}) copy-start(bf16[1,256,1536]{2,1,0:T(8,128)(2,1)} %param.37) | copy-start | bytes 2359300
  600.3 56.9 %copy-start.31 = (f32[1536]{0:T(1024)S(1)}, f32[1536]{0:T(1024)}, u32[]{:S(2)}) copy-start(f32[1536]{0:T(1024)} %copy-done.30) | copy-start | bytes 18436
  600.3 56.9 %copy-start.40 = (f32[256]{0:T(256)S(1)}, f32[256]{0:T(256)}, u32[]{:S(2)}) copy-start(f32[256]{0:T(256)} %copy-done.39) | copy-start | bytes 3076
  600.3 85.5 %copy-start.28 = (f32[256,64]{0,1:T(8,128)S(1)}, f32[256,64]{0,1:T(8,128)}, u32[]{:S(2)}) copy-start(f32[256,64]{0,1:T(8,128)} %copy-done.27) | copy-start | bytes 196612
  600.3 86.6 %copy-start.22 = (f32[256,64]{0,1:T(8,128)S(1)}, f32[256,64]{0,1:T(8,128)}, u32[]{:S(2)}) copy-start(f32[256,64]{0,1:T(8,128)} %copy-done.21) | copy-start | bytes 196612
  600.3 720.9 %reduce-scatter.21.cloned.1.call-start = ((), (), s32[]{:S(2)}) async-start(), calls=%async_computation.20 | async-start | bytes 3244032 | tf_op jit(solution)/shard_map/reduce_scatter | solution.py:316
  660.5 767.0 %reduce-scatter.19.cloned.1.call-start = ((), (), s32[]{:S(2)}) async-start(), calls=%async_computation.19 | async-start | bytes 3244032 | tf_op jit(solution)/shard_map/reduce_scatter | solution.py:315
  690.4 878.2 %reduce-scatter.23.cloned.1.call-start = ((), (), s32[]{:S(2)}) async-start(), calls=%async_computation.21 | async-start | bytes 9732096 | tf_op jit(solution)/shard_map/reduce_scatter | solution.py:319
  696.9 1013.7 %reduce-scatter.17.cloned.1.call-start = ((), (), s32[]{:S(2)}) async-start(), calls=%async_computation.18 | async-start | bytes 9732096 | tf_op jit(solution)/shard_map/reduce_scatter | solution.py:312
  709.0 80.4 %copy-start.29 = (bf16[256,512]{0,1:T(8,128)(2,1)S(1)}, bf16[256,512]{0,1:T(8,128)(2,1)}, u32[]{:S(2)}) copy-start(bf16[256,512]{0,1:T(8,128)(2,1)} %reduce-scatter.15.cloned.1.call-done) | copy-start | bytes 786436
  786.9 49.1 %copy-start.51 = (f32[256]{0:T(256)S(1)}, f32[256]{0:T(256)}, u32[]{:S(2)}) copy-start(f32[256]{0:T(256)} %get-tuple-element.632) | copy-start | bytes 3076
  (32 other events, 209.8 us)
Sparse Core Ops, SparseCore 0:
  16.3 33.5 all-gather.2
  52.0 25.1 all-gather.4
  562.4 94.6 reduce-scatter.14
  660.0 25.7 reduce-scatter.12
  691.3 94.1 reduce-scatter.30
  788.9 140.1 reduce-scatter.28
  932.7 139.0 reduce-scatter.26
  1075.5 139.0 reduce-scatter.24
  1220.6 100.5 reduce-scatter.20
  1327.0 100.3 reduce-scatter.18
  1434.0 134.5 reduce-scatter.22
  1575.9 134.6 reduce-scatter.16
where the time goes:
time: 1730 us; the launch traced here: 1720 us
  waiting for transfers between devices  1230 us (71%)
  local copies, waits for them, and re-layouts  171 us (10%)
  matrix products  162 us (9%)
  other arithmetic  66.6 us (4%)
  blocking collectives  43.3 us (3%)
  starting transfers between devices  23.4 us (1%)
    reduce_scatter x1, waiting for transfers between devices, body(): lax.psum_scatter(grad_w_query, ('expert', 'context', 'dp'), scatter_dimen...  142 us
    reduce_scatter x1, waiting for transfers between devices, body(): lax.psum_scatter(grad_w_out, ('expert', 'context', 'dp'), scatter_dimensi...  141 us
    reduce_scatter x1, waiting for transfers between devices, body(): lax.psum_scatter(grad_up_w.astype(jnp.bfloat16), ('context', 'dp'), scatt...  140 us
    reduce_scatter x1, waiting for transfers between devices, body(): lax.psum_scatter(grad_gate_w.astype(jnp.bfloat16), ('context', 'dp'), sca...  140 us
    reduce_scatter x1, waiting for transfers between devices, body(): lax.psum_scatter(grad_w_key, ('expert', 'context', 'dp'), scatter_dimensi...  106 us
    reduce_scatter x1, waiting for transfers between devices, body(): lax.psum_scatter(grad_w_value, ('expert', 'context', 'dp'), scatter_dimen...  104 us
    reduce_scatter x1, waiting for transfers between devices, body(): lax.psum_scatter(grad_down.astype(jnp.bfloat16), ('context', 'dp'), scatt...  89.9 us
    unnamed x13, waiting for transfers between devices  71.6 us
  transfers between devices with their start and end apart: 16, of which 16 were waited for; matrix products, arithmetic and copies ran while one was open for 15% of the time, Pallas kernels for 0%

commit v1 on v0

v1 whole, which is shorter than its diff:
```python
import functools

import jax
import jax.numpy as jnp
from jax import lax
from jax.experimental import pallas as pl
from jax.experimental.pallas import tpu as pltpu
from jax.sharding import PartitionSpec as P

HEADS = 24
KV_HEADS = 8
HEAD_DIM = 64
GROUP = HEADS // KV_HEADS


EPS = 1e-05
ROPE_BASE = 10000.0
NEG_LARGE = -1e30
F32 = jnp.float32
BF16 = jnp.bfloat16
LANES = 128


def rms_scale(values):
    return lax.rsqrt(jnp.mean(values * values, 0, keepdims=True) + EPS)


def norm_back(grad_out, values, scale, gain):
    weighted = gain * grad_out
    return scale * weighted - values * scale**3 * jnp.mean(weighted * values, 0, keepdims=True)


def mm(a, b, da, db):
    return lax.dot_general(a, b, (((da,), (db,)), ((), ())), preferred_element_type=F32)


class Comm:
    def __init__(self):
        self.n_expert = lax.axis_size("expert")
        self.n_context = lax.axis_size("context")
        self.n_dp = lax.axis_size("dp")
        self.cores = 2 if self.n_expert % 2 == 0 else 1
        self.columns = self.n_expert // self.cores
        self.share = 2 if self.n_context % 2 == 0 else 1

    def peer(self, i, k, j):
        column, core = divmod(i, self.cores)
        return ((column + k) % self.columns) * self.cores + (core + j) % self.cores

    def pull(self, value, k, j):
        pairs = [(self.peer(i, k, j), i) for i in range(self.n_expert)]
        return lax.ppermute(value, "expert", pairs)

    def push(self, value, k, j):
        pairs = [(i, self.peer(i, k, j)) for i in range(self.n_expert)]
        return lax.ppermute(value, "expert", pairs)

    def pair(self, value):
        return lax.ppermute(value, "context", [(i, i ^ 1) for i in range(self.n_context)])

    def gather_expert(self, value):
        row = [value] + [self.pull(value, k, 0) for k in range(1, self.columns)]
        row = jnp.concatenate(row, 1)
        if self.cores == 2:
            row = jnp.concatenate([row, self.pull(row, 0, 1)], 1)
        return row

    def gather_group(self, value):
        if self.share == 1:
            return self.gather_expert(value)
        half = value.shape[0] // 2
        column_blocks = [self.pull(value, k, 0) for k in range(1, self.columns)]
        across = self.pair(value)
        far = []
        for k in range(1, self.columns):
            top = self.pull(across[:half], k, 0)
            bottom = self.pair(column_blocks[k - 1][half:])
            far.append(jnp.concatenate([top, bottom]))
        row = jnp.concatenate([value] + column_blocks + [across] + far, 1)
        if self.cores == 2:
            row = jnp.concatenate([row, self.pull(row, 0, 1)], 1)
        return row

    def return_near(self, parts):
        n = parts.shape[0]
        if self.cores == 1:
            return parts
        other = self.push(parts[n // 2 :], 0, 1)
        return (parts[: n // 2].astype(F32) + other.astype(F32)).astype(BF16)

    def return_far(self, near):
        columns = self.columns
        if self.share == 1:
            total = near[0].astype(F32)
            for k in range(1, columns):
                total = total + self.push(near[k], k, 0).astype(F32)
            return total
        half = near.shape[1] // 2
        near = near.reshape((2, columns) + near.shape[1:])
        top = near[:, 0, :half].astype(F32)
        for k in range(1, columns):
            top = top + self.push(near[:, k, :half], k, 0).astype(F32)
        bottom = near[0, :, half:].astype(F32) + self.pair(near[1, :, half:]).astype(F32)
        top = top[0] + self.pair(top[1].astype(BF16)).astype(F32)
        bottom_low = bottom.astype(BF16)
        bottom = bottom[0]
        for k in range(1, columns):
            bottom = bottom + self.push(bottom_low[k], k, 0).astype(F32)
        return jnp.concatenate([top, bottom])

    def scatter_dp(self, parts):
        me = lax.axis_index("dp")
        n = self.n_dp
        total = lax.dynamic_index_in_dim(parts, me, 0, False).astype(F32)
        for s in range(1, n):
            send = lax.dynamic_index_in_dim(parts, (me + s) % n, 0, False).astype(BF16)
            pairs = [(i, (i + s) % n) for i in range(n)]
            total = total + lax.ppermute(send, "dp", pairs).astype(F32)
        return total

    def scatter_context(self, parts, stride):
        n = self.n_context // stride
        me = lax.axis_index("context") // stride
        total = lax.dynamic_index_in_dim(parts, me, 0, False).astype(F32)
        for s in range(1, n):
            send = lax.dynamic_index_in_dim(parts, (me + s) % n, 0, False).astype(BF16)
            pairs = []
            for i in range(self.n_context):
                k, r = divmod(i, stride)
                pairs.append((i, ((k + s) % n) * stride + r))
            total = total + lax.ppermute(send, "context", pairs).astype(F32)
        return total


def attn_fwd_kernel(blocks, c_ref, q_ref, *refs):
    k_refs, v_refs = refs[:blocks], refs[blocks : 2 * blocks]
    o_ref, ob_ref, lse_ref, scores_ref = refs[2 * blocks :]
    c = c_ref[0]
    n = q_ref.shape[1]
    hd = HEAD_DIM
    for s in range(blocks):
        rows = slice(s * n, (s + 1) * n)

        def fill(s=s, rows=rows):
            for g in range(GROUP):
                scores = mm(k_refs[s][...], q_ref[g * hd : (g + 1) * hd, :], 0, 0)
                if s == 0:
                    key = lax.broadcasted_iota(jnp.int32, scores.shape, 0)
                    query = lax.broadcasted_iota(jnp.int32, scores.shape, 1)
                    scores = jnp.where(key <= query, scores, NEG_LARGE)
                scores_ref[g, rows, :] = scores

        def blank(rows=rows):
            for g in range(GROUP):
                scores_ref[g, rows, :] = jnp.full((n, n), NEG_LARGE, F32)

        if s == 0:
            fill()
        else:
            pl.when(c >= s)(fill)
            pl.when(c < s)(blank)
    lse_ref[...] = jnp.zeros_like(lse_ref)
    for g in range(GROUP):
        scores = scores_ref[g]
        top = jnp.max(scores, 0, keepdims=True)
        weights = jnp.exp(scores - top)
        total = jnp.sum(weights, 0, keepdims=True)
        weights = weights.astype(BF16)
        out = jnp.zeros((hd, n), F32)
        for s in range(blocks):
            out = out + mm(v_refs[s][...], weights[s * n : (s + 1) * n], 1, 0)
        out = out / total
        o_ref[g * hd : (g + 1) * hd, :] = out
        ob_ref[g * hd : (g + 1) * hd, :] = out.astype(BF16)
        lse_ref[0, g : g + 1, :] = top + jnp.log(total)


def kv_specs(blocks, n):
    keys = [pl.BlockSpec((HEAD_DIM, n), lambda h, c: (h, 0))] * blocks
    values = [pl.BlockSpec((HEAD_DIM, n), lambda h, c: (h + KV_HEADS, 0))] * blocks
    return keys + values


def attention_forward(context_index, query_t, kv_blocks):
    blocks = len(kv_blocks)
    n = query_t.shape[1]
    wide = GROUP * HEAD_DIM
    head = pl.BlockSpec((wide, n), lambda h, c: (h, 0))
    return pl.pallas_call(
        functools.partial(attn_fwd_kernel, blocks),
        out_shape=(
            jax.ShapeDtypeStruct(query_t.shape, F32),
            jax.ShapeDtypeStruct(query_t.shape, BF16),
            jax.ShapeDtypeStruct((KV_HEADS, 8, n), F32),
        ),
        grid_spec=pltpu.PrefetchScalarGridSpec(
            num_scalar_prefetch=1,
            grid=(KV_HEADS,),
            in_specs=[head] + kv_specs(blocks, n),
            out_specs=(head, head, pl.BlockSpec((1, 8, n), lambda h, c: (h, 0, 0))),
            scratch_shapes=[pltpu.VMEM((GROUP, blocks * n, n), F32)],
        ),
        compiler_params=pltpu.CompilerParams(vmem_limit_bytes=40 << 20),
        cost_estimate=pl.CostEstimate(
            flops=HEADS * blocks * n * n * 256 * 4,
            transcendentals=HEADS * blocks * n * n,
            bytes_accessed=16 * query_t.size,
        ),
        name="attn_fwd",
    )(context_index.reshape(1), query_t, *kv_blocks, *kv_blocks)


def attn_bwd_kernel(blocks, c_ref, q_ref, do_ref, o_ref, lse_ref, *refs):
    k_refs, v_refs = refs[:blocks], refs[blocks : 2 * blocks]
    dq_ref, dkv_ref = refs[2 * blocks :]
    c = c_ref[0]
    n = q_ref.shape[1]
    hd = HEAD_DIM
    deltas = []
    for g in range(GROUP):
        head = slice(g * hd, (g + 1) * hd)
        both = do_ref[head, :].astype(F32) * o_ref[head, :]
        deltas.append(jnp.sum(both, 0, keepdims=True))
    for s in range(blocks):

        def work(s=s):
            dk = jnp.zeros((hd, n), F32)
            dv = jnp.zeros((hd, n), F32)
            key_t = k_refs[s][...]
            value_t = v_refs[s][...]
            for g in range(GROUP):
                head = slice(g * hd, (g + 1) * hd)
                query, grad = q_ref[head, :], do_ref[head, :]
                scores = mm(key_t, query, 0, 0)
                weights = jnp.exp(scores - lse_ref[0, g : g + 1, :])
                if s == 0:
                    key = lax.broadcasted_iota(jnp.int32, scores.shape, 0)
                    place = lax.broadcasted_iota(jnp.int32, scores.shape, 1)
                    weights = jnp.where(key <= place, weights, 0.0)
                grad_weights = mm(value_t, grad, 0, 0)
                grad_scores = (weights * (grad_weights - deltas[g])).astype(BF16)
                dv = dv + mm(grad, weights.astype(BF16), 1, 1)
                dk = dk + mm(query, grad_scores, 1, 1)
                step = mm(key_t, grad_scores, 1, 0) * (HEAD_DIM**-0.5)
                if s == 0:
                    dq_ref[head, :] = step
                else:
                    dq_ref[head, :] += step
            dkv_ref[s, 0] = dk.astype(BF16)
            dkv_ref[s, 1] = dv.astype(BF16)

        def skip(s=s):
            dkv_ref[s] = jnp.zeros(dkv_ref.shape[1:], BF16)

        if s == 0:
            work()
        else:
            pl.when(c >= s)(work)
            pl.when(c < s)(skip)


def attention_backward(context_index, query_t, grad_t, out_t, lse, kv_blocks):
    blocks = len(kv_blocks)
    n = query_t.shape[1]
    wide = GROUP * HEAD_DIM
    head = pl.BlockSpec((wide, n), lambda h, c: (h, 0))
    return pl.pallas_call(
        functools.partial(attn_bwd_kernel, blocks),
        out_shape=(
            jax.ShapeDtypeStruct(query_t.shape, F32),
            jax.ShapeDtypeStruct((blocks, 2, KV_HEADS * HEAD_DIM, n), BF16),
        ),
        grid_spec=pltpu.PrefetchScalarGridSpec(
            num_scalar_prefetch=1,
            grid=(KV_HEADS,),
            in_specs=[head, head, head, pl.BlockSpec((1, 8, n), lambda h, c: (h, 0, 0))]
            + kv_specs(blocks, n),
            out_specs=(
                head,
                pl.BlockSpec((blocks, 2, HEAD_DIM, n), lambda h, c: (0, 0, h, 0)),
            ),
        ),
        compiler_params=pltpu.CompilerParams(vmem_limit_bytes=40 << 20),
        cost_estimate=pl.CostEstimate(
            flops=HEADS * blocks * n * n * 256 * 10,
            transcendentals=HEADS * blocks * n * n,
            bytes_accessed=20 * query_t.size,
        ),
        name="attn_bwd",
    )(context_index.reshape(1), query_t, grad_t, out_t, lse, *kv_blocks, *kv_blocks)


def rope_tables(positions):
    half_dim = HEAD_DIM // 2
    frequency = ROPE_BASE ** (-2.0 * jnp.arange(half_dim, dtype=F32) / HEAD_DIM)
    angles = frequency[:, None] * positions.astype(F32)[None, :]
    return jnp.cos(angles), jnp.sin(angles)


def rotate_t(values_t, cosine, sine):
    shaped = values_t.reshape(-1, 2, HEAD_DIM // 2, values_t.shape[1])
    low, high = shaped[:, 0], shaped[:, 1]
    turned = jnp.stack([low * cosine - high * sine, high * cosine + low * sine], 1)
    return turned.reshape(values_t.shape)


def prepare_kernel(p_ref, gate_ref, up_ref, down_ref, *outs):
    in_t_ref, gate_out, up_out, down_out, down_t_out = outs
    gate, up, down = gate_ref[0], up_ref[0], down_ref[0]
    in_t_ref[0, 0, 0] = gate.astype(F32).T.astype(BF16)
    in_t_ref[0, 1, 0] = up.astype(F32).T.astype(BF16)
    gate_out[...] = gate
    up_out[...] = up
    down_out[...] = down
    down_t_out[...] = down.astype(F32).T.astype(BF16)


def prepare_weights(parity, w_gate, w_up, w_down, chunk, share):
    experts, width, hidden = w_gate.shape
    chunks = hidden // chunk // share
    units = chunks * chunk

    def column(e, q, p):
        return (e, 0, q * share + p[0])

    def flat(e, q, p):
        return (0, e * chunks + q)

    return pl.pallas_call(
        prepare_kernel,
        out_shape=(
            jax.ShapeDtypeStruct((experts, 2, chunks, chunk, width), BF16),
            jax.ShapeDtypeStruct((width, experts * units), BF16),
            jax.ShapeDtypeStruct((width, experts * units), BF16),
            jax.ShapeDtypeStruct((experts * units, width), BF16),
            jax.ShapeDtypeStruct((width, experts * units), BF16),
        ),
        grid_spec=pltpu.PrefetchScalarGridSpec(
            num_scalar_prefetch=1,
            grid=(experts, chunks),
            in_specs=[
                pl.BlockSpec((1, width, chunk), column),
                pl.BlockSpec((1, width, chunk), column),
                pl.BlockSpec((1, chunk, width), lambda e, q, p: (e, q * share + p[0], 0)),
            ],
            out_specs=(
                pl.BlockSpec((1, 2, 1, chunk, width), lambda e, q, p: (e, 0, q, 0, 0)),
                pl.BlockSpec((width, chunk), flat),
                pl.BlockSpec((width, chunk), flat),
                pl.BlockSpec((chunk, width), lambda e, q, p: (e * chunks + q, 0)),
                pl.BlockSpec((width, chunk), flat),
            ),
        ),
        compiler_params=pltpu.CompilerParams(vmem_limit_bytes=32 << 20),
        cost_estimate=pl.CostEstimate(
            flops=0, transcendentals=0, bytes_accessed=18 * experts * width * units
        ),
        name="prepare_weights",
    )(parity.reshape(1), w_gate, w_up, w_down)


def experts_kernel(
    experts,
    e_ref,
    rows_ref,
    cot_ref,
    chosen_ref,
    kept_ref,
    router_ref,
    in_t_ref,
    gate_w_ref,
    up_w_ref,
    down_ref,
    down_t_ref,
    message_ref,
    back_ref,
    gates_ref,
    act_ref,
    dgate_ref,
    dup_ref,
    kept_gates_ref,
    grads_ref,
):
    width, count = rows_ref.shape
    units = down_ref.shape[0] // experts
    first = e_ref[0] * experts
    chosen = chosen_ref[...] > 0
    logits = jnp.dot(router_ref[...], rows_ref[...], preferred_element_type=F32)
    logits = jnp.where(chosen, logits, NEG_LARGE)
    gates = jnp.exp(logits - jnp.max(logits, 0, keepdims=True))
    gates = jnp.where(chosen, gates, 0.0)
    gates = gates / jnp.sum(gates, 0, keepdims=True)
    gates_ref[...] = gates
    kept_gates_ref[...] = gates * kept_ref[...]
    grads_ref[...] = jnp.zeros_like(grads_ref)

    def one(e, carry):
        both = pl.ds(pl.multiple_of(e * 2 * units, 2 * units), 2 * units)
        mine = pl.ds(pl.multiple_of(e * units, units), units)
        acts = jnp.dot(in_t_ref[both, :], rows_ref[...], preferred_element_type=F32)
        gate, up = acts[:units], acts[units:]
        grad = jnp.dot(down_ref[mine, :], cot_ref[...], preferred_element_type=F32)
        scale = kept_gates_ref[pl.ds(first + e, 1), :]
        keep = kept_ref[pl.ds(first + e, 1), :]
        sigmoid = jax.nn.sigmoid(gate)
        silu = gate * sigmoid
        hidden = silu * up
        grads_ref[pl.ds(first + e, 1), :] = keep * jnp.sum(hidden * grad, 0, keepdims=True)
        act_ref[mine, :] = (hidden * scale).astype(BF16)
        grad = grad * scale
        dup_ref[mine, :] = (grad * silu).astype(BF16)
        dgate_ref[mine, :] = (grad * up * sigmoid * (1.0 + gate * (1.0 - sigmoid))).astype(BF16)
        return carry

    lax.fori_loop(0, experts, one, 0)
    half = width // 2

    def out(i, carry):
        rows = pl.ds(pl.multiple_of(i * half, half), half)
        message_ref[0, rows, :] = jnp.dot(
            down_t_ref[rows, :], act_ref[...], preferred_element_type=F32
        ).astype(BF16)
        back = jnp.dot(gate_w_ref[rows, :], dgate_ref[...], preferred_element_type=F32)
        back = back + jnp.dot(up_w_ref[rows, :], dup_ref[...], preferred_element_type=F32)
        back_ref[0, rows, :] = back.astype(BF16)
        return carry

    lax.fori_loop(0, 2, out, 0)
    grads = grads_ref[...]
    lanes = grads.shape[0]
    high = grads.astype(BF16)
    message_ref[0, width : width + lanes, :] = high
    message_ref[0, width + lanes :, :] = (grads - high.astype(F32)).astype(BF16)


def run_experts(expert_index, experts, count, rows, cots, chosen, kept, router_t, weights):
    in_t, gate_w, up_w, down, down_t = weights
    width, tokens = rows.shape
    blocks = tokens // count
    lanes = router_t.shape[0]
    held = down.shape[0]
    in_t = in_t.reshape(2 * held, width)

    def whole(array):
        return pl.BlockSpec(
            array.shape, lambda b, e: (0, 0), pipeline_mode=pl.Buffered(buffer_count=1)
        )

    def part(height):
        return pl.BlockSpec((height, count), lambda b, e: (0, b))

    return pl.pallas_call(
        functools.partial(experts_kernel, experts),
        out_shape=(
            jax.ShapeDtypeStruct((blocks, width + 2 * lanes, count), BF16),
            jax.ShapeDtypeStruct((blocks, width, count), BF16),
            jax.ShapeDtypeStruct((lanes, tokens), F32),
            jax.ShapeDtypeStruct((held, tokens), BF16),
            jax.ShapeDtypeStruct((held, tokens), BF16),
            jax.ShapeDtypeStruct((held, tokens), BF16),
        ),
        grid_spec=pltpu.PrefetchScalarGridSpec(
            num_scalar_prefetch=1,
            grid=(blocks,),
            in_specs=[
                part(width),
                part(width),
                part(lanes),
                part(lanes),
                whole(router_t),
                whole(in_t),
                whole(gate_w),
                whole(up_w),
                whole(down),
                whole(down_t),
            ],
            out_specs=(
                pl.BlockSpec((1, width + 2 * lanes, count), lambda b, e: (b, 0, 0)),
                pl.BlockSpec((1, width, count), lambda b, e: (b, 0, 0)),
                part(lanes),
                part(held),
                part(held),
                part(held),
            ),
            scratch_shapes=[pltpu.VMEM((lanes, count), F32)] * 2,
        ),
        compiler_params=pltpu.CompilerParams(vmem_limit_bytes=56 << 20),
        cost_estimate=pl.CostEstimate(
            flops=12 * width * held * tokens,
            transcendentals=held * tokens,
            bytes_accessed=12 * width * held + 8 * width * tokens,
        ),
        name="experts",
    )(
        expert_index.reshape(1),
        rows,
        cots,
        chosen,
        kept,
        router_t,
        in_t,
        gate_w,
        up_w,
        down,
        down_t,
    )


def down_grad_kernel(act_ref, cot_ref, out_ref):
    owners, chunks, _, size, _ = out_ref.shape
    grad = mm(act_ref[...], cot_ref[...], 1, 1).astype(BF16)
    for q in range(chunks):
        for d in range(owners):
            at = (q * owners + d) * size
            out_ref[d, q, 0] = grad[at : at + size]


def down_grads(act, cots, experts, width, chunks, owners):
    held, tokens = act.shape
    units = held // experts
    size = units // chunks // owners
    return pl.pallas_call(
        down_grad_kernel,
        out_shape=jax.ShapeDtypeStruct((owners, chunks, experts, size, width), BF16),
        grid=(experts,),
        in_specs=[
            pl.BlockSpec((units, tokens), lambda e: (e, 0)),
            pl.BlockSpec(
                (width, tokens), lambda e: (0, 0), pipeline_mode=pl.Buffered(buffer_count=1)
            ),
        ],
        out_specs=pl.BlockSpec(
            (owners, chunks, 1, size, width), lambda e: (0, 0, e, 0, 0)
        ),
        compiler_params=pltpu.CompilerParams(vmem_limit_bytes=40 << 20),
        cost_estimate=pl.CostEstimate(
            flops=2 * width * held * tokens,
            transcendentals=0,
            bytes_accessed=2 * (held + width) * tokens + 2 * held * width,
        ),
        name="down_grads",
    )(act, cots)


def in_grad_kernel(rows_ref, act_ref, out_ref):
    owners, chunks, _, share, size, _ = out_ref.shape
    for k in range(chunks):
        for q in range(share):
            for d in range(owners):
                at = ((k * share + q) * owners + d) * size
                out_ref[d, k, 0, q] = mm(rows_ref[at : at + size, :], act_ref[...], 1, 1).astype(
                    BF16
                )


def in_grads(rows, grad_act, experts, chunks, share, owners):
    held, tokens = grad_act.shape
    width = rows.shape[0]
    units = held // experts
    size = width // chunks // share // owners
    return pl.pallas_call(
        in_grad_kernel,
        out_shape=jax.ShapeDtypeStruct((owners, chunks, experts, share, size, units), BF16),
        grid=(experts,),
        in_specs=[
            pl.BlockSpec(
                (width, tokens), lambda e: (0, 0), pipeline_mode=pl.Buffered(buffer_count=1)
            ),
            pl.BlockSpec((units, tokens), lambda e: (e, 0)),
        ],
        out_specs=pl.BlockSpec(
            (owners, chunks, 1, share, size, units), lambda e: (0, 0, e, 0, 0, 0)
        ),
        compiler_params=pltpu.CompilerParams(vmem_limit_bytes=40 << 20),
        cost_estimate=pl.CostEstimate(
            flops=2 * width * held * tokens,
            transcendentals=0,
            bytes_accessed=2 * (held + width) * tokens + 2 * held * width,
        ),
        name="in_grads",
    )(rows, grad_act)


def body(
    tokens,
    routes,
    cotangent,
    norm_attn,
    w_query,
    w_key,
    w_value,
    w_out,
    norm_ffn,
    w_router,
    w_gate,
    w_up,
    w_down,
):
    comm = Comm()
    count, width = tokens.shape[1], tokens.shape[2]
    top_k = routes.shape[2]
    experts, _, hidden_units = w_gate.shape
    all_experts = experts * comm.n_expert
    capacity = (9 * count * top_k + 8 * all_experts - 1) // (8 * all_experts)
    n_context, n_dp, share = comm.n_context, comm.n_dp, comm.share
    expert_index = lax.axis_index("expert")
    context_index = lax.axis_index("context")
    dp_index = lax.axis_index("dp")
    parity = context_index % share
    chunks = n_context // share
    lanes = -(-all_experts // 32) * 32

    hidden = tokens[0].T.astype(F32)
    gain_attn = norm_attn.astype(F32)[:, None]
    gain_ffn = norm_ffn.astype(F32)[:, None]
    scale_attn = rms_scale(hidden)
    normed_attn = (hidden * scale_attn * gain_attn).astype(BF16)
    positions = context_index * count + jnp.arange(count, dtype=jnp.int32)
    cosine, sine = rope_tables(positions)
    key_t = rotate_t(mm(w_key, normed_attn, 0, 0), cosine, sine).astype(BF16)
    value_t = mm(w_value, normed_attn, 0, 0).astype(BF16)
    kv_own = jnp.concatenate([key_t, value_t], 0)
    kv_blocks = [kv_own]
    for s in range(1, n_context):
        pairs = [(i, i + s) for i in range(n_context - s)]
        kv_blocks.append(lax.ppermute(kv_own, "context", pairs))
    query_t = rotate_t(mm(w_query, normed_attn, 0, 0), cosine, sine)
    query_t = (query_t * HEAD_DIM**-0.5).astype(BF16)

    cot_t = cotangent[0].T
    routed = (
        routes[0].T[:, None, :] == jnp.arange(lanes, dtype=jnp.int32)[None, :, None]
    ).astype(F32)
    cots_all = comm.gather_group(jnp.concatenate([cot_t, routed.sum(0).astype(BF16)]))
    routed_all = cots_all[width:]
    n_tokens = routed_all.shape[1]
    before = jnp.triu(jnp.ones((count, count), BF16), 1)
    ranking = mm(routed_all.reshape(-1, count), before, 1, 0).reshape(lanes, n_tokens)
    chosen = routed_all.astype(F32)
    kept = jnp.where(ranking < capacity, chosen, 0.0)
    weights = prepare_weights(parity, w_gate, w_up, w_down, hidden_units // n_context, share)
    router_t = jnp.zeros((lanes, width), BF16).at[:all_experts].set(w_router.T)

    out_t, out_low, lse = attention_forward(context_index, query_t, kv_blocks)
    middle = hidden + mm(w_out, out_low, 0, 0)
    scale_ffn = rms_scale(middle)
    normed_ffn = (middle * scale_ffn * gain_ffn).astype(BF16)

    def rows_of(array):
        size = array.shape[0] // comm.n_expert
        blocks = []
        for j in range(comm.cores):
            for k in range(comm.columns):
                column, core = expert_index // comm.cores, expert_index % comm.cores
                column = (column - k) % comm.columns
                target = column * comm.cores + (core + j) % comm.cores
                piece = lax.dynamic_slice_in_dim(array, target * size, size, 0)
                blocks.append(piece if (j, k) == (0, 0) else comm.pull(piece, k, j))
        return jnp.concatenate(blocks, 1)

    h1_rows = rows_of(normed_attn)
    ob_rows = rows_of(out_low)

    rows_all = comm.gather_group(normed_ffn)
    message, back, gates_all, act, grad_gate, grad_up = run_experts(
        expert_index, experts, count, rows_all, cots_all, chosen, kept, router_t, weights
    )
    near = comm.return_near(message)
    near_back = comm.return_near(back)
    down_parts = comm.scatter_dp(down_grads(act, cots_all, experts, width, chunks, n_dp))
    gate_parts = comm.scatter_dp(in_grads(rows_all, grad_gate, experts, chunks, share, n_dp))
    up_parts = comm.scatter_dp(in_grads(rows_all, grad_up, experts, chunks, share, n_dp))
    returned = comm.return_far(near)
    grad_normed_ffn = comm.return_far(near_back)
    result = (middle + returned[:width]).astype(BF16)
    grad_gates = returned[width : width + lanes] + returned[width + lanes :]
    gates_own = gates_all[:, :count]

    upstream = cot_t.astype(F32)
    mean_grad = jnp.sum(gates_own * grad_gates, 0, keepdims=True)
    grad_logits = (gates_own * (grad_gates - mean_grad)).astype(BF16)
    grad_normed_ffn = grad_normed_ffn + mm(router_t, grad_logits, 0, 0)
    grad_gain_ffn = jnp.sum(grad_normed_ffn * middle * scale_ffn, 1)
    grad_middle = upstream + norm_back(grad_normed_ffn, middle, scale_ffn, gain_ffn)
    grad_branch = grad_middle.astype(BF16)

    grad_attn_t = mm(w_out, grad_branch, 1, 0).astype(BF16)
    grad_query_t, grad_kv = attention_backward(
        context_index, query_t, grad_attn_t, out_t, lse, kv_blocks
    )
    kv_width = KV_HEADS * HEAD_DIM
    kv_sum = grad_kv[0].astype(F32)
    for s in range(1, n_context):
        pairs = [(i, i - s) for i in range(s, n_context)]
        kv_sum = kv_sum + lax.ppermute(grad_kv[s], "context", pairs).astype(F32)
    grad_query_raw = rotate_t(grad_query_t, cosine, -sine).astype(BF16)
    grad_key_raw = rotate_t(kv_sum[0], cosine, -sine).astype(BF16)
    grad_value_raw = kv_sum[1].astype(BF16)
    grad_kv_raw = jnp.concatenate([grad_key_raw, grad_value_raw], 0)

    def finish_in(parts):
        total = comm.scatter_context(parts, share)
        if share == 1:
            return total[:, 0]
        keep = lax.dynamic_index_in_dim(total, parity, 1, False)
        send = lax.dynamic_index_in_dim(total, 1 - parity, 1, False)
        other = comm.pair(send.astype(BF16)).astype(F32)
        first = jnp.where(parity == 0, keep, other)
        second = jnp.where(parity == 0, other, keep)
        size = hidden_units // n_context
        pieces = []
        for q in range(chunks):
            pieces += [x[..., q * size : (q + 1) * size] for x in (first, second)]
        return jnp.concatenate(pieces, -1)

    down_sum = comm.scatter_context(down_parts, share)
    gate_sum = finish_in(gate_parts)
    up_sum = finish_in(up_parts)

    def reduce_rows(local):
        parts = local.reshape(n_context, n_dp, -1, local.shape[1])
        total = comm.scatter_dp(jnp.moveaxis(parts, 1, 0))
        return comm.scatter_context(total, 1)

    branch_all = comm.gather_expert(jnp.concatenate([grad_branch, grad_logits]))
    row_count = width // comm.n_expert
    gain_total = grad_gain_ffn.reshape(-1, LANES)
    if comm.cores == 2:
        gain_total = gain_total + comm.pull(gain_total, 0, 1)
    gain_total = sum([comm.pull(gain_total, k, 0) for k in range(1, comm.columns)], gain_total)
    gain_rows = lax.dynamic_slice_in_dim(
        gain_total.reshape(width), expert_index * row_count, row_count, 0
    )
    out_rows = mm(ob_rows, branch_all[:width], 1, 1)
    h2_rows = lax.dynamic_slice_in_dim(rows_all, expert_index * row_count, row_count, 0)
    h2_rows = h2_rows.reshape(row_count, comm.cores, share, comm.columns * count)[:, :, 0]
    router_rows = mm(h2_rows.reshape(row_count, -1), branch_all[width:], 1, 1)
    rest = jnp.zeros((row_count, LANES - lanes - 1), F32)
    first_sum = reduce_rows(
        jnp.concatenate([out_rows, router_rows, gain_rows[:, None], rest], 1)
    )

    def projection_rows(grad_t):
        return reduce_rows(mm(h1_rows, comm.gather_expert(grad_t), 1, 1))

    query_sum = projection_rows(grad_query_raw)
    kv_rows = projection_rows(grad_kv_raw)
    key_sum, value_sum = kv_rows[:, :kv_width], kv_rows[:, kv_width:]

    shard = (expert_index * n_context + context_index) * n_dp + dp_index
    shard_rows = query_sum.shape[0]

    def shard_of(array):
        return lax.dynamic_slice_in_dim(array, shard * shard_rows, shard_rows, 0).astype(F32)

    gain_sum = (
        jnp.sum(shard_of(w_query) * query_sum, 1)
        + jnp.sum(shard_of(w_key) * key_sum, 1)
        + jnp.sum(shard_of(w_value) * value_sum, 1)
    ) / shard_of(norm_attn)

    grad_normed_attn = mm(w_query, grad_query_raw, 1, 0)
    grad_normed_attn = grad_normed_attn + mm(w_key, grad_key_raw, 1, 0)
    grad_normed_attn = grad_normed_attn + mm(w_value, grad_value_raw, 1, 0)
    grad_hidden = grad_middle + norm_back(grad_normed_attn, hidden, scale_attn, gain_attn)
    return (
        result.T[None],
        grad_hidden.astype(BF16).T[None],
        gain_sum,
        query_sum,
        key_sum,
        value_sum,
        first_sum[:, :width],
        first_sum[:, width + lanes],
        first_sum[:, width : width + all_experts],
        gate_sum,
        up_sum,
        down_sum,
    )


def solution(mesh):
    rows = P(("expert", "dp"), "context", None)
    dense = P(("expert", "context", "dp"), None)
    vector = P(("expert", "context", "dp"))
    experts = P("expert", None, None)
    expert_grads = P("expert", ("context", "dp"), None)
    return jax.shard_map(
        body,
        mesh=mesh,
        in_specs=(rows, rows, rows) + (P(),) * 7 + (experts,) * 3,
        out_specs=(rows, rows, vector, dense, dense, dense, dense, vector, dense)
        + (expert_grads,) * 3,
        check_vma=False,
    )
```

time: 1730 us -> 723 us (0.42)
  waiting for transfers between devices: 1230 us -> 258 us
  Pallas kernels: 0 us -> 152 us
  matrix products: 162 us -> 29.3 us
  local copies, waits for them, and re-layouts: 171 us -> 95.8 us
  starting transfers between devices: 23.4 us -> 92.3 us
  blocking collectives: 43.3 us -> 0 us
  other arithmetic: 66.6 us -> 86.8 us
    reduce_scatter x9 -> x0, waiting for transfers between devices: 945 us -> none  [the longest x1 142 us: body(): lax.psum_scatter(grad_w_query, ('expert', 'context', 'dp'), scatter_dimen...]
    ppermute x0 -> x60, waiting for transfers between devices: none -> 258 us  [the longest x6 57.5 us: scatter_dp(): total = total + lax.ppermute(send, 'dp', pairs).astype(F32)]
    all_to_all x4 -> x0, waiting for transfers between devices: 191 us -> none  [the longest x1 59.2 us: body(): lax.all_to_all(send_grads, 'expert', split_axis=0, concat_axis=0, tiled=T...]
    pallas_call x0 -> x7, Pallas kernels: none -> 152 us  [the longest x1 74 us: run_experts(): pl.pallas_call(functools.partial(experts_kernel, experts), out_shape=(jax...]
    dot_general x30 -> x14, matrix products: 161 us -> 29.3 us  [mm(): lax.dot_general(a, b, (((da,), (db,)), ((), ())), preferred_element_type=...]
    ppermute x0 -> x60, starting transfers between devices: none -> 92.3 us  [the longest x12 32.7 us: scatter_context(): total = total + lax.ppermute(send, 'context', pairs).astype(F32)]
    unnamed x13 -> x0, waiting for transfers between devices: 71.6 us -> none
    gather x4 -> x0, local copies, waits for them, and re-layouts: 63.8 us -> none  [the longest x1 19.7 us: body(): padded_grads[pair_of_slot]]
  transfers between devices with their start and end apart: 16 -> 60, of which waited for: 16 -> 27; matrix products, arithmetic and copies ran while one was open for 15% -> 24% of each run, Pallas kernels for 0% -> 8%
where the time goes in v1:
time: 723 us; the launch traced here: 716 us
  waiting for transfers between devices  258 us (36%)
  Pallas kernels  152 us (21%)
  local copies, waits for them, and re-layouts  95.8 us (13%)
  starting transfers between devices  92.3 us (13%)
  other arithmetic  86.8 us (12%)
  matrix products  29.3 us (4%)
    pallas_call x1, Pallas kernels, run_experts(): pl.pallas_call(functools.partial(experts_kernel, experts), out_shape=(jax...  74 us
    ppermute x6, waiting for transfers between devices, scatter_dp(): total = total + lax.ppermute(send, 'dp', pairs).astype(F32)  57.5 us
    ppermute x12, waiting for transfers between devices, scatter_context(): total = total + lax.ppermute(send, 'context', pairs).astype(F32)  51.3 us
    ppermute x3, waiting for transfers between devices, body(): kv_sum = kv_sum + lax.ppermute(grad_kv[s], 'context', pairs).astype(F32)  48.6 us
    ppermute x10, waiting for transfers between devices, pair(): lax.ppermute(value, 'context', [(i, i ^ 1) for i in range(self.n_context)])  40.5 us
    unnamed x215, local copies, waits for them, and re-layouts  38.3 us
    pallas_call x2, Pallas kernels, in_grads(): pl.pallas_call(in_grad_kernel, out_shape=jax.ShapeDtypeStruct((owners, ch...  35.2 us
    ppermute x12, starting transfers between devices, scatter_context(): total = total + lax.ppermute(send, 'context', pairs).astype(F32)  32.7 us
  transfers between devices with their start and end apart: 60, of which 27 were waited for; matrix products, arithmetic and copies ran while one was open for 24% of the time, Pallas kernels for 8%

profile of v1, /device:TPU:0, one launch (start us, length us, event | category | flops | bytes accessed | tf_op | source)
XLA Modules:
  0.0 716.3 jit_solution(16641456621304338514)
XLA Ops:
  9.4 5.0 collective-permute-start
  24.5 4.9 convolution_bitcast_fusion
  37.9 11.3 %collective-permute-done.2.refs_3_.refs_7_ = bf16[1024,256]{1,0:T(8,128)(2,1)S(1)} collective-permute-done((bf16[1024,256]{1,0:T(8,128)(2,1)S(1)}, bf16[1024,256]{1,0:T(8,128)(2,1)S(1)}, u32[]{:S(2)}, u32[]{:S(2)}) %collective-permute-start.2) | collective-permute-done | bytes 524320 | tf_op jit(solution)/shard_map/ppermute | solution.py:626
  51.0 11.1 %attn_fwd.1 = (f32[1536,256]{1,0:T(8,128)S(1)}, bf16[1536,256]{1,0:T(8,128)(2,1)S(1)}, f32[8,8,256]{2,1,0:T(8,128)S(1)}) custom-call(s32[1]{0:T(128)} %bitcast.1.c_ref, bf16[1536,256]{1,0:T(8,128)(2,1)S(1)} %bitcast.265, bf16[1024,256]{1,0:T(8,128)(2,1)S(1)} %pad_maximum_fusion.11.refs_0_.refs_4_, ...), custom_call_target="tpu_custom_call" | custom-call | flops 6442450944 | bytes 6291456 | tf_op jit(solution)/shard_map/attn_fwd/pallas_call | solution.py:189
  71.0 13.5 %collective-permute-start.11 = (bf16[784,256]{1,0:T(8,128)(2,1)S(1)}, bf16[784,256]{1,0:T(8,128)(2,1)S(1)}, u32[]{:S(2)}, u32[]{:S(2)}) collective-permute-start(bf16[784,256]{1,0:T(8,128)(2,1)S(1)} %slice.262), channel_id=1, source_target_pairs={{0,2},{2,0},{4,6},{6,4},{1,3},{3,1},{5,7},{7,5},{8,10},{10,8},{12,... | collective-permute-start | bytes 1204232 | tf_op jit(solution)/shard_map/ppermute | solution.py:59
  86.3 8.4 %collective-permute-done.11 = bf16[784,256]{1,0:T(8,128)(2,1)S(1)} collective-permute-done((bf16[784,256]{1,0:T(8,128)(2,1)S(1)}, bf16[784,256]{1,0:T(8,128)(2,1)S(1)}, u32[]{:S(2)}, u32[]{:S(2)}) %collective-permute-start.11) | collective-permute-done | bytes 401440 | tf_op jit(solution)/shard_map/ppermute | solution.py:59
  94.7 14.7 %maximum_maximum_fusion = bf16[1568,1024]{1,0:T(8,128)(2,1)} fusion(bf16[784,256]{1,0:T(8,128)(2,1)S(1)} %collective-permute-done.11, bf16[784,256]{1,0:T(8,128)(2,1)S(1)} %collective-permute-done.10, bf16[1568,256]{1,0:T(8,128)(2,1)} %collective-permute-done.9, bf16[1568,256]{1,0:T(8,128)(2,1)} %collective-permute-done.8, ...), kind=kLoop, calls=%fused_computation.5 | loop fusion | flops 19267584 | bytes 6422528 | tf_op jit(solution)/shard_map/concatenate | solution.py:79
  112.2 8.8 %collective-permute-done.5 = bf16[768,256]{1,0:T(8,128)(2,1)S(1)} collective-permute-done((bf16[768,256]{1,0:T(8,128)(2,1)S(1)}, bf16[768,256]{1,0:T(8,128)(2,1)S(1)}, u32[]{:S(2)}, u32[]{:S(2)}) %collective-permute-start.5) | collective-permute-done | bytes 393248 | tf_op jit(solution)/shard_map/ppermute | solution.py:52
  121.7 11.9 %maximum_maximum_fusion.1 = bf16[1536,1024]{1,0:T(8,128)(2,1)} fusion(bf16[768,256]{1,0:T(8,128)(2,1)S(1)} %collective-permute-done.6, bf16[768,256]{1,0:T(8,128)(2,1)S(1)} %collective-permute-done.5, bf16[1536,256]{1,0:T(8,128)(2,1)S(1)} %collective-permute-done.4, bf16[1536,256]{1,0:T(8,128)(2,1)S(1)} %collective-permute-done.3, ...), kind=kLoop, calls=%fused_computation.9 | loop fusion | flops 15728640 | bytes 6291456 | tf_op jit(solution)/shard_map/concatenate | solution.py:79
  134.3 11.4 %prepare_weights.1 = (bf16[5,2,2,128,1536]{4,3,2,1,0:T(8,128)(2,1)}, bf16[1536,1280]{1,0:T(8,128)(2,1)S(1)}, bf16[1536,1280]{1,0:T(8,128)(2,1)S(1)}, bf16[1280,1...) custom-call(s32[1]{0:T(128)} %bitcast.17.p_ref, bf16[5,1536,512]{2,1,0:T(8,128)(2,1)} %gate_ref.1, bf16[5,1536,512]{2,1,0:T(8,128)(2,1)} %up_ref.1, ...), custom_call_target="tpu_custom_call" | custom-call | bytes 35389440 | tf_op jit(solution)/shard_map/prepare_weights/pallas_call | solution.py:329
  173.3 74.0 %experts.1 = (bf16[8,1600,256]{2,1,0:T(8,128)(2,1)}, bf16[8,1536,256]{2,1,0:T(8,128)(2,1)}, f32[32,2048]{1,0:T(8,128)}, bf16[1280,2048]{1,0:T(8,128)(2,1)}, bf16...) custom-call(s32[1]{0:T(128)} %bitcast.11.e_ref, bf16[1536,2048]{1,0:T(8,128)(2,1)} %constant_dynamic-update-slice_fusion.rows_ref, ...), custom_call_target="tpu_custom_call" | custom-call | flops 48318382080 | bytes 48758784 | tf_op jit(solution)/shard_map/experts/pallas_call | solution.py:452
  249.8 17.6 %in_grads.3 = bf16[2,2,5,2,192,256]{5,4,3,2,1,0:T(8,128)(2,1)S(1)} custom-call(bf16[1536,2048]{1,0:T(8,128)(2,1)} %constant_dynamic-update-slice_fusion.rows_ref, bf16[1280,2048]{1,0:T(8,128)(2,1)S(1)} %copy-done.16), custom_call_target="tpu_custom_call" | custom-call | flops 8053063680 | bytes 15466496 | tf_op jit(solution)/shard_map/in_grads/pallas_call | solution.py:561
  271.9 17.7 %in_grads.2 = bf16[2,2,5,2,192,256]{5,4,3,2,1,0:T(8,128)(2,1)S(1)} custom-call(bf16[1536,2048]{1,0:T(8,128)(2,1)} %constant_dynamic-update-slice_fusion.rows_ref, bf16[1280,2048]{1,0:T(8,128)(2,1)S(1)} %copy-done.15), custom_call_target="tpu_custom_call" | custom-call | flops 8053063680 | bytes 15466496 | tf_op jit(solution)/shard_map/in_grads/pallas_call | solution.py:561
  293.3 12.1 %down_grads.1 = bf16[2,2,5,64,1536]{4,3,2,1,0:T(8,128)(2,1)S(1)} custom-call(bf16[1280,2048]{1,0:T(8,128)(2,1)S(1)} %bitcast.268, bf16[1568,2048]{1,0:T(8,128)(2,1)} %constant_dynamic-update-slice_fusion.5.cot_ref), custom_call_target="tpu_custom_call" | custom-call | flops 8053063680 | bytes 15466496 | tf_op jit(solution)/shard_map/down_grads/pallas_call | solution.py:522
  327.6 7.2 %collective-permute-start.56 = (bf16[5,2,192,256]{3,2,1,0:T(8,128)(2,1)}, bf16[5,2,192,256]{3,2,1,0:T(8,128)(2,1)}, u32[]{:S(2)}, u32[]{:S(2)}) collective-permute-start(bf16[5,2,192,256]{3,2,1,0:T(8,128)(2,1)} %fusion.35), channel_id=1, source_target_pairs={{0,4},{2,6},{4,0},{6,2},{1,5},{3,7},{5,1},{7,3},{8,12},{10,14},{12... | collective-permute-start | bytes 2949128 | tf_op jit(solution)/shard_map/ppermute | solution.py:131
  334.8 23.7 %collective-permute-done.52 = bf16[2,5,2,192,256]{4,3,1,2,0:T(8,128)(2,1)} collective-permute-done((bf16[2,5,2,192,256]{4,3,1,2,0:T(8,128)(2,1)}, bf16[2,5,2,192,256]{4,3,1,2,0:T(8,128)(2,1)}, u32[]{:S(2)}, u32[]{:S(2)}) %collective-permute-start.52) | collective-permute-done | bytes 1966112 | tf_op jit(solution)/shard_map/ppermute | solution.py:118
  361.9 7.2 %collective-permute-start.53 = (bf16[5,2,192,256]{3,2,0,1:T(8,128)(2,1)}, bf16[5,2,192,256]{3,2,0,1:T(8,128)(2,1)}, u32[]{:S(2)}, u32[]{:S(2)}) collective-permute-start(bf16[5,2,192,256]{3,2,0,1:T(8,128)(2,1)} %fusion.34), channel_id=1, source_target_pairs={{0,4},{2,6},{4,0},{6,2},{1,5},{3,7},{5,1},{7,3},{8,12},{10,14},{12... | collective-permute-start | bytes 2949128 | tf_op jit(solution)/shard_map/ppermute | solution.py:131
  369.1 31.1 %collective-permute-done.58 = bf16[2,5,64,1536]{3,2,1,0:T(8,128)(2,1)} collective-permute-done((bf16[2,5,64,1536]{3,2,1,0:T(8,128)(2,1)}, bf16[2,5,64,1536]{3,2,1,0:T(8,128)(2,1)}, u32[]{:S(2)}, u32[]{:S(2)}) %collective-permute-start.58) | collective-permute-done | bytes 1966112 | tf_op jit(solution)/shard_map/ppermute | solution.py:118
  405.2 7.2 %collective-permute-start.59 = (bf16[5,64,1536]{2,1,0:T(8,128)(2,1)}, bf16[5,64,1536]{2,1,0:T(8,128)(2,1)}, u32[]{:S(2)}, u32[]{:S(2)}) collective-permute-start(bf16[5,64,1536]{2,1,0:T(8,128)(2,1)} %fusion.36), channel_id=1, source_target_pairs={{0,4},{2,6},{4,0},{6,2},{1,5},{3,7},{5,1},{7,3},{8,12},{10,14},{12... | collective-permute-start | bytes 2949128 | tf_op jit(solution)/shard_map/ppermute | solution.py:131
  427.9 14.0 %collective-permute-done.53 = bf16[5,2,192,256]{3,2,0,1:T(8,128)(2,1)} collective-permute-done((bf16[5,2,192,256]{3,2,0,1:T(8,128)(2,1)}, bf16[5,2,192,256]{3,2,0,1:T(8,128)(2,1)}, u32[]{:S(2)}, u32[]{:S(2)}) %collective-permute-start.53) | collective-permute-done | bytes 983072 | tf_op jit(solution)/shard_map/ppermute | solution.py:131
  443.6 18.8 %collective-permute-done.59 = bf16[5,64,1536]{2,1,0:T(8,128)(2,1)} collective-permute-done((bf16[5,64,1536]{2,1,0:T(8,128)(2,1)}, bf16[5,64,1536]{2,1,0:T(8,128)(2,1)}, u32[]{:S(2)}, u32[]{:S(2)}) %collective-permute-start.59) | collective-permute-done | bytes 983072 | tf_op jit(solution)/shard_map/ppermute | solution.py:131
  478.3 5.1 collective-permute-done.54
  485.2 5.1 collective-permute-done.19
  490.3 10.0 %collective-permute-done.21 = bf16[2,768,256]{2,1,0:T(8,128)(2,1)S(1)} collective-permute-done((bf16[2,768,256]{2,1,0:T(8,128)(2,1)S(1)}, bf16[2,768,256]{2,1,0:T(8,128)(2,1)S(1)}, u32[]{:S(2)}, u32[]{:S(2)}) %collective-permute-start.21) | collective-permute-done | bytes 786464 | tf_op jit(solution)/shard_map/ppermute | solution.py:59
  502.3 5.5 collective-permute-done.14
  507.8 10.0 %collective-permute-done.16 = bf16[2,800,256]{2,1,0:T(8,128)(2,1)S(1)} collective-permute-done((bf16[2,800,256]{2,1,0:T(8,128)(2,1)S(1)}, bf16[2,800,256]{2,1,0:T(8,128)(2,1)S(1)}, u32[]{:S(2)}, u32[]{:S(2)}) %collective-permute-start.16) | collective-permute-done | bytes 819232 | tf_op jit(solution)/shard_map/ppermute | solution.py:59
  519.8 6.4 collective-permute-done.20
  536.7 8.0 %attn_bwd.1 = (f32[1536,256]{1,0:T(8,128)S(1)}, bf16[4,2,512,256]{3,2,1,0:T(8,128)(2,1)S(1)}) custom-call(s32[1]{0:T(128)} %bitcast.1.c_ref, bf16[1536,256]{1,0:T(8,128)(2,1)S(1)} %bitcast.266, bf16[1536,256]{1,0:T(8,128)(2,1)S(1)} %fusion.10.do_ref, f32[1536,256]{1,0:T(8,128)S(1)} %copy-done.18, f32[8,8,256]{2,1,0:T(8,128)S(1)} %get-tuple-element.50.lse_ref, ...), custom_call_target="tpu_custom_call" | custom-call | flops 16106127360 | bytes 7864320 | tf_op jit(solution)/shard_map/attn_bwd/pallas_call | solution.py:267
  560.0 6.7 collective-permute-done.23
  568.1 41.9 %collective-permute-done.24 = bf16[2,512,256]{2,1,0:T(8,128)(2,1)} collective-permute-done((bf16[2,512,256]{2,1,0:T(8,128)(2,1)S(1)}, bf16[2,512,256]{2,1,0:T(8,128)(2,1)}, u32[]{:S(2)}, u32[]{:S(2)}) %collective-permute-start.24) | collective-permute-done | bytes 524320 | tf_op jit(solution)/shard_map/ppermute | solution.py:695
  619.2 20.9 %collective-permute-done.35 = bf16[1024,256]{1,0:T(8,128)(2,1)S(1)} collective-permute-done((bf16[1024,256]{1,0:T(8,128)(2,1)S(1)}, bf16[1024,256]{1,0:T(8,128)(2,1)S(1)}, u32[]{:S(2)}, u32[]{:S(2)}) %collective-permute-start.35) | collective-permute-done | bytes 524320 | tf_op jit(solution)/shard_map/ppermute | solution.py:52
  698.9 7.6 %collective-permute-done.33 = bf16[48,1536]{1,0:T(8,128)(2,1)S(1)} collective-permute-done((bf16[48,1536]{1,0:T(8,128)(2,1)S(1)}, bf16[48,1536]{1,0:T(8,128)(2,1)S(1)}, u32[]{:S(2)}, u32[]{:S(2)}) %collective-permute-start.33) | collective-permute-done | bytes 147488 | tf_op jit(solution)/shard_map/ppermute | solution.py:131
  (451 shorter events, 255.1 us)
Async XLA Ops:
  9.4 24.9 %collective-permute-start = (bf16[1024,256]{1,0:T(8,128)(2,1)S(1)}, bf16[1024,256]{1,0:T(8,128)(2,1)S(1)}, u32[]{:S(2)}, u32[]{:S(2)}) collective-permute-start(bf16[1024,256]{1,0:T(8,128)(2,1)S(1)} %pad_maximum_fusion.11.refs_0_.refs_4_), channel_id=1, source_target_pairs={{0,2},{2,4},{4,6},{1,3},{3,5},{5,7},{8,10},{10,12},{12,14},{9,11},... | collective-permute-start | bytes 1572872 | tf_op jit(solution)/shard_map/ppermute | solution.py:626
  18.8 30.3 %collective-permute-start.2 = (bf16[1024,256]{1,0:T(8,128)(2,1)S(1)}, bf16[1024,256]{1,0:T(8,128)(2,1)S(1)}, u32[]{:S(2)}, u32[]{:S(2)}) collective-permute-start(bf16[1024,256]{1,0:T(8,128)(2,1)S(1)} %pad_maximum_fusion.11.refs_0_.refs_4_), channel_id=1, source_target_pairs={{0,6},{1,7},{8,14},{9,15},{16,22},{17,23},{24,30},{25,31}} | collective-permute-start | bytes 1572872 | tf_op jit(solution)/shard_map/ppermute | solution.py:626
  23.0 46.9 %collective-permute-start.8 = (bf16[1568,256]{1,0:T(8,128)(2,1)}, bf16[1568,256]{1,0:T(8,128)(2,1)}, u32[]{:S(2)}, u32[]{:S(2)}) collective-permute-start(bf16[1568,256]{1,0:T(8,128)(2,1)} %get-tuple-element.161), channel_id=1, source_target_pairs={{16,0},{24,8},{0,16},{8,24},{17,1},{25,9},{1,17},{9,25},{18,2},{26... | collective-permute-start | bytes 2408456 | tf_op jit(solution)/shard_map/ppermute | solution.py:52
  24.5 42.6 %collective-permute-start.9 = (bf16[1568,256]{1,0:T(8,128)(2,1)}, bf16[1568,256]{1,0:T(8,128)(2,1)}, u32[]{:S(2)}, u32[]{:S(2)}) collective-permute-start(bf16[1568,256]{1,0:T(8,128)(2,1)} %get-tuple-element.161), channel_id=1, source_target_pairs={{0,2},{2,0},{4,6},{6,4},{1,3},{3,1},{5,7},{7,5},{8,10},{10,8},{12,... | collective-permute-start | bytes 2408456 | tf_op jit(solution)/shard_map/ppermute | solution.py:59
  85.7 23.8 %collective-permute-start.4 = (bf16[1536,256]{1,0:T(8,128)(2,1)S(1)}, bf16[1536,256]{1,0:T(8,128)(2,1)S(1)}, u32[]{:S(2)}, u32[]{:S(2)}) collective-permute-start(bf16[1536,256]{1,0:T(8,128)(2,1)S(1)} %get-tuple-element.125), channel_id=1, source_target_pairs={{0,2},{2,0},{4,6},{6,4},{1,3},{3,1},{5,7},{7,5},{8,10},{10,8},{12,... | collective-permute-start | bytes 2359304 | tf_op jit(solution)/shard_map/ppermute | solution.py:59
  85.7 24.4 %collective-permute-start.3 = (bf16[1536,256]{1,0:T(8,128)(2,1)S(1)}, bf16[1536,256]{1,0:T(8,128)(2,1)S(1)}, u32[]{:S(2)}, u32[]{:S(2)}) collective-permute-start(bf16[1536,256]{1,0:T(8,128)(2,1)S(1)} %get-tuple-element.125), channel_id=1, source_target_pairs={{16,0},{24,8},{0,16},{8,24},{17,1},{25,9},{1,17},{9,25},{18,2},{26... | collective-permute-start | bytes 2359304 | tf_op jit(solution)/shard_map/ppermute | solution.py:52
  109.4 52.4 %collective-permute-start.12 = (bf16[1568,1024]{1,0:T(8,128)(2,1)}, bf16[1568,1024]{1,0:T(8,128)(2,1)}, u32[]{:S(2)}, u32[]{:S(2)}) collective-permute-start(bf16[1568,1024]{1,0:T(8,128)(2,1)} %maximum_maximum_fusion), channel_id=1, source_target_pairs={{8,0},{0,8},{24,16},{16,24},{9,1},{1,9},{25,17},{17,25},{10,2},{2,... | collective-permute-start | bytes 9633800 | tf_op jit(solution)/shard_map/ppermute | solution.py:52
  133.6 35.9 %collective-permute-start.7 = (bf16[1536,1024]{1,0:T(8,128)(2,1)}, bf16[1536,1024]{1,0:T(8,128)(2,1)}, u32[]{:S(2)}, u32[]{:S(2)}) collective-permute-start(bf16[1536,1024]{1,0:T(8,128)(2,1)} %maximum_maximum_fusion.1), channel_id=1, source_target_pairs={{8,0},{0,8},{24,16},{16,24},{9,1},{1,9},{25,17},{17,25},{10,2},{2,... | collective-permute-start | bytes 9437192 | tf_op jit(solution)/shard_map/ppermute | solution.py:52
  270.4 50.4 %collective-permute-start.55 = (bf16[2,5,2,192,256]{4,3,2,1,0:T(8,128)(2,1)}, bf16[2,5,2,192,256]{4,3,2,1,0:T(8,128)(2,1)}, u32[]{:S(2)}, u32[]{:S(2)}) collective-permute-start(bf16[2,5,2,192,256]{4,3,2,1,0:T(8,128)(2,1)} %dynamic-slice_bitcast_fusion.1), channel_id=1, source_target_pairs={{0,1},{1,0},{2,3},{3,2},{4,5},{5,4},{6,7},{7,6},{8,9},{9,8},{10,11... | collective-permute-start | bytes 5898248 | tf_op jit(solution)/shard_map/ppermute | solution.py:118
  292.8 65.7 %collective-permute-start.52 = (bf16[2,5,2,192,256]{4,3,1,2,0:T(8,128)(2,1)}, bf16[2,5,2,192,256]{4,3,1,2,0:T(8,128)(2,1)}, u32[]{:S(2)}, u32[]{:S(2)}) collective-permute-start(bf16[2,5,2,192,256]{4,3,1,2,0:T(8,128)(2,1)} %bitcast.263), channel_id=1, source_target_pairs={{0,1},{1,0},{2,3},{3,2},{4,5},{5,4},{6,7},{7,6},{8,9},{9,8},{10,11... | collective-permute-start | bytes 5898248 | tf_op jit(solution)/shard_map/ppermute | solution.py:118
  308.0 92.2 %collective-permute-start.58 = (bf16[2,5,64,1536]{3,2,1,0:T(8,128)(2,1)}, bf16[2,5,64,1536]{3,2,1,0:T(8,128)(2,1)}, u32[]{:S(2)}, u32[]{:S(2)}) collective-permute-start(bf16[2,5,64,1536]{3,2,1,0:T(8,128)(2,1)} %dynamic-slice_bitcast_fusion), channel_id=1, source_target_pairs={{0,1},{1,0},{2,3},{3,2},{4,5},{5,4},{6,7},{7,6},{8,9},{9,8},{10,11... | collective-permute-start | bytes 5898248 | tf_op jit(solution)/shard_map/ppermute | solution.py:118
  316.3 149.7 %collective-permute-start.18 = (bf16[4,1536,256]{2,1,0:T(8,128)(2,1)}, bf16[4,1536,256]{2,1,0:T(8,128)(2,1)}, u32[]{:S(2)}, u32[]{:S(2)}) collective-permute-start(bf16[4,1536,256]{2,1,0:T(8,128)(2,1)} %slice.217), channel_id=1, source_target_pairs={{0,8},{8,0},{16,24},{24,16},{1,9},{9,1},{17,25},{25,17},{2,10},{10... | collective-permute-start | bytes 9437192 | tf_op jit(solution)/shard_map/ppermute | solution.py:56
  320.3 151.1 %collective-permute-start.13 = (bf16[4,1600,256]{2,1,0:T(8,128)(2,1)}, bf16[4,1600,256]{2,1,0:T(8,128)(2,1)}, u32[]{:S(2)}, u32[]{:S(2)}) collective-permute-start(bf16[4,1600,256]{2,1,0:T(8,128)(2,1)} %slice.206), channel_id=1, source_target_pairs={{0,8},{8,0},{16,24},{24,16},{1,9},{9,1},{17,25},{25,17},{2,10},{10... | collective-permute-start | bytes 9830408 | tf_op jit(solution)/shard_map/ppermute | solution.py:56
  327.6 96.6 %collective-permute-start.56 = (bf16[5,2,192,256]{3,2,1,0:T(8,128)(2,1)}, bf16[5,2,192,256]{3,2,1,0:T(8,128)(2,1)}, u32[]{:S(2)}, u32[]{:S(2)}) collective-permute-start(bf16[5,2,192,256]{3,2,1,0:T(8,128)(2,1)} %fusion.35), channel_id=1, source_target_pairs={{0,4},{2,6},{4,0},{6,2},{1,5},{3,7},{5,1},{7,3},{8,12},{10,14},{12... | collective-permute-start | bytes 2949128 | tf_op jit(solution)/shard_map/ppermute | solution.py:131
  361.9 80.0 %collective-permute-start.53 = (bf16[5,2,192,256]{3,2,0,1:T(8,128)(2,1)}, bf16[5,2,192,256]{3,2,0,1:T(8,128)(2,1)}, u32[]{:S(2)}, u32[]{:S(2)}) collective-permute-start(bf16[5,2,192,256]{3,2,0,1:T(8,128)(2,1)} %fusion.34), channel_id=1, source_target_pairs={{0,4},{2,6},{4,0},{6,2},{1,5},{3,7},{5,1},{7,3},{8,12},{10,14},{12... | collective-permute-start | bytes 2949128 | tf_op jit(solution)/shard_map/ppermute | solution.py:131
  405.2 57.2 %collective-permute-start.59 = (bf16[5,64,1536]{2,1,0:T(8,128)(2,1)}, bf16[5,64,1536]{2,1,0:T(8,128)(2,1)}, u32[]{:S(2)}, u32[]{:S(2)}) collective-permute-start(bf16[5,64,1536]{2,1,0:T(8,128)(2,1)} %fusion.36), channel_id=1, source_target_pairs={{0,4},{2,6},{4,0},{6,2},{1,5},{3,7},{5,1},{7,3},{8,12},{10,14},{12... | collective-permute-start | bytes 2949128 | tf_op jit(solution)/shard_map/ppermute | solution.py:131
  424.2 221.0 %collective-permute-start.26 = (bf16[384,256]{1,0:T(8,128)(2,1)}, bf16[384,256]{1,0:T(8,128)(2,1)}, u32[]{:S(2)}, u32[]{:S(2)}) collective-permute-start(bf16[384,256]{1,0:T(8,128)(2,1)} %get-tuple-element.173), channel_id=1, source_target_pairs={{16,0},{24,8},{0,16},{8,24},{17,1},{25,9},{1,17},{9,25},{18,2},{26... | collective-permute-start | bytes 589832 | tf_op jit(solution)/shard_map/ppermute | solution.py:52
  441.9 33.9 %collective-permute-start.57 = (bf16[5,192,256]{2,1,0:T(8,128)(2,1)S(1)}, bf16[5,192,256]{2,1,0:T(8,128)(2,1)S(1)}, u32[]{:S(2)}, u32[]{:S(2)}) collective-permute-start(bf16[5,192,256]{2,1,0:T(8,128)(2,1)S(1)} %fusion.55), channel_id=1, source_target_pairs={{0,2},{2,0},{4,6},{6,4},{1,3},{3,1},{5,7},{7,5},{8,10},{10,8},{12,... | collective-permute-start | bytes 1474568 | tf_op jit(solution)/shard_map/ppermute | solution.py:59
  471.4 28.8 %collective-permute-start.21 = (bf16[2,768,256]{2,1,0:T(8,128)(2,1)S(1)}, bf16[2,768,256]{2,1,0:T(8,128)(2,1)S(1)}, u32[]{:S(2)}, u32[]{:S(2)}) collective-permute-start(bf16[2,768,256]{2,1,0:T(8,128)(2,1)S(1)} %slice_bitcast_fusion.7), channel_id=1, source_target_pairs={{0,2},{2,0},{4,6},{6,4},{1,3},{3,1},{5,7},{7,5},{8,10},{10,8},{12,... | collective-permute-start | bytes 2359304 | tf_op jit(solution)/shard_map/ppermute | solution.py:59
  475.8 32.0 %collective-permute-start.14 = (bf16[2,800,256]{2,1,0:T(8,128)(2,1)S(1)}, bf16[2,800,256]{2,1,0:T(8,128)(2,1)S(1)}, u32[]{:S(2)}, u32[]{:S(2)}) collective-permute-start(bf16[2,800,256]{2,1,0:T(8,128)(2,1)S(1)} %slice_bitcast_fusion.4), channel_id=1, source_target_pairs={{0,16},{8,24},{16,0},{24,8},{1,17},{9,25},{17,1},{25,9},{2,18},{10... | collective-permute-start | bytes 2457608 | tf_op jit(solution)/shard_map/ppermute | solution.py:56
  483.4 34.4 %collective-permute-start.16 = (bf16[2,800,256]{2,1,0:T(8,128)(2,1)S(1)}, bf16[2,800,256]{2,1,0:T(8,128)(2,1)S(1)}, u32[]{:S(2)}, u32[]{:S(2)}) collective-permute-start(bf16[2,800,256]{2,1,0:T(8,128)(2,1)S(1)} %slice_bitcast_fusion.1), channel_id=1, source_target_pairs={{0,2},{2,0},{4,6},{6,4},{1,3},{3,1},{5,7},{7,5},{8,10},{10,8},{12,... | collective-permute-start | bytes 2457608 | tf_op jit(solution)/shard_map/ppermute | solution.py:59
  500.6 25.6 %collective-permute-start.20 = (bf16[768,256]{1,0:T(8,128)(2,1)S(1)}, bf16[768,256]{1,0:T(8,128)(2,1)S(1)}, u32[]{:S(2)}, u32[]{:S(2)}) collective-permute-start(bf16[768,256]{1,0:T(8,128)(2,1)S(1)} %fusion.59), channel_id=1, source_target_pairs={{0,2},{2,0},{4,6},{6,4},{1,3},{3,1},{5,7},{7,5},{8,10},{10,8},{12,... | collective-permute-start | bytes 1179656 | tf_op jit(solution)/shard_map/ppermute | solution.py:59
  500.8 25.6 %collective-permute-start.22 = (bf16[768,256]{1,0:T(8,128)(2,1)S(1)}, bf16[768,256]{1,0:T(8,128)(2,1)S(1)}, u32[]{:S(2)}, u32[]{:S(2)}) collective-permute-start(bf16[768,256]{1,0:T(8,128)(2,1)S(1)} %fusion.60), channel_id=1, source_target_pairs={{0,16},{8,24},{16,0},{24,8},{1,17},{9,25},{17,1},{25,9},{2,18},{10... | collective-permute-start | bytes 1179656 | tf_op jit(solution)/shard_map/ppermute | solution.py:56
  519.8 33.9 %collective-permute-start.15 = (bf16[800,256]{1,0:T(8,128)(2,1)S(1)}, bf16[800,256]{1,0:T(8,128)(2,1)S(1)}, u32[]{:S(2)}, u32[]{:S(2)}) collective-permute-start(bf16[800,256]{1,0:T(8,128)(2,1)S(1)} %fusion.56), channel_id=1, source_target_pairs={{0,2},{2,0},{4,6},{6,4},{1,3},{3,1},{5,7},{7,5},{8,10},{10,8},{12,... | collective-permute-start | bytes 1228808 | tf_op jit(solution)/shard_map/ppermute | solution.py:59
  547.2 62.9 %collective-permute-start.24 = (bf16[2,512,256]{2,1,0:T(8,128)(2,1)S(1)}, bf16[2,512,256]{2,1,0:T(8,128)(2,1)}, u32[]{:S(2)}, u32[]{:S(2)}) collective-permute-start(bf16[2,512,256]{2,1,0:T(8,128)(2,1)S(1)} %get-tuple-element.140), channel_id=1, source_target_pairs={{4,0},{6,2},{5,1},{7,3},{12,8},{14,10},{13,9},{15,11},{20,16},{22,... | collective-permute-start | bytes 1572872 | tf_op jit(solution)/shard_map/ppermute | solution.py:695
  553.7 57.9 %collective-permute-start.25 = (bf16[2,512,256]{2,1,0:T(8,128)(2,1)}, bf16[2,512,256]{2,1,0:T(8,128)(2,1)}, u32[]{:S(2)}, u32[]{:S(2)}) collective-permute-start(bf16[2,512,256]{2,1,0:T(8,128)(2,1)} %get-tuple-element.139), channel_id=1, source_target_pairs={{6,0},{7,1},{14,8},{15,9},{22,16},{23,17},{30,24},{31,25}} | collective-permute-start | bytes 1572872 | tf_op jit(solution)/shard_map/ppermute | solution.py:695
  559.6 91.2 %collective-permute-start.27 = (bf16[384,256]{1,0:T(8,128)(2,1)}, bf16[384,256]{1,0:T(8,128)(2,1)}, u32[]{:S(2)}, u32[]{:S(2)}) collective-permute-start(bf16[384,256]{1,0:T(8,128)(2,1)} %get-tuple-element.172), channel_id=1, source_target_pairs={{8,0},{0,8},{24,16},{16,24},{9,1},{1,9},{25,17},{17,25},{10,2},{2,... | collective-permute-start | bytes 589832 | tf_op jit(solution)/shard_map/ppermute | solution.py:52
  566.6 49.8 %collective-permute-start.29 = (bf16[1536,256]{1,0:T(8,128)(2,1)}, bf16[1536,256]{1,0:T(8,128)(2,1)S(1)}, u32[]{:S(2)}, u32[]{:S(2)}) collective-permute-start(bf16[1536,256]{1,0:T(8,128)(2,1)} %bitcast.42), channel_id=1, source_target_pairs={{16,0},{24,8},{0,16},{8,24},{17,1},{25,9},{1,17},{9,25},{18,2},{26... | collective-permute-start | bytes 2359304 | tf_op jit(solution)/shard_map/ppermute | solution.py:52
  610.1 32.1 %collective-permute-start.44 = (bf16[1568,256]{1,0:T(8,128)(2,1)}, bf16[1568,256]{1,0:T(8,128)(2,1)S(1)}, u32[]{:S(2)}, u32[]{:S(2)}) collective-permute-start(bf16[1568,256]{1,0:T(8,128)(2,1)} %pad_maximum_fusion.8), channel_id=1, source_target_pairs={{16,0},{24,8},{0,16},{8,24},{17,1},{25,9},{1,17},{9,25},{18,2},{26... | collective-permute-start | bytes 2408456 | tf_op jit(solution)/shard_map/ppermute | solution.py:52
  613.5 26.7 %collective-permute-start.35 = (bf16[1024,256]{1,0:T(8,128)(2,1)S(1)}, bf16[1024,256]{1,0:T(8,128)(2,1)S(1)}, u32[]{:S(2)}, u32[]{:S(2)}) collective-permute-start(bf16[1024,256]{1,0:T(8,128)(2,1)S(1)} %pad_maximum_fusion.12), channel_id=1, source_target_pairs={{16,0},{24,8},{0,16},{8,24},{17,1},{25,9},{1,17},{9,25},{18,2},{26... | collective-permute-start | bytes 1572872 | tf_op jit(solution)/shard_map/ppermute | solution.py:52
  619.2 37.5 %collective-permute-start.30 = (bf16[1536,512]{1,0:T(8,128)(2,1)}, bf16[1536,512]{1,0:T(8,128)(2,1)}, u32[]{:S(2)}, u32[]{:S(2)}) collective-permute-start(bf16[1536,512]{1,0:T(8,128)(2,1)} %pad_maximum_fusion.5), channel_id=1, source_target_pairs={{8,0},{0,8},{24,16},{16,24},{9,1},{1,9},{25,17},{17,25},{10,2},{2,... | collective-permute-start | bytes 4718600 | tf_op jit(solution)/shard_map/ppermute | solution.py:52
  662.6 24.1 %collective-permute-start.31 = (bf16[4,48,1536]{2,1,0:T(8,128)(2,1)}, bf16[4,48,1536]{2,1,0:T(8,128)(2,1)}, u32[]{:S(2)}, u32[]{:S(2)}) collective-permute-start(bf16[4,48,1536]{2,1,0:T(8,128)(2,1)} %fusion.53), channel_id=1, source_target_pairs={{0,1},{1,0},{2,3},{3,2},{4,5},{5,4},{6,7},{7,6},{8,9},{9,8},{10,11... | collective-permute-start | bytes 1769480 | tf_op jit(solution)/shard_map/ppermute | solution.py:118
  (129 other events, 2749.4 us)

commit v2 on v1

v2 whole, which is shorter than its diff:
```python
import functools

import jax
import jax.numpy as jnp
from jax import lax
from jax.experimental import pallas as pl
from jax.experimental.pallas import tpu as pltpu
from jax.sharding import PartitionSpec as P

HEADS = 24
KV_HEADS = 8
HEAD_DIM = 64
GROUP = HEADS // KV_HEADS


EPS = 1e-05
ROPE_BASE = 10000.0
NEG_LARGE = -1e30
F32 = jnp.float32
BF16 = jnp.bfloat16
LANES = 128


def cost(flops, bytes_accessed, transcendentals=0):
    scale = 64
    return pl.CostEstimate(
        flops=flops // scale,
        bytes_accessed=bytes_accessed // scale,
        transcendentals=transcendentals // scale,
    )


def rms_scale(values):
    return lax.rsqrt(jnp.mean(values * values, 0, keepdims=True) + EPS)


def norm_back(grad_out, values, scale, gain):
    weighted = gain * grad_out
    return scale * weighted - values * scale**3 * jnp.mean(weighted * values, 0, keepdims=True)


def mm(a, b, da, db):
    return lax.dot_general(a, b, (((da,), (db,)), ((), ())), preferred_element_type=F32)


class Comm:
    def __init__(self):
        self.n_expert = lax.axis_size("expert")
        self.n_context = lax.axis_size("context")
        self.n_dp = lax.axis_size("dp")
        self.cores = 2 if self.n_expert % 2 == 0 else 1
        self.columns = self.n_expert // self.cores
        self.share = 2 if self.n_context % 2 == 0 else 1

    def peer(self, i, k, j):
        column, core = divmod(i, self.cores)
        return ((column + k) % self.columns) * self.cores + (core + j) % self.cores

    def pull(self, value, k, j):
        pairs = [(self.peer(i, k, j), i) for i in range(self.n_expert)]
        return lax.ppermute(value, "expert", pairs)

    def push(self, value, k, j):
        pairs = [(i, self.peer(i, k, j)) for i in range(self.n_expert)]
        return lax.ppermute(value, "expert", pairs)

    def pair(self, value):
        return lax.ppermute(value, "context", [(i, i ^ 1) for i in range(self.n_context)])

    def from_core(self, blocks):
        arrays = [array for block in blocks for _, array, _ in block]
        moved = self.pull(jnp.concatenate(arrays) if len(arrays) > 1 else arrays[0], 0, 1)
        out, at = [], 0
        for block in blocks:
            pieces = []
            for row, array, _ in block:
                pieces.append((row, moved, at))
                at += array.shape[0]
            out.append(pieces)
        return out

    def gather_columns(self, value):
        return [value] + [self.pull(value, k, 0) for k in range(1, self.columns)]

    def gather_cores(self, near):
        if self.cores == 2:
            near = near + [self.pull(block, 0, 1) for block in near]
        return near

    def gather_expert(self, value):
        return self.gather_cores(self.gather_columns(value))

    def gather_group(self, value):
        columns = [self.pull(value, k, 0) for k in range(1, self.columns)]
        first = [[(0, value, 0)]] + [[(0, block, 0)] for block in columns]
        far = []
        if self.share == 2:
            half = value.shape[0] // 2
            across = self.pair(value)
            first.append([(0, across, 0)])
            for k in range(1, self.columns):
                top = self.pull(across[:half], k, 0)
                bottom = self.pair(columns[k - 1][half:])
                far.append([(0, top, 0), (half, bottom, 0)])
        blocks = first + far
        if self.cores == 2:
            blocks = blocks + self.from_core(first)
            blocks = blocks + (self.from_core(far) if far else [])
        return blocks

    def return_hops(self, near, other):
        columns = self.columns
        shape = (self.share, columns) + near.shape[1:]
        arrays = [x.reshape(shape) for x in (near, other) if x is not None]

        def part(*at):
            return sum(array[at].astype(F32) for array in arrays)

        if self.share == 1:
            sent = [self.push(part(0, k).astype(BF16), k, 0) for k in range(1, columns)]
            return [part(0, 0)] + sent
        half = near.shape[1] // 2
        low, high = slice(0, half), slice(half, 2 * half)
        every = slice(None)
        by_column = [
            self.push(part(every, k, low).astype(BF16), k, 0) for k in range(1, columns)
        ]
        by_pair = self.pair(part(1, every, high).astype(BF16))
        return [part(every, 0, low)] + by_column + [part(0, every, high), by_pair]

    def return_last(self, terms):
        columns = self.columns
        if self.share == 1:
            return sum(term.astype(F32) for term in terms)
        top = terms[:columns]
        bottom = terms[columns : columns + 2]

        def total(parts, at):
            return sum(part[at].astype(F32) for part in parts)

        top_other = self.pair(total(top, 1).astype(BF16))
        others = [
            self.push(total(bottom, k).astype(BF16), k, 0).astype(F32)
            for k in range(1, columns)
        ]
        return jnp.concatenate(
            [total(top, 0) + top_other.astype(F32), sum(others, total(bottom, 0))]
        )

    def send_dp(self, parts):
        n = self.n_dp
        return [
            lax.ppermute(parts[s - 1], "dp", [(i, (i + s) % n) for i in range(n)])
            for s in range(1, n)
        ]

    def send_context(self, parts, stride):
        n = self.n_context // stride
        out = []
        for s in range(1, n):
            pairs = []
            for i in range(self.n_context):
                k, r = divmod(i, stride)
                pairs.append((i, ((k + s) % n) * stride + r))
            out.append(lax.ppermute(parts[s - 1], "context", pairs))
        return out

    def scatter_rows(self, left, right, width):
        n, m = self.n_context, self.n_dp
        c, d = lax.axis_index("context"), lax.axis_index("dp")
        size = left[0].shape[0] // (n * m)
        if size % 16 == 0:
            mine, *parts = row_products(jnp.stack([c, d]), left, right, width, n, m)
        else:
            local = sum(mm(a, b[:width], 1, 1) for a, b in zip(left, right))
            local = local.reshape(n, m, size, width)
            local = jnp.stack(
                [lax.dynamic_index_in_dim(local, (c + k) % n, 0, False) for k in range(n)]
            )
            mine, *parts = [
                lax.dynamic_index_in_dim(local, (d + s) % m, 1, False) for s in range(m)
            ]
        came = self.send_dp([part.astype(BF16) for part in parts])

        def of_context(k):
            return mine[k].astype(F32) + sum(x[k].astype(F32) for x in came)

        came_far = self.send_context([of_context(k).astype(BF16) for k in range(1, n)], 1)
        return of_context(0) + sum(x.astype(F32) for x in came_far)


def row_products_kernel(count, place_ref, *refs):
    left, right, outs, total_s = refs[:count], refs[count : 2 * count], refs[2 * count : -1], refs[-1]
    width = total_s.shape[1]
    total = mm(left[0][...], right[0][:width, :], 1, 1)
    for a, b in zip(left[1:], right[1:]):
        total = total + mm(a[...], b[:width, :], 1, 1)
    total_s[...] = total
    n, size, _ = outs[0].shape
    m = len(outs)
    for k in range(n):
        for s in range(m):
            owner = lax.rem(place_ref[0] + k, n) * m + lax.rem(place_ref[1] + s, m)
            rows = pl.ds(pl.multiple_of(owner * size, size), size)
            outs[s][k] = total_s[rows, :].astype(outs[s].dtype)


def row_products(place, left, right, width, n, m):
    rows = left[0].shape[0]
    size = rows // (n * m)

    def whole(shape):
        return pl.BlockSpec(shape, lambda i, p: (0,) * len(shape))

    return pl.pallas_call(
        functools.partial(row_products_kernel, len(left)),
        out_shape=tuple(
            jax.ShapeDtypeStruct((n, size, width), BF16 if s else F32) for s in range(m)
        ),
        grid_spec=pltpu.PrefetchScalarGridSpec(
            num_scalar_prefetch=1,
            grid=(1,),
            in_specs=[whole(x.shape) for x in left + right],
            out_specs=tuple(whole((n, size, width)) for _ in range(m)),
            scratch_shapes=[pltpu.VMEM((rows, width), F32)],
        ),
        compiler_params=pltpu.CompilerParams(vmem_limit_bytes=32 << 20),
        cost_estimate=cost(
            flops=2 * rows * width * right[0].shape[1] * len(left),
            bytes_accessed=8 * width * right[0].shape[1] + 6 * rows * width,
        ),
        name="row_products",
    )(place, *left, *right)


def attn_fwd_kernel(blocks, c_ref, q_ref, *refs):
    k_refs, v_refs = refs[:blocks], refs[blocks : 2 * blocks]
    o_ref, ob_ref, lse_ref, scores_ref = refs[2 * blocks :]
    c = c_ref[0]
    n = q_ref.shape[1]
    hd = HEAD_DIM
    for s in range(blocks):
        rows = slice(s * n, (s + 1) * n)

        def fill(s=s, rows=rows):
            for g in range(GROUP):
                scores = mm(k_refs[s][...], q_ref[g * hd : (g + 1) * hd, :], 0, 0)
                if s == 0:
                    key = lax.broadcasted_iota(jnp.int32, scores.shape, 0)
                    query = lax.broadcasted_iota(jnp.int32, scores.shape, 1)
                    scores = jnp.where(key <= query, scores, NEG_LARGE)
                scores_ref[g, rows, :] = scores

        def blank(rows=rows):
            for g in range(GROUP):
                scores_ref[g, rows, :] = jnp.full((n, n), NEG_LARGE, F32)

        if s == 0:
            fill()
        else:
            pl.when(c >= s)(fill)
            pl.when(c < s)(blank)
    lse_ref[...] = jnp.zeros_like(lse_ref)
    for g in range(GROUP):
        scores = scores_ref[g]
        top = jnp.max(scores, 0, keepdims=True)
        weights = jnp.exp(scores - top)
        total = jnp.sum(weights, 0, keepdims=True)
        weights = weights.astype(BF16)
        out = jnp.zeros((hd, n), F32)
        for s in range(blocks):
            out = out + mm(v_refs[s][...], weights[s * n : (s + 1) * n], 1, 0)
        out = out / total
        o_ref[g * hd : (g + 1) * hd, :] = out
        ob_ref[g * hd : (g + 1) * hd, :] = out.astype(BF16)
        lse_ref[0, g : g + 1, :] = top + jnp.log(total)


def kv_specs(blocks, n, first=0):
    keys = [pl.BlockSpec((HEAD_DIM, n), lambda h, c: (first + h, 0))] * blocks
    values = [pl.BlockSpec((HEAD_DIM, n), lambda h, c: (first + h + KV_HEADS, 0))] * blocks
    return keys + values


def attention_forward(context_index, query_t, kv_blocks):
    blocks = len(kv_blocks)
    n = query_t.shape[1]
    wide = GROUP * HEAD_DIM
    heads = query_t.shape[0] // wide
    head = pl.BlockSpec((wide, n), lambda h, c: (h, 0))
    return pl.pallas_call(
        functools.partial(attn_fwd_kernel, blocks),
        out_shape=(
            jax.ShapeDtypeStruct(query_t.shape, F32),
            jax.ShapeDtypeStruct(query_t.shape, BF16),
            jax.ShapeDtypeStruct((heads, 8, n), F32),
        ),
        grid_spec=pltpu.PrefetchScalarGridSpec(
            num_scalar_prefetch=1,
            grid=(heads,),
            in_specs=[head] + kv_specs(blocks, n),
            out_specs=(head, head, pl.BlockSpec((1, 8, n), lambda h, c: (h, 0, 0))),
            scratch_shapes=[pltpu.VMEM((GROUP, blocks * n, n), F32)],
        ),
        compiler_params=pltpu.CompilerParams(vmem_limit_bytes=40 << 20),
        cost_estimate=cost(
            flops=heads * GROUP * blocks * n * n * 256 * 4,
            transcendentals=heads * GROUP * blocks * n * n,
            bytes_accessed=16 * query_t.size,
        ),
        name="attn_fwd",
    )(context_index.reshape(1), query_t, *kv_blocks, *kv_blocks)


def attn_bwd_kernel(blocks, c_ref, q_ref, do_ref, o_ref, lse_ref, *refs):
    k_refs, v_refs = refs[:blocks], refs[blocks : 2 * blocks]
    dq_ref, dkv_ref = refs[2 * blocks :]
    c = c_ref[0]
    n = q_ref.shape[1]
    hd = HEAD_DIM
    deltas = []
    for g in range(GROUP):
        head = slice(g * hd, (g + 1) * hd)
        both = do_ref[head, :].astype(F32) * o_ref[head, :]
        deltas.append(jnp.sum(both, 0, keepdims=True))
    for s in range(blocks):

        def work(s=s):
            dk = jnp.zeros((hd, n), F32)
            dv = jnp.zeros((hd, n), F32)
            key_t = k_refs[s][...]
            value_t = v_refs[s][...]
            for g in range(GROUP):
                head = slice(g * hd, (g + 1) * hd)
                query, grad = q_ref[head, :], do_ref[head, :]
                scores = mm(key_t, query, 0, 0)
                weights = jnp.exp(scores - lse_ref[0, g : g + 1, :])
                if s == 0:
                    key = lax.broadcasted_iota(jnp.int32, scores.shape, 0)
                    place = lax.broadcasted_iota(jnp.int32, scores.shape, 1)
                    weights = jnp.where(key <= place, weights, 0.0)
                grad_weights = mm(value_t, grad, 0, 0)
                grad_scores = (weights * (grad_weights - deltas[g])).astype(BF16)
                dv = dv + mm(grad, weights.astype(BF16), 1, 1)
                dk = dk + mm(query, grad_scores, 1, 1)
                step = mm(key_t, grad_scores, 1, 0) * (HEAD_DIM**-0.5)
                if s == 0:
                    dq_ref[head, :] = step
                else:
                    dq_ref[head, :] += step
            owner = lax.rem(c - s + blocks, blocks)
            dkv_ref[owner, 0] = dk.astype(BF16)
            dkv_ref[owner, 1] = dv.astype(BF16)

        def skip(s=s):
            owner = lax.rem(c - s + blocks, blocks)
            dkv_ref[owner] = jnp.zeros(dkv_ref.shape[1:], BF16)

        if s == 0:
            work()
        else:
            pl.when(c >= s)(work)
            pl.when(c < s)(skip)


def attention_backward(context_index, query_t, grad_t, out_t, lse, kv_blocks, first, heads):
    blocks = len(kv_blocks)
    n = query_t.shape[1]
    wide = GROUP * HEAD_DIM
    head = pl.BlockSpec((wide, n), lambda h, c: (first + h, 0))
    out = pl.BlockSpec((wide, n), lambda h, c: (h, 0))
    return pl.pallas_call(
        functools.partial(attn_bwd_kernel, blocks),
        out_shape=(
            jax.ShapeDtypeStruct((heads * wide, n), F32),
            jax.ShapeDtypeStruct((blocks, 2, heads * HEAD_DIM, n), BF16),
        ),
        grid_spec=pltpu.PrefetchScalarGridSpec(
            num_scalar_prefetch=1,
            grid=(heads,),
            in_specs=[head, head, head, pl.BlockSpec((1, 8, n), lambda h, c: (first + h, 0, 0))]
            + kv_specs(blocks, n, first),
            out_specs=(
                out,
                pl.BlockSpec((blocks, 2, HEAD_DIM, n), lambda h, c: (0, 0, h, 0)),
            ),
        ),
        compiler_params=pltpu.CompilerParams(vmem_limit_bytes=40 << 20),
        cost_estimate=cost(
            flops=heads * GROUP * blocks * n * n * 256 * 10,
            transcendentals=heads * GROUP * blocks * n * n,
            bytes_accessed=20 * query_t.size,
        ),
        name="attn_bwd",
    )(context_index.reshape(1), query_t, grad_t, out_t, lse, *kv_blocks, *kv_blocks)


def rope_tables(positions):
    half_dim = HEAD_DIM // 2
    frequency = ROPE_BASE ** (-2.0 * jnp.arange(half_dim, dtype=F32) / HEAD_DIM)
    angles = frequency[:, None] * positions.astype(F32)[None, :]
    return jnp.cos(angles), jnp.sin(angles)


def rotate_t(values_t, cosine, sine):
    shaped = values_t.reshape(-1, 2, HEAD_DIM // 2, values_t.shape[1])
    low, high = shaped[:, 0], shaped[:, 1]
    turned = jnp.stack([low * cosine - high * sine, high * cosine + low * sine], 1)
    return turned.reshape(values_t.shape)


def prepare_kernel(p_ref, gate_ref, up_ref, down_ref, *outs):
    in_t_ref, gate_out, up_out, down_out, down_t_out = outs
    gate, up, down = gate_ref[0], up_ref[0], down_ref[0]
    in_t_ref[0, 0, 0] = gate.astype(F32).T.astype(BF16)
    in_t_ref[0, 1, 0] = up.astype(F32).T.astype(BF16)
    gate_out[...] = gate
    up_out[...] = up
    down_out[...] = down
    down_t_out[...] = down.astype(F32).T.astype(BF16)


def prepare_weights(parity, w_gate, w_up, w_down, chunk, share):
    experts, width, hidden = w_gate.shape
    chunks = hidden // chunk // share
    units = chunks * chunk

    def column(e, q, p):
        return (e, 0, q * share + p[0])

    def flat(e, q, p):
        return (0, e * chunks + q)

    return pl.pallas_call(
        prepare_kernel,
        out_shape=(
            jax.ShapeDtypeStruct((experts, 2, chunks, chunk, width), BF16),
            jax.ShapeDtypeStruct((width, experts * units), BF16),
            jax.ShapeDtypeStruct((width, experts * units), BF16),
            jax.ShapeDtypeStruct((experts * units, width), BF16),
            jax.ShapeDtypeStruct((width, experts * units), BF16),
        ),
        grid_spec=pltpu.PrefetchScalarGridSpec(
            num_scalar_prefetch=1,
            grid=(experts, chunks),
            in_specs=[
                pl.BlockSpec((1, width, chunk), column),
                pl.BlockSpec((1, width, chunk), column),
                pl.BlockSpec((1, chunk, width), lambda e, q, p: (e, q * share + p[0], 0)),
            ],
            out_specs=(
                pl.BlockSpec((1, 2, 1, chunk, width), lambda e, q, p: (e, 0, q, 0, 0)),
                pl.BlockSpec((width, chunk), flat),
                pl.BlockSpec((width, chunk), flat),
                pl.BlockSpec((chunk, width), lambda e, q, p: (e * chunks + q, 0)),
                pl.BlockSpec((width, chunk), flat),
            ),
        ),
        compiler_params=pltpu.CompilerParams(vmem_limit_bytes=60 << 20),
        cost_estimate=cost(
            flops=0, transcendentals=0, bytes_accessed=18 * experts * width * units
        ),
        name="prepare_weights",
    )(parity.reshape(1), w_gate, w_up, w_down)


def piece_copies(blocks, refs, target_ref, sems):
    out, at = [], 0
    count = refs[0].shape[1]
    for b, pieces in enumerate(blocks):
        copies = []
        for i, (first, ref, row) in enumerate(pieces):
            last = pieces[i + 1][0] if i + 1 < len(pieces) else target_ref.shape[0]
            copies.append(
                pltpu.make_async_copy(
                    refs[ref].at[row : row + last - first],
                    target_ref.at[first:last, b * count : (b + 1) * count],
                    sems.at[at],
                )
            )
            at += 1
        out.append(copies)
    return out


def write_grads(rows_ref, cots_ref, act, dgate, dup, place_ref, outs, down_s, in_s, share):
    owners = len(outs)
    chunks, _, _, units = outs[0].shape
    width = rows_ref.shape[0]
    size = units // chunks // owners
    tiles = width // units

    def place(k, s):
        return lax.rem(place_ref[2] + k, chunks), lax.rem(place_ref[1] + s, owners)

    down_s[...] = mm(act, cots_ref[...], 1, 1).astype(BF16)
    for k in range(chunks):
        for s in range(owners):
            at_k, at_d = place(k, s)
            start = pl.multiple_of((at_k * owners + at_d) * size, size)
            for t in range(tiles):
                outs[s][k, 0, t * size : (t + 1) * size, :] = down_s[
                    pl.ds(start, size), t * units : (t + 1) * units
                ]
    base = tiles * size
    size = width // (chunks * share * owners)
    for grad_act in (dgate, dup):
        in_s[...] = mm(rows_ref[...], grad_act, 1, 1).astype(BF16)
        for k in range(chunks):
            for q in range(share):
                for s in range(owners):
                    at_k, at_d = place(k, s)
                    start = pl.multiple_of(((at_k * share + q) * owners + at_d) * size, size)
                    to = base + q * size
                    outs[s][k, 0, to : to + size, :] = in_s[pl.ds(start, size), :]
        base += share * size


class Experts:
    def __init__(self, rows, cots, width, units, share, chunks, owners):
        self.arrays, self.plans = [], []
        for blocks in (rows, cots):
            arrays, plan = [], []
            for block in blocks:
                pieces = []
                for first, array, row in block:
                    known = [i for i, x in enumerate(arrays) if x is array]
                    if not known:
                        arrays.append(array)
                    pieces.append((first, known[0] if known else len(arrays) - 1, row))
                plan.append(pieces)
            self.arrays.append(arrays)
            self.plans.append(plan)
        self.blocks = len(rows)
        self.width, self.count = width, rows[0][0][1].shape[1]
        self.tokens = self.blocks * self.count
        self.units, self.share, self.chunks, self.owners = units, share, chunks, owners
        self.height = self.width // chunks // owners * 3

    def n_arrays(self):
        return sum(map(len, self.arrays))

    def scratch(self):
        wide = pltpu.VMEM((self.width, self.tokens), BF16)
        sems = [pltpu.SemaphoreType.DMA((sum(map(len, plan)),)) for plan in self.plans]
        return [wide, wide] + sems

    def copies(self, refs, rows_ref, cots_ref, row_sems, cot_sems):
        n = len(self.arrays[0])
        row_copies = piece_copies(self.plans[0], refs[:n], rows_ref, row_sems)
        cot_copies = piece_copies(self.plans[1], refs[n:], cots_ref, cot_sems)
        return [a + b for a, b in zip(row_copies, cot_copies)]

    def grads_structs(self, n):
        shape = (self.chunks, n, self.height, self.units)
        spec = pl.BlockSpec(
            (self.chunks, 1, self.height, self.units), lambda i, *_: (0, i, 0, 0)
        )
        return [jax.ShapeDtypeStruct(shape, BF16)] * self.owners, [spec] * self.owners

    def act_kernel(self, first, n, make_gates, e_ref, *refs):
        n_arrays = self.n_arrays()
        kept_ref, scales_ref, in_t_ref, down_ref = refs[:4]
        piece_refs, outs, scratch = refs[4 : 4 + n_arrays], refs[4 + n_arrays : -6], refs[-6:]
        if make_gates:
            chosen_ref = scales_ref
            gates_ref, scales_ref = outs[:2]
            outs = outs[2:]
        act_ref, dgate_ref, dup_ref, dscale_ref = outs[:4]
        rows_ref, cots_ref = scratch[:2]
        units, count, blocks = self.units, self.count, self.blocks
        copies = self.copies(piece_refs, *scratch[:4])
        step = pl.program_id(0)
        row = e_ref[0] + first + step

        def move(wait, start):
            def run():
                for b in start:
                    for copy in copies[b] if b < blocks else ():
                        copy.start()
                for copy in copies[wait]:
                    copy.wait()

            if n == 1:
                run()
            else:
                pl.when(step == 0)(run)

        def products(b):
            move(b, (0, 1, 2) if b == 0 else (b + 2,))
            cols = slice(b * count, (b + 1) * count)
            acts = jnp.dot(in_t_ref[...], rows_ref[:, cols], preferred_element_type=F32)
            grad = jnp.dot(down_ref[...], cots_ref[:, cols], preferred_element_type=F32)
            return acts, grad

        def finish(b, acts, grad):
            cols = slice(b * count, (b + 1) * count)
            gate, up = acts[:units], acts[units : 2 * units]
            if make_gates:
                chosen = chosen_ref[:, cols] > 0
                logits = jnp.where(chosen, acts[2 * units :], NEG_LARGE)
                gates = jnp.exp(logits - jnp.max(logits, 0, keepdims=True))
                gates = jnp.where(chosen, gates, 0.0)
                gates = gates / jnp.sum(gates, 0, keepdims=True)
                gates_ref[:, cols] = gates
                scales_ref[:, cols] = gates * kept_ref[:, cols]
            scale = scales_ref[pl.ds(row, 1), cols]
            keep = kept_ref[pl.ds(row, 1), cols]
            sigmoid = jax.nn.sigmoid(gate)
            silu = gate * sigmoid
            hidden = silu * up
            dscale_ref[0, 0:1, cols] = keep * jnp.sum(hidden * grad, 0, keepdims=True)
            act_ref[:, cols] = (hidden * scale).astype(BF16)
            grad = grad * scale
            dup_ref[:, cols] = (grad * silu).astype(BF16)
            dgate_ref[:, cols] = (grad * up * (sigmoid + silu * (1.0 - sigmoid))).astype(BF16)

        dscale_ref[...] = jnp.zeros_like(dscale_ref)
        ready = products(0)
        for b in range(blocks):
            done = ready
            if b + 1 < blocks:
                ready = products(b + 1)
            finish(b, *done)
        write_grads(
            rows_ref,
            cots_ref,
            act_ref[...],
            dgate_ref[...],
            dup_ref[...],
            e_ref,
            outs[4:],
            *scratch[4:],
            self.share,
        )

    def act(self, places, first, n, kept, scales, in_t, down, make_gates=False):
        units, width, tokens = self.units, self.width, self.tokens
        lanes = kept.shape[0]
        in_rows = 2 * units + (lanes if make_gates else 0)
        table = pl.BlockSpec((lanes, tokens), lambda i, e: (0, 0))
        one = pl.BlockSpec((units, tokens), lambda i, e: (i, 0))
        outs, specs = [], []
        if make_gates:
            outs += [jax.ShapeDtypeStruct((lanes, tokens), F32)] * 2
            specs += [table] * 2
        outs += [jax.ShapeDtypeStruct((n * units, tokens), BF16)] * 3
        specs += [one] * 3
        outs.append(jax.ShapeDtypeStruct((n, 8, tokens), F32))
        specs.append(pl.BlockSpec((1, 8, tokens), lambda i, e: (i, 0, 0)))
        structs, grad_specs = self.grads_structs(n)
        extra = [pltpu.VMEM((units, width), BF16), pltpu.VMEM((width, units), BF16)]
        return pl.pallas_call(
            functools.partial(self.act_kernel, first, n, make_gates),
            out_shape=tuple(outs + structs),
            grid_spec=pltpu.PrefetchScalarGridSpec(
                num_scalar_prefetch=1,
                grid=(n,),
                in_specs=[
                    table,
                    table,
                    pl.BlockSpec((in_rows, width), lambda i, e: (first + i, 0)),
                    pl.BlockSpec((units, width), lambda i, e: (first + i, 0)),
                ]
                + [pl.BlockSpec(memory_space=pl.ANY)] * self.n_arrays(),
                out_specs=tuple(specs + grad_specs),
                scratch_shapes=self.scratch() + extra,
            ),
            compiler_params=pltpu.CompilerParams(vmem_limit_bytes=60 << 20),
            cost_estimate=cost(
                flops=12 * width * units * tokens * n,
                transcendentals=units * tokens * n,
                bytes_accessed=4 * width * tokens + 6 * n * units * (width + tokens),
            ),
            name="experts_act",
        )(places, kept, scales, in_t, down, *self.arrays[0], *self.arrays[1])

    def out_kernel(self, parts, e_ref, weight_ref, *refs):
        act_refs, dscale_refs = refs[:parts], refs[parts : 2 * parts]
        message_ref, act_s, dscale_s = refs[2 * parts :]
        at = row = 0
        dscale_s[...] = jnp.zeros_like(dscale_s)
        for act_ref, dscale_ref in zip(act_refs, dscale_refs):
            act_s[at : at + act_ref.shape[0], :] = act_ref[...]
            at += act_ref.shape[0]
            for i in range(dscale_ref.shape[0]):
                dscale_s[pl.ds(e_ref[0] + row, 1), :] = dscale_ref[i, 0:1, :]
                row += 1
        width, lanes = self.width, dscale_s.shape[0]
        message_ref[0, :width, :] = jnp.dot(
            weight_ref[...], act_s[...], preferred_element_type=F32
        ).astype(BF16)
        grads = dscale_s[...]
        high = grads.astype(BF16)
        message_ref[0, width : width + lanes, :] = high
        message_ref[0, width + lanes :, :] = (grads - high.astype(F32)).astype(BF16)

    def out(self, places, lanes, weight, acts, dscales, first_block, n_blocks):
        rows = weight.shape[1]
        parts = len(acts)
        width, count = self.width, self.count

        def column(shape):
            return pl.BlockSpec(
                shape, lambda b, e: (0,) * (len(shape) - 1) + (first_block + b,)
            )

        return pl.pallas_call(
            functools.partial(self.out_kernel, parts),
            out_shape=jax.ShapeDtypeStruct((n_blocks, width + 2 * lanes, count), BF16),
            grid_spec=pltpu.PrefetchScalarGridSpec(
                num_scalar_prefetch=1,
                grid=(n_blocks,),
                in_specs=[
                    pl.BlockSpec(
                        (width, rows),
                        lambda b, e: (0, 0),
                        pipeline_mode=pl.Buffered(buffer_count=1),
                    )
                ]
                + [column((a.shape[0], count)) for a in acts]
                + [column((a.shape[0], 8, count)) for a in dscales],
                out_specs=pl.BlockSpec((1, width + 2 * lanes, count), lambda b, e: (b, 0, 0)),
                scratch_shapes=[pltpu.VMEM((rows, count), BF16), pltpu.VMEM((lanes, count), F32)],
            ),
            compiler_params=pltpu.CompilerParams(vmem_limit_bytes=60 << 20),
            cost_estimate=cost(
                flops=2 * width * rows * count * n_blocks,
                transcendentals=0,
                bytes_accessed=2 * width * rows + 4 * width * count * n_blocks,
            ),
            name="experts_out",
        )(places, weight, *acts, *dscales)

    def back_kernel(self, parts, gate_w_ref, up_w_ref, *refs):
        dgate_refs, dup_refs = refs[:parts], refs[parts : 2 * parts]
        back_ref, dgate_s, dup_s = refs[2 * parts :]
        for target, pieces in ((dgate_s, dgate_refs), (dup_s, dup_refs)):
            at = 0
            for piece in pieces:
                target[at : at + piece.shape[0], :] = piece[...]
                at += piece.shape[0]
        back = jnp.dot(gate_w_ref[...], dgate_s[...], preferred_element_type=F32)
        back = back + jnp.dot(up_w_ref[...], dup_s[...], preferred_element_type=F32)
        back_ref[0] = back.astype(BF16)

    def back(self, gate_w, up_w, dgates, dups, first_block, n_blocks):
        width, count = self.width, self.count
        rows = gate_w.shape[1]
        parts = len(dgates)
        whole = pl.BlockSpec(
            (width, rows), lambda b: (0, 0), pipeline_mode=pl.Buffered(buffer_count=1)
        )
        column = [pl.BlockSpec((a.shape[0], count), lambda b: (0, first_block + b)) for a in dgates]
        return pl.pallas_call(
            functools.partial(self.back_kernel, parts),
            out_shape=jax.ShapeDtypeStruct((n_blocks, width, count), BF16),
            grid=(n_blocks,),
            in_specs=[whole, whole] + column * 2,
            out_specs=pl.BlockSpec((1, width, count), lambda b: (b, 0, 0)),
            scratch_shapes=[pltpu.VMEM((rows, count), BF16)] * 2,
            compiler_params=pltpu.CompilerParams(vmem_limit_bytes=60 << 20),
            cost_estimate=cost(
                flops=4 * width * rows * count * n_blocks,
                transcendentals=0,
                bytes_accessed=4 * width * rows + 4 * width * count * n_blocks,
            ),
            name="experts_back",
        )(gate_w, up_w, *dgates, *dups)


def body(
    tokens,
    routes,
    cotangent,
    norm_attn,
    w_query,
    w_key,
    w_value,
    w_out,
    norm_ffn,
    w_router,
    w_gate,
    w_up,
    w_down,
):
    comm = Comm()
    hold = lax.optimization_barrier
    count, width = tokens.shape[1], tokens.shape[2]
    top_k = routes.shape[2]
    n_experts, _, hidden_units = w_gate.shape
    all_experts = n_experts * comm.n_expert
    capacity = (9 * count * top_k + 8 * all_experts - 1) // (8 * all_experts)
    n_context, n_dp, share = comm.n_context, comm.n_dp, comm.share
    expert_index = lax.axis_index("expert")
    context_index = lax.axis_index("context")
    dp_index = lax.axis_index("dp")
    parity = context_index % share
    chunks = n_context // share
    units = hidden_units // share
    lanes = -(-all_experts // 32) * 32
    places = jnp.stack([expert_index * n_experts, dp_index, context_index // share])

    hidden = tokens[0].T.astype(F32)
    gain_attn = norm_attn.astype(F32)[:, None]
    gain_ffn = norm_ffn.astype(F32)[:, None]
    scale_attn = rms_scale(hidden)
    normed_attn = (hidden * scale_attn * gain_attn).astype(BF16)
    positions = context_index * count + jnp.arange(count, dtype=jnp.int32)
    cosine, sine = rope_tables(positions)
    key_t = rotate_t(mm(w_key, normed_attn, 0, 0), cosine, sine).astype(BF16)
    value_t = mm(w_value, normed_attn, 0, 0).astype(BF16)
    kv_width = key_t.shape[0]
    kv_own = jnp.concatenate([key_t, value_t], 0)
    kv_blocks = [kv_own]
    for s in range(1, n_context):
        pairs = [(i, i + s) for i in range(n_context - s)]
        kv_blocks.append(lax.ppermute(kv_own, "context", pairs))
    query_t = rotate_t(mm(w_query, normed_attn, 0, 0), cosine, sine)
    query_t = (query_t * HEAD_DIM**-0.5).astype(BF16)

    cot_t = cotangent[0].T
    routed = (
        routes[0].T[:, None, :] == jnp.arange(lanes, dtype=jnp.int32)[None, :, None]
    ).astype(F32)
    cot_message = jnp.concatenate([cot_t, routed.sum(0).astype(BF16)])
    cots = [cot_message] + [comm.pull(cot_message, k, 0) for k in range(1, comm.columns)]
    weights = prepare_weights(parity, w_gate, w_up, w_down, hidden_units // n_context, share)
    router_t = jnp.zeros((lanes, width), BF16).at[:all_experts].set(w_router.T)
    in_t, gate_w, up_w, down, down_t = weights
    in_t = in_t.reshape(n_experts * 2 * units, width)
    in_first = jnp.concatenate([in_t[: 2 * units], router_t])
    far = []
    if share == 2:
        across = comm.pair(cot_message)
        cots, across, in_t, in_first = hold((cots, across, in_t, in_first))
        far = [comm.pull(across, k, 0) for k in range(1, comm.columns)]
        cots = cots + [across]
    cots, far = [[[(0, x, 0)] for x in part] for part in (cots, far)]
    others = comm.from_core(cots) if comm.cores == 2 else []
    kv_blocks, in_t, in_first, gate_w, up_w, down, down_t = hold(
        (kv_blocks, in_t, in_first, gate_w, up_w, down, down_t)
    )
    out_t, out_low, lse = attention_forward(context_index, query_t, kv_blocks)
    middle = hidden + mm(w_out, out_low, 0, 0)
    scale_ffn = rms_scale(middle)
    normed_ffn = (middle * scale_ffn * gain_ffn).astype(BF16)
    if comm.cores == 2 and far:
        far_arrays, normed_ffn = hold(([block[0][1] for block in far], normed_ffn))
        far = [[(0, array, 0)] for array in far_arrays]
        others = others + comm.from_core(far)
    cots = cots + far + others
    rows = comm.gather_group(normed_ffn)

    routed_all = jnp.concatenate(
        [block[0][1][block[0][2] + width : block[0][2] + width + lanes] for block in cots]
    )
    n_blocks = len(cots)
    before = jnp.triu(jnp.ones((count, count), BF16), 1)
    ranking = mm(routed_all, before, 1, 0)
    chosen = routed_all.astype(F32)
    kept = jnp.where(ranking < capacity, chosen, 0.0)

    def side_by_side(array):
        array = array.reshape(n_blocks, lanes, count)
        return jnp.concatenate([array[b] for b in range(n_blocks)], 1)

    chosen, kept = side_by_side(chosen), side_by_side(kept)

    row_count = width // comm.n_expert

    def to_experts(*arrays):
        blocks = []
        for j in range(comm.cores):
            for k in range(comm.columns):
                column, core = expert_index // comm.cores, expert_index % comm.cores
                column = (column - k) % comm.columns
                target = column * comm.cores + (core + j) % comm.cores
                pieces = jnp.concatenate(
                    [
                        lax.dynamic_slice_in_dim(array, target * row_count, row_count, 0)
                        for array in arrays
                    ]
                )
                blocks.append(pieces if (j, k) == (0, 0) else comm.pull(pieces, k, j))
        return blocks

    own = Experts(rows, cots, width, units, share, chunks, n_dp)
    groups, at = [], 0
    for n in (1, (n_experts - 1) // 2, n_experts - 1 - (n_experts - 1) // 2):
        if n:
            groups.append((at, n))
            at += n
    acts, dgates, dups, dscales, kept_parts, arrived, crossing = ([] for _ in range(7))
    scales = None

    def pass_on(g, values):
        if g >= len(groups):
            return values
        terms, values = hold((arrived[g], values))
        terms = [kept_parts[g]] + terms

        def part(k):
            return sum(term[k].astype(F32) for term in terms)

        sent = comm.send_context([part(k).astype(BF16) for k in range(1, chunks)], share)
        crossing.append([part(0).astype(BF16)] + sent)
        return values

    for g, (first, n) in enumerate(groups):
        if g == 0:
            gates_all, scales, *done = own.act(
                places, first, n, kept, chosen, in_first, down, make_gates=True
            )
        else:
            done = own.act(places, first, n, kept, scales, in_t, down)
        for target, value in zip((acts, dgates, dups, dscales, kept_parts), done):
            target.append(value)
        arrived.append(comm.send_dp(done[5:]))
        if g == 0:
            scales, normed_attn, out_low = hold((scales, normed_attn, out_low))
            columns_got = to_experts(normed_attn, out_low)
        if g == 1:
            scales = pass_on(0, scales)

    columns_got, acts = hold((columns_got, acts))
    h1_rows = [x[:row_count] for x in columns_got]
    ob_rows = [x[row_count:] for x in columns_got]
    near_count = n_blocks // comm.cores

    def both_cores(call):
        other = None
        if comm.cores == 2:
            other = comm.push(call(near_count, near_count), 0, 1)
        return call(0, near_count), other

    message = both_cores(
        lambda first, n: own.out(places, lanes, down_t, acts, dscales, first, n)
    )
    back_other = None
    if comm.cores == 2:
        back_other = own.back(gate_w, up_w, dgates, dups, near_count, near_count)
        back_other = comm.push(back_other, 0, 1)
    message, dgates = hold((message, dgates))
    dgates, crossing[0] = pass_on(1, (dgates, crossing[0]))
    back_near = own.back(gate_w, up_w, dgates, dups, 0, near_count)
    message = comm.return_hops(*message)
    message, back_near = hold((message, back_near))
    back = comm.return_hops(back_near, back_other)
    returned = comm.return_last(message)
    back = pass_on(2, back)
    grad_normed_ffn = comm.return_last(back)
    result = (middle + returned[:width]).astype(BF16)
    grad_gates = returned[width : width + lanes] + returned[width + lanes :]
    gates_own = gates_all[:, :count]

    upstream = cot_t.astype(F32)
    mean_grad = jnp.sum(gates_own * grad_gates, 0, keepdims=True)
    grad_logits = (gates_own * (grad_gates - mean_grad)).astype(BF16)
    grad_normed_ffn = grad_normed_ffn + mm(router_t, grad_logits, 0, 0)
    grad_gain_ffn = jnp.sum(grad_normed_ffn * middle * scale_ffn, 1)
    grad_middle = upstream + norm_back(grad_normed_ffn, middle, scale_ffn, gain_ffn)
    grad_branch = grad_middle.astype(BF16)

    gain_grid = grad_gain_ffn.reshape(-1, count)
    gain_lines = gain_grid.shape[0]
    gain_high = lax.reduce_precision(gain_grid, 8, 7)
    gain_rows = jnp.concatenate([gain_high, gain_grid - gain_high]).astype(BF16)
    gain_rows = jnp.pad(gain_rows, ((0, -2 * gain_lines % 16), (0, 0)))
    branch_all = comm.gather_columns(jnp.concatenate([grad_branch, grad_logits, gain_rows]))
    grad_attn_t = mm(w_out, grad_branch, 1, 0).astype(BF16)

    def attention_half(first, heads):
        return attention_backward(
            context_index, query_t, grad_attn_t, out_t, lse, kv_blocks, first, heads
        )

    def to_keys(grad_kv):
        return lax.all_to_all(grad_kv, "context", 0, 0, tiled=True)

    size_down = units // chunks // n_dp
    tiles = width // units

    def total_of(terms):
        total = jnp.concatenate([sum(x.astype(F32) for x in group) for group in terms])
        n = total.shape[0]
        part = total[:, : tiles * size_down].reshape(n, tiles, size_down, units)
        down = jnp.swapaxes(part, 1, 2).reshape(n, size_down, width)
        part = total[:, tiles * size_down :]
        return down, part.reshape(n, 2, share, part.shape[1] // 2 // share, units)

    def send_pair(part):
        if share == 1:
            return part[:, :, 0], None
        keep = lax.dynamic_index_in_dim(part, parity, 2, False)
        send = lax.dynamic_index_in_dim(part, 1 - parity, 2, False)
        return keep, comm.pair(send.astype(BF16))

    def both_columns(keep, other):
        if other is None:
            return keep
        other = other.astype(F32)
        first = jnp.where(parity == 0, keep, other)
        second = jnp.where(parity == 0, other, keep)
        chunk = hidden_units // n_context
        pieces = []
        for q in range(chunks):
            pieces += [x[..., q * chunk : (q + 1) * chunk] for x in (first, second)]
        return jnp.concatenate(pieces, -1)

    early = crossing[:-1]
    early, grad_attn_t = hold((early, grad_attn_t))
    totals = [total_of(early)] if early else []
    pairs = [send_pair(part) for _, part in totals]
    half = KV_HEADS // 2
    grad_query_a, grad_kv_a = attention_half(0, half)
    kv_a = to_keys(grad_kv_a)
    branch_all, grad_attn_t = hold((branch_all, grad_attn_t))
    branch_all = comm.gather_cores(branch_all)
    grad_query_b, grad_kv_b = attention_half(half, half)
    kv_a, grad_kv_b, branch_all, pairs, crossing[-1] = hold(
        (kv_a, grad_kv_b, branch_all, pairs, crossing[-1])
    )
    kv_b = to_keys(grad_kv_b)

    out_sum = comm.scatter_rows(ob_rows, branch_all, width)
    h2_rows = [
        lax.dynamic_slice_in_dim(array, at + expert_index * row_count, row_count, 0)
        for j in range(comm.cores)
        for ((_, array, at),) in rows[j * near_count : j * near_count + comm.columns]
    ]
    router_rows = sum(mm(a, b[width : width + lanes], 1, 1) for a, b in zip(h2_rows, branch_all))
    gain_total = sum(x[width + lanes :].astype(F32) for x in branch_all)
    gain_total = gain_total[:gain_lines] + gain_total[gain_lines : 2 * gain_lines]
    gain_part = lax.dynamic_slice_in_dim(
        gain_total.reshape(width), expert_index * row_count, row_count, 0
    )
    rest = jnp.zeros((row_count, LANES - lanes - 1), F32)
    extra = jnp.concatenate([router_rows, gain_part[:, None], rest], 1).astype(BF16)
    extra = extra.reshape(n_context * n_dp, -1, LANES)
    extra, kv_b = hold((extra, kv_b))
    extra = lax.all_to_all(extra, ("context", "dp"), 0, 0, tiled=True)
    extra = jnp.sum(extra.astype(F32), 0)

    grad_query_raw = jnp.concatenate(
        [rotate_t(x, cosine, -sine).astype(BF16) for x in (grad_query_a, grad_query_b)]
    )
    query_sum = comm.scatter_rows(h1_rows, comm.gather_expert(grad_query_raw), width)
    late, kv_b = hold((crossing[-1], kv_b))
    totals.append(total_of([late]))
    pairs.append(send_pair(totals[-1][1]))
    kv_sums = [jnp.sum(x.astype(F32), 0) for x in (kv_a, kv_b)]
    grad_key_raw = [rotate_t(kv_sum[0], cosine, -sine).astype(BF16) for kv_sum in kv_sums]
    grad_kv_raw = jnp.concatenate(grad_key_raw + [kv_sum[1].astype(BF16) for kv_sum in kv_sums])
    kv_rows = comm.scatter_rows(h1_rows, comm.gather_expert(grad_kv_raw), 2 * kv_width)
    key_sum, value_sum = kv_rows[:, :kv_width], kv_rows[:, kv_width:]

    down_sum = jnp.concatenate([down for down, _ in totals])
    parts = [both_columns(*pair) for pair in pairs]
    gate_sum = jnp.concatenate([part[:, 0] for part in parts])
    up_sum = jnp.concatenate([part[:, 1] for part in parts])

    shard = (expert_index * n_context + context_index) * n_dp + dp_index
    shard_rows = query_sum.shape[0]

    def shard_of(array):
        return lax.dynamic_slice_in_dim(array, shard * shard_rows, shard_rows, 0).astype(F32)

    gain_sum = (
        jnp.sum(shard_of(w_query) * query_sum, 1)
        + jnp.sum(shard_of(w_key) * key_sum, 1)
        + jnp.sum(shard_of(w_value) * value_sum, 1)
    ) / shard_of(norm_attn)

    grad_normed_attn = mm(w_query, grad_query_raw, 1, 0)
    grad_normed_attn = grad_normed_attn + mm(w_key, grad_kv_raw[:kv_width], 1, 0)
    grad_normed_attn = grad_normed_attn + mm(w_value, grad_kv_raw[kv_width:], 1, 0)
    grad_hidden = grad_middle + norm_back(grad_normed_attn, hidden, scale_attn, gain_attn)
    return (
        result.T[None],
        grad_hidden.astype(BF16).T[None],
        gain_sum,
        query_sum,
        key_sum,
        value_sum,
        out_sum,
        extra[:, lanes],
        extra[:, :all_experts],
        gate_sum,
        up_sum,
        down_sum,
    )


def solution(mesh):
    rows = P(("expert", "dp"), "context", None)
    dense = P(("expert", "context", "dp"), None)
    vector = P(("expert", "context", "dp"))
    experts = P("expert", None, None)
    expert_grads = P("expert", ("context", "dp"), None)
    return jax.shard_map(
        body,
        mesh=mesh,
        in_specs=(rows, rows, rows) + (P(),) * 7 + (experts,) * 3,
        out_specs=(rows, rows, vector, dense, dense, dense, dense, vector, dense)
        + (expert_grads,) * 3,
        check_vma=False,
    )
```

time: 723 us -> 609 us (0.84)
  waiting for transfers between devices: 258 us -> 132 us
  local copies, waits for them, and re-layouts: 95.8 us -> 64.3 us
  Pallas kernels: 152 us -> 183 us
  starting transfers between devices: 92.3 us -> 104 us
    ppermute x21 -> x18, waiting for transfers between devices: 157 us -> 35.2 us  [the longest x12 19 us: send_context(): out.append(lax.ppermute(parts[s - 1], 'context', pairs))]
    ppermute x10 -> x9, waiting for transfers between devices: 40.5 us -> 81.1 us  [pair(): lax.ppermute(value, 'context', [(i, i ^ 1) for i in range(self.n_context)])]
    pallas_call x4 -> x10, Pallas kernels: 121 us -> 148 us  [the longest x3 91.1 us: act(): pl.pallas_call(functools.partial(self.act_kernel, first, n, make_gates),...]
    all_to_all x0 -> x3, starting transfers between devices: none -> 26.1 us  [the longest x2 22.1 us: to_keys(): return lax.all_to_all(grad_kv, 'context', 0, 0, tiled=True)]
    concatenate x11 -> x21, other arithmetic: 39.5 us -> 17.2 us  [the longest x4 2.38 us: to_experts(): jnp.concatenate([lax.dynamic_slice_in_dim(array, target * row_count, row_...]
    ppermute x20, waiting for transfers between devices: 31 us -> 11 us  [pull(): return lax.ppermute(value, 'expert', pairs)]
    convert_element_type x2 -> x16, other arithmetic: 6.56 us -> 25.1 us  [the longest x3 10.2 us: pass_on(): part(k).astype(BF16)]
    ppermute x3, waiting for transfers between devices: 14.9 us -> 0.01 us  [body(): kv_blocks.append(lax.ppermute(kv_own, 'context', pairs))]
  transfers between devices with their start and end apart: 60 -> 59, of which waited for: 27 -> 21; matrix products, arithmetic and copies ran while one was open for 24% -> 25% of each run, Pallas kernels for 8% -> 25%
where the time goes in v2:
time: 609 us; the launch traced here: 600 us
  Pallas kernels  183 us (30%)
  waiting for transfers between devices  132 us (22%)
  starting transfers between devices  104 us (17%)
  other arithmetic  83.3 us (14%)
  local copies, waits for them, and re-layouts  64.3 us (11%)
  matrix products  30.9 us (5%)
    pallas_call x3, Pallas kernels, act(): pl.pallas_call(functools.partial(self.act_kernel, first, n, make_gates),...  91.1 us
    ppermute x9, waiting for transfers between devices, pair(): lax.ppermute(value, 'context', [(i, i ^ 1) for i in range(self.n_context)])  81.1 us
    dot_general x14, matrix products, mm(): lax.dot_general(a, b, (((da,), (db,)), ((), ())), preferred_element_type=...  30.9 us
    ppermute x12, starting transfers between devices, send_context(): out.append(lax.ppermute(parts[s - 1], 'context', pairs))  28.3 us
    unnamed x196, local copies, waits for them, and re-layouts  28.3 us
    pallas_call x2, Pallas kernels, back(): pl.pallas_call(functools.partial(self.back_kernel, parts), out_shape=jax....  27.9 us
    all_to_all x2, starting transfers between devices, to_keys(): return lax.all_to_all(grad_kv, 'context', 0, 0, tiled=True)  22.1 us
    ppermute x12, waiting for transfers between devices, send_context(): out.append(lax.ppermute(parts[s - 1], 'context', pairs))  19 us
  transfers between devices with their start and end apart: 59, of which 21 were waited for; matrix products, arithmetic and copies ran while one was open for 25% of the time, Pallas kernels for 25%

profile of v2, /device:TPU:0, one launch (start us, length us, event | category | flops | bytes accessed | tf_op | source)
XLA Modules:
  0.0 599.9 jit_solution(753613728012833118)
XLA Ops:
  8.4 7.0 %collective-permute-start.2 = (bf16[1024,256]{1,0:T(8,128)(2,1)S(1)}, bf16[1024,256]{1,0:T(8,128)(2,1)S(1)}, u32[]{:S(2)}, u32[]{:S(2)}) collective-permute-start(bf16[1024,256]{1,0:T(8,128)(2,1)S(1)} %pad_maximum_fusion.14.refs_0_.refs_4_), channel_id=1, source_target_pairs={{0,6},{1,7},{8,14},{9,15},{16,22},{17,23},{24,30},{25,31}} | collective-permute-start | bytes 1572872 | tf_op jit(solution)/shard_map/ppermute | solution.py:818
  25.2 5.0 convolution_bitcast_fusion
  33.2 15.1 %prepare_weights.1 = (bf16[5,2,2,128,1536]{4,3,2,1,0:T(8,128)(2,1)}, bf16[1536,1280]{1,0:T(8,128)(2,1)}, bf16[1536,1280]{1,0:T(8,128)(2,1)}, bf16[1280,1536]{1,0:T(8,128)(2,1)}, bf16[1536,1280]{1,0:T(8,128)(2,1)}) custom-call(s32[1]{0:T(128)} %bitcast.14.p_ref, bf16[5,1536,512]{2,1,0:T(8,128)(2,1)} %gate_ref.1, bf16[5,1536,512]{2,1,0:T(8,128)(2,1)} %up_ref.1, ...), custom_call_target="tpu_custom_call" | custom-call | bytes 552960 | tf_op jit(solution)/shard_map/prepare_weights/pallas_call | solution.py:434
  55.3 11.1 %collective-permute-done.4.refs_13_ = bf16[1568,256]{1,0:T(8,128)(2,1)} collective-permute-done((bf16[1568,256]{1,0:T(8,128)(2,1)}, bf16[1568,256]{1,0:T(8,128)(2,1)}, u32[]{:S(2)}, u32[]{:S(2)}) %collective-permute-start.4) | collective-permute-done | bytes 802848 | tf_op jit(solution)/shard_map/ppermute | solution.py:68
  69.8 11.0 %attn_fwd.1 = (f32[1536,256]{1,0:T(8,128)S(1)}, bf16[1536,256]{1,0:T(8,128)(2,1)S(1)}, f32[8,8,256]{2,1,0:T(8,128)S(1)}) custom-call(s32[1]{0:T(128)} %bitcast.1.c_ref, bf16[1536,256]{1,0:T(8,128)(2,1)S(1)} %bitcast.213, bf16[1024,256]{1,0:T(8,128)(2,1)S(1)} %pad_maximum_fusion.14.refs_0_.refs_4_, ...), custom_call_target="tpu_custom_call" | custom-call | flops 100663296 | bytes 98304 | tf_op jit(solution)/shard_map/attn_fwd/pallas_call | solution.py:291
  91.6 14.9 %collective-permute-done.9.refs_6_ = bf16[1536,256]{1,0:T(8,128)(2,1)S(1)} collective-permute-done((bf16[1536,256]{1,0:T(8,128)(2,1)S(1)}, bf16[1536,256]{1,0:T(8,128)(2,1)S(1)}, u32[]{:S(2)}, u32[]{:S(2)}) %collective-permute-start.9) | collective-permute-done | bytes 786464 | tf_op jit(solution)/shard_map/ppermute | solution.py:68
  109.3 8.2 %collective-permute-done.10.refs_7_ = bf16[768,256]{1,0:T(8,128)(2,1)S(1)} collective-permute-done((bf16[768,256]{1,0:T(8,128)(2,1)S(1)}, bf16[768,256]{1,0:T(8,128)(2,1)S(1)}, u32[]{:S(2)}, u32[]{:S(2)}) %collective-permute-start.10) | collective-permute-done | bytes 393248 | tf_op jit(solution)/shard_map/ppermute | solution.py:61
  126.8 21.7 %experts_act.3 = (f32[32,2048]{1,0:T(8,128)}, f32[32,2048]{1,0:T(8,128)}, bf16[256,2048]{1,0:T(8,128)(2,1)}, bf16[256,2048]{1,0:T(8,128)(2,1)}, bf16[256,2048]{1...) custom-call(s32[3]{0:T(128)} %pad_add_fusion.e_ref, ...), custom_call_target="tpu_custom_call" | custom-call | flops 150994944 | bytes 282624 | tf_op jit(solution)/shard_map/experts_act/pallas_call | solution.py:653
  158.5 34.5 %experts_act.4 = (bf16[512,2048]{1,0:T(8,128)(2,1)}, bf16[512,2048]{1,0:T(8,128)(2,1)}, bf16[512,2048]{1,0:T(8,128)(2,1)}, f32[2,8,2048]{2,1,0:T(8,128)}, bf16[2...) custom-call(s32[3]{0:T(128)} %pad_add_fusion.e_ref, f32[32,2048]{1,0:T(8,128)} %get-tuple-element.401.refs_0_, ...), custom_call_target="tpu_custom_call" | custom-call | flops 301989888 | bytes 368640 | tf_op jit(solution)/shard_map/experts_act/pallas_call | solution.py:653
  193.0 34.8 %experts_act.5 = (bf16[512,2048]{1,0:T(8,128)(2,1)}, bf16[512,2048]{1,0:T(8,128)(2,1)}, bf16[512,2048]{1,0:T(8,128)(2,1)}, f32[2,8,2048]{2,1,0:T(8,128)}, bf16[2...) custom-call(s32[3]{0:T(128)} %pad_add_fusion.e_ref, f32[32,2048]{1,0:T(8,128)} %get-tuple-element.401.refs_0_, ...), custom_call_target="tpu_custom_call" | custom-call | flops 301989888 | bytes 368640 | tf_op jit(solution)/shard_map/experts_act/pallas_call | solution.py:653
  227.9 9.4 %experts_out.3 = bf16[4,1600,256]{2,1,0:T(8,128)(2,1)} custom-call(s32[3]{0:T(128)} %pad_add_fusion.e_ref, bf16[1536,1280]{1,0:T(8,128)(2,1)} %get-tuple-element.147.weight_ref, bf16[256,2048]{1,0:T(8,128)(2,1)} %get-tuple-element.165.refs_0_, bf16[512,2048]{1,0:T(8,128)(2,1)} %get-tuple-element.166.refs_1_, bf16[512,2048]{1,0:T(8,128)(2,1)} %get-tuple-element.167.refs_2_, ...), custom_call_target="tpu_custom_call" | custom-call | flops 62914560 | bytes 159744 | tf_op jit(solution)/shard_map/experts_out/pallas_call | solution.py:708
  237.9 13.8 %experts_back.3 = bf16[4,1536,256]{2,1,0:T(8,128)(2,1)} custom-call(bf16[1536,1280]{1,0:T(8,128)(2,1)} %get-tuple-element.176.gate_w_ref, bf16[1536,1280]{1,0:T(8,128)(2,1)} %get-tuple-element.177.up_w_ref, bf16[256,2048]{1,0:T(8,128)(2,1)} %get-tuple-element.184.refs_0_, bf16[512,2048]{1,0:T(8,128)(2,1)} %get-tuple-element.185.refs_1_, ...), custom_call_target="tpu_custom_call" | custom-call | flops 125829120 | bytes 221184 | tf_op jit(solution)/shard_map/experts_back/pallas_call | solution.py:755
  255.5 6.1 %collective-permute-start.22 = (bf16[1,1152,256]{2,1,0:T(8,128)(2,1)}, bf16[1,1152,256]{2,1,0:T(8,128)(2,1)}, u32[]{:S(2)}, u32[]{:S(2)}) collective-permute-start(bf16[1,1152,256]{2,1,0:T(8,128)(2,1)} %get-tuple-element.326), channel_id=1, source_target_pairs={{0,4},{2,6},{4,0},{6,2},{1,5},{3,7},{5,1},{7,3},{8,12},{10,14},{12... | collective-permute-start | bytes 1769480 | tf_op jit(solution)/shard_map/ppermute | solution.py:165
  261.5 9.4 %experts_out.2 = bf16[4,1600,256]{2,1,0:T(8,128)(2,1)} custom-call(s32[3]{0:T(128)} %pad_add_fusion.e_ref, bf16[1536,1280]{1,0:T(8,128)(2,1)} %get-tuple-element.147.weight_ref, bf16[256,2048]{1,0:T(8,128)(2,1)} %get-tuple-element.165.refs_0_, bf16[512,2048]{1,0:T(8,128)(2,1)} %get-tuple-element.166.refs_1_, bf16[512,2048]{1,0:T(8,128)(2,1)} %get-tuple-element.167.refs_2_, ...), custom_call_target="tpu_custom_call" | custom-call | flops 62914560 | bytes 159744 | tf_op jit(solution)/shard_map/experts_out/pallas_call | solution.py:708
  295.1 6.3 %collective-permute-start.31 = (bf16[2,1152,256]{2,1,0:T(8,128)(2,1)}, bf16[2,1152,256]{2,1,0:T(8,128)(2,1)}, u32[]{:S(2)}, u32[]{:S(2)}) collective-permute-start(bf16[2,1152,256]{2,1,0:T(8,128)(2,1)} %get-tuple-element.322), channel_id=1, source_target_pairs={{0,4},{2,6},{4,0},{6,2},{1,5},{3,7},{5,1},{7,3},{8,12},{10,14},{12... | collective-permute-start | bytes 3538952 | tf_op jit(solution)/shard_map/ppermute | solution.py:165
  301.4 14.1 %experts_back.2 = bf16[4,1536,256]{2,1,0:T(8,128)(2,1)} custom-call(bf16[1536,1280]{1,0:T(8,128)(2,1)} %get-tuple-element.176.gate_w_ref, bf16[1536,1280]{1,0:T(8,128)(2,1)} %get-tuple-element.177.up_w_ref, bf16[256,2048]{1,0:T(8,128)(2,1)} %get-tuple-element.184.refs_0_, bf16[512,2048]{1,0:T(8,128)(2,1)} %get-tuple-element.185.refs_1_, ...), custom_call_target="tpu_custom_call" | custom-call | flops 125829120 | bytes 221184 | tf_op jit(solution)/shard_map/experts_back/pallas_call | solution.py:755
  333.3 26.3 %collective-permute-done.23 = bf16[800,256]{1,0:T(8,128)(2,1)S(1)} collective-permute-done((bf16[800,256]{1,0:T(8,128)(2,1)S(1)}, bf16[800,256]{1,0:T(8,128)(2,1)S(1)}, u32[]{:S(2)}, u32[]{:S(2)}) %collective-permute-start.23) | collective-permute-done | bytes 409632 | tf_op jit(solution)/shard_map/ppermute | solution.py:68
  361.7 12.4 %collective-permute-done.28 = bf16[2,768,256]{2,1,0:T(8,128)(2,1)S(1)} collective-permute-done((bf16[2,768,256]{2,1,0:T(8,128)(2,1)S(1)}, bf16[2,768,256]{2,1,0:T(8,128)(2,1)S(1)}, u32[]{:S(2)}, u32[]{:S(2)}) %collective-permute-start.28) | collective-permute-done | bytes 786464 | tf_op jit(solution)/shard_map/ppermute | solution.py:68
  400.9 4.1 attn_bwd.2
  406.9 14.5 %all-to-all-start = ((bf16[4,2,256,256]{3,2,1,0:T(8,128)(2,1)}), bf16[4,2,256,256]{3,2,1,0:T(8,128)(2,1)}, u32[]{:S(2)}, u32[]{:S(2)}) async-start(bf16[4,2,256,256]{3,2,1,0:T(8,128)(2,1)} %copy-done.6), calls=%async_computation | async-start | bytes 2097152 | tf_op jit(solution)/shard_map/all_to_all | solution.py:979
  427.1 4.7 attn_bwd.3
  436.5 5.9 collective-permute-start.35
  444.8 4.9 fusion.87
  449.7 12.3 %collective-permute-done.35 = bf16[3,2,192,256]{3,2,0,1:T(8,128)(2,1)S(1)} collective-permute-done((bf16[3,2,192,256]{3,2,0,1:T(8,128)(2,1)S(1)}, bf16[3,2,192,256]{3,2,0,1:T(8,128)(2,1)S(1)}, u32[]{:S(2)}, u32[]{:S(2)}) %collective-permute-start.35) | collective-permute-done | bytes 589856 | tf_op jit(solution)/shard_map/ppermute | solution.py:68
  464.0 7.6 %all-to-all-start.1 = ((bf16[4,2,256,256]{3,2,1,0:T(8,128)(2,1)}), bf16[4,2,256,256]{3,2,1,0:T(8,128)(2,1)}, u32[]{:S(2)}, u32[]{:S(2)}) async-start(bf16[4,2,256,256]{3,2,1,0:T(8,128)(2,1)} %get-tuple-element.228), calls=%async_computation.1 | async-start | bytes 2097152 | tf_op jit(solution)/shard_map/all_to_all | solution.py:979
  477.4 4.8 row_products.5
  504.5 6.4 %collective-permute-done.40 = bf16[4,48,1536]{2,1,0:T(8,128)(2,1)S(1)} collective-permute-done((bf16[4,48,1536]{2,1,0:T(8,128)(2,1)S(1)}, bf16[4,48,1536]{2,1,0:T(8,128)(2,1)S(1)}, u32[]{:S(2)}, u32[]{:S(2)}) %collective-permute-start.40) | collective-permute-done | bytes 589856 | tf_op jit(solution)/shard_map/ppermute | solution.py:153
  515.8 5.6 collective-permute-done.53
  523.1 5.4 collective-permute-done.42
  553.8 5.1 fusion.29
  576.4 8.1 %collective-permute-done.47 = bf16[4,48,1024]{2,1,0:T(8,128)(2,1)S(1)} collective-permute-done((bf16[4,48,1024]{2,1,0:T(8,128)(2,1)S(1)}, bf16[4,48,1024]{2,1,0:T(8,128)(2,1)S(1)}, u32[]{:S(2)}, u32[]{:S(2)}) %collective-permute-start.47) | collective-permute-done | bytes 393248 | tf_op jit(solution)/shard_map/ppermute | solution.py:153
  592.2 4.5 collective-permute-done.49
  (440 shorter events, 242.6 us)
Async XLA Ops:
  8.4 58.0 %collective-permute-start.2 = (bf16[1024,256]{1,0:T(8,128)(2,1)S(1)}, bf16[1024,256]{1,0:T(8,128)(2,1)S(1)}, u32[]{:S(2)}, u32[]{:S(2)}) collective-permute-start(bf16[1024,256]{1,0:T(8,128)(2,1)S(1)} %pad_maximum_fusion.14.refs_0_.refs_4_), channel_id=1, source_target_pairs={{0,6},{1,7},{8,14},{9,15},{16,22},{17,23},{24,30},{25,31}} | collective-permute-start | bytes 1572872 | tf_op jit(solution)/shard_map/ppermute | solution.py:818
  15.4 51.0 %collective-permute-start.1 = (bf16[1024,256]{1,0:T(8,128)(2,1)S(1)}, bf16[1024,256]{1,0:T(8,128)(2,1)S(1)}, u32[]{:S(2)}, u32[]{:S(2)}) collective-permute-start(bf16[1024,256]{1,0:T(8,128)(2,1)S(1)} %pad_maximum_fusion.14.refs_0_.refs_4_), channel_id=1, source_target_pairs={{0,4},{2,6},{1,5},{3,7},{8,12},{10,14},{9,13},{11,15},{16,20},{18,... | collective-permute-start | bytes 1572872 | tf_op jit(solution)/shard_map/ppermute | solution.py:818
  16.7 49.7 %collective-permute-start = (bf16[1024,256]{1,0:T(8,128)(2,1)S(1)}, bf16[1024,256]{1,0:T(8,128)(2,1)S(1)}, u32[]{:S(2)}, u32[]{:S(2)}) collective-permute-start(bf16[1024,256]{1,0:T(8,128)(2,1)S(1)} %pad_maximum_fusion.14.refs_0_.refs_4_), channel_id=1, source_target_pairs={{0,2},{2,4},{4,6},{1,3},{3,5},{5,7},{8,10},{10,12},{12,14},{9,11},... | collective-permute-start | bytes 1572872 | tf_op jit(solution)/shard_map/ppermute | solution.py:818
  23.6 42.7 %collective-permute-start.4 = (bf16[1568,256]{1,0:T(8,128)(2,1)}, bf16[1568,256]{1,0:T(8,128)(2,1)}, u32[]{:S(2)}, u32[]{:S(2)}) collective-permute-start(bf16[1568,256]{1,0:T(8,128)(2,1)} %pad_maximum_fusion.11.refs_11_), channel_id=1, source_target_pairs={{0,2},{2,0},{4,6},{6,4},{1,3},{3,1},{5,7},{7,5},{8,10},{10,8},{12,... | collective-permute-start | bytes 2408456 | tf_op jit(solution)/shard_map/ppermute | solution.py:68
  23.7 42.7 %collective-permute-start.3 = (bf16[1568,256]{1,0:T(8,128)(2,1)}, bf16[1568,256]{1,0:T(8,128)(2,1)}, u32[]{:S(2)}, u32[]{:S(2)}) collective-permute-start(bf16[1568,256]{1,0:T(8,128)(2,1)} %pad_maximum_fusion.11.refs_11_), channel_id=1, source_target_pairs={{16,0},{24,8},{0,16},{8,24},{17,1},{25,9},{1,17},{9,25},{18,2},{26... | collective-permute-start | bytes 2408456 | tf_op jit(solution)/shard_map/ppermute | solution.py:61
  69.8 48.8 %collective-permute-start.6 = (bf16[4704,256]{1,0:T(8,128)(2,1)S(1)}, bf16[4704,256]{1,0:T(8,128)(2,1)S(1)}, u32[]{:S(2)}, u32[]{:S(2)}) collective-permute-start(bf16[4704,256]{1,0:T(8,128)(2,1)S(1)} %pad_maximum_fusion), channel_id=1, source_target_pairs={{8,0},{0,8},{24,16},{16,24},{9,1},{1,9},{25,17},{17,25},{10,2},{2,... | collective-permute-start | bytes 7225352 | tf_op jit(solution)/shard_map/ppermute | solution.py:61
  91.6 28.4 %collective-permute-start.7 = (bf16[1568,256]{1,0:T(8,128)(2,1)S(1)}, bf16[1568,256]{1,0:T(8,128)(2,1)S(1)}, u32[]{:S(2)}, u32[]{:S(2)}) collective-permute-start(bf16[1568,256]{1,0:T(8,128)(2,1)S(1)} %collective-permute-done.5.refs_14_), channel_id=1, source_target_pairs={{8,0},{0,8},{24,16},{16,24},{9,1},{1,9},{25,17},{17,25},{10,2},{2,... | collective-permute-start | bytes 2408456 | tf_op jit(solution)/shard_map/ppermute | solution.py:61
  148.6 44.5 %collective-permute-start.17 = (bf16[2,1,1152,256]{3,2,1,0:T(8,128)(2,1)}, bf16[2,1,1152,256]{3,2,1,0:T(8,128)(2,1)}, u32[]{:S(2)}, u32[]{:S(2)}) collective-permute-start(bf16[2,1,1152,256]{3,2,1,0:T(8,128)(2,1)} %get-tuple-element.162), channel_id=1, source_target_pairs={{0,1},{1,0},{2,3},{3,2},{4,5},{5,4},{6,7},{7,6},{8,9},{9,8},{10,11... | collective-permute-start | bytes 3538952 | tf_op jit(solution)/shard_map/ppermute | solution.py:153
  154.7 73.2 %collective-permute-start.14 = (bf16[768,256]{1,0:T(8,128)(2,1)}, bf16[768,256]{1,0:T(8,128)(2,1)}, u32[]{:S(2)}, u32[]{:S(2)}) collective-permute-start(bf16[768,256]{1,0:T(8,128)(2,1)} %pad_maximum_fusion.17), channel_id=1, source_target_pairs={{16,0},{24,8},{0,16},{8,24},{17,1},{25,9},{1,17},{9,25},{18,2},{26... | collective-permute-start | bytes 1179656 | tf_op jit(solution)/shard_map/ppermute | solution.py:61
  156.5 71.4 %collective-permute-start.15 = (bf16[768,256]{1,0:T(8,128)(2,1)}, bf16[768,256]{1,0:T(8,128)(2,1)}, u32[]{:S(2)}, u32[]{:S(2)}) collective-permute-start(bf16[768,256]{1,0:T(8,128)(2,1)} %pad_maximum_fusion.18), channel_id=1, source_target_pairs={{8,0},{0,8},{24,16},{16,24},{9,1},{1,9},{25,17},{17,25},{10,2},{2,... | collective-permute-start | bytes 1179656 | tf_op jit(solution)/shard_map/ppermute | solution.py:61
  157.2 70.7 %collective-permute-start.16 = (bf16[768,256]{1,0:T(8,128)(2,1)}, bf16[768,256]{1,0:T(8,128)(2,1)}, u32[]{:S(2)}, u32[]{:S(2)}) collective-permute-start(bf16[768,256]{1,0:T(8,128)(2,1)} %pad_maximum_fusion.19), channel_id=1, source_target_pairs={{24,0},{16,8},{8,16},{0,24},{25,1},{17,9},{9,17},{1,25},{26,2},{18... | collective-permute-start | bytes 1179656 | tf_op jit(solution)/shard_map/ppermute | solution.py:61
  237.4 37.7 %collective-permute-start.18 = (bf16[4,1600,256]{2,1,0:T(8,128)(2,1)}, bf16[4,1600,256]{2,1,0:T(8,128)(2,1)}, u32[]{:S(2)}, u32[]{:S(2)}) collective-permute-start(bf16[4,1600,256]{2,1,0:T(8,128)(2,1)} %experts_out.3), channel_id=1, source_target_pairs={{0,8},{8,0},{16,24},{24,16},{1,9},{9,1},{17,25},{25,17},{2,10},{10... | collective-permute-start | bytes 9830408 | tf_op jit(solution)/shard_map/ppermute | solution.py:65
  237.4 54.2 %collective-permute-start.21 = (bf16[2,2,1152,256]{3,2,1,0:T(8,128)(2,1)}, bf16[2,2,1152,256]{3,2,1,0:T(8,128)(2,1)}, u32[]{:S(2)}, u32[]{:S(2)}) collective-permute-start(bf16[2,2,1152,256]{3,2,1,0:T(8,128)(2,1)} %get-tuple-element.178), channel_id=1, source_target_pairs={{0,1},{1,0},{2,3},{3,2},{4,5},{5,4},{6,7},{7,6},{8,9},{9,8},{10,11... | collective-permute-start | bytes 7077896 | tf_op jit(solution)/shard_map/ppermute | solution.py:153
  251.7 66.3 %collective-permute-start.26 = (bf16[4,1536,256]{2,1,0:T(8,128)(2,1)}, bf16[4,1536,256]{2,1,0:T(8,128)(2,1)}, u32[]{:S(2)}, u32[]{:S(2)}) collective-permute-start(bf16[4,1536,256]{2,1,0:T(8,128)(2,1)} %experts_back.3), channel_id=1, source_target_pairs={{0,8},{8,0},{16,24},{24,16},{1,9},{9,1},{17,25},{25,17},{2,10},{10... | collective-permute-start | bytes 9437192 | tf_op jit(solution)/shard_map/ppermute | solution.py:65
  255.5 33.0 %collective-permute-start.22 = (bf16[1,1152,256]{2,1,0:T(8,128)(2,1)}, bf16[1,1152,256]{2,1,0:T(8,128)(2,1)}, u32[]{:S(2)}, u32[]{:S(2)}) collective-permute-start(bf16[1,1152,256]{2,1,0:T(8,128)(2,1)} %get-tuple-element.326), channel_id=1, source_target_pairs={{0,4},{2,6},{4,0},{6,2},{1,5},{3,7},{5,1},{7,3},{8,12},{10,14},{12... | collective-permute-start | bytes 1769480 | tf_op jit(solution)/shard_map/ppermute | solution.py:165
  278.9 36.7 %collective-permute-start.20 = (bf16[2,800,256]{2,1,0:T(8,128)(2,1)}, bf16[2,800,256]{2,1,0:T(8,128)(2,1)}, u32[]{:S(2)}, u32[]{:S(2)}) collective-permute-start(bf16[2,800,256]{2,1,0:T(8,128)(2,1)} %get-tuple-element.314), channel_id=1, source_target_pairs={{0,2},{2,0},{4,6},{6,4},{1,3},{3,1},{5,7},{7,5},{8,10},{10,8},{12,... | collective-permute-start | bytes 2457608 | tf_op jit(solution)/shard_map/ppermute | solution.py:68
  283.4 32.2 %collective-permute-start.19 = (bf16[2,800,256]{2,1,0:T(8,128)(2,1)}, bf16[2,800,256]{2,1,0:T(8,128)(2,1)}, u32[]{:S(2)}, u32[]{:S(2)}) collective-permute-start(bf16[2,800,256]{2,1,0:T(8,128)(2,1)} %get-tuple-element.316), channel_id=1, source_target_pairs={{0,16},{8,24},{16,0},{24,8},{1,17},{9,25},{17,1},{25,9},{2,18},{10... | collective-permute-start | bytes 2457608 | tf_op jit(solution)/shard_map/ppermute | solution.py:65
  288.4 73.2 %collective-permute-start.25 = (bf16[2,2,1152,256]{3,2,1,0:T(8,128)(2,1)}, bf16[2,2,1152,256]{3,2,1,0:T(8,128)(2,1)}, u32[]{:S(2)}, u32[]{:S(2)}) collective-permute-start(bf16[2,2,1152,256]{3,2,1,0:T(8,128)(2,1)} %get-tuple-element.194), channel_id=1, source_target_pairs={{0,1},{1,0},{2,3},{3,2},{4,5},{5,4},{6,7},{7,6},{8,9},{9,8},{10,11... | collective-permute-start | bytes 7077896 | tf_op jit(solution)/shard_map/ppermute | solution.py:153
  295.1 103.8 %collective-permute-start.31 = (bf16[2,1152,256]{2,1,0:T(8,128)(2,1)}, bf16[2,1152,256]{2,1,0:T(8,128)(2,1)}, u32[]{:S(2)}, u32[]{:S(2)}) collective-permute-start(bf16[2,1152,256]{2,1,0:T(8,128)(2,1)} %get-tuple-element.322), channel_id=1, source_target_pairs={{0,4},{2,6},{4,0},{6,2},{1,5},{3,7},{5,1},{7,3},{8,12},{10,14},{12... | collective-permute-start | bytes 3538952 | tf_op jit(solution)/shard_map/ppermute | solution.py:165
  322.4 37.2 %collective-permute-start.23 = (bf16[800,256]{1,0:T(8,128)(2,1)S(1)}, bf16[800,256]{1,0:T(8,128)(2,1)S(1)}, u32[]{:S(2)}, u32[]{:S(2)}) collective-permute-start(bf16[800,256]{1,0:T(8,128)(2,1)S(1)} %fusion.33), channel_id=1, source_target_pairs={{0,2},{2,0},{4,6},{6,4},{1,3},{3,1},{5,7},{7,5},{8,10},{10,8},{12,... | collective-permute-start | bytes 1228808 | tf_op jit(solution)/shard_map/ppermute | solution.py:68
  324.0 37.6 %collective-permute-start.27 = (bf16[2,768,256]{2,1,0:T(8,128)(2,1)S(1)}, bf16[2,768,256]{2,1,0:T(8,128)(2,1)S(1)}, u32[]{:S(2)}, u32[]{:S(2)}) collective-permute-start(bf16[2,768,256]{2,1,0:T(8,128)(2,1)S(1)} %fusion.26), channel_id=1, source_target_pairs={{0,16},{8,24},{16,0},{24,8},{1,17},{9,25},{17,1},{25,9},{2,18},{10... | collective-permute-start | bytes 2359304 | tf_op jit(solution)/shard_map/ppermute | solution.py:65
  329.6 44.5 %collective-permute-start.28 = (bf16[2,768,256]{2,1,0:T(8,128)(2,1)S(1)}, bf16[2,768,256]{2,1,0:T(8,128)(2,1)S(1)}, u32[]{:S(2)}, u32[]{:S(2)}) collective-permute-start(bf16[2,768,256]{2,1,0:T(8,128)(2,1)S(1)} %get-tuple-element.318), channel_id=1, source_target_pairs={{0,2},{2,0},{4,6},{6,4},{1,3},{3,1},{5,7},{7,5},{8,10},{10,8},{12,... | collective-permute-start | bytes 2359304 | tf_op jit(solution)/shard_map/ppermute | solution.py:68
  379.4 83.1 %collective-permute-start.36 = (bf16[2,1152,256]{2,1,0:T(8,128)(2,1)}, bf16[2,1152,256]{2,1,0:T(8,128)(2,1)}, u32[]{:S(2)}, u32[]{:S(2)}) collective-permute-start(bf16[2,1152,256]{2,1,0:T(8,128)(2,1)} %get-tuple-element.320), channel_id=1, source_target_pairs={{0,4},{2,6},{4,0},{6,2},{1,5},{3,7},{5,1},{7,3},{8,12},{10,14},{12... | collective-permute-start | bytes 3538952 | tf_op jit(solution)/shard_map/ppermute | solution.py:165
  406.9 55.7 %all-to-all-start = ((bf16[4,2,256,256]{3,2,1,0:T(8,128)(2,1)}), bf16[4,2,256,256]{3,2,1,0:T(8,128)(2,1)}, u32[]{:S(2)}, u32[]{:S(2)}) async-start(bf16[4,2,256,256]{3,2,1,0:T(8,128)(2,1)} %copy-done.6), calls=%async_computation | async-start | bytes 2097152 | tf_op jit(solution)/shard_map/all_to_all | solution.py:979
  426.2 36.3 %collective-permute-start.33 = (bf16[1584,256]{1,0:T(8,128)(2,1)}, bf16[1584,256]{1,0:T(8,128)(2,1)}, u32[]{:S(2)}, u32[]{:S(2)}) collective-permute-start(bf16[1584,256]{1,0:T(8,128)(2,1)} %pad_maximum_fusion.10.refs_4_), channel_id=1, source_target_pairs={{8,0},{0,8},{24,16},{16,24},{9,1},{1,9},{25,17},{17,25},{10,2},{2,... | collective-permute-start | bytes 2433032 | tf_op jit(solution)/shard_map/ppermute | solution.py:61
  426.3 36.3 %collective-permute-start.34 = (bf16[1584,256]{1,0:T(8,128)(2,1)}, bf16[1584,256]{1,0:T(8,128)(2,1)}, u32[]{:S(2)}, u32[]{:S(2)}) collective-permute-start(bf16[1584,256]{1,0:T(8,128)(2,1)} %collective-permute-done.32.refs_5_), channel_id=1, source_target_pairs={{8,0},{0,8},{24,16},{16,24},{9,1},{1,9},{25,17},{17,25},{10,2},{2,... | collective-permute-start | bytes 2433032 | tf_op jit(solution)/shard_map/ppermute | solution.py:61
  432.2 29.8 %collective-permute-start.37 = (bf16[1536,256]{1,0:T(8,128)(2,1)S(1)}, bf16[1536,256]{1,0:T(8,128)(2,1)}, u32[]{:S(2)}, u32[]{:S(2)}) collective-permute-start(bf16[1536,256]{1,0:T(8,128)(2,1)S(1)} %pad_maximum_fusion.13.refs_4_), channel_id=1, source_target_pairs={{16,0},{24,8},{0,16},{8,24},{17,1},{25,9},{1,17},{9,25},{18,2},{26... | collective-permute-start | bytes 2359304 | tf_op jit(solution)/shard_map/ppermute | solution.py:61
  462.0 30.2 %collective-permute-start.38 = (bf16[1536,256]{1,0:T(8,128)(2,1)S(1)}, bf16[1536,256]{1,0:T(8,128)(2,1)}, u32[]{:S(2)}, u32[]{:S(2)}) collective-permute-start(bf16[1536,256]{1,0:T(8,128)(2,1)S(1)} %pad_maximum_fusion.13.refs_4_), channel_id=1, source_target_pairs={{8,0},{0,8},{24,16},{16,24},{9,1},{1,9},{25,17},{17,25},{10,2},{2,... | collective-permute-start | bytes 2359304 | tf_op jit(solution)/shard_map/ppermute | solution.py:61
  462.0 30.2 %collective-permute-start.39 = (bf16[1536,256]{1,0:T(8,128)(2,1)}, bf16[1536,256]{1,0:T(8,128)(2,1)}, u32[]{:S(2)}, u32[]{:S(2)}) collective-permute-start(bf16[1536,256]{1,0:T(8,128)(2,1)} %collective-permute-done.37.refs_5_), channel_id=1, source_target_pairs={{8,0},{0,8},{24,16},{16,24},{9,1},{1,9},{25,17},{17,25},{10,2},{2,... | collective-permute-start | bytes 2359304 | tf_op jit(solution)/shard_map/ppermute | solution.py:61
  464.0 66.3 %all-to-all-start.1 = ((bf16[4,2,256,256]{3,2,1,0:T(8,128)(2,1)}), bf16[4,2,256,256]{3,2,1,0:T(8,128)(2,1)}, u32[]{:S(2)}, u32[]{:S(2)}) async-start(bf16[4,2,256,256]{3,2,1,0:T(8,128)(2,1)} %get-tuple-element.228), calls=%async_computation.1 | async-start | bytes 2097152 | tf_op jit(solution)/shard_map/all_to_all | solution.py:979
  532.7 35.2 %collective-permute-start.45 = (bf16[1024,256]{1,0:T(8,128)(2,1)S(1)}, bf16[1024,256]{1,0:T(8,128)(2,1)S(1)}, u32[]{:S(2)}, u32[]{:S(2)}) collective-permute-start(bf16[1024,256]{1,0:T(8,128)(2,1)S(1)} %pad_maximum_fusion.15.refs_4_), channel_id=1, source_target_pairs={{8,0},{0,8},{24,16},{16,24},{9,1},{1,9},{25,17},{17,25},{10,2},{2,... | collective-permute-start | bytes 1572872 | tf_op jit(solution)/shard_map/ppermute | solution.py:61
  532.8 34.8 %collective-permute-start.44 = (bf16[1024,256]{1,0:T(8,128)(2,1)S(1)}, bf16[1024,256]{1,0:T(8,128)(2,1)S(1)}, u32[]{:S(2)}, u32[]{:S(2)}) collective-permute-start(bf16[1024,256]{1,0:T(8,128)(2,1)S(1)} %pad_maximum_fusion.15.refs_4_), channel_id=1, source_target_pairs={{16,0},{24,8},{0,16},{8,24},{17,1},{25,9},{1,17},{9,25},{18,2},{26... | collective-permute-start | bytes 1572872 | tf_op jit(solution)/shard_map/ppermute | solution.py:61
  (113 other events, 1182.8 us)

commit v3 on v2

--- a/solution.py
+++ b/solution.py
@@ -90,13 +90,15 @@
     def gather_expert(self, value):
         return self.gather_cores(self.gather_columns(value))
 
-    def gather_group(self, value):
+    def gather_group(self, value, beside):
         columns = [self.pull(value, k, 0) for k in range(1, self.columns)]
-        first = [[(0, value, 0)]] + [[(0, block, 0)] for block in columns]
         far = []
         if self.share == 2:
             half = value.shape[0] // 2
             across = self.pair(value)
+            columns, across, beside = lax.optimization_barrier((columns, across, beside))
+        first = [[(0, value, 0)]] + [[(0, block, 0)] for block in columns]
+        if self.share == 2:
             first.append([(0, across, 0)])
             for k in range(1, self.columns):
                 top = self.pull(across[:half], k, 0)
@@ -106,7 +108,7 @@
         if self.cores == 2:
             blocks = blocks + self.from_core(first)
             blocks = blocks + (self.from_core(far) if far else [])
-        return blocks
+        return blocks, beside
 
     def return_hops(self, near, other):
         columns = self.columns
@@ -576,7 +578,7 @@
         def move(wait, start):
             def run():
                 for b in start:
-                    for copy in copies[b] if b < blocks else ():
+                    for copy in copies[b]:
                         copy.start()
                 for copy in copies[wait]:
                     copy.wait()
@@ -587,7 +589,7 @@
                 pl.when(step == 0)(run)
 
         def products(b):
-            move(b, (0, 1, 2) if b == 0 else (b + 2,))
+            move(b, range(blocks) if b == 0 else ())
             cols = slice(b * count, (b + 1) * count)
             acts = jnp.dot(in_t_ref[...], rows_ref[:, cols], preferred_element_type=F32)
             grad = jnp.dot(down_ref[...], cots_ref[:, cols], preferred_element_type=F32)
@@ -616,12 +618,8 @@
             dgate_ref[:, cols] = (grad * up * (sigmoid + silu * (1.0 - sigmoid))).astype(BF16)
 
         dscale_ref[...] = jnp.zeros_like(dscale_ref)
-        ready = products(0)
         for b in range(blocks):
-            done = ready
-            if b + 1 < blocks:
-                ready = products(b + 1)
-            finish(b, *done)
+            finish(b, *products(b))
         write_grads(
             rows_ref,
             cots_ref,
@@ -801,6 +799,15 @@
     lanes = -(-all_experts // 32) * 32
     places = jnp.stack([expert_index * n_experts, dp_index, context_index // share])
 
+    cot_t = cotangent[0].T
+    routed = (
+        routes[0].T[:, None, :] == jnp.arange(lanes, dtype=jnp.int32)[None, :, None]
+    ).astype(F32)
+    cot_message = jnp.concatenate([cot_t, routed.sum(0).astype(BF16)])
+    tokens, cot_message = hold((tokens, cot_message))
+    across = [comm.pair(cot_message)] if share == 2 else []
+    cots = [cot_message] + [comm.pull(cot_message, k, 0) for k in range(1, comm.columns)]
+
     hidden = tokens[0].T.astype(F32)
     gain_attn = norm_attn.astype(F32)[:, None]
     gain_ffn = norm_ffn.astype(F32)[:, None]
@@ -819,24 +826,16 @@
     query_t = rotate_t(mm(w_query, normed_attn, 0, 0), cosine, sine)
     query_t = (query_t * HEAD_DIM**-0.5).astype(BF16)
 
-    cot_t = cotangent[0].T
-    routed = (
-        routes[0].T[:, None, :] == jnp.arange(lanes, dtype=jnp.int32)[None, :, None]
-    ).astype(F32)
-    cot_message = jnp.concatenate([cot_t, routed.sum(0).astype(BF16)])
-    cots = [cot_message] + [comm.pull(cot_message, k, 0) for k in range(1, comm.columns)]
     weights = prepare_weights(parity, w_gate, w_up, w_down, hidden_units // n_context, share)
     router_t = jnp.zeros((lanes, width), BF16).at[:all_experts].set(w_router.T)
     in_t, gate_w, up_w, down, down_t = weights
     in_t = in_t.reshape(n_experts * 2 * units, width)
     in_first = jnp.concatenate([in_t[: 2 * units], router_t])
-    far = []
-    if share == 2:
-        across = comm.pair(cot_message)
-        cots, across, in_t, in_first = hold((cots, across, in_t, in_first))
-        far = [comm.pull(across, k, 0) for k in range(1, comm.columns)]
-        cots = cots + [across]
-    cots, far = [[[(0, x, 0)] for x in part] for part in (cots, far)]
+    if across:
+        across, in_t, in_first = hold((across, in_t, in_first))
+        across = across + [comm.pull(across[0], k, 0) for k in range(1, comm.columns)]
+        cots, across[0], in_t = hold((cots, across[0], in_t))
+    cots, across = [[[(0, x, 0)] for x in part] for part in (cots, across)]
     others = comm.from_core(cots) if comm.cores == 2 else []
     kv_blocks, in_t, in_first, gate_w, up_w, down, down_t = hold(
         (kv_blocks, in_t, in_first, gate_w, up_w, down, down_t)
@@ -845,12 +844,13 @@
     middle = hidden + mm(w_out, out_low, 0, 0)
     scale_ffn = rms_scale(middle)
     normed_ffn = (middle * scale_ffn * gain_ffn).astype(BF16)
-    if comm.cores == 2 and far:
-        far_arrays, normed_ffn = hold(([block[0][1] for block in far], normed_ffn))
-        far = [[(0, array, 0)] for array in far_arrays]
-        others = others + comm.from_core(far)
-    cots = cots + far + others
-    rows = comm.gather_group(normed_ffn)
+    across = [block[0][1] for block in across]
+    across, normed_ffn = hold((across, normed_ffn))
+    rows, across = comm.gather_group(normed_ffn, across)
+    across = [[(0, x, 0)] for x in across]
+    if comm.cores == 2 and across:
+        others = others + comm.from_core(across)
+    cots = cots + across + others
 
     routed_all = jnp.concatenate(
         [block[0][1][block[0][2] + width : block[0][2] + width + lanes] for block in cots]
@@ -869,21 +869,26 @@
 
     row_count = width // comm.n_expert
 
-    def to_experts(*arrays):
-        blocks = []
+    def for_experts(*arrays):
+        out = []
         for j in range(comm.cores):
             for k in range(comm.columns):
                 column, core = expert_index // comm.cores, expert_index % comm.cores
                 column = (column - k) % comm.columns
                 target = column * comm.cores + (core + j) % comm.cores
-                pieces = jnp.concatenate(
-                    [
-                        lax.dynamic_slice_in_dim(array, target * row_count, row_count, 0)
-                        for array in arrays
-                    ]
-                )
-                blocks.append(pieces if (j, k) == (0, 0) else comm.pull(pieces, k, j))
-        return blocks
+                pieces = [
+                    lax.dynamic_slice_in_dim(array, target * row_count, row_count, 0)
+                    for array in arrays
+                ]
+                out.append(jnp.concatenate(pieces))
+        return out
+
+    def to_experts(pieces):
+        peers = [(j, k) for j in range(comm.cores) for k in range(comm.columns)]
+        return pieces[:1] + [comm.pull(x, k, j) for x, (j, k) in zip(pieces[1:], peers[1:])]
+
+    columns_sent = for_experts(normed_attn, out_low)
+    chosen, columns_sent = hold((chosen, columns_sent))
 
     own = Experts(rows, cots, width, units, share, chunks, n_dp)
     groups, at = [], 0
@@ -918,8 +923,8 @@
             target.append(value)
         arrived.append(comm.send_dp(done[5:]))
         if g == 0:
-            scales, normed_attn, out_low = hold((scales, normed_attn, out_low))
-            columns_got = to_experts(normed_attn, out_low)
+            scales, columns_sent = hold((scales, columns_sent))
+            columns_got = to_experts(columns_sent)
         if g == 1:
             scales = pass_on(0, scales)
 
@@ -1018,9 +1023,7 @@
     branch_all, grad_attn_t = hold((branch_all, grad_attn_t))
     branch_all = comm.gather_cores(branch_all)
     grad_query_b, grad_kv_b = attention_half(half, half)
-    kv_a, grad_kv_b, branch_all, pairs, crossing[-1] = hold(
-        (kv_a, grad_kv_b, branch_all, pairs, crossing[-1])
-    )
+    kv_a, grad_kv_b, branch_all, crossing[-1] = hold((kv_a, grad_kv_b, branch_all, crossing[-1]))
     kv_b = to_keys(grad_kv_b)
 
     out_sum = comm.scatter_rows(ob_rows, branch_all, width)
@@ -1046,7 +1049,7 @@
         [rotate_t(x, cosine, -sine).astype(BF16) for x in (grad_query_a, grad_query_b)]
     )
     query_sum = comm.scatter_rows(h1_rows, comm.gather_expert(grad_query_raw), width)
-    late, kv_b = hold((crossing[-1], kv_b))
+    late, pairs, kv_b = hold((crossing[-1], pairs, kv_b))
     totals.append(total_of([late]))
     pairs.append(send_pair(totals[-1][1]))
     kv_sums = [jnp.sum(x.astype(F32), 0) for x in (kv_a, kv_b)]

time: 609 us -> 595 us (0.977)
  local copies, waits for them, and re-layouts: 64.3 us -> 52.4 us
  starting transfers between devices: 104 us -> 113 us
  other arithmetic: 83.3 us -> 76.3 us
    unnamed x196 -> x207, local copies, waits for them, and re-layouts: 28.3 us -> 18.8 us
    ppermute x6, waiting for transfers between devices: 16.1 us -> 24.2 us  [send_dp(): lax.ppermute(parts[s - 1], 'dp', [(i, (i + s) % n) for i in range(n)])]
    ppermute x20, waiting for transfers between devices: 11 us -> 3.97 us  [pull(): return lax.ppermute(value, 'expert', pairs)]
    all_to_all x2, starting transfers between devices: 22.1 us -> 28.4 us  [to_keys(): return lax.all_to_all(grad_kv, 'context', 0, 0, tiled=True)]
  transfers between devices with their start and end apart: 59 -> 59, of which waited for: 21 -> 23; matrix products, arithmetic and copies ran while one was open for 25% -> 23% of each run, Pallas kernels for 25% -> 25%
where the time goes in v3:
time: 595 us; the launch traced here: 586 us
  Pallas kernels  177 us (30%)
  waiting for transfers between devices  133 us (22%)
  starting transfers between devices  113 us (19%)
  other arithmetic  76.3 us (13%)
  local copies, waits for them, and re-layouts  52.4 us (9%)
  matrix products  31.3 us (5%)
    pallas_call x3, Pallas kernels, act(): pl.pallas_call(functools.partial(self.act_kernel, first, n, make_gates),...  86.3 us
    ppermute x9, waiting for transfers between devices, pair(): lax.ppermute(value, 'context', [(i, i ^ 1) for i in range(self.n_context)])  79.1 us
    dot_general x14, matrix products, mm(): lax.dot_general(a, b, (((da,), (db,)), ((), ())), preferred_element_type=...  31.3 us
    ppermute x12, starting transfers between devices, send_context(): out.append(lax.ppermute(parts[s - 1], 'context', pairs))  29.2 us
    all_to_all x2, starting transfers between devices, to_keys(): return lax.all_to_all(grad_kv, 'context', 0, 0, tiled=True)  28.4 us
    pallas_call x2, Pallas kernels, back(): pl.pallas_call(functools.partial(self.back_kernel, parts), out_shape=jax....  28.2 us
    ppermute x6, waiting for transfers between devices, send_dp(): lax.ppermute(parts[s - 1], 'dp', [(i, (i + s) % n) for i in range(n)])  24.2 us
    ppermute x12, waiting for transfers between devices, send_context(): out.append(lax.ppermute(parts[s - 1], 'context', pairs))  21.7 us
  transfers between devices with their start and end apart: 59, of which 23 were waited for; matrix products, arithmetic and copies ran while one was open for 23% of the time, Pallas kernels for 25%

profile of v3, /device:TPU:0, one launch (start us, length us, event | category | flops | bytes accessed | tf_op | source)
XLA Modules:
  0.0 586.1 jit_solution(9743250562420760688)
XLA Ops:
  10.9 7.0 %collective-permute-start.2 = (bf16[1024,256]{1,0:T(8,128)(2,1)S(1)}, bf16[1024,256]{1,0:T(8,128)(2,1)S(1)}, u32[]{:S(2)}, u32[]{:S(2)}) collective-permute-start(bf16[1024,256]{1,0:T(8,128)(2,1)S(1)} %pad_maximum_fusion.15.refs_0_.refs_4_), channel_id=1, source_target_pairs={{0,6},{1,7},{8,14},{9,15},{16,22},{17,23},{24,30},{25,31}} | collective-permute-start | bytes 1572872 | tf_op jit(solution)/shard_map/ppermute | solution.py:825
  23.3 4.9 convolution_bitcast_fusion
  31.2 15.1 %prepare_weights.1 = (bf16[5,2,2,128,1536]{4,3,2,1,0:T(8,128)(2,1)}, bf16[1536,1280]{1,0:T(8,128)(2,1)}, bf16[1536,1280]{1,0:T(8,128)(2,1)}, bf16[1280,1536]{1,0:T(8,128)(2,1)}, bf16[1536,1280]{1,0:T(8,128)(2,1)}) custom-call(s32[1]{0:T(128)} %bitcast.14.p_ref, bf16[5,1536,512]{2,1,0:T(8,128)(2,1)} %gate_ref.1, bf16[5,1536,512]{2,1,0:T(8,128)(2,1)} %up_ref.1, ...), custom_call_target="tpu_custom_call" | custom-call | bytes 552960 | tf_op jit(solution)/shard_map/prepare_weights/pallas_call | solution.py:436
  53.6 15.3 %collective-permute-done.4.refs_13_ = bf16[1568,256]{1,0:T(8,128)(2,1)} collective-permute-done((bf16[1568,256]{1,0:T(8,128)(2,1)}, bf16[1568,256]{1,0:T(8,128)(2,1)}, u32[]{:S(2)}, u32[]{:S(2)}) %collective-permute-start.4) | collective-permute-done | bytes 802848 | tf_op jit(solution)/shard_map/ppermute | solution.py:68
  72.0 11.1 %attn_fwd.1 = (f32[1536,256]{1,0:T(8,128)S(1)}, bf16[1536,256]{1,0:T(8,128)(2,1)S(1)}, f32[8,8,256]{2,1,0:T(8,128)S(1)}) custom-call(s32[1]{0:T(128)} %bitcast.5.c_ref, bf16[1536,256]{1,0:T(8,128)(2,1)S(1)} %bitcast.217, bf16[1024,256]{1,0:T(8,128)(2,1)S(1)} %pad_maximum_fusion.15.refs_0_.refs_4_, ...), custom_call_target="tpu_custom_call" | custom-call | flops 100663296 | bytes 98304 | tf_op jit(solution)/shard_map/attn_fwd/pallas_call | solution.py:293
  83.1 4.9 multiply_reduce_fusion.2
  88.9 4.3 collective-permute-start.7
  97.2 14.2 %collective-permute-done.7.refs_6_ = bf16[1536,256]{1,0:T(8,128)(2,1)S(1)} collective-permute-done((bf16[1536,256]{1,0:T(8,128)(2,1)S(1)}, bf16[1536,256]{1,0:T(8,128)(2,1)S(1)}, u32[]{:S(2)}, u32[]{:S(2)}) %collective-permute-start.7) | collective-permute-done | bytes 786464 | tf_op jit(solution)/shard_map/ppermute | solution.py:68
  116.7 6.7 %collective-permute-done.11.refs_8_ = bf16[768,256]{1,0:T(8,128)(2,1)S(1)} collective-permute-done((bf16[768,256]{1,0:T(8,128)(2,1)S(1)}, bf16[768,256]{1,0:T(8,128)(2,1)S(1)}, u32[]{:S(2)}, u32[]{:S(2)}) %collective-permute-start.11) | collective-permute-done | bytes 393248 | tf_op jit(solution)/shard_map/ppermute | solution.py:68
  127.1 21.4 %experts_act.3 = (f32[32,2048]{1,0:T(8,128)}, f32[32,2048]{1,0:T(8,128)}, bf16[256,2048]{1,0:T(8,128)(2,1)}, bf16[256,2048]{1,0:T(8,128)(2,1)}, bf16[256,2048]{1...) custom-call(s32[3]{0:T(128)} %pad_add_fusion.e_ref, ...), custom_call_target="tpu_custom_call" | custom-call | flops 150994944 | bytes 282624 | tf_op jit(solution)/shard_map/experts_act/pallas_call | solution.py:651
  152.2 32.3 %experts_act.4 = (bf16[512,2048]{1,0:T(8,128)(2,1)}, bf16[512,2048]{1,0:T(8,128)(2,1)}, bf16[512,2048]{1,0:T(8,128)(2,1)}, f32[2,8,2048]{2,1,0:T(8,128)}, bf16[2...) custom-call(s32[3]{0:T(128)} %pad_add_fusion.e_ref, f32[32,2048]{1,0:T(8,128)} %copy-done.53, ...), custom_call_target="tpu_custom_call" | custom-call | flops 301989888 | bytes 368640 | tf_op jit(solution)/shard_map/experts_act/pallas_call | solution.py:651
  184.5 32.7 %experts_act.5 = (bf16[512,2048]{1,0:T(8,128)(2,1)}, bf16[512,2048]{1,0:T(8,128)(2,1)}, bf16[512,2048]{1,0:T(8,128)(2,1)}, f32[2,8,2048]{2,1,0:T(8,128)}, bf16[2...) custom-call(s32[3]{0:T(128)} %pad_add_fusion.e_ref, f32[32,2048]{1,0:T(8,128)} %copy-done.53, ...), custom_call_target="tpu_custom_call" | custom-call | flops 301989888 | bytes 368640 | tf_op jit(solution)/shard_map/experts_act/pallas_call | solution.py:651
  217.2 9.2 %experts_out.3 = bf16[4,1600,256]{2,1,0:T(8,128)(2,1)} custom-call(s32[3]{0:T(128)} %pad_add_fusion.e_ref, bf16[1536,1280]{1,0:T(8,128)(2,1)} %get-tuple-element.167.weight_ref, bf16[256,2048]{1,0:T(8,128)(2,1)} %get-tuple-element.197.refs_0_, bf16[512,2048]{1,0:T(8,128)(2,1)} %get-tuple-element.198.refs_1_, bf16[512,2048]{1,0:T(8,128)(2,1)} %get-tuple-element.199.refs_2_, ...), custom_call_target="tpu_custom_call" | custom-call | flops 62914560 | bytes 159744 | tf_op jit(solution)/shard_map/experts_out/pallas_call | solution.py:706
  227.1 14.0 %experts_back.3 = bf16[4,1536,256]{2,1,0:T(8,128)(2,1)} custom-call(bf16[1536,1280]{1,0:T(8,128)(2,1)} %get-tuple-element.208.gate_w_ref, bf16[1536,1280]{1,0:T(8,128)(2,1)} %get-tuple-element.209.up_w_ref, bf16[256,2048]{1,0:T(8,128)(2,1)} %get-tuple-element.216.refs_0_, bf16[512,2048]{1,0:T(8,128)(2,1)} %get-tuple-element.217.refs_1_, ...), custom_call_target="tpu_custom_call" | custom-call | flops 125829120 | bytes 221184 | tf_op jit(solution)/shard_map/experts_back/pallas_call | solution.py:753
  244.9 6.0 %collective-permute-start.22 = (bf16[1,1152,256]{2,1,0:T(8,128)(2,1)}, bf16[1,1152,256]{2,1,0:T(8,128)(2,1)}, u32[]{:S(2)}, u32[]{:S(2)}) collective-permute-start(bf16[1,1152,256]{2,1,0:T(8,128)(2,1)} %get-tuple-element.358), channel_id=1, source_target_pairs={{0,4},{2,6},{4,0},{6,2},{1,5},{3,7},{5,1},{7,3},{8,12},{10,14},{12... | collective-permute-start | bytes 1769480 | tf_op jit(solution)/shard_map/ppermute | solution.py:167
  250.9 9.4 %experts_out.2 = bf16[4,1600,256]{2,1,0:T(8,128)(2,1)} custom-call(s32[3]{0:T(128)} %pad_add_fusion.e_ref, bf16[1536,1280]{1,0:T(8,128)(2,1)} %get-tuple-element.167.weight_ref, bf16[256,2048]{1,0:T(8,128)(2,1)} %get-tuple-element.197.refs_0_, bf16[512,2048]{1,0:T(8,128)(2,1)} %get-tuple-element.198.refs_1_, bf16[512,2048]{1,0:T(8,128)(2,1)} %get-tuple-element.199.refs_2_, ...), custom_call_target="tpu_custom_call" | custom-call | flops 62914560 | bytes 159744 | tf_op jit(solution)/shard_map/experts_out/pallas_call | solution.py:706
  273.3 4.5 collective-permute-done.22
  284.1 6.5 %collective-permute-start.31 = (bf16[2,1152,256]{2,1,0:T(8,128)(2,1)}, bf16[2,1152,256]{2,1,0:T(8,128)(2,1)}, u32[]{:S(2)}, u32[]{:S(2)}) collective-permute-start(bf16[2,1152,256]{2,1,0:T(8,128)(2,1)} %get-tuple-element.354), channel_id=1, source_target_pairs={{0,4},{2,6},{4,0},{6,2},{1,5},{3,7},{5,1},{7,3},{8,12},{10,14},{12... | collective-permute-start | bytes 3538952 | tf_op jit(solution)/shard_map/ppermute | solution.py:167
  290.6 14.2 %experts_back.2 = bf16[4,1536,256]{2,1,0:T(8,128)(2,1)} custom-call(bf16[1536,1280]{1,0:T(8,128)(2,1)} %get-tuple-element.208.gate_w_ref, bf16[1536,1280]{1,0:T(8,128)(2,1)} %get-tuple-element.209.up_w_ref, bf16[256,2048]{1,0:T(8,128)(2,1)} %get-tuple-element.216.refs_0_, bf16[512,2048]{1,0:T(8,128)(2,1)} %get-tuple-element.217.refs_1_, ...), custom_call_target="tpu_custom_call" | custom-call | flops 125829120 | bytes 221184 | tf_op jit(solution)/shard_map/experts_back/pallas_call | solution.py:753
  322.9 25.3 %collective-permute-done.23 = bf16[800,256]{1,0:T(8,128)(2,1)S(1)} collective-permute-done((bf16[800,256]{1,0:T(8,128)(2,1)S(1)}, bf16[800,256]{1,0:T(8,128)(2,1)S(1)}, u32[]{:S(2)}, u32[]{:S(2)}) %collective-permute-start.23) | collective-permute-done | bytes 409632 | tf_op jit(solution)/shard_map/ppermute | solution.py:68
  350.2 12.4 %collective-permute-done.28 = bf16[2,768,256]{2,1,0:T(8,128)(2,1)S(1)} collective-permute-done((bf16[2,768,256]{2,1,0:T(8,128)(2,1)S(1)}, bf16[2,768,256]{2,1,0:T(8,128)(2,1)S(1)}, u32[]{:S(2)}, u32[]{:S(2)}) %collective-permute-start.28) | collective-permute-done | bytes 786464 | tf_op jit(solution)/shard_map/ppermute | solution.py:68
  371.6 5.2 collective-permute-done.29
  395.6 14.5 %all-to-all-start = ((bf16[4,2,256,256]{3,2,1,0:T(8,128)(2,1)}), bf16[4,2,256,256]{3,2,1,0:T(8,128)(2,1)}, u32[]{:S(2)}, u32[]{:S(2)}) async-start(bf16[4,2,256,256]{3,2,1,0:T(8,128)(2,1)} %copy-done.6), calls=%async_computation | async-start | bytes 2097152 | tf_op jit(solution)/shard_map/all_to_all | solution.py:984
  415.8 4.8 attn_bwd.3
  429.7 5.8 collective-permute-start.36
  437.9 4.9 fusion.87
  443.3 13.9 %all-to-all-start.1 = ((bf16[4,2,256,256]{3,2,1,0:T(8,128)(2,1)}), bf16[4,2,256,256]{3,2,1,0:T(8,128)(2,1)}, u32[]{:S(2)}, u32[]{:S(2)}) async-start(bf16[4,2,256,256]{3,2,1,0:T(8,128)(2,1)} %get-tuple-element.260), calls=%async_computation.1 | async-start | bytes 2097152 | tf_op jit(solution)/shard_map/all_to_all | solution.py:984
  476.3 8.1 %collective-permute-done.51 = bf16[4,48,1536]{2,1,0:T(8,128)(2,1)S(1)} collective-permute-done((bf16[4,48,1536]{2,1,0:T(8,128)(2,1)S(1)}, bf16[4,48,1536]{2,1,0:T(8,128)(2,1)S(1)}, u32[]{:S(2)}, u32[]{:S(2)}) %collective-permute-start.51) | collective-permute-done | bytes 589856 | tf_op jit(solution)/shard_map/ppermute | solution.py:155
  489.5 6.8 %collective-permute-done.40 = bf16[4,48,1536]{2,1,0:T(8,128)(2,1)S(1)} collective-permute-done((bf16[4,48,1536]{2,1,0:T(8,128)(2,1)S(1)}, bf16[4,48,1536]{2,1,0:T(8,128)(2,1)S(1)}, u32[]{:S(2)}, u32[]{:S(2)}) %collective-permute-start.40) | collective-permute-done | bytes 589856 | tf_op jit(solution)/shard_map/ppermute | solution.py:155
  506.7 6.4 %collective-permute-done.42 = bf16[48,1536]{1,0:T(8,128)(2,1)S(1)} collective-permute-done((bf16[48,1536]{1,0:T(8,128)(2,1)S(1)}, bf16[48,1536]{1,0:T(8,128)(2,1)S(1)}, u32[]{:S(2)}, u32[]{:S(2)}) %collective-permute-start.42) | collective-permute-done | bytes 147488 | tf_op jit(solution)/shard_map/ppermute | solution.py:167
  562.5 8.1 %collective-permute-done.47 = bf16[4,48,1024]{2,1,0:T(8,128)(2,1)S(1)} collective-permute-done((bf16[4,48,1024]{2,1,0:T(8,128)(2,1)S(1)}, bf16[4,48,1024]{2,1,0:T(8,128)(2,1)S(1)}, u32[]{:S(2)}, u32[]{:S(2)}) %collective-permute-start.47) | collective-permute-done | bytes 393248 | tf_op jit(solution)/shard_map/ppermute | solution.py:155
  578.4 4.5 collective-permute-done.49
  (451 shorter events, 229.3 us)
Async XLA Ops:
  10.9 59.5 %collective-permute-start.2 = (bf16[1024,256]{1,0:T(8,128)(2,1)S(1)}, bf16[1024,256]{1,0:T(8,128)(2,1)S(1)}, u32[]{:S(2)}, u32[]{:S(2)}) collective-permute-start(bf16[1024,256]{1,0:T(8,128)(2,1)S(1)} %pad_maximum_fusion.15.refs_0_.refs_4_), channel_id=1, source_target_pairs={{0,6},{1,7},{8,14},{9,15},{16,22},{17,23},{24,30},{25,31}} | collective-permute-start | bytes 1572872 | tf_op jit(solution)/shard_map/ppermute | solution.py:825
  17.9 52.5 %collective-permute-start.1 = (bf16[1024,256]{1,0:T(8,128)(2,1)S(1)}, bf16[1024,256]{1,0:T(8,128)(2,1)S(1)}, u32[]{:S(2)}, u32[]{:S(2)}) collective-permute-start(bf16[1024,256]{1,0:T(8,128)(2,1)S(1)} %pad_maximum_fusion.15.refs_0_.refs_4_), channel_id=1, source_target_pairs={{0,4},{2,6},{1,5},{3,7},{8,12},{10,14},{9,13},{11,15},{16,20},{18,... | collective-permute-start | bytes 1572872 | tf_op jit(solution)/shard_map/ppermute | solution.py:825
  19.2 51.2 %collective-permute-start = (bf16[1024,256]{1,0:T(8,128)(2,1)S(1)}, bf16[1024,256]{1,0:T(8,128)(2,1)S(1)}, u32[]{:S(2)}, u32[]{:S(2)}) collective-permute-start(bf16[1024,256]{1,0:T(8,128)(2,1)S(1)} %pad_maximum_fusion.15.refs_0_.refs_4_), channel_id=1, source_target_pairs={{0,2},{2,4},{4,6},{1,3},{3,5},{5,7},{8,10},{10,12},{12,14},{9,11},... | collective-permute-start | bytes 1572872 | tf_op jit(solution)/shard_map/ppermute | solution.py:825
  21.7 47.2 %collective-permute-start.4 = (bf16[1568,256]{1,0:T(8,128)(2,1)}, bf16[1568,256]{1,0:T(8,128)(2,1)}, u32[]{:S(2)}, u32[]{:S(2)}) collective-permute-start(bf16[1568,256]{1,0:T(8,128)(2,1)} %pad_maximum_fusion.12.refs_11_), channel_id=1, source_target_pairs={{0,2},{2,0},{4,6},{6,4},{1,3},{3,1},{5,7},{7,5},{8,10},{10,8},{12,... | collective-permute-start | bytes 2408456 | tf_op jit(solution)/shard_map/ppermute | solution.py:68
  21.8 48.6 %collective-permute-start.3 = (bf16[1568,256]{1,0:T(8,128)(2,1)}, bf16[1568,256]{1,0:T(8,128)(2,1)}, u32[]{:S(2)}, u32[]{:S(2)}) collective-permute-start(bf16[1568,256]{1,0:T(8,128)(2,1)} %pad_maximum_fusion.12.refs_11_), channel_id=1, source_target_pairs={{16,0},{24,8},{0,16},{8,24},{17,1},{25,9},{1,17},{9,25},{18,2},{26... | collective-permute-start | bytes 2408456 | tf_op jit(solution)/shard_map/ppermute | solution.py:61
  71.9 44.8 %collective-permute-start.8 = (bf16[3136,256]{1,0:T(8,128)(2,1)S(1)}, bf16[3136,256]{1,0:T(8,128)(2,1)S(1)}, u32[]{:S(2)}, u32[]{:S(2)}) collective-permute-start(bf16[3136,256]{1,0:T(8,128)(2,1)S(1)} %pad_maximum_fusion.6), channel_id=1, source_target_pairs={{8,0},{0,8},{24,16},{16,24},{9,1},{1,9},{25,17},{17,25},{10,2},{2,... | collective-permute-start | bytes 4816904 | tf_op jit(solution)/shard_map/ppermute | solution.py:61
  148.4 36.0 %collective-permute-start.17 = (bf16[2,1,1152,256]{3,2,1,0:T(8,128)(2,1)}, bf16[2,1,1152,256]{3,2,1,0:T(8,128)(2,1)}, u32[]{:S(2)}, u32[]{:S(2)}) collective-permute-start(bf16[2,1,1152,256]{3,2,1,0:T(8,128)(2,1)} %get-tuple-element.194), channel_id=1, source_target_pairs={{0,1},{1,0},{2,3},{3,2},{4,5},{5,4},{6,7},{7,6},{8,9},{9,8},{10,11... | collective-permute-start | bytes 3538952 | tf_op jit(solution)/shard_map/ppermute | solution.py:155
  150.0 67.2 %collective-permute-start.14 = (bf16[768,256]{1,0:T(8,128)(2,1)}, bf16[768,256]{1,0:T(8,128)(2,1)S(1)}, u32[]{:S(2)}, u32[]{:S(2)}) collective-permute-start(bf16[768,256]{1,0:T(8,128)(2,1)} %get-tuple-element.187), channel_id=1, source_target_pairs={{16,0},{24,8},{0,16},{8,24},{17,1},{25,9},{1,17},{9,25},{18,2},{26... | collective-permute-start | bytes 1179656 | tf_op jit(solution)/shard_map/ppermute | solution.py:61
  150.6 66.7 %collective-permute-start.15 = (bf16[768,256]{1,0:T(8,128)(2,1)}, bf16[768,256]{1,0:T(8,128)(2,1)}, u32[]{:S(2)}, u32[]{:S(2)}) collective-permute-start(bf16[768,256]{1,0:T(8,128)(2,1)} %get-tuple-element.188), channel_id=1, source_target_pairs={{8,0},{0,8},{24,16},{16,24},{9,1},{1,9},{25,17},{17,25},{10,2},{2,... | collective-permute-start | bytes 1179656 | tf_op jit(solution)/shard_map/ppermute | solution.py:61
  150.6 66.7 %collective-permute-start.16 = (bf16[768,256]{1,0:T(8,128)(2,1)}, bf16[768,256]{1,0:T(8,128)(2,1)S(1)}, u32[]{:S(2)}, u32[]{:S(2)}) collective-permute-start(bf16[768,256]{1,0:T(8,128)(2,1)} %get-tuple-element.189), channel_id=1, source_target_pairs={{24,0},{16,8},{8,16},{0,24},{25,1},{17,9},{9,17},{1,25},{26,2},{18... | collective-permute-start | bytes 1179656 | tf_op jit(solution)/shard_map/ppermute | solution.py:61
  226.5 37.0 %collective-permute-start.18 = (bf16[4,1600,256]{2,1,0:T(8,128)(2,1)}, bf16[4,1600,256]{2,1,0:T(8,128)(2,1)}, u32[]{:S(2)}, u32[]{:S(2)}) collective-permute-start(bf16[4,1600,256]{2,1,0:T(8,128)(2,1)} %experts_out.3), channel_id=1, source_target_pairs={{0,8},{8,0},{16,24},{24,16},{1,9},{9,1},{17,25},{25,17},{2,10},{10... | collective-permute-start | bytes 9830408 | tf_op jit(solution)/shard_map/ppermute | solution.py:65
  226.5 54.0 %collective-permute-start.21 = (bf16[2,2,1152,256]{3,2,1,0:T(8,128)(2,1)}, bf16[2,2,1152,256]{3,2,1,0:T(8,128)(2,1)}, u32[]{:S(2)}, u32[]{:S(2)}) collective-permute-start(bf16[2,2,1152,256]{3,2,1,0:T(8,128)(2,1)} %get-tuple-element.210), channel_id=1, source_target_pairs={{0,1},{1,0},{2,3},{3,2},{4,5},{5,4},{6,7},{7,6},{8,9},{9,8},{10,11... | collective-permute-start | bytes 7077896 | tf_op jit(solution)/shard_map/ppermute | solution.py:155
  241.1 65.8 %collective-permute-start.26 = (bf16[4,1536,256]{2,1,0:T(8,128)(2,1)}, bf16[4,1536,256]{2,1,0:T(8,128)(2,1)}, u32[]{:S(2)}, u32[]{:S(2)}) collective-permute-start(bf16[4,1536,256]{2,1,0:T(8,128)(2,1)} %experts_back.3), channel_id=1, source_target_pairs={{0,8},{8,0},{16,24},{24,16},{1,9},{9,1},{17,25},{25,17},{2,10},{10... | collective-permute-start | bytes 9437192 | tf_op jit(solution)/shard_map/ppermute | solution.py:65
  244.9 32.9 %collective-permute-start.22 = (bf16[1,1152,256]{2,1,0:T(8,128)(2,1)}, bf16[1,1152,256]{2,1,0:T(8,128)(2,1)}, u32[]{:S(2)}, u32[]{:S(2)}) collective-permute-start(bf16[1,1152,256]{2,1,0:T(8,128)(2,1)} %get-tuple-element.358), channel_id=1, source_target_pairs={{0,4},{2,6},{4,0},{6,2},{1,5},{3,7},{5,1},{7,3},{8,12},{10,14},{12... | collective-permute-start | bytes 1769480 | tf_op jit(solution)/shard_map/ppermute | solution.py:167
  267.2 37.5 %collective-permute-start.20 = (bf16[2,800,256]{2,1,0:T(8,128)(2,1)}, bf16[2,800,256]{2,1,0:T(8,128)(2,1)}, u32[]{:S(2)}, u32[]{:S(2)}) collective-permute-start(bf16[2,800,256]{2,1,0:T(8,128)(2,1)} %get-tuple-element.346), channel_id=1, source_target_pairs={{0,2},{2,0},{4,6},{6,4},{1,3},{3,1},{5,7},{7,5},{8,10},{10,8},{12,... | collective-permute-start | bytes 2457608 | tf_op jit(solution)/shard_map/ppermute | solution.py:68
  272.0 32.8 %collective-permute-start.19 = (bf16[2,800,256]{2,1,0:T(8,128)(2,1)}, bf16[2,800,256]{2,1,0:T(8,128)(2,1)}, u32[]{:S(2)}, u32[]{:S(2)}) collective-permute-start(bf16[2,800,256]{2,1,0:T(8,128)(2,1)} %get-tuple-element.348), channel_id=1, source_target_pairs={{0,16},{8,24},{16,0},{24,8},{1,17},{9,25},{17,1},{25,9},{2,18},{10... | collective-permute-start | bytes 2457608 | tf_op jit(solution)/shard_map/ppermute | solution.py:65
  277.8 72.4 %collective-permute-start.25 = (bf16[2,2,1152,256]{3,2,1,0:T(8,128)(2,1)}, bf16[2,2,1152,256]{3,2,1,0:T(8,128)(2,1)}, u32[]{:S(2)}, u32[]{:S(2)}) collective-permute-start(bf16[2,2,1152,256]{3,2,1,0:T(8,128)(2,1)} %get-tuple-element.226), channel_id=1, source_target_pairs={{0,1},{1,0},{2,3},{3,2},{4,5},{5,4},{6,7},{7,6},{8,9},{9,8},{10,11... | collective-permute-start | bytes 7077896 | tf_op jit(solution)/shard_map/ppermute | solution.py:155
  284.1 105.3 %collective-permute-start.31 = (bf16[2,1152,256]{2,1,0:T(8,128)(2,1)}, bf16[2,1152,256]{2,1,0:T(8,128)(2,1)}, u32[]{:S(2)}, u32[]{:S(2)}) collective-permute-start(bf16[2,1152,256]{2,1,0:T(8,128)(2,1)} %get-tuple-element.354), channel_id=1, source_target_pairs={{0,4},{2,6},{4,0},{6,2},{1,5},{3,7},{5,1},{7,3},{8,12},{10,14},{12... | collective-permute-start | bytes 3538952 | tf_op jit(solution)/shard_map/ppermute | solution.py:167
  311.3 36.9 %collective-permute-start.23 = (bf16[800,256]{1,0:T(8,128)(2,1)S(1)}, bf16[800,256]{1,0:T(8,128)(2,1)S(1)}, u32[]{:S(2)}, u32[]{:S(2)}) collective-permute-start(bf16[800,256]{1,0:T(8,128)(2,1)S(1)} %fusion.33), channel_id=1, source_target_pairs={{0,2},{2,0},{4,6},{6,4},{1,3},{3,1},{5,7},{7,5},{8,10},{10,8},{12,... | collective-permute-start | bytes 1228808 | tf_op jit(solution)/shard_map/ppermute | solution.py:68
  312.7 37.5 %collective-permute-start.27 = (bf16[2,768,256]{2,1,0:T(8,128)(2,1)S(1)}, bf16[2,768,256]{2,1,0:T(8,128)(2,1)S(1)}, u32[]{:S(2)}, u32[]{:S(2)}) collective-permute-start(bf16[2,768,256]{2,1,0:T(8,128)(2,1)S(1)} %fusion.26), channel_id=1, source_target_pairs={{0,16},{8,24},{16,0},{24,8},{1,17},{9,25},{17,1},{25,9},{2,18},{10... | collective-permute-start | bytes 2359304 | tf_op jit(solution)/shard_map/ppermute | solution.py:65
  318.8 43.8 %collective-permute-start.28 = (bf16[2,768,256]{2,1,0:T(8,128)(2,1)S(1)}, bf16[2,768,256]{2,1,0:T(8,128)(2,1)S(1)}, u32[]{:S(2)}, u32[]{:S(2)}) collective-permute-start(bf16[2,768,256]{2,1,0:T(8,128)(2,1)S(1)} %get-tuple-element.350), channel_id=1, source_target_pairs={{0,2},{2,0},{4,6},{6,4},{1,3},{3,1},{5,7},{7,5},{8,10},{10,8},{12,... | collective-permute-start | bytes 2359304 | tf_op jit(solution)/shard_map/ppermute | solution.py:68
  368.2 74.6 %collective-permute-start.35 = (bf16[2,1152,256]{2,1,0:T(8,128)(2,1)}, bf16[2,1152,256]{2,1,0:T(8,128)(2,1)}, u32[]{:S(2)}, u32[]{:S(2)}) collective-permute-start(bf16[2,1152,256]{2,1,0:T(8,128)(2,1)} %get-tuple-element.352), channel_id=1, source_target_pairs={{0,4},{2,6},{4,0},{6,2},{1,5},{3,7},{5,1},{7,3},{8,12},{10,14},{12... | collective-permute-start | bytes 3538952 | tf_op jit(solution)/shard_map/ppermute | solution.py:167
  395.6 47.7 %all-to-all-start = ((bf16[4,2,256,256]{3,2,1,0:T(8,128)(2,1)}), bf16[4,2,256,256]{3,2,1,0:T(8,128)(2,1)}, u32[]{:S(2)}, u32[]{:S(2)}) async-start(bf16[4,2,256,256]{3,2,1,0:T(8,128)(2,1)} %copy-done.6), calls=%async_computation | async-start | bytes 2097152 | tf_op jit(solution)/shard_map/all_to_all | solution.py:984
  414.9 28.4 %collective-permute-start.33 = (bf16[1584,256]{1,0:T(8,128)(2,1)}, bf16[1584,256]{1,0:T(8,128)(2,1)}, u32[]{:S(2)}, u32[]{:S(2)}) collective-permute-start(bf16[1584,256]{1,0:T(8,128)(2,1)} %pad_maximum_fusion.11.refs_4_), channel_id=1, source_target_pairs={{8,0},{0,8},{24,16},{16,24},{9,1},{1,9},{25,17},{17,25},{10,2},{2,... | collective-permute-start | bytes 2433032 | tf_op jit(solution)/shard_map/ppermute | solution.py:61
  415.0 28.3 %collective-permute-start.34 = (bf16[1584,256]{1,0:T(8,128)(2,1)}, bf16[1584,256]{1,0:T(8,128)(2,1)}, u32[]{:S(2)}, u32[]{:S(2)}) collective-permute-start(bf16[1584,256]{1,0:T(8,128)(2,1)} %collective-permute-done.32.refs_5_), channel_id=1, source_target_pairs={{8,0},{0,8},{24,16},{16,24},{9,1},{1,9},{25,17},{17,25},{10,2},{2,... | collective-permute-start | bytes 2433032 | tf_op jit(solution)/shard_map/ppermute | solution.py:61
  429.7 85.2 %collective-permute-start.36 = (bf16[3,2,192,256]{3,2,0,1:T(8,128)(2,1)}, bf16[3,2,192,256]{3,2,0,1:T(8,128)(2,1)S(1)}, u32[]{:S(2)}, u32[]{:S(2)}) collective-permute-start(bf16[3,2,192,256]{3,2,0,1:T(8,128)(2,1)} %fusion.32), channel_id=1, source_target_pairs={{0,2},{2,0},{4,6},{6,4},{1,3},{3,1},{5,7},{7,5},{8,10},{10,8},{12,... | collective-permute-start | bytes 1769480 | tf_op jit(solution)/shard_map/ppermute | solution.py:68
  442.7 27.4 %collective-permute-start.38 = (bf16[1536,256]{1,0:T(8,128)(2,1)S(1)}, bf16[1536,256]{1,0:T(8,128)(2,1)}, u32[]{:S(2)}, u32[]{:S(2)}) collective-permute-start(bf16[1536,256]{1,0:T(8,128)(2,1)S(1)} %pad_maximum_fusion.14.refs_4_), channel_id=1, source_target_pairs={{8,0},{0,8},{24,16},{16,24},{9,1},{1,9},{25,17},{17,25},{10,2},{2,... | collective-permute-start | bytes 2359304 | tf_op jit(solution)/shard_map/ppermute | solution.py:61
  442.8 27.4 %collective-permute-start.39 = (bf16[1536,256]{1,0:T(8,128)(2,1)}, bf16[1536,256]{1,0:T(8,128)(2,1)}, u32[]{:S(2)}, u32[]{:S(2)}) collective-permute-start(bf16[1536,256]{1,0:T(8,128)(2,1)} %collective-permute-done.37.refs_5_), channel_id=1, source_target_pairs={{8,0},{0,8},{24,16},{16,24},{9,1},{1,9},{25,17},{17,25},{10,2},{2,... | collective-permute-start | bytes 2359304 | tf_op jit(solution)/shard_map/ppermute | solution.py:61
  443.3 71.6 %all-to-all-start.1 = ((bf16[4,2,256,256]{3,2,1,0:T(8,128)(2,1)}), bf16[4,2,256,256]{3,2,1,0:T(8,128)(2,1)}, u32[]{:S(2)}, u32[]{:S(2)}) async-start(bf16[4,2,256,256]{3,2,1,0:T(8,128)(2,1)} %get-tuple-element.260), calls=%async_computation.1 | async-start | bytes 2097152 | tf_op jit(solution)/shard_map/all_to_all | solution.py:984
  517.5 39.2 %collective-permute-start.45 = (bf16[1024,256]{1,0:T(8,128)(2,1)S(1)}, bf16[1024,256]{1,0:T(8,128)(2,1)S(1)}, u32[]{:S(2)}, u32[]{:S(2)}) collective-permute-start(bf16[1024,256]{1,0:T(8,128)(2,1)S(1)} %pad_maximum_fusion.16.refs_4_), channel_id=1, source_target_pairs={{8,0},{0,8},{24,16},{16,24},{9,1},{1,9},{25,17},{17,25},{10,2},{2,... | collective-permute-start | bytes 1572872 | tf_op jit(solution)/shard_map/ppermute | solution.py:61
  517.6 38.2 %collective-permute-start.44 = (bf16[1024,256]{1,0:T(8,128)(2,1)S(1)}, bf16[1024,256]{1,0:T(8,128)(2,1)S(1)}, u32[]{:S(2)}, u32[]{:S(2)}) collective-permute-start(bf16[1024,256]{1,0:T(8,128)(2,1)S(1)} %pad_maximum_fusion.16.refs_4_), channel_id=1, source_target_pairs={{16,0},{24,8},{0,16},{8,24},{17,1},{25,9},{1,17},{9,25},{18,2},{26... | collective-permute-start | bytes 1572872 | tf_op jit(solution)/shard_map/ppermute | solution.py:61
  523.1 28.9 %all-to-all-start.2 = ((bf16[8,48,128]{2,1,0:T(8,128)(2,1)}), bf16[8,48,128]{2,1,0:T(8,128)(2,1)}, u32[]{:S(2)}, u32[]{:S(2)}) async-start(bf16[8,48,128]{2,1,0:T(8,128)(2,1)} %maximum_maximum_fusion), calls=%async_computation.2 | async-start | bytes 196608 | tf_op jit(solution)/shard_map/all_to_all | solution.py:1045
  (119 other events, 1030.9 us)

commit v4 on v3

--- a/solution.py
+++ b/solution.py
@@ -194,10 +194,12 @@
 def row_products_kernel(count, place_ref, *refs):
     left, right, outs, total_s = refs[:count], refs[count : 2 * count], refs[2 * count : -1], refs[-1]
     width = total_s.shape[1]
-    total = mm(left[0][...], right[0][:width, :], 1, 1)
-    for a, b in zip(left[1:], right[1:]):
-        total = total + mm(a[...], b[:width, :], 1, 1)
-    total_s[...] = total
+    total_s[...] = mm(
+        jnp.concatenate([a[...] for a in left], 1),
+        jnp.concatenate([b[:width, :] for b in right], 1),
+        1,
+        1,
+    )
     n, size, _ = outs[0].shape
     m = len(outs)
     for k in range(n):
@@ -235,27 +237,35 @@
     )(place, *left, *right)
 
 
+def heads_side_by_side(ref):
+    hd = HEAD_DIM
+    return jnp.concatenate([ref[g * hd : (g + 1) * hd, :] for g in range(GROUP)], 1)
+
+
+def causal(shape, n):
+    key = lax.broadcasted_iota(jnp.int32, shape, 0)
+    query = lax.rem(lax.broadcasted_iota(jnp.int32, shape, 1), n)
+    return key <= query
+
+
 def attn_fwd_kernel(blocks, c_ref, q_ref, *refs):
     k_refs, v_refs = refs[:blocks], refs[blocks : 2 * blocks]
     o_ref, ob_ref, lse_ref, scores_ref = refs[2 * blocks :]
     c = c_ref[0]
     n = q_ref.shape[1]
     hd = HEAD_DIM
+    queries = heads_side_by_side(q_ref)
     for s in range(blocks):
         rows = slice(s * n, (s + 1) * n)
 
         def fill(s=s, rows=rows):
-            for g in range(GROUP):
-                scores = mm(k_refs[s][...], q_ref[g * hd : (g + 1) * hd, :], 0, 0)
-                if s == 0:
-                    key = lax.broadcasted_iota(jnp.int32, scores.shape, 0)
-                    query = lax.broadcasted_iota(jnp.int32, scores.shape, 1)
-                    scores = jnp.where(key <= query, scores, NEG_LARGE)
-                scores_ref[g, rows, :] = scores
+            scores = mm(k_refs[s][...], queries, 0, 0)
+            if s == 0:
+                scores = jnp.where(causal(scores.shape, n), scores, NEG_LARGE)
+            scores_ref[rows, :] = scores
 
         def blank(rows=rows):
-            for g in range(GROUP):
-                scores_ref[g, rows, :] = jnp.full((n, n), NEG_LARGE, F32)
+            scores_ref[rows, :] = jnp.full((n, GROUP * n), NEG_LARGE, F32)
 
         if s == 0:
             fill()
@@ -264,7 +274,8 @@
             pl.when(c < s)(blank)
     lse_ref[...] = jnp.zeros_like(lse_ref)
     for g in range(GROUP):
-        scores = scores_ref[g]
+        cols = slice(g * n, (g + 1) * n)
+        scores = scores_ref[:, cols]
         top = jnp.max(scores, 0, keepdims=True)
         weights = jnp.exp(scores - top)
         total = jnp.sum(weights, 0, keepdims=True)
@@ -302,7 +313,7 @@
             grid=(heads,),
             in_specs=[head] + kv_specs(blocks, n),
             out_specs=(head, head, pl.BlockSpec((1, 8, n), lambda h, c: (h, 0, 0))),
-            scratch_shapes=[pltpu.VMEM((GROUP, blocks * n, n), F32)],
+            scratch_shapes=[pltpu.VMEM((blocks * n, GROUP * n), F32)],
         ),
         compiler_params=pltpu.CompilerParams(vmem_limit_bytes=40 << 20),
         cost_estimate=cost(
@@ -320,39 +331,33 @@
     c = c_ref[0]
     n = q_ref.shape[1]
     hd = HEAD_DIM
-    deltas = []
+    queries, grads = heads_side_by_side(q_ref), heads_side_by_side(do_ref)
+    deltas, lses = [], []
     for g in range(GROUP):
         head = slice(g * hd, (g + 1) * hd)
         both = do_ref[head, :].astype(F32) * o_ref[head, :]
         deltas.append(jnp.sum(both, 0, keepdims=True))
+        lses.append(lse_ref[0, g : g + 1, :])
+    delta, lse = jnp.concatenate(deltas, 1), jnp.concatenate(lses, 1)
     for s in range(blocks):
 
         def work(s=s):
-            dk = jnp.zeros((hd, n), F32)
-            dv = jnp.zeros((hd, n), F32)
             key_t = k_refs[s][...]
-            value_t = v_refs[s][...]
+            weights = jnp.exp(mm(key_t, queries, 0, 0) - lse)
+            if s == 0:
+                weights = jnp.where(causal(weights.shape, n), weights, 0.0)
+            grad_weights = mm(v_refs[s][...], grads, 0, 0)
+            grad_scores = (weights * (grad_weights - delta)).astype(BF16)
+            owner = lax.rem(c - s + blocks, blocks)
+            dkv_ref[owner, 0] = mm(queries, grad_scores, 1, 1).astype(BF16)
+            dkv_ref[owner, 1] = mm(grads, weights.astype(BF16), 1, 1).astype(BF16)
+            step = mm(key_t, grad_scores, 1, 0) * (HEAD_DIM**-0.5)
             for g in range(GROUP):
-                head = slice(g * hd, (g + 1) * hd)
-                query, grad = q_ref[head, :], do_ref[head, :]
-                scores = mm(key_t, query, 0, 0)
-                weights = jnp.exp(scores - lse_ref[0, g : g + 1, :])
+                head, cols = slice(g * hd, (g + 1) * hd), slice(g * n, (g + 1) * n)
                 if s == 0:
-                    key = lax.broadcasted_iota(jnp.int32, scores.shape, 0)
-                    place = lax.broadcasted_iota(jnp.int32, scores.shape, 1)
-                    weights = jnp.where(key <= place, weights, 0.0)
-                grad_weights = mm(value_t, grad, 0, 0)
-                grad_scores = (weights * (grad_weights - deltas[g])).astype(BF16)
-                dv = dv + mm(grad, weights.astype(BF16), 1, 1)
-                dk = dk + mm(query, grad_scores, 1, 1)
-                step = mm(key_t, grad_scores, 1, 0) * (HEAD_DIM**-0.5)
-                if s == 0:
-                    dq_ref[head, :] = step
+                    dq_ref[head, :] = step[:, cols]
                 else:
-                    dq_ref[head, :] += step
-            owner = lax.rem(c - s + blocks, blocks)
-            dkv_ref[owner, 0] = dk.astype(BF16)
-            dkv_ref[owner, 1] = dv.astype(BF16)
+                    dq_ref[head, :] += step[:, cols]
 
         def skip(s=s):
             owner = lax.rem(c - s + blocks, blocks)

time: 595 us -> 587 us (0.987)
  starting transfers between devices: 113 us -> 102 us
    all_to_all x2, starting transfers between devices: 28.4 us -> 17.9 us  [to_keys(): return lax.all_to_all(grad_kv, 'context', 0, 0, tiled=True)]
  transfers between devices with their start and end apart: 59 -> 59, of which waited for: 23 -> 24; matrix products, arithmetic and copies ran while one was open for 23% -> 24% of each run, Pallas kernels for 25% -> 25%
where the time goes in v4:
time: 587 us; the launch traced here: 578 us
  Pallas kernels  175 us (30%)
  waiting for transfers between devices  138 us (24%)
  starting transfers between devices  102 us (17%)
  other arithmetic  76.3 us (13%)
  local copies, waits for them, and re-layouts  52.4 us (9%)
  matrix products  31.3 us (5%)
    pallas_call x3, Pallas kernels, act(): pl.pallas_call(functools.partial(self.act_kernel, first, n, make_gates),...  86.3 us
    ppermute x9, waiting for transfers between devices, pair(): lax.ppermute(value, 'context', [(i, i ^ 1) for i in range(self.n_context)])  79 us
    dot_general x14, matrix products, mm(): lax.dot_general(a, b, (((da,), (db,)), ((), ())), preferred_element_type=...  31.3 us
    ppermute x12, starting transfers between devices, send_context(): out.append(lax.ppermute(parts[s - 1], 'context', pairs))  29 us
    pallas_call x2, Pallas kernels, back(): pl.pallas_call(functools.partial(self.back_kernel, parts), out_shape=jax....  28 us
    ppermute x6, waiting for transfers between devices, send_dp(): lax.ppermute(parts[s - 1], 'dp', [(i, (i + s) % n) for i in range(n)])  24 us
    ppermute x12, waiting for transfers between devices, send_context(): out.append(lax.ppermute(parts[s - 1], 'context', pairs))  21.9 us
    unnamed x207, local copies, waits for them, and re-layouts  18.8 us
  transfers between devices with their start and end apart: 59, of which 24 were waited for; matrix products, arithmetic and copies ran while one was open for 24% of the time, Pallas kernels for 25%

profile of v4, /device:TPU:0, one launch (start us, length us, event | category | flops | bytes accessed | tf_op | source)
XLA Modules:
  0.0 577.9 jit_solution(16607676510921582256)
XLA Ops:
  10.9 7.0 %collective-permute-start.2 = (bf16[1024,256]{1,0:T(8,128)(2,1)S(1)}, bf16[1024,256]{1,0:T(8,128)(2,1)S(1)}, u32[]{:S(2)}, u32[]{:S(2)}) collective-permute-start(bf16[1024,256]{1,0:T(8,128)(2,1)S(1)} %pad_maximum_fusion.15.refs_0_.refs_4_), channel_id=1, source_target_pairs={{0,6},{1,7},{8,14},{9,15},{16,22},{17,23},{24,30},{25,31}} | collective-permute-start | bytes 1572872 | tf_op jit(solution)/shard_map/ppermute | solution.py:830
  23.3 4.9 convolution_bitcast_fusion
  31.2 15.1 %prepare_weights.1 = (bf16[5,2,2,128,1536]{4,3,2,1,0:T(8,128)(2,1)}, bf16[1536,1280]{1,0:T(8,128)(2,1)}, bf16[1536,1280]{1,0:T(8,128)(2,1)}, bf16[1280,1536]{1,0:T(8,128)(2,1)}, bf16[1536,1280]{1,0:T(8,128)(2,1)}) custom-call(s32[1]{0:T(128)} %bitcast.14.p_ref, bf16[5,1536,512]{2,1,0:T(8,128)(2,1)} %gate_ref.1, bf16[5,1536,512]{2,1,0:T(8,128)(2,1)} %up_ref.1, ...), custom_call_target="tpu_custom_call" | custom-call | bytes 552960 | tf_op jit(solution)/shard_map/prepare_weights/pallas_call | solution.py:441
  53.6 15.3 %collective-permute-done.4.refs_13_ = bf16[1568,256]{1,0:T(8,128)(2,1)} collective-permute-done((bf16[1568,256]{1,0:T(8,128)(2,1)}, bf16[1568,256]{1,0:T(8,128)(2,1)}, u32[]{:S(2)}, u32[]{:S(2)}) %collective-permute-start.4) | collective-permute-done | bytes 802848 | tf_op jit(solution)/shard_map/ppermute | solution.py:68
  72.0 11.0 %attn_fwd.1 = (f32[1536,256]{1,0:T(8,128)S(1)}, bf16[1536,256]{1,0:T(8,128)(2,1)S(1)}, f32[8,8,256]{2,1,0:T(8,128)S(1)}) custom-call(s32[1]{0:T(128)} %bitcast.5.c_ref, bf16[1536,256]{1,0:T(8,128)(2,1)S(1)} %bitcast.217, bf16[1024,256]{1,0:T(8,128)(2,1)S(1)} %pad_maximum_fusion.15.refs_0_.refs_4_, ...), custom_call_target="tpu_custom_call" | custom-call | flops 100663296 | bytes 98304 | tf_op jit(solution)/shard_map/attn_fwd/pallas_call | solution.py:304
  83.0 4.9 multiply_reduce_fusion.2
  88.8 4.4 collective-permute-start.7
  97.1 14.3 %collective-permute-done.7.refs_6_ = bf16[1536,256]{1,0:T(8,128)(2,1)S(1)} collective-permute-done((bf16[1536,256]{1,0:T(8,128)(2,1)S(1)}, bf16[1536,256]{1,0:T(8,128)(2,1)S(1)}, u32[]{:S(2)}, u32[]{:S(2)}) %collective-permute-start.7) | collective-permute-done | bytes 786464 | tf_op jit(solution)/shard_map/ppermute | solution.py:68
  116.7 6.7 %collective-permute-done.11.refs_8_ = bf16[768,256]{1,0:T(8,128)(2,1)S(1)} collective-permute-done((bf16[768,256]{1,0:T(8,128)(2,1)S(1)}, bf16[768,256]{1,0:T(8,128)(2,1)S(1)}, u32[]{:S(2)}, u32[]{:S(2)}) %collective-permute-start.11) | collective-permute-done | bytes 393248 | tf_op jit(solution)/shard_map/ppermute | solution.py:68
  127.1 21.4 %experts_act.3 = (f32[32,2048]{1,0:T(8,128)}, f32[32,2048]{1,0:T(8,128)}, bf16[256,2048]{1,0:T(8,128)(2,1)}, bf16[256,2048]{1,0:T(8,128)(2,1)}, bf16[256,2048]{1...) custom-call(s32[3]{0:T(128)} %pad_add_fusion.e_ref, ...), custom_call_target="tpu_custom_call" | custom-call | flops 150994944 | bytes 282624 | tf_op jit(solution)/shard_map/experts_act/pallas_call | solution.py:656
  152.1 32.3 %experts_act.4 = (bf16[512,2048]{1,0:T(8,128)(2,1)}, bf16[512,2048]{1,0:T(8,128)(2,1)}, bf16[512,2048]{1,0:T(8,128)(2,1)}, f32[2,8,2048]{2,1,0:T(8,128)}, bf16[2...) custom-call(s32[3]{0:T(128)} %pad_add_fusion.e_ref, f32[32,2048]{1,0:T(8,128)} %copy-done.53, ...), custom_call_target="tpu_custom_call" | custom-call | flops 301989888 | bytes 368640 | tf_op jit(solution)/shard_map/experts_act/pallas_call | solution.py:656
  184.4 32.7 %experts_act.5 = (bf16[512,2048]{1,0:T(8,128)(2,1)}, bf16[512,2048]{1,0:T(8,128)(2,1)}, bf16[512,2048]{1,0:T(8,128)(2,1)}, f32[2,8,2048]{2,1,0:T(8,128)}, bf16[2...) custom-call(s32[3]{0:T(128)} %pad_add_fusion.e_ref, f32[32,2048]{1,0:T(8,128)} %copy-done.53, ...), custom_call_target="tpu_custom_call" | custom-call | flops 301989888 | bytes 368640 | tf_op jit(solution)/shard_map/experts_act/pallas_call | solution.py:656
  217.2 9.2 %experts_out.3 = bf16[4,1600,256]{2,1,0:T(8,128)(2,1)} custom-call(s32[3]{0:T(128)} %pad_add_fusion.e_ref, bf16[1536,1280]{1,0:T(8,128)(2,1)} %get-tuple-element.167.weight_ref, bf16[256,2048]{1,0:T(8,128)(2,1)} %get-tuple-element.197.refs_0_, bf16[512,2048]{1,0:T(8,128)(2,1)} %get-tuple-element.198.refs_1_, bf16[512,2048]{1,0:T(8,128)(2,1)} %get-tuple-element.199.refs_2_, ...), custom_call_target="tpu_custom_call" | custom-call | flops 62914560 | bytes 159744 | tf_op jit(solution)/shard_map/experts_out/pallas_call | solution.py:711
  227.1 14.2 %experts_back.3 = bf16[4,1536,256]{2,1,0:T(8,128)(2,1)} custom-call(bf16[1536,1280]{1,0:T(8,128)(2,1)} %get-tuple-element.208.gate_w_ref, bf16[1536,1280]{1,0:T(8,128)(2,1)} %get-tuple-element.209.up_w_ref, bf16[256,2048]{1,0:T(8,128)(2,1)} %get-tuple-element.216.refs_0_, bf16[512,2048]{1,0:T(8,128)(2,1)} %get-tuple-element.217.refs_1_, ...), custom_call_target="tpu_custom_call" | custom-call | flops 125829120 | bytes 221184 | tf_op jit(solution)/shard_map/experts_back/pallas_call | solution.py:758
  245.0 6.0 %collective-permute-start.22 = (bf16[1,1152,256]{2,1,0:T(8,128)(2,1)}, bf16[1,1152,256]{2,1,0:T(8,128)(2,1)}, u32[]{:S(2)}, u32[]{:S(2)}) collective-permute-start(bf16[1,1152,256]{2,1,0:T(8,128)(2,1)} %get-tuple-element.358), channel_id=1, source_target_pairs={{0,4},{2,6},{4,0},{6,2},{1,5},{3,7},{5,1},{7,3},{8,12},{10,14},{12... | collective-permute-start | bytes 1769480 | tf_op jit(solution)/shard_map/ppermute | solution.py:167
  251.0 9.4 %experts_out.2 = bf16[4,1600,256]{2,1,0:T(8,128)(2,1)} custom-call(s32[3]{0:T(128)} %pad_add_fusion.e_ref, bf16[1536,1280]{1,0:T(8,128)(2,1)} %get-tuple-element.167.weight_ref, bf16[256,2048]{1,0:T(8,128)(2,1)} %get-tuple-element.197.refs_0_, bf16[512,2048]{1,0:T(8,128)(2,1)} %get-tuple-element.198.refs_1_, bf16[512,2048]{1,0:T(8,128)(2,1)} %get-tuple-element.199.refs_2_, ...), custom_call_target="tpu_custom_call" | custom-call | flops 62914560 | bytes 159744 | tf_op jit(solution)/shard_map/experts_out/pallas_call | solution.py:711
  273.4 4.5 collective-permute-done.22
  284.1 6.5 %collective-permute-start.31 = (bf16[2,1152,256]{2,1,0:T(8,128)(2,1)}, bf16[2,1152,256]{2,1,0:T(8,128)(2,1)}, u32[]{:S(2)}, u32[]{:S(2)}) collective-permute-start(bf16[2,1152,256]{2,1,0:T(8,128)(2,1)} %get-tuple-element.354), channel_id=1, source_target_pairs={{0,4},{2,6},{4,0},{6,2},{1,5},{3,7},{5,1},{7,3},{8,12},{10,14},{12... | collective-permute-start | bytes 3538952 | tf_op jit(solution)/shard_map/ppermute | solution.py:167
  290.5 13.8 %experts_back.2 = bf16[4,1536,256]{2,1,0:T(8,128)(2,1)} custom-call(bf16[1536,1280]{1,0:T(8,128)(2,1)} %get-tuple-element.208.gate_w_ref, bf16[1536,1280]{1,0:T(8,128)(2,1)} %get-tuple-element.209.up_w_ref, bf16[256,2048]{1,0:T(8,128)(2,1)} %get-tuple-element.216.refs_0_, bf16[512,2048]{1,0:T(8,128)(2,1)} %get-tuple-element.217.refs_1_, ...), custom_call_target="tpu_custom_call" | custom-call | flops 125829120 | bytes 221184 | tf_op jit(solution)/shard_map/experts_back/pallas_call | solution.py:758
  322.4 25.3 %collective-permute-done.23 = bf16[800,256]{1,0:T(8,128)(2,1)S(1)} collective-permute-done((bf16[800,256]{1,0:T(8,128)(2,1)S(1)}, bf16[800,256]{1,0:T(8,128)(2,1)S(1)}, u32[]{:S(2)}, u32[]{:S(2)}) %collective-permute-start.23) | collective-permute-done | bytes 409632 | tf_op jit(solution)/shard_map/ppermute | solution.py:68
  349.7 12.4 %collective-permute-done.28 = bf16[2,768,256]{2,1,0:T(8,128)(2,1)S(1)} collective-permute-done((bf16[2,768,256]{2,1,0:T(8,128)(2,1)S(1)}, bf16[2,768,256]{2,1,0:T(8,128)(2,1)S(1)}, u32[]{:S(2)}, u32[]{:S(2)}) %collective-permute-start.28) | collective-permute-done | bytes 786464 | tf_op jit(solution)/shard_map/ppermute | solution.py:68
  371.2 5.1 collective-permute-done.29
  394.0 11.6 %all-to-all-start = ((bf16[4,2,256,256]{3,2,1,0:T(8,128)(2,1)}), bf16[4,2,256,256]{3,2,1,0:T(8,128)(2,1)}, u32[]{:S(2)}, u32[]{:S(2)}) async-start(bf16[4,2,256,256]{3,2,1,0:T(8,128)(2,1)} %copy-done.6), calls=%async_computation | async-start | bytes 2097152 | tf_op jit(solution)/shard_map/all_to_all | solution.py:989
  424.2 4.8 collective-permute-start.36
  431.4 4.9 fusion.87
  436.8 5.5 all-to-all-done
  442.4 6.4 %all-to-all-start.1 = ((bf16[4,2,256,256]{3,2,1,0:T(8,128)(2,1)}), bf16[4,2,256,256]{3,2,1,0:T(8,128)(2,1)}, u32[]{:S(2)}, u32[]{:S(2)}) async-start(bf16[4,2,256,256]{3,2,1,0:T(8,128)(2,1)} %get-tuple-element.260), calls=%async_computation.1 | async-start | bytes 2097152 | tf_op jit(solution)/shard_map/all_to_all | solution.py:989
  467.9 8.1 %collective-permute-done.51 = bf16[4,48,1536]{2,1,0:T(8,128)(2,1)S(1)} collective-permute-done((bf16[4,48,1536]{2,1,0:T(8,128)(2,1)S(1)}, bf16[4,48,1536]{2,1,0:T(8,128)(2,1)S(1)}, u32[]{:S(2)}, u32[]{:S(2)}) %collective-permute-start.51) | collective-permute-done | bytes 589856 | tf_op jit(solution)/shard_map/ppermute | solution.py:155
  481.1 6.8 %collective-permute-done.40 = bf16[4,48,1536]{2,1,0:T(8,128)(2,1)S(1)} collective-permute-done((bf16[4,48,1536]{2,1,0:T(8,128)(2,1)S(1)}, bf16[4,48,1536]{2,1,0:T(8,128)(2,1)S(1)}, u32[]{:S(2)}, u32[]{:S(2)}) %collective-permute-start.40) | collective-permute-done | bytes 589856 | tf_op jit(solution)/shard_map/ppermute | solution.py:155
  498.2 6.4 %collective-permute-done.42 = bf16[48,1536]{1,0:T(8,128)(2,1)S(1)} collective-permute-done((bf16[48,1536]{1,0:T(8,128)(2,1)S(1)}, bf16[48,1536]{1,0:T(8,128)(2,1)S(1)}, u32[]{:S(2)}, u32[]{:S(2)}) %collective-permute-start.42) | collective-permute-done | bytes 147488 | tf_op jit(solution)/shard_map/ppermute | solution.py:167
  554.3 8.1 %collective-permute-done.47 = bf16[4,48,1024]{2,1,0:T(8,128)(2,1)S(1)} collective-permute-done((bf16[4,48,1024]{2,1,0:T(8,128)(2,1)S(1)}, bf16[4,48,1024]{2,1,0:T(8,128)(2,1)S(1)}, u32[]{:S(2)}, u32[]{:S(2)}) %collective-permute-start.47) | collective-permute-done | bytes 393248 | tf_op jit(solution)/shard_map/ppermute | solution.py:155
  570.2 4.5 collective-permute-done.49
  (451 shorter events, 232.2 us)
Async XLA Ops:
  10.9 59.5 %collective-permute-start.2 = (bf16[1024,256]{1,0:T(8,128)(2,1)S(1)}, bf16[1024,256]{1,0:T(8,128)(2,1)S(1)}, u32[]{:S(2)}, u32[]{:S(2)}) collective-permute-start(bf16[1024,256]{1,0:T(8,128)(2,1)S(1)} %pad_maximum_fusion.15.refs_0_.refs_4_), channel_id=1, source_target_pairs={{0,6},{1,7},{8,14},{9,15},{16,22},{17,23},{24,30},{25,31}} | collective-permute-start | bytes 1572872 | tf_op jit(solution)/shard_map/ppermute | solution.py:830
  17.9 52.5 %collective-permute-start.1 = (bf16[1024,256]{1,0:T(8,128)(2,1)S(1)}, bf16[1024,256]{1,0:T(8,128)(2,1)S(1)}, u32[]{:S(2)}, u32[]{:S(2)}) collective-permute-start(bf16[1024,256]{1,0:T(8,128)(2,1)S(1)} %pad_maximum_fusion.15.refs_0_.refs_4_), channel_id=1, source_target_pairs={{0,4},{2,6},{1,5},{3,7},{8,12},{10,14},{9,13},{11,15},{16,20},{18,... | collective-permute-start | bytes 1572872 | tf_op jit(solution)/shard_map/ppermute | solution.py:830
  19.2 51.2 %collective-permute-start = (bf16[1024,256]{1,0:T(8,128)(2,1)S(1)}, bf16[1024,256]{1,0:T(8,128)(2,1)S(1)}, u32[]{:S(2)}, u32[]{:S(2)}) collective-permute-start(bf16[1024,256]{1,0:T(8,128)(2,1)S(1)} %pad_maximum_fusion.15.refs_0_.refs_4_), channel_id=1, source_target_pairs={{0,2},{2,4},{4,6},{1,3},{3,5},{5,7},{8,10},{10,12},{12,14},{9,11},... | collective-permute-start | bytes 1572872 | tf_op jit(solution)/shard_map/ppermute | solution.py:830
  21.7 47.2 %collective-permute-start.4 = (bf16[1568,256]{1,0:T(8,128)(2,1)}, bf16[1568,256]{1,0:T(8,128)(2,1)}, u32[]{:S(2)}, u32[]{:S(2)}) collective-permute-start(bf16[1568,256]{1,0:T(8,128)(2,1)} %pad_maximum_fusion.12.refs_11_), channel_id=1, source_target_pairs={{0,2},{2,0},{4,6},{6,4},{1,3},{3,1},{5,7},{7,5},{8,10},{10,8},{12,... | collective-permute-start | bytes 2408456 | tf_op jit(solution)/shard_map/ppermute | solution.py:68
  21.8 48.6 %collective-permute-start.3 = (bf16[1568,256]{1,0:T(8,128)(2,1)}, bf16[1568,256]{1,0:T(8,128)(2,1)}, u32[]{:S(2)}, u32[]{:S(2)}) collective-permute-start(bf16[1568,256]{1,0:T(8,128)(2,1)} %pad_maximum_fusion.12.refs_11_), channel_id=1, source_target_pairs={{16,0},{24,8},{0,16},{8,24},{17,1},{25,9},{1,17},{9,25},{18,2},{26... | collective-permute-start | bytes 2408456 | tf_op jit(solution)/shard_map/ppermute | solution.py:61
  71.9 44.7 %collective-permute-start.8 = (bf16[3136,256]{1,0:T(8,128)(2,1)S(1)}, bf16[3136,256]{1,0:T(8,128)(2,1)S(1)}, u32[]{:S(2)}, u32[]{:S(2)}) collective-permute-start(bf16[3136,256]{1,0:T(8,128)(2,1)S(1)} %pad_maximum_fusion.6), channel_id=1, source_target_pairs={{8,0},{0,8},{24,16},{16,24},{9,1},{1,9},{25,17},{17,25},{10,2},{2,... | collective-permute-start | bytes 4816904 | tf_op jit(solution)/shard_map/ppermute | solution.py:61
  148.4 36.0 %collective-permute-start.17 = (bf16[2,1,1152,256]{3,2,1,0:T(8,128)(2,1)}, bf16[2,1,1152,256]{3,2,1,0:T(8,128)(2,1)}, u32[]{:S(2)}, u32[]{:S(2)}) collective-permute-start(bf16[2,1,1152,256]{3,2,1,0:T(8,128)(2,1)} %get-tuple-element.194), channel_id=1, source_target_pairs={{0,1},{1,0},{2,3},{3,2},{4,5},{5,4},{6,7},{7,6},{8,9},{9,8},{10,11... | collective-permute-start | bytes 3538952 | tf_op jit(solution)/shard_map/ppermute | solution.py:155
  150.0 67.1 %collective-permute-start.14 = (bf16[768,256]{1,0:T(8,128)(2,1)}, bf16[768,256]{1,0:T(8,128)(2,1)S(1)}, u32[]{:S(2)}, u32[]{:S(2)}) collective-permute-start(bf16[768,256]{1,0:T(8,128)(2,1)} %get-tuple-element.187), channel_id=1, source_target_pairs={{16,0},{24,8},{0,16},{8,24},{17,1},{25,9},{1,17},{9,25},{18,2},{26... | collective-permute-start | bytes 1179656 | tf_op jit(solution)/shard_map/ppermute | solution.py:61
  150.6 66.6 %collective-permute-start.15 = (bf16[768,256]{1,0:T(8,128)(2,1)}, bf16[768,256]{1,0:T(8,128)(2,1)}, u32[]{:S(2)}, u32[]{:S(2)}) collective-permute-start(bf16[768,256]{1,0:T(8,128)(2,1)} %get-tuple-element.188), channel_id=1, source_target_pairs={{8,0},{0,8},{24,16},{16,24},{9,1},{1,9},{25,17},{17,25},{10,2},{2,... | collective-permute-start | bytes 1179656 | tf_op jit(solution)/shard_map/ppermute | solution.py:61
  150.6 66.6 %collective-permute-start.16 = (bf16[768,256]{1,0:T(8,128)(2,1)}, bf16[768,256]{1,0:T(8,128)(2,1)S(1)}, u32[]{:S(2)}, u32[]{:S(2)}) collective-permute-start(bf16[768,256]{1,0:T(8,128)(2,1)} %get-tuple-element.189), channel_id=1, source_target_pairs={{24,0},{16,8},{8,16},{0,24},{25,1},{17,9},{9,17},{1,25},{26,2},{18... | collective-permute-start | bytes 1179656 | tf_op jit(solution)/shard_map/ppermute | solution.py:61
  226.4 37.1 %collective-permute-start.18 = (bf16[4,1600,256]{2,1,0:T(8,128)(2,1)}, bf16[4,1600,256]{2,1,0:T(8,128)(2,1)}, u32[]{:S(2)}, u32[]{:S(2)}) collective-permute-start(bf16[4,1600,256]{2,1,0:T(8,128)(2,1)} %experts_out.3), channel_id=1, source_target_pairs={{0,8},{8,0},{16,24},{24,16},{1,9},{9,1},{17,25},{25,17},{2,10},{10... | collective-permute-start | bytes 9830408 | tf_op jit(solution)/shard_map/ppermute | solution.py:65
  226.5 54.0 %collective-permute-start.21 = (bf16[2,2,1152,256]{3,2,1,0:T(8,128)(2,1)}, bf16[2,2,1152,256]{3,2,1,0:T(8,128)(2,1)}, u32[]{:S(2)}, u32[]{:S(2)}) collective-permute-start(bf16[2,2,1152,256]{3,2,1,0:T(8,128)(2,1)} %get-tuple-element.210), channel_id=1, source_target_pairs={{0,1},{1,0},{2,3},{3,2},{4,5},{5,4},{6,7},{7,6},{8,9},{9,8},{10,11... | collective-permute-start | bytes 7077896 | tf_op jit(solution)/shard_map/ppermute | solution.py:155
  241.3 65.1 %collective-permute-start.26 = (bf16[4,1536,256]{2,1,0:T(8,128)(2,1)}, bf16[4,1536,256]{2,1,0:T(8,128)(2,1)}, u32[]{:S(2)}, u32[]{:S(2)}) collective-permute-start(bf16[4,1536,256]{2,1,0:T(8,128)(2,1)} %experts_back.3), channel_id=1, source_target_pairs={{0,8},{8,0},{16,24},{24,16},{1,9},{9,1},{17,25},{25,17},{2,10},{10... | collective-permute-start | bytes 9437192 | tf_op jit(solution)/shard_map/ppermute | solution.py:65
  245.0 32.9 %collective-permute-start.22 = (bf16[1,1152,256]{2,1,0:T(8,128)(2,1)}, bf16[1,1152,256]{2,1,0:T(8,128)(2,1)}, u32[]{:S(2)}, u32[]{:S(2)}) collective-permute-start(bf16[1,1152,256]{2,1,0:T(8,128)(2,1)} %get-tuple-element.358), channel_id=1, source_target_pairs={{0,4},{2,6},{4,0},{6,2},{1,5},{3,7},{5,1},{7,3},{8,12},{10,14},{12... | collective-permute-start | bytes 1769480 | tf_op jit(solution)/shard_map/ppermute | solution.py:167
  267.4 36.9 %collective-permute-start.20 = (bf16[2,800,256]{2,1,0:T(8,128)(2,1)}, bf16[2,800,256]{2,1,0:T(8,128)(2,1)}, u32[]{:S(2)}, u32[]{:S(2)}) collective-permute-start(bf16[2,800,256]{2,1,0:T(8,128)(2,1)} %get-tuple-element.346), channel_id=1, source_target_pairs={{0,2},{2,0},{4,6},{6,4},{1,3},{3,1},{5,7},{7,5},{8,10},{10,8},{12,... | collective-permute-start | bytes 2457608 | tf_op jit(solution)/shard_map/ppermute | solution.py:68
  272.1 32.2 %collective-permute-start.19 = (bf16[2,800,256]{2,1,0:T(8,128)(2,1)}, bf16[2,800,256]{2,1,0:T(8,128)(2,1)}, u32[]{:S(2)}, u32[]{:S(2)}) collective-permute-start(bf16[2,800,256]{2,1,0:T(8,128)(2,1)} %get-tuple-element.348), channel_id=1, source_target_pairs={{0,16},{8,24},{16,0},{24,8},{1,17},{9,25},{17,1},{25,9},{2,18},{10... | collective-permute-start | bytes 2457608 | tf_op jit(solution)/shard_map/ppermute | solution.py:65
  277.9 71.8 %collective-permute-start.25 = (bf16[2,2,1152,256]{3,2,1,0:T(8,128)(2,1)}, bf16[2,2,1152,256]{3,2,1,0:T(8,128)(2,1)}, u32[]{:S(2)}, u32[]{:S(2)}) collective-permute-start(bf16[2,2,1152,256]{3,2,1,0:T(8,128)(2,1)} %get-tuple-element.226), channel_id=1, source_target_pairs={{0,1},{1,0},{2,3},{3,2},{4,5},{5,4},{6,7},{7,6},{8,9},{9,8},{10,11... | collective-permute-start | bytes 7077896 | tf_op jit(solution)/shard_map/ppermute | solution.py:155
  284.1 104.8 %collective-permute-start.31 = (bf16[2,1152,256]{2,1,0:T(8,128)(2,1)}, bf16[2,1152,256]{2,1,0:T(8,128)(2,1)}, u32[]{:S(2)}, u32[]{:S(2)}) collective-permute-start(bf16[2,1152,256]{2,1,0:T(8,128)(2,1)} %get-tuple-element.354), channel_id=1, source_target_pairs={{0,4},{2,6},{4,0},{6,2},{1,5},{3,7},{5,1},{7,3},{8,12},{10,14},{12... | collective-permute-start | bytes 3538952 | tf_op jit(solution)/shard_map/ppermute | solution.py:167
  310.8 36.9 %collective-permute-start.23 = (bf16[800,256]{1,0:T(8,128)(2,1)S(1)}, bf16[800,256]{1,0:T(8,128)(2,1)S(1)}, u32[]{:S(2)}, u32[]{:S(2)}) collective-permute-start(bf16[800,256]{1,0:T(8,128)(2,1)S(1)} %fusion.33), channel_id=1, source_target_pairs={{0,2},{2,0},{4,6},{6,4},{1,3},{3,1},{5,7},{7,5},{8,10},{10,8},{12,... | collective-permute-start | bytes 1228808 | tf_op jit(solution)/shard_map/ppermute | solution.py:68
  312.2 37.5 %collective-permute-start.27 = (bf16[2,768,256]{2,1,0:T(8,128)(2,1)S(1)}, bf16[2,768,256]{2,1,0:T(8,128)(2,1)S(1)}, u32[]{:S(2)}, u32[]{:S(2)}) collective-permute-start(bf16[2,768,256]{2,1,0:T(8,128)(2,1)S(1)} %fusion.26), channel_id=1, source_target_pairs={{0,16},{8,24},{16,0},{24,8},{1,17},{9,25},{17,1},{25,9},{2,18},{10... | collective-permute-start | bytes 2359304 | tf_op jit(solution)/shard_map/ppermute | solution.py:65
  318.3 43.8 %collective-permute-start.28 = (bf16[2,768,256]{2,1,0:T(8,128)(2,1)S(1)}, bf16[2,768,256]{2,1,0:T(8,128)(2,1)S(1)}, u32[]{:S(2)}, u32[]{:S(2)}) collective-permute-start(bf16[2,768,256]{2,1,0:T(8,128)(2,1)S(1)} %get-tuple-element.350), channel_id=1, source_target_pairs={{0,2},{2,0},{4,6},{6,4},{1,3},{3,1},{5,7},{7,5},{8,10},{10,8},{12,... | collective-permute-start | bytes 2359304 | tf_op jit(solution)/shard_map/ppermute | solution.py:68
  367.7 68.6 %collective-permute-start.35 = (bf16[2,1152,256]{2,1,0:T(8,128)(2,1)}, bf16[2,1152,256]{2,1,0:T(8,128)(2,1)}, u32[]{:S(2)}, u32[]{:S(2)}) collective-permute-start(bf16[2,1152,256]{2,1,0:T(8,128)(2,1)} %get-tuple-element.352), channel_id=1, source_target_pairs={{0,4},{2,6},{4,0},{6,2},{1,5},{3,7},{5,1},{7,3},{8,12},{10,14},{12... | collective-permute-start | bytes 3538952 | tf_op jit(solution)/shard_map/ppermute | solution.py:167
  394.0 48.3 %all-to-all-start = ((bf16[4,2,256,256]{3,2,1,0:T(8,128)(2,1)}), bf16[4,2,256,256]{3,2,1,0:T(8,128)(2,1)}, u32[]{:S(2)}, u32[]{:S(2)}) async-start(bf16[4,2,256,256]{3,2,1,0:T(8,128)(2,1)} %copy-done.6), calls=%async_computation | async-start | bytes 2097152 | tf_op jit(solution)/shard_map/all_to_all | solution.py:989
  410.4 31.9 %collective-permute-start.33 = (bf16[1584,256]{1,0:T(8,128)(2,1)}, bf16[1584,256]{1,0:T(8,128)(2,1)}, u32[]{:S(2)}, u32[]{:S(2)}) collective-permute-start(bf16[1584,256]{1,0:T(8,128)(2,1)} %pad_maximum_fusion.11.refs_4_), channel_id=1, source_target_pairs={{8,0},{0,8},{24,16},{16,24},{9,1},{1,9},{25,17},{17,25},{10,2},{2,... | collective-permute-start | bytes 2433032 | tf_op jit(solution)/shard_map/ppermute | solution.py:61
  410.5 31.9 %collective-permute-start.34 = (bf16[1584,256]{1,0:T(8,128)(2,1)}, bf16[1584,256]{1,0:T(8,128)(2,1)}, u32[]{:S(2)}, u32[]{:S(2)}) collective-permute-start(bf16[1584,256]{1,0:T(8,128)(2,1)} %collective-permute-done.32.refs_5_), channel_id=1, source_target_pairs={{8,0},{0,8},{24,16},{16,24},{9,1},{1,9},{25,17},{17,25},{10,2},{2,... | collective-permute-start | bytes 2433032 | tf_op jit(solution)/shard_map/ppermute | solution.py:61
  424.2 82.2 %collective-permute-start.36 = (bf16[3,2,192,256]{3,2,0,1:T(8,128)(2,1)}, bf16[3,2,192,256]{3,2,0,1:T(8,128)(2,1)S(1)}, u32[]{:S(2)}, u32[]{:S(2)}) collective-permute-start(bf16[3,2,192,256]{3,2,0,1:T(8,128)(2,1)} %fusion.32), channel_id=1, source_target_pairs={{0,2},{2,0},{4,6},{6,4},{1,3},{3,1},{5,7},{7,5},{8,10},{10,8},{12,... | collective-permute-start | bytes 1769480 | tf_op jit(solution)/shard_map/ppermute | solution.py:68
  436.3 25.5 %collective-permute-start.38 = (bf16[1536,256]{1,0:T(8,128)(2,1)S(1)}, bf16[1536,256]{1,0:T(8,128)(2,1)}, u32[]{:S(2)}, u32[]{:S(2)}) collective-permute-start(bf16[1536,256]{1,0:T(8,128)(2,1)S(1)} %pad_maximum_fusion.14.refs_4_), channel_id=1, source_target_pairs={{8,0},{0,8},{24,16},{16,24},{9,1},{1,9},{25,17},{17,25},{10,2},{2,... | collective-permute-start | bytes 2359304 | tf_op jit(solution)/shard_map/ppermute | solution.py:61
  436.3 25.5 %collective-permute-start.39 = (bf16[1536,256]{1,0:T(8,128)(2,1)}, bf16[1536,256]{1,0:T(8,128)(2,1)}, u32[]{:S(2)}, u32[]{:S(2)}) collective-permute-start(bf16[1536,256]{1,0:T(8,128)(2,1)} %collective-permute-done.37.refs_5_), channel_id=1, source_target_pairs={{8,0},{0,8},{24,16},{16,24},{9,1},{1,9},{25,17},{17,25},{10,2},{2,... | collective-permute-start | bytes 2359304 | tf_op jit(solution)/shard_map/ppermute | solution.py:61
  442.4 64.1 %all-to-all-start.1 = ((bf16[4,2,256,256]{3,2,1,0:T(8,128)(2,1)}), bf16[4,2,256,256]{3,2,1,0:T(8,128)(2,1)}, u32[]{:S(2)}, u32[]{:S(2)}) async-start(bf16[4,2,256,256]{3,2,1,0:T(8,128)(2,1)} %get-tuple-element.260), calls=%async_computation.1 | async-start | bytes 2097152 | tf_op jit(solution)/shard_map/all_to_all | solution.py:989
  509.0 39.5 %collective-permute-start.45 = (bf16[1024,256]{1,0:T(8,128)(2,1)S(1)}, bf16[1024,256]{1,0:T(8,128)(2,1)S(1)}, u32[]{:S(2)}, u32[]{:S(2)}) collective-permute-start(bf16[1024,256]{1,0:T(8,128)(2,1)S(1)} %pad_maximum_fusion.16.refs_4_), channel_id=1, source_target_pairs={{8,0},{0,8},{24,16},{16,24},{9,1},{1,9},{25,17},{17,25},{10,2},{2,... | collective-permute-start | bytes 1572872 | tf_op jit(solution)/shard_map/ppermute | solution.py:61
  509.1 38.5 %collective-permute-start.44 = (bf16[1024,256]{1,0:T(8,128)(2,1)S(1)}, bf16[1024,256]{1,0:T(8,128)(2,1)S(1)}, u32[]{:S(2)}, u32[]{:S(2)}) collective-permute-start(bf16[1024,256]{1,0:T(8,128)(2,1)S(1)} %pad_maximum_fusion.16.refs_4_), channel_id=1, source_target_pairs={{16,0},{24,8},{0,16},{8,24},{17,1},{25,9},{1,17},{9,25},{18,2},{26... | collective-permute-start | bytes 1572872 | tf_op jit(solution)/shard_map/ppermute | solution.py:61
  514.7 29.2 %all-to-all-start.2 = ((bf16[8,48,128]{2,1,0:T(8,128)(2,1)}), bf16[8,48,128]{2,1,0:T(8,128)(2,1)}, u32[]{:S(2)}, u32[]{:S(2)}) async-start(bf16[8,48,128]{2,1,0:T(8,128)(2,1)} %maximum_maximum_fusion), calls=%async_computation.2 | async-start | bytes 196608 | tf_op jit(solution)/shard_map/all_to_all | solution.py:1050
  (119 other events, 991.3 us)

commit v5 on v4

--- a/solution.py
+++ b/solution.py
@@ -1054,7 +1054,8 @@
         [rotate_t(x, cosine, -sine).astype(BF16) for x in (grad_query_a, grad_query_b)]
     )
     query_sum = comm.scatter_rows(h1_rows, comm.gather_expert(grad_query_raw), width)
-    late, pairs, kv_b = hold((crossing[-1], pairs, kv_b))
+    late = crossing[-1]
+    pairs, kv_b = hold((pairs, kv_b))
     totals.append(total_of([late]))
     pairs.append(send_pair(totals[-1][1]))
     kv_sums = [jnp.sum(x.astype(F32), 0) for x in (kv_a, kv_b)]

time: 587 us -> 582 us (level)
  waiting for transfers between devices: 138 us -> 132 us
    ppermute x6, waiting for transfers between devices: 24 us -> 7.2 us  [send_dp(): lax.ppermute(parts[s - 1], 'dp', [(i, (i + s) % n) for i in range(n)])]
    ppermute x9, waiting for transfers between devices: 79 us -> 85 us  [pair(): lax.ppermute(value, 'context', [(i, i ^ 1) for i in range(self.n_context)])]
    unnamed x207 -> x201, local copies, waits for them, and re-layouts: 18.8 us -> 20 us
  transfers between devices with their start and end apart: 59 -> 59, of which waited for: 24 -> 22; matrix products, arithmetic and copies ran while one was open for 24% -> 25% of each run, Pallas kernels for 25% -> 26%
where the time goes in v5:
time: 582 us; the launch traced here: 573 us
  Pallas kernels  177 us (30%)
  waiting for transfers between devices  132 us (23%)
  starting transfers between devices  102 us (18%)
  other arithmetic  79.8 us (14%)
  local copies, waits for them, and re-layouts  50.3 us (9%)
  matrix products  30.2 us (5%)
    pallas_call x3, Pallas kernels, act(): pl.pallas_call(functools.partial(self.act_kernel, first, n, make_gates),...  86.3 us
    ppermute x9, waiting for transfers between devices, pair(): lax.ppermute(value, 'context', [(i, i ^ 1) for i in range(self.n_context)])  85 us
    dot_general x14, matrix products, mm(): lax.dot_general(a, b, (((da,), (db,)), ((), ())), preferred_element_type=...  30.2 us
    ppermute x12, starting transfers between devices, send_context(): out.append(lax.ppermute(parts[s - 1], 'context', pairs))  29.4 us
    pallas_call x2, Pallas kernels, back(): pl.pallas_call(functools.partial(self.back_kernel, parts), out_shape=jax....  28 us
    ppermute x12, waiting for transfers between devices, send_context(): out.append(lax.ppermute(parts[s - 1], 'context', pairs))  23.8 us
    unnamed x201, local copies, waits for them, and re-layouts  20 us
    pallas_call x2, Pallas kernels, out(): pl.pallas_call(functools.partial(self.out_kernel, parts), out_shape=jax.S...  18.6 us
  transfers between devices with their start and end apart: 59, of which 22 were waited for; matrix products, arithmetic and copies ran while one was open for 25% of the time, Pallas kernels for 26%

profile of v5, /device:TPU:0, one launch (start us, length us, event | category | flops | bytes accessed | tf_op | source)
XLA Modules:
  0.0 572.8 jit_solution(8994447045648949094)
XLA Ops:
  10.9 7.0 %collective-permute-start.2 = (bf16[1024,256]{1,0:T(8,128)(2,1)S(1)}, bf16[1024,256]{1,0:T(8,128)(2,1)S(1)}, u32[]{:S(2)}, u32[]{:S(2)}) collective-permute-start(bf16[1024,256]{1,0:T(8,128)(2,1)S(1)} %pad_maximum_fusion.15.refs_0_.refs_4_), channel_id=1, source_target_pairs={{0,6},{1,7},{8,14},{9,15},{16,22},{17,23},{24,30},{25,31}} | collective-permute-start | bytes 1572872 | tf_op jit(solution)/shard_map/ppermute | solution.py:830
  23.4 4.9 convolution_bitcast_fusion
  31.3 15.1 %prepare_weights.1 = (bf16[5,2,2,128,1536]{4,3,2,1,0:T(8,128)(2,1)}, bf16[1536,1280]{1,0:T(8,128)(2,1)}, bf16[1536,1280]{1,0:T(8,128)(2,1)}, bf16[1280,1536]{1,0:T(8,128)(2,1)}, bf16[1536,1280]{1,0:T(8,128)(2,1)}) custom-call(s32[1]{0:T(128)} %bitcast.14.p_ref, bf16[5,1536,512]{2,1,0:T(8,128)(2,1)} %gate_ref.1, bf16[5,1536,512]{2,1,0:T(8,128)(2,1)} %up_ref.1, ...), custom_call_target="tpu_custom_call" | custom-call | bytes 552960 | tf_op jit(solution)/shard_map/prepare_weights/pallas_call | solution.py:441
  53.6 15.3 %collective-permute-done.4.refs_13_ = bf16[1568,256]{1,0:T(8,128)(2,1)} collective-permute-done((bf16[1568,256]{1,0:T(8,128)(2,1)}, bf16[1568,256]{1,0:T(8,128)(2,1)}, u32[]{:S(2)}, u32[]{:S(2)}) %collective-permute-start.4) | collective-permute-done | bytes 802848 | tf_op jit(solution)/shard_map/ppermute | solution.py:68
  72.0 11.0 %attn_fwd.1 = (f32[1536,256]{1,0:T(8,128)S(1)}, bf16[1536,256]{1,0:T(8,128)(2,1)S(1)}, f32[8,8,256]{2,1,0:T(8,128)S(1)}) custom-call(s32[1]{0:T(128)} %bitcast.5.c_ref, bf16[1536,256]{1,0:T(8,128)(2,1)S(1)} %bitcast.217, bf16[1024,256]{1,0:T(8,128)(2,1)S(1)} %pad_maximum_fusion.15.refs_0_.refs_4_, ...), custom_call_target="tpu_custom_call" | custom-call | flops 100663296 | bytes 98304 | tf_op jit(solution)/shard_map/attn_fwd/pallas_call | solution.py:304
  83.0 4.9 multiply_reduce_fusion.2
  97.2 14.2 %collective-permute-done.7.refs_6_ = bf16[1536,256]{1,0:T(8,128)(2,1)S(1)} collective-permute-done((bf16[1536,256]{1,0:T(8,128)(2,1)S(1)}, bf16[1536,256]{1,0:T(8,128)(2,1)S(1)}, u32[]{:S(2)}, u32[]{:S(2)}) %collective-permute-start.7) | collective-permute-done | bytes 786464 | tf_op jit(solution)/shard_map/ppermute | solution.py:68
  116.7 6.7 %collective-permute-done.11.refs_8_ = bf16[768,256]{1,0:T(8,128)(2,1)S(1)} collective-permute-done((bf16[768,256]{1,0:T(8,128)(2,1)S(1)}, bf16[768,256]{1,0:T(8,128)(2,1)S(1)}, u32[]{:S(2)}, u32[]{:S(2)}) %collective-permute-start.11) | collective-permute-done | bytes 393248 | tf_op jit(solution)/shard_map/ppermute | solution.py:68
  129.5 21.4 %experts_act.3 = (f32[32,2048]{1,0:T(8,128)}, f32[32,2048]{1,0:T(8,128)}, bf16[256,2048]{1,0:T(8,128)(2,1)}, bf16[256,2048]{1,0:T(8,128)(2,1)}, bf16[256,2048]{1...) custom-call(s32[3]{0:T(128)} %pad_add_fusion.e_ref, ...), custom_call_target="tpu_custom_call" | custom-call | flops 150994944 | bytes 282624 | tf_op jit(solution)/shard_map/experts_act/pallas_call | solution.py:656
  154.6 32.3 %experts_act.4 = (bf16[512,2048]{1,0:T(8,128)(2,1)}, bf16[512,2048]{1,0:T(8,128)(2,1)}, bf16[512,2048]{1,0:T(8,128)(2,1)}, f32[2,8,2048]{2,1,0:T(8,128)}, bf16[2...) custom-call(s32[3]{0:T(128)} %pad_add_fusion.e_ref, ...), custom_call_target="tpu_custom_call" | custom-call | flops 301989888 | bytes 368640 | tf_op jit(solution)/shard_map/experts_act/pallas_call | solution.py:656
  186.9 32.6 %experts_act.5 = (bf16[512,2048]{1,0:T(8,128)(2,1)}, bf16[512,2048]{1,0:T(8,128)(2,1)}, bf16[512,2048]{1,0:T(8,128)(2,1)}, f32[2,8,2048]{2,1,0:T(8,128)}, bf16[2...) custom-call(s32[3]{0:T(128)} %pad_add_fusion.e_ref, ...), custom_call_target="tpu_custom_call" | custom-call | flops 301989888 | bytes 368640 | tf_op jit(solution)/shard_map/experts_act/pallas_call | solution.py:656
  219.6 9.2 %experts_out.3 = bf16[4,1600,256]{2,1,0:T(8,128)(2,1)} custom-call(s32[3]{0:T(128)} %pad_add_fusion.e_ref, bf16[1536,1280]{1,0:T(8,128)(2,1)} %get-tuple-element.165.weight_ref, bf16[256,2048]{1,0:T(8,128)(2,1)} %get-tuple-element.195.refs_0_, bf16[512,2048]{1,0:T(8,128)(2,1)} %get-tuple-element.196.refs_1_, bf16[512,2048]{1,0:T(8,128)(2,1)} %get-tuple-element.197.refs_2_, ...), custom_call_target="tpu_custom_call" | custom-call | flops 62914560 | bytes 159744 | tf_op jit(solution)/shard_map/experts_out/pallas_call | solution.py:711
  229.5 14.2 %experts_back.3 = bf16[4,1536,256]{2,1,0:T(8,128)(2,1)} custom-call(bf16[1536,1280]{1,0:T(8,128)(2,1)} %get-tuple-element.206.gate_w_ref, bf16[1536,1280]{1,0:T(8,128)(2,1)} %get-tuple-element.207.up_w_ref, bf16[256,2048]{1,0:T(8,128)(2,1)} %get-tuple-element.214.refs_0_, bf16[512,2048]{1,0:T(8,128)(2,1)} %get-tuple-element.215.refs_1_, ...), custom_call_target="tpu_custom_call" | custom-call | flops 125829120 | bytes 221184 | tf_op jit(solution)/shard_map/experts_back/pallas_call | solution.py:758
  247.5 6.0 %collective-permute-start.22 = (bf16[1,1152,256]{2,1,0:T(8,128)(2,1)}, bf16[1,1152,256]{2,1,0:T(8,128)(2,1)}, u32[]{:S(2)}, u32[]{:S(2)}) collective-permute-start(bf16[1,1152,256]{2,1,0:T(8,128)(2,1)} %get-tuple-element.354), channel_id=1, source_target_pairs={{0,4},{2,6},{4,0},{6,2},{1,5},{3,7},{5,1},{7,3},{8,12},{10,14},{12... | collective-permute-start | bytes 1769480 | tf_op jit(solution)/shard_map/ppermute | solution.py:167
  253.5 9.4 %experts_out.2 = bf16[4,1600,256]{2,1,0:T(8,128)(2,1)} custom-call(s32[3]{0:T(128)} %pad_add_fusion.e_ref, bf16[1536,1280]{1,0:T(8,128)(2,1)} %get-tuple-element.165.weight_ref, bf16[256,2048]{1,0:T(8,128)(2,1)} %get-tuple-element.195.refs_0_, bf16[512,2048]{1,0:T(8,128)(2,1)} %get-tuple-element.196.refs_1_, bf16[512,2048]{1,0:T(8,128)(2,1)} %get-tuple-element.197.refs_2_, ...), custom_call_target="tpu_custom_call" | custom-call | flops 62914560 | bytes 159744 | tf_op jit(solution)/shard_map/experts_out/pallas_call | solution.py:711
  286.5 6.5 %collective-permute-start.31 = (bf16[2,1152,256]{2,1,0:T(8,128)(2,1)}, bf16[2,1152,256]{2,1,0:T(8,128)(2,1)}, u32[]{:S(2)}, u32[]{:S(2)}) collective-permute-start(bf16[2,1152,256]{2,1,0:T(8,128)(2,1)} %get-tuple-element.350), channel_id=1, source_target_pairs={{0,4},{2,6},{4,0},{6,2},{1,5},{3,7},{5,1},{7,3},{8,12},{10,14},{12... | collective-permute-start | bytes 3538952 | tf_op jit(solution)/shard_map/ppermute | solution.py:167
  293.0 13.8 %experts_back.2 = bf16[4,1536,256]{2,1,0:T(8,128)(2,1)} custom-call(bf16[1536,1280]{1,0:T(8,128)(2,1)} %get-tuple-element.206.gate_w_ref, bf16[1536,1280]{1,0:T(8,128)(2,1)} %get-tuple-element.207.up_w_ref, bf16[256,2048]{1,0:T(8,128)(2,1)} %get-tuple-element.214.refs_0_, bf16[512,2048]{1,0:T(8,128)(2,1)} %get-tuple-element.215.refs_1_, ...), custom_call_target="tpu_custom_call" | custom-call | flops 125829120 | bytes 221184 | tf_op jit(solution)/shard_map/experts_back/pallas_call | solution.py:758
  324.8 25.3 %collective-permute-done.23 = bf16[800,256]{1,0:T(8,128)(2,1)S(1)} collective-permute-done((bf16[800,256]{1,0:T(8,128)(2,1)S(1)}, bf16[800,256]{1,0:T(8,128)(2,1)S(1)}, u32[]{:S(2)}, u32[]{:S(2)}) %collective-permute-start.23) | collective-permute-done | bytes 409632 | tf_op jit(solution)/shard_map/ppermute | solution.py:68
  352.1 12.4 %collective-permute-done.28 = bf16[2,768,256]{2,1,0:T(8,128)(2,1)S(1)} collective-permute-done((bf16[2,768,256]{2,1,0:T(8,128)(2,1)S(1)}, bf16[2,768,256]{2,1,0:T(8,128)(2,1)S(1)}, u32[]{:S(2)}, u32[]{:S(2)}) %collective-permute-start.28) | collective-permute-done | bytes 786464 | tf_op jit(solution)/shard_map/ppermute | solution.py:68
  373.6 5.1 collective-permute-done.29
  396.5 11.5 %all-to-all-start = ((bf16[4,2,256,256]{3,2,1,0:T(8,128)(2,1)}), bf16[4,2,256,256]{3,2,1,0:T(8,128)(2,1)}, u32[]{:S(2)}, u32[]{:S(2)}) async-start(bf16[4,2,256,256]{3,2,1,0:T(8,128)(2,1)} %copy-done.6), calls=%async_computation | async-start | bytes 2097152 | tf_op jit(solution)/shard_map/all_to_all | solution.py:989
  424.2 4.8 collective-permute-start.36
  431.5 4.9 fusion.87
  437.5 7.2 %all-to-all-done = bf16[4,2,256,256]{3,2,1,0:T(8,128)(2,1)} async-done(((bf16[4,2,256,256]{3,2,1,0:T(8,128)(2,1)}), bf16[4,2,256,256]{3,2,1,0:T(8,128)(2,1)}, u32[]{:S(2)}, u32[]{:S(2)}) %all-to-all-start) | async-done | bytes 1048608 | tf_op jit(solution)/shard_map/all_to_all | solution.py:989
  446.9 6.3 %all-to-all-start.1 = ((bf16[4,2,256,256]{3,2,1,0:T(8,128)(2,1)}), bf16[4,2,256,256]{3,2,1,0:T(8,128)(2,1)}, u32[]{:S(2)}, u32[]{:S(2)}) async-start(bf16[4,2,256,256]{3,2,1,0:T(8,128)(2,1)} %get-tuple-element.256), calls=%async_computation.1 | async-start | bytes 2097152 | tf_op jit(solution)/shard_map/all_to_all | solution.py:989
  460.3 4.8 row_products.5
  477.9 6.0 %collective-permute-done.55 = bf16[2,2,192,256]{3,2,0,1:T(8,128)(2,1)S(1)} collective-permute-done((bf16[2,2,192,256]{3,2,0,1:T(8,128)(2,1)}, bf16[2,2,192,256]{3,2,0,1:T(8,128)(2,1)S(1)}, u32[]{:S(2)}, u32[]{:S(2)}) %collective-permute-start.55) | collective-permute-done | bytes 393248 | tf_op jit(solution)/shard_map/ppermute | solution.py:68
  497.7 5.5 collective-permute-done.40
  503.4 4.8 collective-permute-start.43
  508.8 6.0 %collective-permute-done.53 = bf16[48,1536]{1,0:T(8,128)(2,1)S(1)} collective-permute-done((bf16[48,1536]{1,0:T(8,128)(2,1)S(1)}, bf16[48,1536]{1,0:T(8,128)(2,1)S(1)}, u32[]{:S(2)}, u32[]{:S(2)}) %collective-permute-start.53) | collective-permute-done | bytes 147488 | tf_op jit(solution)/shard_map/ppermute | solution.py:167
  516.6 6.1 %collective-permute-done.42 = bf16[48,1536]{1,0:T(8,128)(2,1)S(1)} collective-permute-done((bf16[48,1536]{1,0:T(8,128)(2,1)S(1)}, bf16[48,1536]{1,0:T(8,128)(2,1)S(1)}, u32[]{:S(2)}, u32[]{:S(2)}) %collective-permute-start.42) | collective-permute-done | bytes 147488 | tf_op jit(solution)/shard_map/ppermute | solution.py:167
  565.0 4.6 collective-permute-done.49
  (444 shorter events, 230.5 us)
Async XLA Ops:
  10.9 59.5 %collective-permute-start.2 = (bf16[1024,256]{1,0:T(8,128)(2,1)S(1)}, bf16[1024,256]{1,0:T(8,128)(2,1)S(1)}, u32[]{:S(2)}, u32[]{:S(2)}) collective-permute-start(bf16[1024,256]{1,0:T(8,128)(2,1)S(1)} %pad_maximum_fusion.15.refs_0_.refs_4_), channel_id=1, source_target_pairs={{0,6},{1,7},{8,14},{9,15},{16,22},{17,23},{24,30},{25,31}} | collective-permute-start | bytes 1572872 | tf_op jit(solution)/shard_map/ppermute | solution.py:830
  17.9 52.5 %collective-permute-start.1 = (bf16[1024,256]{1,0:T(8,128)(2,1)S(1)}, bf16[1024,256]{1,0:T(8,128)(2,1)S(1)}, u32[]{:S(2)}, u32[]{:S(2)}) collective-permute-start(bf16[1024,256]{1,0:T(8,128)(2,1)S(1)} %pad_maximum_fusion.15.refs_0_.refs_4_), channel_id=1, source_target_pairs={{0,4},{2,6},{1,5},{3,7},{8,12},{10,14},{9,13},{11,15},{16,20},{18,... | collective-permute-start | bytes 1572872 | tf_op jit(solution)/shard_map/ppermute | solution.py:830
  19.2 51.2 %collective-permute-start = (bf16[1024,256]{1,0:T(8,128)(2,1)S(1)}, bf16[1024,256]{1,0:T(8,128)(2,1)S(1)}, u32[]{:S(2)}, u32[]{:S(2)}) collective-permute-start(bf16[1024,256]{1,0:T(8,128)(2,1)S(1)} %pad_maximum_fusion.15.refs_0_.refs_4_), channel_id=1, source_target_pairs={{0,2},{2,4},{4,6},{1,3},{3,5},{5,7},{8,10},{10,12},{12,14},{9,11},... | collective-permute-start | bytes 1572872 | tf_op jit(solution)/shard_map/ppermute | solution.py:830
  21.7 47.2 %collective-permute-start.4 = (bf16[1568,256]{1,0:T(8,128)(2,1)}, bf16[1568,256]{1,0:T(8,128)(2,1)}, u32[]{:S(2)}, u32[]{:S(2)}) collective-permute-start(bf16[1568,256]{1,0:T(8,128)(2,1)} %pad_maximum_fusion.12.refs_11_), channel_id=1, source_target_pairs={{0,2},{2,0},{4,6},{6,4},{1,3},{3,1},{5,7},{7,5},{8,10},{10,8},{12,... | collective-permute-start | bytes 2408456 | tf_op jit(solution)/shard_map/ppermute | solution.py:68
  21.8 48.6 %collective-permute-start.3 = (bf16[1568,256]{1,0:T(8,128)(2,1)}, bf16[1568,256]{1,0:T(8,128)(2,1)}, u32[]{:S(2)}, u32[]{:S(2)}) collective-permute-start(bf16[1568,256]{1,0:T(8,128)(2,1)} %pad_maximum_fusion.12.refs_11_), channel_id=1, source_target_pairs={{16,0},{24,8},{0,16},{8,24},{17,1},{25,9},{1,17},{9,25},{18,2},{26... | collective-permute-start | bytes 2408456 | tf_op jit(solution)/shard_map/ppermute | solution.py:61
  71.9 44.8 %collective-permute-start.8 = (bf16[3136,256]{1,0:T(8,128)(2,1)S(1)}, bf16[3136,256]{1,0:T(8,128)(2,1)S(1)}, u32[]{:S(2)}, u32[]{:S(2)}) collective-permute-start(bf16[3136,256]{1,0:T(8,128)(2,1)S(1)} %pad_maximum_fusion.6), channel_id=1, source_target_pairs={{8,0},{0,8},{24,16},{16,24},{9,1},{1,9},{25,17},{17,25},{10,2},{2,... | collective-permute-start | bytes 4816904 | tf_op jit(solution)/shard_map/ppermute | solution.py:61
  88.8 22.5 %collective-permute-start.7 = (bf16[1536,256]{1,0:T(8,128)(2,1)S(1)}, bf16[1536,256]{1,0:T(8,128)(2,1)S(1)}, u32[]{:S(2)}, u32[]{:S(2)}) collective-permute-start(bf16[1536,256]{1,0:T(8,128)(2,1)S(1)} %multiply_convert_fusion.refs_4_), channel_id=1, source_target_pairs={{0,2},{2,0},{4,6},{6,4},{1,3},{3,1},{5,7},{7,5},{8,10},{10,8},{12,... | collective-permute-start | bytes 2359304 | tf_op jit(solution)/shard_map/ppermute | solution.py:68
  150.9 36.0 %collective-permute-start.17 = (bf16[2,1,1152,256]{3,2,1,0:T(8,128)(2,1)}, bf16[2,1,1152,256]{3,2,1,0:T(8,128)(2,1)}, u32[]{:S(2)}, u32[]{:S(2)}) collective-permute-start(bf16[2,1,1152,256]{3,2,1,0:T(8,128)(2,1)} %get-tuple-element.192), channel_id=1, source_target_pairs={{0,1},{1,0},{2,3},{3,2},{4,5},{5,4},{6,7},{7,6},{8,9},{9,8},{10,11... | collective-permute-start | bytes 3538952 | tf_op jit(solution)/shard_map/ppermute | solution.py:155
  152.5 67.1 %collective-permute-start.14 = (bf16[768,256]{1,0:T(8,128)(2,1)}, bf16[768,256]{1,0:T(8,128)(2,1)S(1)}, u32[]{:S(2)}, u32[]{:S(2)}) collective-permute-start(bf16[768,256]{1,0:T(8,128)(2,1)} %get-tuple-element.185), channel_id=1, source_target_pairs={{16,0},{24,8},{0,16},{8,24},{17,1},{25,9},{1,17},{9,25},{18,2},{26... | collective-permute-start | bytes 1179656 | tf_op jit(solution)/shard_map/ppermute | solution.py:61
  153.2 66.4 %collective-permute-start.15 = (bf16[768,256]{1,0:T(8,128)(2,1)}, bf16[768,256]{1,0:T(8,128)(2,1)}, u32[]{:S(2)}, u32[]{:S(2)}) collective-permute-start(bf16[768,256]{1,0:T(8,128)(2,1)} %get-tuple-element.186), channel_id=1, source_target_pairs={{8,0},{0,8},{24,16},{16,24},{9,1},{1,9},{25,17},{17,25},{10,2},{2,... | collective-permute-start | bytes 1179656 | tf_op jit(solution)/shard_map/ppermute | solution.py:61
  153.2 66.4 %collective-permute-start.16 = (bf16[768,256]{1,0:T(8,128)(2,1)}, bf16[768,256]{1,0:T(8,128)(2,1)S(1)}, u32[]{:S(2)}, u32[]{:S(2)}) collective-permute-start(bf16[768,256]{1,0:T(8,128)(2,1)} %get-tuple-element.187), channel_id=1, source_target_pairs={{24,0},{16,8},{8,16},{0,24},{25,1},{17,9},{9,17},{1,25},{26,2},{18... | collective-permute-start | bytes 1179656 | tf_op jit(solution)/shard_map/ppermute | solution.py:61
  228.9 37.1 %collective-permute-start.18 = (bf16[4,1600,256]{2,1,0:T(8,128)(2,1)}, bf16[4,1600,256]{2,1,0:T(8,128)(2,1)}, u32[]{:S(2)}, u32[]{:S(2)}) collective-permute-start(bf16[4,1600,256]{2,1,0:T(8,128)(2,1)} %experts_out.3), channel_id=1, source_target_pairs={{0,8},{8,0},{16,24},{24,16},{1,9},{9,1},{17,25},{25,17},{2,10},{10... | collective-permute-start | bytes 9830408 | tf_op jit(solution)/shard_map/ppermute | solution.py:65
  228.9 54.0 %collective-permute-start.21 = (bf16[2,2,1152,256]{3,2,1,0:T(8,128)(2,1)}, bf16[2,2,1152,256]{3,2,1,0:T(8,128)(2,1)}, u32[]{:S(2)}, u32[]{:S(2)}) collective-permute-start(bf16[2,2,1152,256]{3,2,1,0:T(8,128)(2,1)} %get-tuple-element.208), channel_id=1, source_target_pairs={{0,1},{1,0},{2,3},{3,2},{4,5},{5,4},{6,7},{7,6},{8,9},{9,8},{10,11... | collective-permute-start | bytes 7077896 | tf_op jit(solution)/shard_map/ppermute | solution.py:155
  243.7 65.1 %collective-permute-start.26 = (bf16[4,1536,256]{2,1,0:T(8,128)(2,1)}, bf16[4,1536,256]{2,1,0:T(8,128)(2,1)}, u32[]{:S(2)}, u32[]{:S(2)}) collective-permute-start(bf16[4,1536,256]{2,1,0:T(8,128)(2,1)} %experts_back.3), channel_id=1, source_target_pairs={{0,8},{8,0},{16,24},{24,16},{1,9},{9,1},{17,25},{25,17},{2,10},{10... | collective-permute-start | bytes 9437192 | tf_op jit(solution)/shard_map/ppermute | solution.py:65
  247.5 32.9 %collective-permute-start.22 = (bf16[1,1152,256]{2,1,0:T(8,128)(2,1)}, bf16[1,1152,256]{2,1,0:T(8,128)(2,1)}, u32[]{:S(2)}, u32[]{:S(2)}) collective-permute-start(bf16[1,1152,256]{2,1,0:T(8,128)(2,1)} %get-tuple-element.354), channel_id=1, source_target_pairs={{0,4},{2,6},{4,0},{6,2},{1,5},{3,7},{5,1},{7,3},{8,12},{10,14},{12... | collective-permute-start | bytes 1769480 | tf_op jit(solution)/shard_map/ppermute | solution.py:167
  269.8 36.9 %collective-permute-start.20 = (bf16[2,800,256]{2,1,0:T(8,128)(2,1)}, bf16[2,800,256]{2,1,0:T(8,128)(2,1)}, u32[]{:S(2)}, u32[]{:S(2)}) collective-permute-start(bf16[2,800,256]{2,1,0:T(8,128)(2,1)} %get-tuple-element.342), channel_id=1, source_target_pairs={{0,2},{2,0},{4,6},{6,4},{1,3},{3,1},{5,7},{7,5},{8,10},{10,8},{12,... | collective-permute-start | bytes 2457608 | tf_op jit(solution)/shard_map/ppermute | solution.py:68
  274.5 32.2 %collective-permute-start.19 = (bf16[2,800,256]{2,1,0:T(8,128)(2,1)}, bf16[2,800,256]{2,1,0:T(8,128)(2,1)}, u32[]{:S(2)}, u32[]{:S(2)}) collective-permute-start(bf16[2,800,256]{2,1,0:T(8,128)(2,1)} %get-tuple-element.344), channel_id=1, source_target_pairs={{0,16},{8,24},{16,0},{24,8},{1,17},{9,25},{17,1},{25,9},{2,18},{10... | collective-permute-start | bytes 2457608 | tf_op jit(solution)/shard_map/ppermute | solution.py:65
  280.4 71.8 %collective-permute-start.25 = (bf16[2,2,1152,256]{3,2,1,0:T(8,128)(2,1)}, bf16[2,2,1152,256]{3,2,1,0:T(8,128)(2,1)}, u32[]{:S(2)}, u32[]{:S(2)}) collective-permute-start(bf16[2,2,1152,256]{3,2,1,0:T(8,128)(2,1)} %get-tuple-element.224), channel_id=1, source_target_pairs={{0,1},{1,0},{2,3},{3,2},{4,5},{5,4},{6,7},{7,6},{8,9},{9,8},{10,11... | collective-permute-start | bytes 7077896 | tf_op jit(solution)/shard_map/ppermute | solution.py:155
  286.5 104.8 %collective-permute-start.31 = (bf16[2,1152,256]{2,1,0:T(8,128)(2,1)}, bf16[2,1152,256]{2,1,0:T(8,128)(2,1)}, u32[]{:S(2)}, u32[]{:S(2)}) collective-permute-start(bf16[2,1152,256]{2,1,0:T(8,128)(2,1)} %get-tuple-element.350), channel_id=1, source_target_pairs={{0,4},{2,6},{4,0},{6,2},{1,5},{3,7},{5,1},{7,3},{8,12},{10,14},{12... | collective-permute-start | bytes 3538952 | tf_op jit(solution)/shard_map/ppermute | solution.py:167
  313.2 36.8 %collective-permute-start.23 = (bf16[800,256]{1,0:T(8,128)(2,1)S(1)}, bf16[800,256]{1,0:T(8,128)(2,1)S(1)}, u32[]{:S(2)}, u32[]{:S(2)}) collective-permute-start(bf16[800,256]{1,0:T(8,128)(2,1)S(1)} %fusion.33), channel_id=1, source_target_pairs={{0,2},{2,0},{4,6},{6,4},{1,3},{3,1},{5,7},{7,5},{8,10},{10,8},{12,... | collective-permute-start | bytes 1228808 | tf_op jit(solution)/shard_map/ppermute | solution.py:68
  314.7 37.5 %collective-permute-start.27 = (bf16[2,768,256]{2,1,0:T(8,128)(2,1)S(1)}, bf16[2,768,256]{2,1,0:T(8,128)(2,1)S(1)}, u32[]{:S(2)}, u32[]{:S(2)}) collective-permute-start(bf16[2,768,256]{2,1,0:T(8,128)(2,1)S(1)} %fusion.26), channel_id=1, source_target_pairs={{0,16},{8,24},{16,0},{24,8},{1,17},{9,25},{17,1},{25,9},{2,18},{10... | collective-permute-start | bytes 2359304 | tf_op jit(solution)/shard_map/ppermute | solution.py:65
  320.7 43.8 %collective-permute-start.28 = (bf16[2,768,256]{2,1,0:T(8,128)(2,1)S(1)}, bf16[2,768,256]{2,1,0:T(8,128)(2,1)S(1)}, u32[]{:S(2)}, u32[]{:S(2)}) collective-permute-start(bf16[2,768,256]{2,1,0:T(8,128)(2,1)S(1)} %get-tuple-element.346), channel_id=1, source_target_pairs={{0,2},{2,0},{4,6},{6,4},{1,3},{3,1},{5,7},{7,5},{8,10},{10,8},{12,... | collective-permute-start | bytes 2359304 | tf_op jit(solution)/shard_map/ppermute | solution.py:68
  370.1 66.3 %collective-permute-start.35 = (bf16[2,1152,256]{2,1,0:T(8,128)(2,1)}, bf16[2,1152,256]{2,1,0:T(8,128)(2,1)}, u32[]{:S(2)}, u32[]{:S(2)}) collective-permute-start(bf16[2,1152,256]{2,1,0:T(8,128)(2,1)} %get-tuple-element.348), channel_id=1, source_target_pairs={{0,4},{2,6},{4,0},{6,2},{1,5},{3,7},{5,1},{7,3},{8,12},{10,14},{12... | collective-permute-start | bytes 3538952 | tf_op jit(solution)/shard_map/ppermute | solution.py:167
  396.5 48.2 %all-to-all-start = ((bf16[4,2,256,256]{3,2,1,0:T(8,128)(2,1)}), bf16[4,2,256,256]{3,2,1,0:T(8,128)(2,1)}, u32[]{:S(2)}, u32[]{:S(2)}) async-start(bf16[4,2,256,256]{3,2,1,0:T(8,128)(2,1)} %copy-done.6), calls=%async_computation | async-start | bytes 2097152 | tf_op jit(solution)/shard_map/all_to_all | solution.py:989
  412.8 31.9 %collective-permute-start.33 = (bf16[1584,256]{1,0:T(8,128)(2,1)}, bf16[1584,256]{1,0:T(8,128)(2,1)}, u32[]{:S(2)}, u32[]{:S(2)}) collective-permute-start(bf16[1584,256]{1,0:T(8,128)(2,1)} %pad_maximum_fusion.11.refs_4_), channel_id=1, source_target_pairs={{8,0},{0,8},{24,16},{16,24},{9,1},{1,9},{25,17},{17,25},{10,2},{2,... | collective-permute-start | bytes 2433032 | tf_op jit(solution)/shard_map/ppermute | solution.py:61
  412.9 31.8 %collective-permute-start.34 = (bf16[1584,256]{1,0:T(8,128)(2,1)}, bf16[1584,256]{1,0:T(8,128)(2,1)}, u32[]{:S(2)}, u32[]{:S(2)}) collective-permute-start(bf16[1584,256]{1,0:T(8,128)(2,1)} %collective-permute-done.32.refs_5_), channel_id=1, source_target_pairs={{8,0},{0,8},{24,16},{16,24},{9,1},{1,9},{25,17},{17,25},{10,2},{2,... | collective-permute-start | bytes 2433032 | tf_op jit(solution)/shard_map/ppermute | solution.py:61
  424.2 100.8 %collective-permute-start.36 = (bf16[3,2,192,256]{3,2,0,1:T(8,128)(2,1)}, bf16[3,2,192,256]{3,2,0,1:T(8,128)(2,1)}, u32[]{:S(2)}, u32[]{:S(2)}) collective-permute-start(bf16[3,2,192,256]{3,2,0,1:T(8,128)(2,1)} %fusion.32), channel_id=1, source_target_pairs={{0,2},{2,0},{4,6},{6,4},{1,3},{3,1},{5,7},{7,5},{8,10},{10,8},{12,... | collective-permute-start | bytes 1769480 | tf_op jit(solution)/shard_map/ppermute | solution.py:68
  436.4 48.0 %collective-permute-start.38 = (bf16[1536,256]{1,0:T(8,128)(2,1)S(1)}, bf16[1536,256]{1,0:T(8,128)(2,1)}, u32[]{:S(2)}, u32[]{:S(2)}) collective-permute-start(bf16[1536,256]{1,0:T(8,128)(2,1)S(1)} %pad_maximum_fusion.14.refs_4_), channel_id=1, source_target_pairs={{8,0},{0,8},{24,16},{16,24},{9,1},{1,9},{25,17},{17,25},{10,2},{2,... | collective-permute-start | bytes 2359304 | tf_op jit(solution)/shard_map/ppermute | solution.py:61
  437.5 46.9 %collective-permute-start.39 = (bf16[1536,256]{1,0:T(8,128)(2,1)}, bf16[1536,256]{1,0:T(8,128)(2,1)}, u32[]{:S(2)}, u32[]{:S(2)}) collective-permute-start(bf16[1536,256]{1,0:T(8,128)(2,1)} %collective-permute-done.37.refs_5_), channel_id=1, source_target_pairs={{8,0},{0,8},{24,16},{16,24},{9,1},{1,9},{25,17},{17,25},{10,2},{2,... | collective-permute-start | bytes 2359304 | tf_op jit(solution)/shard_map/ppermute | solution.py:61
  446.9 78.1 %all-to-all-start.1 = ((bf16[4,2,256,256]{3,2,1,0:T(8,128)(2,1)}), bf16[4,2,256,256]{3,2,1,0:T(8,128)(2,1)}, u32[]{:S(2)}, u32[]{:S(2)}) async-start(bf16[4,2,256,256]{3,2,1,0:T(8,128)(2,1)} %get-tuple-element.256), calls=%async_computation.1 | async-start | bytes 2097152 | tf_op jit(solution)/shard_map/all_to_all | solution.py:989
  465.1 26.6 %collective-permute-start.51 = (bf16[4,48,1536]{2,1,0:T(8,128)(2,1)}, bf16[4,48,1536]{2,1,0:T(8,128)(2,1)}, u32[]{:S(2)}, u32[]{:S(2)}) collective-permute-start(bf16[4,48,1536]{2,1,0:T(8,128)(2,1)} %get-tuple-element.268), channel_id=1, source_target_pairs={{0,1},{1,0},{2,3},{3,2},{4,5},{5,4},{6,7},{7,6},{8,9},{9,8},{10,11... | collective-permute-start | bytes 1769480 | tf_op jit(solution)/shard_map/ppermute | solution.py:155
  528.6 26.5 %all-to-all-start.2 = ((bf16[8,48,128]{2,1,0:T(8,128)(2,1)}), bf16[8,48,128]{2,1,0:T(8,128)(2,1)}, u32[]{:S(2)}, u32[]{:S(2)}) async-start(bf16[8,48,128]{2,1,0:T(8,128)(2,1)} %maximum_maximum_fusion), calls=%async_computation.2 | async-start | bytes 196608 | tf_op jit(solution)/shard_map/all_to_all | solution.py:1050
  (115 other events, 1061.9 us)

commit v6 on v5

--- a/solution.py
+++ b/solution.py
@@ -182,10 +182,13 @@
             mine, *parts = [
                 lax.dynamic_index_in_dim(local, (d + s) % m, 1, False) for s in range(m)
             ]
-        came = self.send_dp([part.astype(BF16) for part in parts])
+        return [mine] + self.send_dp([part.astype(BF16) for part in parts])
+
+    def scatter_rest(self, terms):
+        n = self.n_context
 
         def of_context(k):
-            return mine[k].astype(F32) + sum(x[k].astype(F32) for x in came)
+            return sum(x[k].astype(F32) for x in terms)
 
         came_far = self.send_context([of_context(k).astype(BF16) for k in range(1, n)], 1)
         return of_context(0) + sum(x.astype(F32) for x in came_far)
@@ -1031,7 +1034,7 @@
     kv_a, grad_kv_b, branch_all, crossing[-1] = hold((kv_a, grad_kv_b, branch_all, crossing[-1]))
     kv_b = to_keys(grad_kv_b)
 
-    out_sum = comm.scatter_rows(ob_rows, branch_all, width)
+    out_terms = comm.scatter_rows(ob_rows, branch_all, width)
     h2_rows = [
         lax.dynamic_slice_in_dim(array, at + expert_index * row_count, row_count, 0)
         for j in range(comm.cores)
@@ -1053,7 +1056,7 @@
     grad_query_raw = jnp.concatenate(
         [rotate_t(x, cosine, -sine).astype(BF16) for x in (grad_query_a, grad_query_b)]
     )
-    query_sum = comm.scatter_rows(h1_rows, comm.gather_expert(grad_query_raw), width)
+    query_terms = comm.scatter_rows(h1_rows, comm.gather_expert(grad_query_raw), width)
     late = crossing[-1]
     pairs, kv_b = hold((pairs, kv_b))
     totals.append(total_of([late]))
@@ -1061,7 +1064,11 @@
     kv_sums = [jnp.sum(x.astype(F32), 0) for x in (kv_a, kv_b)]
     grad_key_raw = [rotate_t(kv_sum[0], cosine, -sine).astype(BF16) for kv_sum in kv_sums]
     grad_kv_raw = jnp.concatenate(grad_key_raw + [kv_sum[1].astype(BF16) for kv_sum in kv_sums])
-    kv_rows = comm.scatter_rows(h1_rows, comm.gather_expert(grad_kv_raw), 2 * kv_width)
+    near_kv = comm.gather_columns(grad_kv_raw)
+    near_kv, out_terms, query_terms = hold((near_kv, out_terms, query_terms))
+    out_sum, query_sum = comm.scatter_rest(out_terms), comm.scatter_rest(query_terms)
+    kv_terms = comm.scatter_rows(h1_rows, comm.gather_cores(near_kv), 2 * kv_width)
+    kv_rows = comm.scatter_rest(kv_terms)
     key_sum, value_sum = kv_rows[:, :kv_width], kv_rows[:, kv_width:]
 
     down_sum = jnp.concatenate([down for down, _ in totals])

time: 582 us -> 576 us (0.990)
  waiting for transfers between devices: 132 us -> 119 us
    ppermute x12, waiting for transfers between devices: 23.8 us -> 16.6 us  [send_context(): out.append(lax.ppermute(parts[s - 1], 'context', pairs))]
    unnamed x201 -> x195, local copies, waits for them, and re-layouts: 20 us -> 24.2 us
  transfers between devices with their start and end apart: 59 -> 59, of which waited for: 22 -> 20; matrix products, arithmetic and copies ran while one was open for 25% -> 24% of each run, Pallas kernels for 26% -> 26%
where the time goes in v6:
time: 576 us; the launch traced here: 567 us
  Pallas kernels  177 us (31%)
  waiting for transfers between devices  119 us (21%)
  starting transfers between devices  105 us (18%)
  other arithmetic  80.9 us (14%)
  local copies, waits for them, and re-layouts  52.3 us (9%)
  matrix products  30.1 us (5%)
    pallas_call x3, Pallas kernels, act(): pl.pallas_call(functools.partial(self.act_kernel, first, n, make_gates),...  86.3 us
    ppermute x9, waiting for transfers between devices, pair(): lax.ppermute(value, 'context', [(i, i ^ 1) for i in range(self.n_context)])  86.1 us
    ppermute x12, starting transfers between devices, send_context(): out.append(lax.ppermute(parts[s - 1], 'context', pairs))  32.8 us
    dot_general x14, matrix products, mm(): lax.dot_general(a, b, (((da,), (db,)), ((), ())), preferred_element_type=...  30.1 us
    pallas_call x2, Pallas kernels, back(): pl.pallas_call(functools.partial(self.back_kernel, parts), out_shape=jax....  28 us
    unnamed x195, local copies, waits for them, and re-layouts  24.2 us
    pallas_call x2, Pallas kernels, out(): pl.pallas_call(functools.partial(self.out_kernel, parts), out_shape=jax.S...  18.6 us
    all_to_all x2, starting transfers between devices, to_keys(): return lax.all_to_all(grad_kv, 'context', 0, 0, tiled=True)  17.9 us
  transfers between devices with their start and end apart: 59, of which 20 were waited for; matrix products, arithmetic and copies ran while one was open for 24% of the time, Pallas kernels for 26%

profile of v6, /device:TPU:0, one launch (start us, length us, event | category | flops | bytes accessed | tf_op | source)
XLA Modules:
  0.0 567.1 jit_solution(3710707670765649526)
XLA Ops:
  10.9 7.0 %collective-permute-start.2 = (bf16[1024,256]{1,0:T(8,128)(2,1)S(1)}, bf16[1024,256]{1,0:T(8,128)(2,1)S(1)}, u32[]{:S(2)}, u32[]{:S(2)}) collective-permute-start(bf16[1024,256]{1,0:T(8,128)(2,1)S(1)} %pad_maximum_fusion.15.refs_0_.refs_4_), channel_id=1, source_target_pairs={{0,6},{1,7},{8,14},{9,15},{16,22},{17,23},{24,30},{25,31}} | collective-permute-start | bytes 1572872 | tf_op jit(solution)/shard_map/ppermute | solution.py:833
  23.4 4.9 convolution_bitcast_fusion
  31.3 15.2 %prepare_weights.1 = (bf16[5,2,2,128,1536]{4,3,2,1,0:T(8,128)(2,1)}, bf16[1536,1280]{1,0:T(8,128)(2,1)}, bf16[1536,1280]{1,0:T(8,128)(2,1)}, bf16[1280,1536]{1,0:T(8,128)(2,1)}, bf16[1536,1280]{1,0:T(8,128)(2,1)}) custom-call(s32[1]{0:T(128)} %bitcast.14.p_ref, bf16[5,1536,512]{2,1,0:T(8,128)(2,1)} %gate_ref.1, bf16[5,1536,512]{2,1,0:T(8,128)(2,1)} %up_ref.1, ...), custom_call_target="tpu_custom_call" | custom-call | bytes 552960 | tf_op jit(solution)/shard_map/prepare_weights/pallas_call | solution.py:444
  53.7 15.2 %collective-permute-done.4.refs_13_ = bf16[1568,256]{1,0:T(8,128)(2,1)} collective-permute-done((bf16[1568,256]{1,0:T(8,128)(2,1)}, bf16[1568,256]{1,0:T(8,128)(2,1)}, u32[]{:S(2)}, u32[]{:S(2)}) %collective-permute-start.4) | collective-permute-done | bytes 802848 | tf_op jit(solution)/shard_map/ppermute | solution.py:68
  72.0 11.0 %attn_fwd.1 = (f32[1536,256]{1,0:T(8,128)S(1)}, bf16[1536,256]{1,0:T(8,128)(2,1)S(1)}, f32[8,8,256]{2,1,0:T(8,128)S(1)}) custom-call(s32[1]{0:T(128)} %bitcast.5.c_ref, bf16[1536,256]{1,0:T(8,128)(2,1)S(1)} %bitcast.217, bf16[1024,256]{1,0:T(8,128)(2,1)S(1)} %pad_maximum_fusion.15.refs_0_.refs_4_, ...), custom_call_target="tpu_custom_call" | custom-call | flops 100663296 | bytes 98304 | tf_op jit(solution)/shard_map/attn_fwd/pallas_call | solution.py:307
  83.0 4.9 multiply_reduce_fusion.2
  88.9 4.4 collective-permute-start.7
  97.2 14.2 %collective-permute-done.7.refs_6_ = bf16[1536,256]{1,0:T(8,128)(2,1)S(1)} collective-permute-done((bf16[1536,256]{1,0:T(8,128)(2,1)S(1)}, bf16[1536,256]{1,0:T(8,128)(2,1)S(1)}, u32[]{:S(2)}, u32[]{:S(2)}) %collective-permute-start.7) | collective-permute-done | bytes 786464 | tf_op jit(solution)/shard_map/ppermute | solution.py:68
  116.7 6.7 %collective-permute-done.11.refs_8_ = bf16[768,256]{1,0:T(8,128)(2,1)S(1)} collective-permute-done((bf16[768,256]{1,0:T(8,128)(2,1)S(1)}, bf16[768,256]{1,0:T(8,128)(2,1)S(1)}, u32[]{:S(2)}, u32[]{:S(2)}) %collective-permute-start.11) | collective-permute-done | bytes 393248 | tf_op jit(solution)/shard_map/ppermute | solution.py:68
  127.1 21.4 %experts_act.3 = (f32[32,2048]{1,0:T(8,128)}, f32[32,2048]{1,0:T(8,128)}, bf16[256,2048]{1,0:T(8,128)(2,1)}, bf16[256,2048]{1,0:T(8,128)(2,1)}, bf16[256,2048]{1...) custom-call(s32[3]{0:T(128)} %pad_add_fusion.e_ref, ...), custom_call_target="tpu_custom_call" | custom-call | flops 150994944 | bytes 282624 | tf_op jit(solution)/shard_map/experts_act/pallas_call | solution.py:659
  152.2 32.3 %experts_act.4 = (bf16[512,2048]{1,0:T(8,128)(2,1)}, bf16[512,2048]{1,0:T(8,128)(2,1)}, bf16[512,2048]{1,0:T(8,128)(2,1)}, f32[2,8,2048]{2,1,0:T(8,128)}, bf16[2...) custom-call(s32[3]{0:T(128)} %pad_add_fusion.e_ref, f32[32,2048]{1,0:T(8,128)} %copy-done.50, ...), custom_call_target="tpu_custom_call" | custom-call | flops 301989888 | bytes 368640 | tf_op jit(solution)/shard_map/experts_act/pallas_call | solution.py:659
  184.5 32.6 %experts_act.5 = (bf16[512,2048]{1,0:T(8,128)(2,1)}, bf16[512,2048]{1,0:T(8,128)(2,1)}, bf16[512,2048]{1,0:T(8,128)(2,1)}, f32[2,8,2048]{2,1,0:T(8,128)}, bf16[2...) custom-call(s32[3]{0:T(128)} %pad_add_fusion.e_ref, f32[32,2048]{1,0:T(8,128)} %copy-done.50, ...), custom_call_target="tpu_custom_call" | custom-call | flops 301989888 | bytes 368640 | tf_op jit(solution)/shard_map/experts_act/pallas_call | solution.py:659
  217.2 9.2 %experts_out.3 = bf16[4,1600,256]{2,1,0:T(8,128)(2,1)} custom-call(s32[3]{0:T(128)} %pad_add_fusion.e_ref, bf16[1536,1280]{1,0:T(8,128)(2,1)} %get-tuple-element.171.weight_ref, bf16[256,2048]{1,0:T(8,128)(2,1)} %get-tuple-element.201.refs_0_, bf16[512,2048]{1,0:T(8,128)(2,1)} %get-tuple-element.202.refs_1_, bf16[512,2048]{1,0:T(8,128)(2,1)} %get-tuple-element.203.refs_2_, ...), custom_call_target="tpu_custom_call" | custom-call | flops 62914560 | bytes 159744 | tf_op jit(solution)/shard_map/experts_out/pallas_call | solution.py:714
  227.1 14.2 %experts_back.3 = bf16[4,1536,256]{2,1,0:T(8,128)(2,1)} custom-call(bf16[1536,1280]{1,0:T(8,128)(2,1)} %get-tuple-element.212.gate_w_ref, bf16[1536,1280]{1,0:T(8,128)(2,1)} %get-tuple-element.213.up_w_ref, bf16[256,2048]{1,0:T(8,128)(2,1)} %get-tuple-element.220.refs_0_, bf16[512,2048]{1,0:T(8,128)(2,1)} %get-tuple-element.221.refs_1_, ...), custom_call_target="tpu_custom_call" | custom-call | flops 125829120 | bytes 221184 | tf_op jit(solution)/shard_map/experts_back/pallas_call | solution.py:761
  245.0 6.0 %collective-permute-start.22 = (bf16[1,1152,256]{2,1,0:T(8,128)(2,1)}, bf16[1,1152,256]{2,1,0:T(8,128)(2,1)}, u32[]{:S(2)}, u32[]{:S(2)}) collective-permute-start(bf16[1,1152,256]{2,1,0:T(8,128)(2,1)} %get-tuple-element.366), channel_id=1, source_target_pairs={{0,4},{2,6},{4,0},{6,2},{1,5},{3,7},{5,1},{7,3},{8,12},{10,14},{12... | collective-permute-start | bytes 1769480 | tf_op jit(solution)/shard_map/ppermute | solution.py:167
  251.1 9.3 %experts_out.2 = bf16[4,1600,256]{2,1,0:T(8,128)(2,1)} custom-call(s32[3]{0:T(128)} %pad_add_fusion.e_ref, bf16[1536,1280]{1,0:T(8,128)(2,1)} %get-tuple-element.171.weight_ref, bf16[256,2048]{1,0:T(8,128)(2,1)} %get-tuple-element.201.refs_0_, bf16[512,2048]{1,0:T(8,128)(2,1)} %get-tuple-element.202.refs_1_, bf16[512,2048]{1,0:T(8,128)(2,1)} %get-tuple-element.203.refs_2_, ...), custom_call_target="tpu_custom_call" | custom-call | flops 62914560 | bytes 159744 | tf_op jit(solution)/shard_map/experts_out/pallas_call | solution.py:714
  273.4 4.6 collective-permute-done.22
  284.0 6.5 %collective-permute-start.31 = (bf16[2,1152,256]{2,1,0:T(8,128)(2,1)}, bf16[2,1152,256]{2,1,0:T(8,128)(2,1)}, u32[]{:S(2)}, u32[]{:S(2)}) collective-permute-start(bf16[2,1152,256]{2,1,0:T(8,128)(2,1)} %get-tuple-element.362), channel_id=1, source_target_pairs={{0,4},{2,6},{4,0},{6,2},{1,5},{3,7},{5,1},{7,3},{8,12},{10,14},{12... | collective-permute-start | bytes 3538952 | tf_op jit(solution)/shard_map/ppermute | solution.py:167
  290.5 13.7 %experts_back.2 = bf16[4,1536,256]{2,1,0:T(8,128)(2,1)} custom-call(bf16[1536,1280]{1,0:T(8,128)(2,1)} %get-tuple-element.212.gate_w_ref, bf16[1536,1280]{1,0:T(8,128)(2,1)} %get-tuple-element.213.up_w_ref, bf16[256,2048]{1,0:T(8,128)(2,1)} %get-tuple-element.220.refs_0_, bf16[512,2048]{1,0:T(8,128)(2,1)} %get-tuple-element.221.refs_1_, ...), custom_call_target="tpu_custom_call" | custom-call | flops 125829120 | bytes 221184 | tf_op jit(solution)/shard_map/experts_back/pallas_call | solution.py:761
  322.4 25.3 %collective-permute-done.23 = bf16[800,256]{1,0:T(8,128)(2,1)S(1)} collective-permute-done((bf16[800,256]{1,0:T(8,128)(2,1)S(1)}, bf16[800,256]{1,0:T(8,128)(2,1)S(1)}, u32[]{:S(2)}, u32[]{:S(2)}) %collective-permute-start.23) | collective-permute-done | bytes 409632 | tf_op jit(solution)/shard_map/ppermute | solution.py:68
  349.6 12.5 %collective-permute-done.28 = bf16[2,768,256]{2,1,0:T(8,128)(2,1)S(1)} collective-permute-done((bf16[2,768,256]{2,1,0:T(8,128)(2,1)S(1)}, bf16[2,768,256]{2,1,0:T(8,128)(2,1)S(1)}, u32[]{:S(2)}, u32[]{:S(2)}) %collective-permute-start.28) | collective-permute-done | bytes 786464 | tf_op jit(solution)/shard_map/ppermute | solution.py:68
  371.1 5.1 collective-permute-done.29
  394.1 11.6 %all-to-all-start = ((bf16[4,2,256,256]{3,2,1,0:T(8,128)(2,1)}), bf16[4,2,256,256]{3,2,1,0:T(8,128)(2,1)}, u32[]{:S(2)}, u32[]{:S(2)}) async-start(bf16[4,2,256,256]{3,2,1,0:T(8,128)(2,1)} %copy-done.8), calls=%async_computation | async-start | bytes 2097152 | tf_op jit(solution)/shard_map/all_to_all | solution.py:992
  422.0 4.8 collective-permute-start.36
  429.2 4.9 fusion.87
  435.2 7.1 %all-to-all-done = bf16[4,2,256,256]{3,2,1,0:T(8,128)(2,1)} async-done(((bf16[4,2,256,256]{3,2,1,0:T(8,128)(2,1)}), bf16[4,2,256,256]{3,2,1,0:T(8,128)(2,1)}, u32[]{:S(2)}, u32[]{:S(2)}) %all-to-all-start) | async-done | bytes 1048608 | tf_op jit(solution)/shard_map/all_to_all | solution.py:992
  444.4 6.3 %all-to-all-start.1 = ((bf16[4,2,256,256]{3,2,1,0:T(8,128)(2,1)}), bf16[4,2,256,256]{3,2,1,0:T(8,128)(2,1)}, u32[]{:S(2)}, u32[]{:S(2)}) async-start(bf16[4,2,256,256]{3,2,1,0:T(8,128)(2,1)} %get-tuple-element.262), calls=%async_computation.1 | async-start | bytes 2097152 | tf_op jit(solution)/shard_map/all_to_all | solution.py:992
  460.8 4.8 row_products.3
  477.4 7.2 %collective-permute-done.55 = bf16[2,2,192,256]{3,2,0,1:T(8,128)(2,1)} collective-permute-done((bf16[2,2,192,256]{3,2,0,1:T(8,128)(2,1)}, bf16[2,2,192,256]{3,2,0,1:T(8,128)(2,1)}, u32[]{:S(2)}, u32[]{:S(2)}) %collective-permute-start.55) | collective-permute-done | bytes 393248 | tf_op jit(solution)/shard_map/ppermute | solution.py:68
  487.3 4.6 row_products.4
  542.6 4.1 collective-permute-done.53
  554.1 5.7 %collective-permute-done.44 = bf16[48,1536]{1,0:T(8,128)(2,1)S(1)} collective-permute-done((bf16[48,1536]{1,0:T(8,128)(2,1)S(1)}, bf16[48,1536]{1,0:T(8,128)(2,1)S(1)}, u32[]{:S(2)}, u32[]{:S(2)}) %collective-permute-start.44) | collective-permute-done | bytes 147488 | tf_op jit(solution)/shard_map/ppermute | solution.py:167
  (439 shorter events, 227.4 us)
Async XLA Ops:
  10.9 59.5 %collective-permute-start.2 = (bf16[1024,256]{1,0:T(8,128)(2,1)S(1)}, bf16[1024,256]{1,0:T(8,128)(2,1)S(1)}, u32[]{:S(2)}, u32[]{:S(2)}) collective-permute-start(bf16[1024,256]{1,0:T(8,128)(2,1)S(1)} %pad_maximum_fusion.15.refs_0_.refs_4_), channel_id=1, source_target_pairs={{0,6},{1,7},{8,14},{9,15},{16,22},{17,23},{24,30},{25,31}} | collective-permute-start | bytes 1572872 | tf_op jit(solution)/shard_map/ppermute | solution.py:833
  17.9 52.5 %collective-permute-start.1 = (bf16[1024,256]{1,0:T(8,128)(2,1)S(1)}, bf16[1024,256]{1,0:T(8,128)(2,1)S(1)}, u32[]{:S(2)}, u32[]{:S(2)}) collective-permute-start(bf16[1024,256]{1,0:T(8,128)(2,1)S(1)} %pad_maximum_fusion.15.refs_0_.refs_4_), channel_id=1, source_target_pairs={{0,4},{2,6},{1,5},{3,7},{8,12},{10,14},{9,13},{11,15},{16,20},{18,... | collective-permute-start | bytes 1572872 | tf_op jit(solution)/shard_map/ppermute | solution.py:833
  19.2 51.2 %collective-permute-start = (bf16[1024,256]{1,0:T(8,128)(2,1)S(1)}, bf16[1024,256]{1,0:T(8,128)(2,1)S(1)}, u32[]{:S(2)}, u32[]{:S(2)}) collective-permute-start(bf16[1024,256]{1,0:T(8,128)(2,1)S(1)} %pad_maximum_fusion.15.refs_0_.refs_4_), channel_id=1, source_target_pairs={{0,2},{2,4},{4,6},{1,3},{3,5},{5,7},{8,10},{10,12},{12,14},{9,11},... | collective-permute-start | bytes 1572872 | tf_op jit(solution)/shard_map/ppermute | solution.py:833
  21.7 47.2 %collective-permute-start.4 = (bf16[1568,256]{1,0:T(8,128)(2,1)}, bf16[1568,256]{1,0:T(8,128)(2,1)}, u32[]{:S(2)}, u32[]{:S(2)}) collective-permute-start(bf16[1568,256]{1,0:T(8,128)(2,1)} %pad_maximum_fusion.12.refs_11_), channel_id=1, source_target_pairs={{0,2},{2,0},{4,6},{6,4},{1,3},{3,1},{5,7},{7,5},{8,10},{10,8},{12,... | collective-permute-start | bytes 2408456 | tf_op jit(solution)/shard_map/ppermute | solution.py:68
  21.8 48.6 %collective-permute-start.3 = (bf16[1568,256]{1,0:T(8,128)(2,1)}, bf16[1568,256]{1,0:T(8,128)(2,1)}, u32[]{:S(2)}, u32[]{:S(2)}) collective-permute-start(bf16[1568,256]{1,0:T(8,128)(2,1)} %pad_maximum_fusion.12.refs_11_), channel_id=1, source_target_pairs={{16,0},{24,8},{0,16},{8,24},{17,1},{25,9},{1,17},{9,25},{18,2},{26... | collective-permute-start | bytes 2408456 | tf_op jit(solution)/shard_map/ppermute | solution.py:61
  71.9 44.8 %collective-permute-start.8 = (bf16[3136,256]{1,0:T(8,128)(2,1)S(1)}, bf16[3136,256]{1,0:T(8,128)(2,1)S(1)}, u32[]{:S(2)}, u32[]{:S(2)}) collective-permute-start(bf16[3136,256]{1,0:T(8,128)(2,1)S(1)} %pad_maximum_fusion.6), channel_id=1, source_target_pairs={{8,0},{0,8},{24,16},{16,24},{9,1},{1,9},{25,17},{17,25},{10,2},{2,... | collective-permute-start | bytes 4816904 | tf_op jit(solution)/shard_map/ppermute | solution.py:61
  148.5 36.0 %collective-permute-start.17 = (bf16[2,1,1152,256]{3,2,1,0:T(8,128)(2,1)}, bf16[2,1,1152,256]{3,2,1,0:T(8,128)(2,1)}, u32[]{:S(2)}, u32[]{:S(2)}) collective-permute-start(bf16[2,1,1152,256]{3,2,1,0:T(8,128)(2,1)} %get-tuple-element.198), channel_id=1, source_target_pairs={{0,1},{1,0},{2,3},{3,2},{4,5},{5,4},{6,7},{7,6},{8,9},{9,8},{10,11... | collective-permute-start | bytes 3538952 | tf_op jit(solution)/shard_map/ppermute | solution.py:155
  150.0 67.1 %collective-permute-start.14 = (bf16[768,256]{1,0:T(8,128)(2,1)}, bf16[768,256]{1,0:T(8,128)(2,1)S(1)}, u32[]{:S(2)}, u32[]{:S(2)}) collective-permute-start(bf16[768,256]{1,0:T(8,128)(2,1)} %get-tuple-element.191), channel_id=1, source_target_pairs={{16,0},{24,8},{0,16},{8,24},{17,1},{25,9},{1,17},{9,25},{18,2},{26... | collective-permute-start | bytes 1179656 | tf_op jit(solution)/shard_map/ppermute | solution.py:61
  150.6 66.6 %collective-permute-start.15 = (bf16[768,256]{1,0:T(8,128)(2,1)}, bf16[768,256]{1,0:T(8,128)(2,1)}, u32[]{:S(2)}, u32[]{:S(2)}) collective-permute-start(bf16[768,256]{1,0:T(8,128)(2,1)} %get-tuple-element.192), channel_id=1, source_target_pairs={{8,0},{0,8},{24,16},{16,24},{9,1},{1,9},{25,17},{17,25},{10,2},{2,... | collective-permute-start | bytes 1179656 | tf_op jit(solution)/shard_map/ppermute | solution.py:61
  150.6 66.6 %collective-permute-start.16 = (bf16[768,256]{1,0:T(8,128)(2,1)}, bf16[768,256]{1,0:T(8,128)(2,1)S(1)}, u32[]{:S(2)}, u32[]{:S(2)}) collective-permute-start(bf16[768,256]{1,0:T(8,128)(2,1)} %get-tuple-element.193), channel_id=1, source_target_pairs={{24,0},{16,8},{8,16},{0,24},{25,1},{17,9},{9,17},{1,25},{26,2},{18... | collective-permute-start | bytes 1179656 | tf_op jit(solution)/shard_map/ppermute | solution.py:61
  226.4 37.2 %collective-permute-start.18 = (bf16[4,1600,256]{2,1,0:T(8,128)(2,1)}, bf16[4,1600,256]{2,1,0:T(8,128)(2,1)}, u32[]{:S(2)}, u32[]{:S(2)}) collective-permute-start(bf16[4,1600,256]{2,1,0:T(8,128)(2,1)} %experts_out.3), channel_id=1, source_target_pairs={{0,8},{8,0},{16,24},{24,16},{1,9},{9,1},{17,25},{25,17},{2,10},{10... | collective-permute-start | bytes 9830408 | tf_op jit(solution)/shard_map/ppermute | solution.py:65
  226.5 54.0 %collective-permute-start.21 = (bf16[2,2,1152,256]{3,2,1,0:T(8,128)(2,1)}, bf16[2,2,1152,256]{3,2,1,0:T(8,128)(2,1)}, u32[]{:S(2)}, u32[]{:S(2)}) collective-permute-start(bf16[2,2,1152,256]{3,2,1,0:T(8,128)(2,1)} %get-tuple-element.214), channel_id=1, source_target_pairs={{0,1},{1,0},{2,3},{3,2},{4,5},{5,4},{6,7},{7,6},{8,9},{9,8},{10,11... | collective-permute-start | bytes 7077896 | tf_op jit(solution)/shard_map/ppermute | solution.py:155
  241.3 65.1 %collective-permute-start.26 = (bf16[4,1536,256]{2,1,0:T(8,128)(2,1)}, bf16[4,1536,256]{2,1,0:T(8,128)(2,1)}, u32[]{:S(2)}, u32[]{:S(2)}) collective-permute-start(bf16[4,1536,256]{2,1,0:T(8,128)(2,1)} %experts_back.3), channel_id=1, source_target_pairs={{0,8},{8,0},{16,24},{24,16},{1,9},{9,1},{17,25},{25,17},{2,10},{10... | collective-permute-start | bytes 9437192 | tf_op jit(solution)/shard_map/ppermute | solution.py:65
  245.0 32.9 %collective-permute-start.22 = (bf16[1,1152,256]{2,1,0:T(8,128)(2,1)}, bf16[1,1152,256]{2,1,0:T(8,128)(2,1)}, u32[]{:S(2)}, u32[]{:S(2)}) collective-permute-start(bf16[1,1152,256]{2,1,0:T(8,128)(2,1)} %get-tuple-element.366), channel_id=1, source_target_pairs={{0,4},{2,6},{4,0},{6,2},{1,5},{3,7},{5,1},{7,3},{8,12},{10,14},{12... | collective-permute-start | bytes 1769480 | tf_op jit(solution)/shard_map/ppermute | solution.py:167
  267.4 36.9 %collective-permute-start.20 = (bf16[2,800,256]{2,1,0:T(8,128)(2,1)}, bf16[2,800,256]{2,1,0:T(8,128)(2,1)}, u32[]{:S(2)}, u32[]{:S(2)}) collective-permute-start(bf16[2,800,256]{2,1,0:T(8,128)(2,1)} %get-tuple-element.354), channel_id=1, source_target_pairs={{0,2},{2,0},{4,6},{6,4},{1,3},{3,1},{5,7},{7,5},{8,10},{10,8},{12,... | collective-permute-start | bytes 2457608 | tf_op jit(solution)/shard_map/ppermute | solution.py:68
  272.1 32.2 %collective-permute-start.19 = (bf16[2,800,256]{2,1,0:T(8,128)(2,1)}, bf16[2,800,256]{2,1,0:T(8,128)(2,1)}, u32[]{:S(2)}, u32[]{:S(2)}) collective-permute-start(bf16[2,800,256]{2,1,0:T(8,128)(2,1)} %get-tuple-element.356), channel_id=1, source_target_pairs={{0,16},{8,24},{16,0},{24,8},{1,17},{9,25},{17,1},{25,9},{2,18},{10... | collective-permute-start | bytes 2457608 | tf_op jit(solution)/shard_map/ppermute | solution.py:65
  278.0 71.6 %collective-permute-start.25 = (bf16[2,2,1152,256]{3,2,1,0:T(8,128)(2,1)}, bf16[2,2,1152,256]{3,2,1,0:T(8,128)(2,1)}, u32[]{:S(2)}, u32[]{:S(2)}) collective-permute-start(bf16[2,2,1152,256]{3,2,1,0:T(8,128)(2,1)} %get-tuple-element.230), channel_id=1, source_target_pairs={{0,1},{1,0},{2,3},{3,2},{4,5},{5,4},{6,7},{7,6},{8,9},{9,8},{10,11... | collective-permute-start | bytes 7077896 | tf_op jit(solution)/shard_map/ppermute | solution.py:155
  284.0 104.8 %collective-permute-start.31 = (bf16[2,1152,256]{2,1,0:T(8,128)(2,1)}, bf16[2,1152,256]{2,1,0:T(8,128)(2,1)}, u32[]{:S(2)}, u32[]{:S(2)}) collective-permute-start(bf16[2,1152,256]{2,1,0:T(8,128)(2,1)} %get-tuple-element.362), channel_id=1, source_target_pairs={{0,4},{2,6},{4,0},{6,2},{1,5},{3,7},{5,1},{7,3},{8,12},{10,14},{12... | collective-permute-start | bytes 3538952 | tf_op jit(solution)/shard_map/ppermute | solution.py:167
  310.8 36.9 %collective-permute-start.23 = (bf16[800,256]{1,0:T(8,128)(2,1)S(1)}, bf16[800,256]{1,0:T(8,128)(2,1)S(1)}, u32[]{:S(2)}, u32[]{:S(2)}) collective-permute-start(bf16[800,256]{1,0:T(8,128)(2,1)S(1)} %fusion.33), channel_id=1, source_target_pairs={{0,2},{2,0},{4,6},{6,4},{1,3},{3,1},{5,7},{7,5},{8,10},{10,8},{12,... | collective-permute-start | bytes 1228808 | tf_op jit(solution)/shard_map/ppermute | solution.py:68
  312.2 37.5 %collective-permute-start.27 = (bf16[2,768,256]{2,1,0:T(8,128)(2,1)S(1)}, bf16[2,768,256]{2,1,0:T(8,128)(2,1)S(1)}, u32[]{:S(2)}, u32[]{:S(2)}) collective-permute-start(bf16[2,768,256]{2,1,0:T(8,128)(2,1)S(1)} %fusion.26), channel_id=1, source_target_pairs={{0,16},{8,24},{16,0},{24,8},{1,17},{9,25},{17,1},{25,9},{2,18},{10... | collective-permute-start | bytes 2359304 | tf_op jit(solution)/shard_map/ppermute | solution.py:65
  318.3 43.8 %collective-permute-start.28 = (bf16[2,768,256]{2,1,0:T(8,128)(2,1)S(1)}, bf16[2,768,256]{2,1,0:T(8,128)(2,1)S(1)}, u32[]{:S(2)}, u32[]{:S(2)}) collective-permute-start(bf16[2,768,256]{2,1,0:T(8,128)(2,1)S(1)} %get-tuple-element.358), channel_id=1, source_target_pairs={{0,2},{2,0},{4,6},{6,4},{1,3},{3,1},{5,7},{7,5},{8,10},{10,8},{12,... | collective-permute-start | bytes 2359304 | tf_op jit(solution)/shard_map/ppermute | solution.py:68
  367.6 66.4 %collective-permute-start.35 = (bf16[2,1152,256]{2,1,0:T(8,128)(2,1)}, bf16[2,1152,256]{2,1,0:T(8,128)(2,1)}, u32[]{:S(2)}, u32[]{:S(2)}) collective-permute-start(bf16[2,1152,256]{2,1,0:T(8,128)(2,1)} %get-tuple-element.360), channel_id=1, source_target_pairs={{0,4},{2,6},{4,0},{6,2},{1,5},{3,7},{5,1},{7,3},{8,12},{10,14},{12... | collective-permute-start | bytes 3538952 | tf_op jit(solution)/shard_map/ppermute | solution.py:167
  394.1 48.1 %all-to-all-start = ((bf16[4,2,256,256]{3,2,1,0:T(8,128)(2,1)}), bf16[4,2,256,256]{3,2,1,0:T(8,128)(2,1)}, u32[]{:S(2)}, u32[]{:S(2)}) async-start(bf16[4,2,256,256]{3,2,1,0:T(8,128)(2,1)} %copy-done.8), calls=%async_computation | async-start | bytes 2097152 | tf_op jit(solution)/shard_map/all_to_all | solution.py:992
  410.4 31.8 %collective-permute-start.33 = (bf16[1584,256]{1,0:T(8,128)(2,1)}, bf16[1584,256]{1,0:T(8,128)(2,1)}, u32[]{:S(2)}, u32[]{:S(2)}) collective-permute-start(bf16[1584,256]{1,0:T(8,128)(2,1)} %pad_maximum_fusion.11.refs_4_), channel_id=1, source_target_pairs={{8,0},{0,8},{24,16},{16,24},{9,1},{1,9},{25,17},{17,25},{10,2},{2,... | collective-permute-start | bytes 2433032 | tf_op jit(solution)/shard_map/ppermute | solution.py:61
  410.5 31.7 %collective-permute-start.34 = (bf16[1584,256]{1,0:T(8,128)(2,1)}, bf16[1584,256]{1,0:T(8,128)(2,1)}, u32[]{:S(2)}, u32[]{:S(2)}) collective-permute-start(bf16[1584,256]{1,0:T(8,128)(2,1)} %collective-permute-done.32.refs_5_), channel_id=1, source_target_pairs={{8,0},{0,8},{24,16},{16,24},{9,1},{1,9},{25,17},{17,25},{10,2},{2,... | collective-permute-start | bytes 2433032 | tf_op jit(solution)/shard_map/ppermute | solution.py:61
  422.0 72.3 %collective-permute-start.36 = (bf16[3,2,192,256]{3,2,0,1:T(8,128)(2,1)}, bf16[3,2,192,256]{3,2,0,1:T(8,128)(2,1)}, u32[]{:S(2)}, u32[]{:S(2)}) collective-permute-start(bf16[3,2,192,256]{3,2,0,1:T(8,128)(2,1)} %fusion.32), channel_id=1, source_target_pairs={{0,2},{2,0},{4,6},{6,4},{1,3},{3,1},{5,7},{7,5},{8,10},{10,8},{12,... | collective-permute-start | bytes 1769480 | tf_op jit(solution)/shard_map/ppermute | solution.py:68
  434.1 53.2 %collective-permute-start.40 = (bf16[1536,256]{1,0:T(8,128)(2,1)S(1)}, bf16[1536,256]{1,0:T(8,128)(2,1)}, u32[]{:S(2)}, u32[]{:S(2)}) collective-permute-start(bf16[1536,256]{1,0:T(8,128)(2,1)S(1)} %pad_maximum_fusion.14.refs_4_), channel_id=1, source_target_pairs={{8,0},{0,8},{24,16},{16,24},{9,1},{1,9},{25,17},{17,25},{10,2},{2,... | collective-permute-start | bytes 2359304 | tf_op jit(solution)/shard_map/ppermute | solution.py:61
  435.2 52.1 %collective-permute-start.41 = (bf16[1536,256]{1,0:T(8,128)(2,1)}, bf16[1536,256]{1,0:T(8,128)(2,1)}, u32[]{:S(2)}, u32[]{:S(2)}) collective-permute-start(bf16[1536,256]{1,0:T(8,128)(2,1)} %collective-permute-done.39.refs_5_), channel_id=1, source_target_pairs={{8,0},{0,8},{24,16},{16,24},{9,1},{1,9},{25,17},{17,25},{10,2},{2,... | collective-permute-start | bytes 2359304 | tf_op jit(solution)/shard_map/ppermute | solution.py:61
  444.4 49.9 %all-to-all-start.1 = ((bf16[4,2,256,256]{3,2,1,0:T(8,128)(2,1)}), bf16[4,2,256,256]{3,2,1,0:T(8,128)(2,1)}, u32[]{:S(2)}, u32[]{:S(2)}) async-start(bf16[4,2,256,256]{3,2,1,0:T(8,128)(2,1)} %get-tuple-element.262), calls=%async_computation.1 | async-start | bytes 2097152 | tf_op jit(solution)/shard_map/all_to_all | solution.py:992
  465.6 58.1 %collective-permute-start.38 = (bf16[4,48,1536]{2,1,0:T(8,128)(2,1)}, bf16[4,48,1536]{2,1,0:T(8,128)(2,1)}, u32[]{:S(2)}, u32[]{:S(2)}) collective-permute-start(bf16[4,48,1536]{2,1,0:T(8,128)(2,1)} %get-tuple-element.270), channel_id=1, source_target_pairs={{0,1},{1,0},{2,3},{3,2},{4,5},{5,4},{6,7},{7,6},{8,9},{9,8},{10,11... | collective-permute-start | bytes 1769480 | tf_op jit(solution)/shard_map/ppermute | solution.py:155
  492.9 30.8 %collective-permute-start.42 = (bf16[4,48,1536]{2,1,0:T(8,128)(2,1)}, bf16[4,48,1536]{2,1,0:T(8,128)(2,1)}, u32[]{:S(2)}, u32[]{:S(2)}) collective-permute-start(bf16[4,48,1536]{2,1,0:T(8,128)(2,1)} %get-tuple-element.272), channel_id=1, source_target_pairs={{0,1},{1,0},{2,3},{3,2},{4,5},{5,4},{6,7},{7,6},{8,9},{9,8},{10,11... | collective-permute-start | bytes 1769480 | tf_op jit(solution)/shard_map/ppermute | solution.py:155
  495.8 26.5 %all-to-all-start.2 = ((bf16[8,48,128]{2,1,0:T(8,128)(2,1)}), bf16[8,48,128]{2,1,0:T(8,128)(2,1)S(1)}, u32[]{:S(2)}, u32[]{:S(2)}) async-start(bf16[8,48,128]{2,1,0:T(8,128)(2,1)} %maximum_maximum_fusion), calls=%async_computation.2 | async-start | bytes 196608 | tf_op jit(solution)/shard_map/all_to_all | solution.py:1053
  (113 other events, 904.6 us)

commit v7 on v6

--- a/solution.py
+++ b/solution.py
@@ -1049,9 +1049,6 @@
     rest = jnp.zeros((row_count, LANES - lanes - 1), F32)
     extra = jnp.concatenate([router_rows, gain_part[:, None], rest], 1).astype(BF16)
     extra = extra.reshape(n_context * n_dp, -1, LANES)
-    extra, kv_b = hold((extra, kv_b))
-    extra = lax.all_to_all(extra, ("context", "dp"), 0, 0, tiled=True)
-    extra = jnp.sum(extra.astype(F32), 0)
 
     grad_query_raw = jnp.concatenate(
         [rotate_t(x, cosine, -sine).astype(BF16) for x in (grad_query_a, grad_query_b)]
@@ -1068,6 +1065,9 @@
     near_kv, out_terms, query_terms = hold((near_kv, out_terms, query_terms))
     out_sum, query_sum = comm.scatter_rest(out_terms), comm.scatter_rest(query_terms)
     kv_terms = comm.scatter_rows(h1_rows, comm.gather_cores(near_kv), 2 * kv_width)
+    extra, kv_terms[0] = hold((extra, kv_terms[0]))
+    extra = lax.all_to_all(extra, ("context", "dp"), 0, 0, tiled=True)
+    extra = jnp.sum(extra.astype(F32), 0)
     kv_rows = comm.scatter_rest(kv_terms)
     key_sum, value_sum = kv_rows[:, :kv_width], kv_rows[:, kv_width:]
 

time: 576 us -> 573 us (level)
    unnamed x195 -> x203, local copies, waits for them, and re-layouts: 24.2 us -> 21.2 us
  transfers between devices with their start and end apart: 59 -> 59, of which waited for: 20 -> 21; matrix products, arithmetic and copies ran while one was open for 24% -> 24% of each run, Pallas kernels for 26% -> 26%
where the time goes in v7:
time: 573 us; the launch traced here: 564 us
  Pallas kernels  178 us (31%)
  waiting for transfers between devices  122 us (21%)
  starting transfers between devices  104 us (18%)
  other arithmetic  80.2 us (14%)
  local copies, waits for them, and re-layouts  48.3 us (8%)
  matrix products  29.6 us (5%)
    pallas_call x3, Pallas kernels, act(): pl.pallas_call(functools.partial(self.act_kernel, first, n, make_gates),...  86.3 us
    ppermute x9, waiting for transfers between devices, pair(): lax.ppermute(value, 'context', [(i, i ^ 1) for i in range(self.n_context)])  84 us
    dot_general x14, matrix products, mm(): lax.dot_general(a, b, (((da,), (db,)), ((), ())), preferred_element_type=...  29.6 us
    ppermute x12, starting transfers between devices, send_context(): out.append(lax.ppermute(parts[s - 1], 'context', pairs))  28.8 us
    pallas_call x2, Pallas kernels, back(): pl.pallas_call(functools.partial(self.back_kernel, parts), out_shape=jax....  28 us
    unnamed x203, local copies, waits for them, and re-layouts  21.2 us
    all_to_all x2, starting transfers between devices, to_keys(): return lax.all_to_all(grad_kv, 'context', 0, 0, tiled=True)  18.7 us
    pallas_call x2, Pallas kernels, out(): pl.pallas_call(functools.partial(self.out_kernel, parts), out_shape=jax.S...  18.6 us
  transfers between devices with their start and end apart: 59, of which 21 were waited for; matrix products, arithmetic and copies ran while one was open for 24% of the time, Pallas kernels for 26%

profile of v7, /device:TPU:0, one launch (start us, length us, event | category | flops | bytes accessed | tf_op | source)
XLA Modules:
  0.0 563.7 jit_solution(7691672696152207648)
XLA Ops:
  10.9 7.0 %collective-permute-start.2 = (bf16[1024,256]{1,0:T(8,128)(2,1)S(1)}, bf16[1024,256]{1,0:T(8,128)(2,1)S(1)}, u32[]{:S(2)}, u32[]{:S(2)}) collective-permute-start(bf16[1024,256]{1,0:T(8,128)(2,1)S(1)} %pad_maximum_fusion.15.refs_0_.refs_4_), channel_id=1, source_target_pairs={{0,6},{1,7},{8,14},{9,15},{16,22},{17,23},{24,30},{25,31}} | collective-permute-start | bytes 1572872 | tf_op jit(solution)/shard_map/ppermute | solution.py:833
  23.3 4.9 convolution_bitcast_fusion
  31.2 15.1 %prepare_weights.1 = (bf16[5,2,2,128,1536]{4,3,2,1,0:T(8,128)(2,1)}, bf16[1536,1280]{1,0:T(8,128)(2,1)}, bf16[1536,1280]{1,0:T(8,128)(2,1)}, bf16[1280,1536]{1,0:T(8,128)(2,1)}, bf16[1536,1280]{1,0:T(8,128)(2,1)}) custom-call(s32[1]{0:T(128)} %bitcast.14.p_ref, bf16[5,1536,512]{2,1,0:T(8,128)(2,1)} %gate_ref.1, bf16[5,1536,512]{2,1,0:T(8,128)(2,1)} %up_ref.1, ...), custom_call_target="tpu_custom_call" | custom-call | bytes 552960 | tf_op jit(solution)/shard_map/prepare_weights/pallas_call | solution.py:444
  53.6 15.3 %collective-permute-done.4.refs_13_ = bf16[1568,256]{1,0:T(8,128)(2,1)} collective-permute-done((bf16[1568,256]{1,0:T(8,128)(2,1)}, bf16[1568,256]{1,0:T(8,128)(2,1)}, u32[]{:S(2)}, u32[]{:S(2)}) %collective-permute-start.4) | collective-permute-done | bytes 802848 | tf_op jit(solution)/shard_map/ppermute | solution.py:68
  72.0 11.0 %attn_fwd.1 = (f32[1536,256]{1,0:T(8,128)S(1)}, bf16[1536,256]{1,0:T(8,128)(2,1)S(1)}, f32[8,8,256]{2,1,0:T(8,128)S(1)}) custom-call(s32[1]{0:T(128)} %bitcast.5.c_ref, bf16[1536,256]{1,0:T(8,128)(2,1)S(1)} %bitcast.217, bf16[1024,256]{1,0:T(8,128)(2,1)S(1)} %pad_maximum_fusion.15.refs_0_.refs_4_, ...), custom_call_target="tpu_custom_call" | custom-call | flops 100663296 | bytes 98304 | tf_op jit(solution)/shard_map/attn_fwd/pallas_call | solution.py:307
  83.0 4.9 multiply_reduce_fusion.2
  88.9 4.4 collective-permute-start.7
  97.2 14.2 %collective-permute-done.7.refs_6_ = bf16[1536,256]{1,0:T(8,128)(2,1)S(1)} collective-permute-done((bf16[1536,256]{1,0:T(8,128)(2,1)S(1)}, bf16[1536,256]{1,0:T(8,128)(2,1)S(1)}, u32[]{:S(2)}, u32[]{:S(2)}) %collective-permute-start.7) | collective-permute-done | bytes 786464 | tf_op jit(solution)/shard_map/ppermute | solution.py:68
  116.7 6.7 %collective-permute-done.11.refs_8_ = bf16[768,256]{1,0:T(8,128)(2,1)S(1)} collective-permute-done((bf16[768,256]{1,0:T(8,128)(2,1)S(1)}, bf16[768,256]{1,0:T(8,128)(2,1)S(1)}, u32[]{:S(2)}, u32[]{:S(2)}) %collective-permute-start.11) | collective-permute-done | bytes 393248 | tf_op jit(solution)/shard_map/ppermute | solution.py:68
  127.1 21.4 %experts_act.3 = (f32[32,2048]{1,0:T(8,128)}, f32[32,2048]{1,0:T(8,128)}, bf16[256,2048]{1,0:T(8,128)(2,1)}, bf16[256,2048]{1,0:T(8,128)(2,1)}, bf16[256,2048]{1...) custom-call(s32[3]{0:T(128)} %pad_add_fusion.e_ref, ...), custom_call_target="tpu_custom_call" | custom-call | flops 150994944 | bytes 282624 | tf_op jit(solution)/shard_map/experts_act/pallas_call | solution.py:659
  152.2 32.3 %experts_act.4 = (bf16[512,2048]{1,0:T(8,128)(2,1)}, bf16[512,2048]{1,0:T(8,128)(2,1)}, bf16[512,2048]{1,0:T(8,128)(2,1)}, f32[2,8,2048]{2,1,0:T(8,128)}, bf16[2...) custom-call(s32[3]{0:T(128)} %pad_add_fusion.e_ref, f32[32,2048]{1,0:T(8,128)} %copy-done.53, ...), custom_call_target="tpu_custom_call" | custom-call | flops 301989888 | bytes 368640 | tf_op jit(solution)/shard_map/experts_act/pallas_call | solution.py:659
  184.5 32.7 %experts_act.5 = (bf16[512,2048]{1,0:T(8,128)(2,1)}, bf16[512,2048]{1,0:T(8,128)(2,1)}, bf16[512,2048]{1,0:T(8,128)(2,1)}, f32[2,8,2048]{2,1,0:T(8,128)}, bf16[2...) custom-call(s32[3]{0:T(128)} %pad_add_fusion.e_ref, f32[32,2048]{1,0:T(8,128)} %copy-done.53, ...), custom_call_target="tpu_custom_call" | custom-call | flops 301989888 | bytes 368640 | tf_op jit(solution)/shard_map/experts_act/pallas_call | solution.py:659
  217.2 9.2 %experts_out.3 = bf16[4,1600,256]{2,1,0:T(8,128)(2,1)} custom-call(s32[3]{0:T(128)} %pad_add_fusion.e_ref, bf16[1536,1280]{1,0:T(8,128)(2,1)} %get-tuple-element.171.weight_ref, bf16[256,2048]{1,0:T(8,128)(2,1)} %get-tuple-element.201.refs_0_, bf16[512,2048]{1,0:T(8,128)(2,1)} %get-tuple-element.202.refs_1_, bf16[512,2048]{1,0:T(8,128)(2,1)} %get-tuple-element.203.refs_2_, ...), custom_call_target="tpu_custom_call" | custom-call | flops 62914560 | bytes 159744 | tf_op jit(solution)/shard_map/experts_out/pallas_call | solution.py:714
  227.1 14.0 %experts_back.3 = bf16[4,1536,256]{2,1,0:T(8,128)(2,1)} custom-call(bf16[1536,1280]{1,0:T(8,128)(2,1)} %get-tuple-element.212.gate_w_ref, bf16[1536,1280]{1,0:T(8,128)(2,1)} %get-tuple-element.213.up_w_ref, bf16[256,2048]{1,0:T(8,128)(2,1)} %get-tuple-element.220.refs_0_, bf16[512,2048]{1,0:T(8,128)(2,1)} %get-tuple-element.221.refs_1_, ...), custom_call_target="tpu_custom_call" | custom-call | flops 125829120 | bytes 221184 | tf_op jit(solution)/shard_map/experts_back/pallas_call | solution.py:761
  244.9 6.0 %collective-permute-start.22 = (bf16[1,1152,256]{2,1,0:T(8,128)(2,1)}, bf16[1,1152,256]{2,1,0:T(8,128)(2,1)}, u32[]{:S(2)}, u32[]{:S(2)}) collective-permute-start(bf16[1,1152,256]{2,1,0:T(8,128)(2,1)} %get-tuple-element.366), channel_id=1, source_target_pairs={{0,4},{2,6},{4,0},{6,2},{1,5},{3,7},{5,1},{7,3},{8,12},{10,14},{12... | collective-permute-start | bytes 1769480 | tf_op jit(solution)/shard_map/ppermute | solution.py:167
  250.9 9.4 %experts_out.2 = bf16[4,1600,256]{2,1,0:T(8,128)(2,1)} custom-call(s32[3]{0:T(128)} %pad_add_fusion.e_ref, bf16[1536,1280]{1,0:T(8,128)(2,1)} %get-tuple-element.171.weight_ref, bf16[256,2048]{1,0:T(8,128)(2,1)} %get-tuple-element.201.refs_0_, bf16[512,2048]{1,0:T(8,128)(2,1)} %get-tuple-element.202.refs_1_, bf16[512,2048]{1,0:T(8,128)(2,1)} %get-tuple-element.203.refs_2_, ...), custom_call_target="tpu_custom_call" | custom-call | flops 62914560 | bytes 159744 | tf_op jit(solution)/shard_map/experts_out/pallas_call | solution.py:714
  273.3 4.4 collective-permute-done.22
  284.2 6.4 %collective-permute-start.31 = (bf16[2,1152,256]{2,1,0:T(8,128)(2,1)}, bf16[2,1152,256]{2,1,0:T(8,128)(2,1)}, u32[]{:S(2)}, u32[]{:S(2)}) collective-permute-start(bf16[2,1152,256]{2,1,0:T(8,128)(2,1)} %get-tuple-element.362), channel_id=1, source_target_pairs={{0,4},{2,6},{4,0},{6,2},{1,5},{3,7},{5,1},{7,3},{8,12},{10,14},{12... | collective-permute-start | bytes 3538952 | tf_op jit(solution)/shard_map/ppermute | solution.py:167
  290.6 14.0 %experts_back.2 = bf16[4,1536,256]{2,1,0:T(8,128)(2,1)} custom-call(bf16[1536,1280]{1,0:T(8,128)(2,1)} %get-tuple-element.212.gate_w_ref, bf16[1536,1280]{1,0:T(8,128)(2,1)} %get-tuple-element.213.up_w_ref, bf16[256,2048]{1,0:T(8,128)(2,1)} %get-tuple-element.220.refs_0_, bf16[512,2048]{1,0:T(8,128)(2,1)} %get-tuple-element.221.refs_1_, ...), custom_call_target="tpu_custom_call" | custom-call | flops 125829120 | bytes 221184 | tf_op jit(solution)/shard_map/experts_back/pallas_call | solution.py:761
  322.7 25.3 %collective-permute-done.23 = bf16[800,256]{1,0:T(8,128)(2,1)S(1)} collective-permute-done((bf16[800,256]{1,0:T(8,128)(2,1)S(1)}, bf16[800,256]{1,0:T(8,128)(2,1)S(1)}, u32[]{:S(2)}, u32[]{:S(2)}) %collective-permute-start.23) | collective-permute-done | bytes 409632 | tf_op jit(solution)/shard_map/ppermute | solution.py:68
  350.0 12.4 %collective-permute-done.28 = bf16[2,768,256]{2,1,0:T(8,128)(2,1)S(1)} collective-permute-done((bf16[2,768,256]{2,1,0:T(8,128)(2,1)S(1)}, bf16[2,768,256]{2,1,0:T(8,128)(2,1)S(1)}, u32[]{:S(2)}, u32[]{:S(2)}) %collective-permute-start.28) | collective-permute-done | bytes 786464 | tf_op jit(solution)/shard_map/ppermute | solution.py:68
  371.5 5.2 collective-permute-done.29
  394.4 11.8 %all-to-all-start = ((bf16[4,2,256,256]{3,2,1,0:T(8,128)(2,1)}), bf16[4,2,256,256]{3,2,1,0:T(8,128)(2,1)}, u32[]{:S(2)}, u32[]{:S(2)}) async-start(bf16[4,2,256,256]{3,2,1,0:T(8,128)(2,1)} %copy-done.8), calls=%async_computation | async-start | bytes 2097152 | tf_op jit(solution)/shard_map/all_to_all | solution.py:992
  422.5 4.8 collective-permute-start.36
  429.8 4.9 fusion.87
  435.8 6.8 %all-to-all-done = bf16[4,2,256,256]{3,2,1,0:T(8,128)(2,1)} async-done(((bf16[4,2,256,256]{3,2,1,0:T(8,128)(2,1)}), bf16[4,2,256,256]{3,2,1,0:T(8,128)(2,1)}, u32[]{:S(2)}, u32[]{:S(2)}) %all-to-all-start) | async-done | bytes 1048608 | tf_op jit(solution)/shard_map/all_to_all | solution.py:992
  444.0 6.9 %all-to-all-start.1 = ((bf16[4,2,256,256]{3,2,1,0:T(8,128)(2,1)}), bf16[4,2,256,256]{3,2,1,0:T(8,128)(2,1)}, u32[]{:S(2)}, u32[]{:S(2)}) async-start(bf16[4,2,256,256]{3,2,1,0:T(8,128)(2,1)} %get-tuple-element.258), calls=%async_computation.1 | async-start | bytes 2097152 | tf_op jit(solution)/shard_map/all_to_all | solution.py:992
  463.3 4.8 row_products.3
  474.3 5.0 collective-permute-done.55
  482.0 4.5 row_products.4
  536.1 6.9 %all-to-all-start.2 = ((bf16[8,48,128]{2,1,0:T(8,128)(2,1)}), bf16[8,48,128]{2,1,0:T(8,128)(2,1)S(1)}, u32[]{:S(2)}, u32[]{:S(2)}) async-start(bf16[8,48,128]{2,1,0:T(8,128)(2,1)} %maximum_maximum_fusion), calls=%async_computation.2 | async-start | bytes 196608 | tf_op jit(solution)/shard_map/all_to_all | solution.py:1069
  545.1 5.0 all-to-all-done.2
  (448 shorter events, 223.7 us)
Async XLA Ops:
  10.9 59.5 %collective-permute-start.2 = (bf16[1024,256]{1,0:T(8,128)(2,1)S(1)}, bf16[1024,256]{1,0:T(8,128)(2,1)S(1)}, u32[]{:S(2)}, u32[]{:S(2)}) collective-permute-start(bf16[1024,256]{1,0:T(8,128)(2,1)S(1)} %pad_maximum_fusion.15.refs_0_.refs_4_), channel_id=1, source_target_pairs={{0,6},{1,7},{8,14},{9,15},{16,22},{17,23},{24,30},{25,31}} | collective-permute-start | bytes 1572872 | tf_op jit(solution)/shard_map/ppermute | solution.py:833
  17.9 52.5 %collective-permute-start.1 = (bf16[1024,256]{1,0:T(8,128)(2,1)S(1)}, bf16[1024,256]{1,0:T(8,128)(2,1)S(1)}, u32[]{:S(2)}, u32[]{:S(2)}) collective-permute-start(bf16[1024,256]{1,0:T(8,128)(2,1)S(1)} %pad_maximum_fusion.15.refs_0_.refs_4_), channel_id=1, source_target_pairs={{0,4},{2,6},{1,5},{3,7},{8,12},{10,14},{9,13},{11,15},{16,20},{18,... | collective-permute-start | bytes 1572872 | tf_op jit(solution)/shard_map/ppermute | solution.py:833
  19.2 51.2 %collective-permute-start = (bf16[1024,256]{1,0:T(8,128)(2,1)S(1)}, bf16[1024,256]{1,0:T(8,128)(2,1)S(1)}, u32[]{:S(2)}, u32[]{:S(2)}) collective-permute-start(bf16[1024,256]{1,0:T(8,128)(2,1)S(1)} %pad_maximum_fusion.15.refs_0_.refs_4_), channel_id=1, source_target_pairs={{0,2},{2,4},{4,6},{1,3},{3,5},{5,7},{8,10},{10,12},{12,14},{9,11},... | collective-permute-start | bytes 1572872 | tf_op jit(solution)/shard_map/ppermute | solution.py:833
  21.7 47.2 %collective-permute-start.4 = (bf16[1568,256]{1,0:T(8,128)(2,1)}, bf16[1568,256]{1,0:T(8,128)(2,1)}, u32[]{:S(2)}, u32[]{:S(2)}) collective-permute-start(bf16[1568,256]{1,0:T(8,128)(2,1)} %pad_maximum_fusion.12.refs_11_), channel_id=1, source_target_pairs={{0,2},{2,0},{4,6},{6,4},{1,3},{3,1},{5,7},{7,5},{8,10},{10,8},{12,... | collective-permute-start | bytes 2408456 | tf_op jit(solution)/shard_map/ppermute | solution.py:68
  21.8 48.6 %collective-permute-start.3 = (bf16[1568,256]{1,0:T(8,128)(2,1)}, bf16[1568,256]{1,0:T(8,128)(2,1)}, u32[]{:S(2)}, u32[]{:S(2)}) collective-permute-start(bf16[1568,256]{1,0:T(8,128)(2,1)} %pad_maximum_fusion.12.refs_11_), channel_id=1, source_target_pairs={{16,0},{24,8},{0,16},{8,24},{17,1},{25,9},{1,17},{9,25},{18,2},{26... | collective-permute-start | bytes 2408456 | tf_op jit(solution)/shard_map/ppermute | solution.py:61
  71.9 44.8 %collective-permute-start.8 = (bf16[3136,256]{1,0:T(8,128)(2,1)S(1)}, bf16[3136,256]{1,0:T(8,128)(2,1)S(1)}, u32[]{:S(2)}, u32[]{:S(2)}) collective-permute-start(bf16[3136,256]{1,0:T(8,128)(2,1)S(1)} %pad_maximum_fusion.6), channel_id=1, source_target_pairs={{8,0},{0,8},{24,16},{16,24},{9,1},{1,9},{25,17},{17,25},{10,2},{2,... | collective-permute-start | bytes 4816904 | tf_op jit(solution)/shard_map/ppermute | solution.py:61
  148.5 36.0 %collective-permute-start.17 = (bf16[2,1,1152,256]{3,2,1,0:T(8,128)(2,1)}, bf16[2,1,1152,256]{3,2,1,0:T(8,128)(2,1)}, u32[]{:S(2)}, u32[]{:S(2)}) collective-permute-start(bf16[2,1,1152,256]{3,2,1,0:T(8,128)(2,1)} %get-tuple-element.198), channel_id=1, source_target_pairs={{0,1},{1,0},{2,3},{3,2},{4,5},{5,4},{6,7},{7,6},{8,9},{9,8},{10,11... | collective-permute-start | bytes 3538952 | tf_op jit(solution)/shard_map/ppermute | solution.py:155
  150.0 67.1 %collective-permute-start.14 = (bf16[768,256]{1,0:T(8,128)(2,1)}, bf16[768,256]{1,0:T(8,128)(2,1)S(1)}, u32[]{:S(2)}, u32[]{:S(2)}) collective-permute-start(bf16[768,256]{1,0:T(8,128)(2,1)} %get-tuple-element.191), channel_id=1, source_target_pairs={{16,0},{24,8},{0,16},{8,24},{17,1},{25,9},{1,17},{9,25},{18,2},{26... | collective-permute-start | bytes 1179656 | tf_op jit(solution)/shard_map/ppermute | solution.py:61
  150.6 66.6 %collective-permute-start.15 = (bf16[768,256]{1,0:T(8,128)(2,1)}, bf16[768,256]{1,0:T(8,128)(2,1)}, u32[]{:S(2)}, u32[]{:S(2)}) collective-permute-start(bf16[768,256]{1,0:T(8,128)(2,1)} %get-tuple-element.192), channel_id=1, source_target_pairs={{8,0},{0,8},{24,16},{16,24},{9,1},{1,9},{25,17},{17,25},{10,2},{2,... | collective-permute-start | bytes 1179656 | tf_op jit(solution)/shard_map/ppermute | solution.py:61
  150.6 66.6 %collective-permute-start.16 = (bf16[768,256]{1,0:T(8,128)(2,1)}, bf16[768,256]{1,0:T(8,128)(2,1)S(1)}, u32[]{:S(2)}, u32[]{:S(2)}) collective-permute-start(bf16[768,256]{1,0:T(8,128)(2,1)} %get-tuple-element.193), channel_id=1, source_target_pairs={{24,0},{16,8},{8,16},{0,24},{25,1},{17,9},{9,17},{1,25},{26,2},{18... | collective-permute-start | bytes 1179656 | tf_op jit(solution)/shard_map/ppermute | solution.py:61
  226.5 36.9 %collective-permute-start.18 = (bf16[4,1600,256]{2,1,0:T(8,128)(2,1)}, bf16[4,1600,256]{2,1,0:T(8,128)(2,1)}, u32[]{:S(2)}, u32[]{:S(2)}) collective-permute-start(bf16[4,1600,256]{2,1,0:T(8,128)(2,1)} %experts_out.3), channel_id=1, source_target_pairs={{0,8},{8,0},{16,24},{24,16},{1,9},{9,1},{17,25},{25,17},{2,10},{10... | collective-permute-start | bytes 9830408 | tf_op jit(solution)/shard_map/ppermute | solution.py:65
  226.5 54.0 %collective-permute-start.21 = (bf16[2,2,1152,256]{3,2,1,0:T(8,128)(2,1)}, bf16[2,2,1152,256]{3,2,1,0:T(8,128)(2,1)}, u32[]{:S(2)}, u32[]{:S(2)}) collective-permute-start(bf16[2,2,1152,256]{3,2,1,0:T(8,128)(2,1)} %get-tuple-element.214), channel_id=1, source_target_pairs={{0,1},{1,0},{2,3},{3,2},{4,5},{5,4},{6,7},{7,6},{8,9},{9,8},{10,11... | collective-permute-start | bytes 7077896 | tf_op jit(solution)/shard_map/ppermute | solution.py:155
  241.1 65.6 %collective-permute-start.26 = (bf16[4,1536,256]{2,1,0:T(8,128)(2,1)}, bf16[4,1536,256]{2,1,0:T(8,128)(2,1)}, u32[]{:S(2)}, u32[]{:S(2)}) collective-permute-start(bf16[4,1536,256]{2,1,0:T(8,128)(2,1)} %experts_back.3), channel_id=1, source_target_pairs={{0,8},{8,0},{16,24},{24,16},{1,9},{9,1},{17,25},{25,17},{2,10},{10... | collective-permute-start | bytes 9437192 | tf_op jit(solution)/shard_map/ppermute | solution.py:65
  244.9 32.9 %collective-permute-start.22 = (bf16[1,1152,256]{2,1,0:T(8,128)(2,1)}, bf16[1,1152,256]{2,1,0:T(8,128)(2,1)}, u32[]{:S(2)}, u32[]{:S(2)}) collective-permute-start(bf16[1,1152,256]{2,1,0:T(8,128)(2,1)} %get-tuple-element.366), channel_id=1, source_target_pairs={{0,4},{2,6},{4,0},{6,2},{1,5},{3,7},{5,1},{7,3},{8,12},{10,14},{12... | collective-permute-start | bytes 1769480 | tf_op jit(solution)/shard_map/ppermute | solution.py:167
  267.2 37.4 %collective-permute-start.20 = (bf16[2,800,256]{2,1,0:T(8,128)(2,1)}, bf16[2,800,256]{2,1,0:T(8,128)(2,1)}, u32[]{:S(2)}, u32[]{:S(2)}) collective-permute-start(bf16[2,800,256]{2,1,0:T(8,128)(2,1)} %get-tuple-element.354), channel_id=1, source_target_pairs={{0,2},{2,0},{4,6},{6,4},{1,3},{3,1},{5,7},{7,5},{8,10},{10,8},{12,... | collective-permute-start | bytes 2457608 | tf_op jit(solution)/shard_map/ppermute | solution.py:68
  272.0 32.6 %collective-permute-start.19 = (bf16[2,800,256]{2,1,0:T(8,128)(2,1)}, bf16[2,800,256]{2,1,0:T(8,128)(2,1)}, u32[]{:S(2)}, u32[]{:S(2)}) collective-permute-start(bf16[2,800,256]{2,1,0:T(8,128)(2,1)} %get-tuple-element.356), channel_id=1, source_target_pairs={{0,16},{8,24},{16,0},{24,8},{1,17},{9,25},{17,1},{25,9},{2,18},{10... | collective-permute-start | bytes 2457608 | tf_op jit(solution)/shard_map/ppermute | solution.py:65
  277.8 72.2 %collective-permute-start.25 = (bf16[2,2,1152,256]{3,2,1,0:T(8,128)(2,1)}, bf16[2,2,1152,256]{3,2,1,0:T(8,128)(2,1)}, u32[]{:S(2)}, u32[]{:S(2)}) collective-permute-start(bf16[2,2,1152,256]{3,2,1,0:T(8,128)(2,1)} %get-tuple-element.230), channel_id=1, source_target_pairs={{0,1},{1,0},{2,3},{3,2},{4,5},{5,4},{6,7},{7,6},{8,9},{9,8},{10,11... | collective-permute-start | bytes 7077896 | tf_op jit(solution)/shard_map/ppermute | solution.py:155
  284.2 105.0 %collective-permute-start.31 = (bf16[2,1152,256]{2,1,0:T(8,128)(2,1)}, bf16[2,1152,256]{2,1,0:T(8,128)(2,1)}, u32[]{:S(2)}, u32[]{:S(2)}) collective-permute-start(bf16[2,1152,256]{2,1,0:T(8,128)(2,1)} %get-tuple-element.362), channel_id=1, source_target_pairs={{0,4},{2,6},{4,0},{6,2},{1,5},{3,7},{5,1},{7,3},{8,12},{10,14},{12... | collective-permute-start | bytes 3538952 | tf_op jit(solution)/shard_map/ppermute | solution.py:167
  311.1 36.9 %collective-permute-start.23 = (bf16[800,256]{1,0:T(8,128)(2,1)S(1)}, bf16[800,256]{1,0:T(8,128)(2,1)S(1)}, u32[]{:S(2)}, u32[]{:S(2)}) collective-permute-start(bf16[800,256]{1,0:T(8,128)(2,1)S(1)} %fusion.33), channel_id=1, source_target_pairs={{0,2},{2,0},{4,6},{6,4},{1,3},{3,1},{5,7},{7,5},{8,10},{10,8},{12,... | collective-permute-start | bytes 1228808 | tf_op jit(solution)/shard_map/ppermute | solution.py:68
  312.5 37.5 %collective-permute-start.27 = (bf16[2,768,256]{2,1,0:T(8,128)(2,1)S(1)}, bf16[2,768,256]{2,1,0:T(8,128)(2,1)S(1)}, u32[]{:S(2)}, u32[]{:S(2)}) collective-permute-start(bf16[2,768,256]{2,1,0:T(8,128)(2,1)S(1)} %fusion.26), channel_id=1, source_target_pairs={{0,16},{8,24},{16,0},{24,8},{1,17},{9,25},{17,1},{25,9},{2,18},{10... | collective-permute-start | bytes 2359304 | tf_op jit(solution)/shard_map/ppermute | solution.py:65
  318.6 43.8 %collective-permute-start.28 = (bf16[2,768,256]{2,1,0:T(8,128)(2,1)S(1)}, bf16[2,768,256]{2,1,0:T(8,128)(2,1)S(1)}, u32[]{:S(2)}, u32[]{:S(2)}) collective-permute-start(bf16[2,768,256]{2,1,0:T(8,128)(2,1)S(1)} %get-tuple-element.358), channel_id=1, source_target_pairs={{0,2},{2,0},{4,6},{6,4},{1,3},{3,1},{5,7},{7,5},{8,10},{10,8},{12,... | collective-permute-start | bytes 2359304 | tf_op jit(solution)/shard_map/ppermute | solution.py:68
  368.0 66.7 %collective-permute-start.35 = (bf16[2,1152,256]{2,1,0:T(8,128)(2,1)}, bf16[2,1152,256]{2,1,0:T(8,128)(2,1)}, u32[]{:S(2)}, u32[]{:S(2)}) collective-permute-start(bf16[2,1152,256]{2,1,0:T(8,128)(2,1)} %get-tuple-element.360), channel_id=1, source_target_pairs={{0,4},{2,6},{4,0},{6,2},{1,5},{3,7},{5,1},{7,3},{8,12},{10,14},{12... | collective-permute-start | bytes 3538952 | tf_op jit(solution)/shard_map/ppermute | solution.py:167
  394.4 48.2 %all-to-all-start = ((bf16[4,2,256,256]{3,2,1,0:T(8,128)(2,1)}), bf16[4,2,256,256]{3,2,1,0:T(8,128)(2,1)}, u32[]{:S(2)}, u32[]{:S(2)}) async-start(bf16[4,2,256,256]{3,2,1,0:T(8,128)(2,1)} %copy-done.8), calls=%async_computation | async-start | bytes 2097152 | tf_op jit(solution)/shard_map/all_to_all | solution.py:992
  411.0 31.6 %collective-permute-start.33 = (bf16[1584,256]{1,0:T(8,128)(2,1)}, bf16[1584,256]{1,0:T(8,128)(2,1)}, u32[]{:S(2)}, u32[]{:S(2)}) collective-permute-start(bf16[1584,256]{1,0:T(8,128)(2,1)} %pad_maximum_fusion.11.refs_4_), channel_id=1, source_target_pairs={{8,0},{0,8},{24,16},{16,24},{9,1},{1,9},{25,17},{17,25},{10,2},{2,... | collective-permute-start | bytes 2433032 | tf_op jit(solution)/shard_map/ppermute | solution.py:61
  411.1 31.5 %collective-permute-start.34 = (bf16[1584,256]{1,0:T(8,128)(2,1)}, bf16[1584,256]{1,0:T(8,128)(2,1)}, u32[]{:S(2)}, u32[]{:S(2)}) collective-permute-start(bf16[1584,256]{1,0:T(8,128)(2,1)} %collective-permute-done.32.refs_5_), channel_id=1, source_target_pairs={{8,0},{0,8},{24,16},{16,24},{9,1},{1,9},{25,17},{17,25},{10,2},{2,... | collective-permute-start | bytes 2433032 | tf_op jit(solution)/shard_map/ppermute | solution.py:61
  422.5 65.5 %collective-permute-start.36 = (bf16[3,2,192,256]{3,2,0,1:T(8,128)(2,1)}, bf16[3,2,192,256]{3,2,0,1:T(8,128)(2,1)}, u32[]{:S(2)}, u32[]{:S(2)}) collective-permute-start(bf16[3,2,192,256]{3,2,0,1:T(8,128)(2,1)} %fusion.32), channel_id=1, source_target_pairs={{0,2},{2,0},{4,6},{6,4},{1,3},{3,1},{5,7},{7,5},{8,10},{10,8},{12,... | collective-permute-start | bytes 1769480 | tf_op jit(solution)/shard_map/ppermute | solution.py:68
  434.6 47.4 %collective-permute-start.40 = (bf16[1536,256]{1,0:T(8,128)(2,1)S(1)}, bf16[1536,256]{1,0:T(8,128)(2,1)}, u32[]{:S(2)}, u32[]{:S(2)}) collective-permute-start(bf16[1536,256]{1,0:T(8,128)(2,1)S(1)} %pad_maximum_fusion.14.refs_4_), channel_id=1, source_target_pairs={{8,0},{0,8},{24,16},{16,24},{9,1},{1,9},{25,17},{17,25},{10,2},{2,... | collective-permute-start | bytes 2359304 | tf_op jit(solution)/shard_map/ppermute | solution.py:61
  435.7 46.3 %collective-permute-start.41 = (bf16[1536,256]{1,0:T(8,128)(2,1)}, bf16[1536,256]{1,0:T(8,128)(2,1)}, u32[]{:S(2)}, u32[]{:S(2)}) collective-permute-start(bf16[1536,256]{1,0:T(8,128)(2,1)} %collective-permute-done.39.refs_5_), channel_id=1, source_target_pairs={{8,0},{0,8},{24,16},{16,24},{9,1},{1,9},{25,17},{17,25},{10,2},{2,... | collective-permute-start | bytes 2359304 | tf_op jit(solution)/shard_map/ppermute | solution.py:61
  444.0 44.0 %all-to-all-start.1 = ((bf16[4,2,256,256]{3,2,1,0:T(8,128)(2,1)}), bf16[4,2,256,256]{3,2,1,0:T(8,128)(2,1)}, u32[]{:S(2)}, u32[]{:S(2)}) async-start(bf16[4,2,256,256]{3,2,1,0:T(8,128)(2,1)} %get-tuple-element.258), calls=%async_computation.1 | async-start | bytes 2097152 | tf_op jit(solution)/shard_map/all_to_all | solution.py:992
  468.1 40.6 %collective-permute-start.38 = (bf16[4,48,1536]{2,1,0:T(8,128)(2,1)}, bf16[4,48,1536]{2,1,0:T(8,128)(2,1)}, u32[]{:S(2)}, u32[]{:S(2)}) collective-permute-start(bf16[4,48,1536]{2,1,0:T(8,128)(2,1)} %get-tuple-element.269), channel_id=1, source_target_pairs={{0,1},{1,0},{2,3},{3,2},{4,5},{5,4},{6,7},{7,6},{8,9},{9,8},{10,11... | collective-permute-start | bytes 1769480 | tf_op jit(solution)/shard_map/ppermute | solution.py:155
  519.5 23.5 %collective-permute-start.43 = (bf16[48,1536]{1,0:T(8,128)(2,1)}, bf16[48,1536]{1,0:T(8,128)(2,1)S(1)}, u32[]{:S(2)}, u32[]{:S(2)}) collective-permute-start(bf16[48,1536]{1,0:T(8,128)(2,1)} %get-tuple-element.373), channel_id=1, source_target_pairs={{0,2},{2,4},{4,6},{6,0},{1,3},{3,5},{5,7},{7,1},{8,10},{10,12},{12... | collective-permute-start | bytes 442376 | tf_op jit(solution)/shard_map/ppermute | solution.py:167
  520.4 22.6 %collective-permute-start.45 = (bf16[48,1536]{1,0:T(8,128)(2,1)}, bf16[48,1536]{1,0:T(8,128)(2,1)}, u32[]{:S(2)}, u32[]{:S(2)}) collective-permute-start(bf16[48,1536]{1,0:T(8,128)(2,1)} %get-tuple-element.374), channel_id=1, source_target_pairs={{0,6},{2,0},{4,2},{6,4},{1,7},{3,1},{5,3},{7,5},{8,14},{10,8},{12,... | collective-permute-start | bytes 442376 | tf_op jit(solution)/shard_map/ppermute | solution.py:167
  (118 other events, 919.3 us)

commit v8 on v7

--- a/solution.py
+++ b/solution.py
@@ -475,7 +475,7 @@
 
 
 def piece_copies(blocks, refs, target_ref, sems):
-    out, at = [], 0
+    out = []
     count = refs[0].shape[1]
     for b, pieces in enumerate(blocks):
         copies = []
@@ -485,10 +485,9 @@
                 pltpu.make_async_copy(
                     refs[ref].at[row : row + last - first],
                     target_ref.at[first:last, b * count : (b + 1) * count],
-                    sems.at[at],
+                    sems.at[b],
                 )
             )
-            at += 1
         out.append(copies)
     return out
 
@@ -552,7 +551,7 @@
 
     def scratch(self):
         wide = pltpu.VMEM((self.width, self.tokens), BF16)
-        sems = [pltpu.SemaphoreType.DMA((sum(map(len, plan)),)) for plan in self.plans]
+        sems = [pltpu.SemaphoreType.DMA((self.blocks,))] * 2
         return [wide, wide] + sems
 
     def copies(self, refs, rows_ref, cots_ref, row_sems, cot_sems):
@@ -583,28 +582,30 @@
         step = pl.program_id(0)
         row = e_ref[0] + first + step
 
-        def move(wait, start):
-            def run():
-                for b in start:
-                    for copy in copies[b]:
-                        copy.start()
-                for copy in copies[wait]:
-                    copy.wait()
-
-            if n == 1:
-                run()
-            else:
-                pl.when(step == 0)(run)
+        def start():
+            for block in copies:
+                for copy in block:
+                    copy.start()
+
+        pl.when(step == 0)(start)
+
+        def columns(b):
+            return pl.ds(pl.multiple_of(b * count, count), count)
+
+        def arrive(b):
+            whole = piece_refs[0].at[0 : self.width]
+            for target, sems in zip(scratch[:2], scratch[2:4]):
+                pltpu.make_async_copy(whole, target.at[:, columns(b)], sems.at[b]).wait()
 
         def products(b):
-            move(b, range(blocks) if b == 0 else ())
-            cols = slice(b * count, (b + 1) * count)
+            pl.when(step == 0)(lambda: arrive(b))
+            cols = columns(b)
             acts = jnp.dot(in_t_ref[...], rows_ref[:, cols], preferred_element_type=F32)
             grad = jnp.dot(down_ref[...], cots_ref[:, cols], preferred_element_type=F32)
             return acts, grad
 
         def finish(b, acts, grad):
-            cols = slice(b * count, (b + 1) * count)
+            cols = columns(b)
             gate, up = acts[:units], acts[units : 2 * units]
             if make_gates:
                 chosen = chosen_ref[:, cols] > 0
@@ -626,8 +627,15 @@
             dgate_ref[:, cols] = (grad * up * (sigmoid + silu * (1.0 - sigmoid))).astype(BF16)
 
         dscale_ref[...] = jnp.zeros_like(dscale_ref)
-        for b in range(blocks):
-            finish(b, *products(b))
+
+        unroll = 4 if blocks % 4 == 0 else 1
+
+        def some(i, carry):
+            for u in range(unroll):
+                finish(i * unroll + u, *products(i * unroll + u))
+            return carry
+
+        lax.fori_loop(0, blocks // unroll, some, 0)
         write_grads(
             rows_ref,
             cots_ref,

time: 573 us -> 572 us (level)
  transfers between devices with their start and end apart: 59 -> 59, of which waited for: 21 -> 21; matrix products, arithmetic and copies ran while one was open for 24% -> 24% of each run, Pallas kernels for 26% -> 27%
where the time goes in v8:
time: 572 us; the launch traced here: 566 us
  Pallas kernels  180 us (31%)
  waiting for transfers between devices  122 us (21%)
  starting transfers between devices  103 us (18%)
  other arithmetic  80.2 us (14%)
  local copies, waits for them, and re-layouts  48.3 us (8%)
  matrix products  29.6 us (5%)
    pallas_call x3, Pallas kernels, act(): pl.pallas_call(functools.partial(self.act_kernel, first, n, make_gates),...  89.2 us
    ppermute x9, waiting for transfers between devices, pair(): lax.ppermute(value, 'context', [(i, i ^ 1) for i in range(self.n_context)])  83.7 us
    dot_general x14, matrix products, mm(): lax.dot_general(a, b, (((da,), (db,)), ((), ())), preferred_element_type=...  29.6 us
    ppermute x12, starting transfers between devices, send_context(): out.append(lax.ppermute(parts[s - 1], 'context', pairs))  28.6 us
    pallas_call x2, Pallas kernels, back(): pl.pallas_call(functools.partial(self.back_kernel, parts), out_shape=jax....  27.6 us
    unnamed x203, local copies, waits for them, and re-layouts  21.2 us
    pallas_call x2, Pallas kernels, out(): pl.pallas_call(functools.partial(self.out_kernel, parts), out_shape=jax.S...  18.7 us
    all_to_all x2, starting transfers between devices, to_keys(): return lax.all_to_all(grad_kv, 'context', 0, 0, tiled=True)  17.8 us
  transfers between devices with their start and end apart: 59, of which 21 were waited for; matrix products, arithmetic and copies ran while one was open for 24% of the time, Pallas kernels for 27%

profile of v8, /device:TPU:0, one launch (start us, length us, event | category | flops | bytes accessed | tf_op | source)
XLA Modules:
  0.0 565.6 jit_solution(12332985014443532412)
XLA Ops:
  10.9 7.0 %collective-permute-start.2 = (bf16[1024,256]{1,0:T(8,128)(2,1)S(1)}, bf16[1024,256]{1,0:T(8,128)(2,1)S(1)}, u32[]{:S(2)}, u32[]{:S(2)}) collective-permute-start(bf16[1024,256]{1,0:T(8,128)(2,1)S(1)} %pad_maximum_fusion.15.refs_0_.refs_4_), channel_id=1, source_target_pairs={{0,6},{1,7},{8,14},{9,15},{16,22},{17,23},{24,30},{25,31}} | collective-permute-start | bytes 1572872 | tf_op jit(solution)/shard_map/ppermute | solution.py:841
  23.5 4.9 convolution_bitcast_fusion
  31.4 15.1 %prepare_weights.1 = (bf16[5,2,2,128,1536]{4,3,2,1,0:T(8,128)(2,1)}, bf16[1536,1280]{1,0:T(8,128)(2,1)}, bf16[1536,1280]{1,0:T(8,128)(2,1)}, bf16[1280,1536]{1,0:T(8,128)(2,1)}, bf16[1536,1280]{1,0:T(8,128)(2,1)}) custom-call(s32[1]{0:T(128)} %bitcast.14.p_ref, bf16[5,1536,512]{2,1,0:T(8,128)(2,1)} %gate_ref.1, bf16[5,1536,512]{2,1,0:T(8,128)(2,1)} %up_ref.1, ...), custom_call_target="tpu_custom_call" | custom-call | bytes 552960 | tf_op jit(solution)/shard_map/prepare_weights/pallas_call | solution.py:444
  53.7 15.2 %collective-permute-done.4.refs_13_ = bf16[1568,256]{1,0:T(8,128)(2,1)} collective-permute-done((bf16[1568,256]{1,0:T(8,128)(2,1)}, bf16[1568,256]{1,0:T(8,128)(2,1)}, u32[]{:S(2)}, u32[]{:S(2)}) %collective-permute-start.4) | collective-permute-done | bytes 802848 | tf_op jit(solution)/shard_map/ppermute | solution.py:68
  72.0 10.8 %attn_fwd.1 = (f32[1536,256]{1,0:T(8,128)S(1)}, bf16[1536,256]{1,0:T(8,128)(2,1)S(1)}, f32[8,8,256]{2,1,0:T(8,128)S(1)}) custom-call(s32[1]{0:T(128)} %bitcast.5.c_ref, bf16[1536,256]{1,0:T(8,128)(2,1)S(1)} %bitcast.217, bf16[1024,256]{1,0:T(8,128)(2,1)S(1)} %pad_maximum_fusion.15.refs_0_.refs_4_, ...), custom_call_target="tpu_custom_call" | custom-call | flops 100663296 | bytes 98304 | tf_op jit(solution)/shard_map/attn_fwd/pallas_call | solution.py:307
  82.8 4.9 multiply_reduce_fusion.2
  88.7 4.4 collective-permute-start.7
  97.0 14.2 %collective-permute-done.7.refs_6_ = bf16[1536,256]{1,0:T(8,128)(2,1)S(1)} collective-permute-done((bf16[1536,256]{1,0:T(8,128)(2,1)S(1)}, bf16[1536,256]{1,0:T(8,128)(2,1)S(1)}, u32[]{:S(2)}, u32[]{:S(2)}) %collective-permute-start.7) | collective-permute-done | bytes 786464 | tf_op jit(solution)/shard_map/ppermute | solution.py:68
  116.5 6.7 %collective-permute-done.11.refs_8_ = bf16[768,256]{1,0:T(8,128)(2,1)S(1)} collective-permute-done((bf16[768,256]{1,0:T(8,128)(2,1)S(1)}, bf16[768,256]{1,0:T(8,128)(2,1)S(1)}, u32[]{:S(2)}, u32[]{:S(2)}) %collective-permute-start.11) | collective-permute-done | bytes 393248 | tf_op jit(solution)/shard_map/ppermute | solution.py:68
  126.9 20.7 %experts_act.3 = (f32[32,2048]{1,0:T(8,128)}, f32[32,2048]{1,0:T(8,128)}, bf16[256,2048]{1,0:T(8,128)(2,1)}, bf16[256,2048]{1,0:T(8,128)(2,1)}, bf16[256,2048]{1...) custom-call(s32[3]{0:T(128)} %pad_add_fusion.e_ref, ...), custom_call_target="tpu_custom_call" | custom-call | flops 150994944 | bytes 282624 | tf_op jit(solution)/shard_map/experts_act/pallas_call | solution.py:667
  151.4 33.9 %experts_act.4 = (bf16[512,2048]{1,0:T(8,128)(2,1)}, bf16[512,2048]{1,0:T(8,128)(2,1)}, bf16[512,2048]{1,0:T(8,128)(2,1)}, f32[2,8,2048]{2,1,0:T(8,128)}, bf16[2...) custom-call(s32[3]{0:T(128)} %pad_add_fusion.e_ref, f32[32,2048]{1,0:T(8,128)} %copy-done.53, ...), custom_call_target="tpu_custom_call" | custom-call | flops 301989888 | bytes 368640 | tf_op jit(solution)/shard_map/experts_act/pallas_call | solution.py:667
  185.3 34.6 %experts_act.5 = (bf16[512,2048]{1,0:T(8,128)(2,1)}, bf16[512,2048]{1,0:T(8,128)(2,1)}, bf16[512,2048]{1,0:T(8,128)(2,1)}, f32[2,8,2048]{2,1,0:T(8,128)}, bf16[2...) custom-call(s32[3]{0:T(128)} %pad_add_fusion.e_ref, f32[32,2048]{1,0:T(8,128)} %copy-done.53, ...), custom_call_target="tpu_custom_call" | custom-call | flops 301989888 | bytes 368640 | tf_op jit(solution)/shard_map/experts_act/pallas_call | solution.py:667
  219.9 9.2 %experts_out.3 = bf16[4,1600,256]{2,1,0:T(8,128)(2,1)} custom-call(s32[3]{0:T(128)} %pad_add_fusion.e_ref, bf16[1536,1280]{1,0:T(8,128)(2,1)} %get-tuple-element.171.weight_ref, bf16[256,2048]{1,0:T(8,128)(2,1)} %get-tuple-element.201.refs_0_, bf16[512,2048]{1,0:T(8,128)(2,1)} %get-tuple-element.202.refs_1_, bf16[512,2048]{1,0:T(8,128)(2,1)} %get-tuple-element.203.refs_2_, ...), custom_call_target="tpu_custom_call" | custom-call | flops 62914560 | bytes 159744 | tf_op jit(solution)/shard_map/experts_out/pallas_call | solution.py:722
  229.8 13.8 %experts_back.3 = bf16[4,1536,256]{2,1,0:T(8,128)(2,1)} custom-call(bf16[1536,1280]{1,0:T(8,128)(2,1)} %get-tuple-element.212.gate_w_ref, bf16[1536,1280]{1,0:T(8,128)(2,1)} %get-tuple-element.213.up_w_ref, bf16[256,2048]{1,0:T(8,128)(2,1)} %get-tuple-element.220.refs_0_, bf16[512,2048]{1,0:T(8,128)(2,1)} %get-tuple-element.221.refs_1_, ...), custom_call_target="tpu_custom_call" | custom-call | flops 125829120 | bytes 221184 | tf_op jit(solution)/shard_map/experts_back/pallas_call | solution.py:769
  247.3 6.0 %collective-permute-start.22 = (bf16[1,1152,256]{2,1,0:T(8,128)(2,1)}, bf16[1,1152,256]{2,1,0:T(8,128)(2,1)}, u32[]{:S(2)}, u32[]{:S(2)}) collective-permute-start(bf16[1,1152,256]{2,1,0:T(8,128)(2,1)} %get-tuple-element.366), channel_id=1, source_target_pairs={{0,4},{2,6},{4,0},{6,2},{1,5},{3,7},{5,1},{7,3},{8,12},{10,14},{12... | collective-permute-start | bytes 1769480 | tf_op jit(solution)/shard_map/ppermute | solution.py:167
  253.4 9.5 %experts_out.2 = bf16[4,1600,256]{2,1,0:T(8,128)(2,1)} custom-call(s32[3]{0:T(128)} %pad_add_fusion.e_ref, bf16[1536,1280]{1,0:T(8,128)(2,1)} %get-tuple-element.171.weight_ref, bf16[256,2048]{1,0:T(8,128)(2,1)} %get-tuple-element.201.refs_0_, bf16[512,2048]{1,0:T(8,128)(2,1)} %get-tuple-element.202.refs_1_, bf16[512,2048]{1,0:T(8,128)(2,1)} %get-tuple-element.203.refs_2_, ...), custom_call_target="tpu_custom_call" | custom-call | flops 62914560 | bytes 159744 | tf_op jit(solution)/shard_map/experts_out/pallas_call | solution.py:722
  287.0 6.2 %collective-permute-start.31 = (bf16[2,1152,256]{2,1,0:T(8,128)(2,1)}, bf16[2,1152,256]{2,1,0:T(8,128)(2,1)}, u32[]{:S(2)}, u32[]{:S(2)}) collective-permute-start(bf16[2,1152,256]{2,1,0:T(8,128)(2,1)} %get-tuple-element.362), channel_id=1, source_target_pairs={{0,4},{2,6},{4,0},{6,2},{1,5},{3,7},{5,1},{7,3},{8,12},{10,14},{12... | collective-permute-start | bytes 3538952 | tf_op jit(solution)/shard_map/ppermute | solution.py:167
  293.2 13.8 %experts_back.2 = bf16[4,1536,256]{2,1,0:T(8,128)(2,1)} custom-call(bf16[1536,1280]{1,0:T(8,128)(2,1)} %get-tuple-element.212.gate_w_ref, bf16[1536,1280]{1,0:T(8,128)(2,1)} %get-tuple-element.213.up_w_ref, bf16[256,2048]{1,0:T(8,128)(2,1)} %get-tuple-element.220.refs_0_, bf16[512,2048]{1,0:T(8,128)(2,1)} %get-tuple-element.221.refs_1_, ...), custom_call_target="tpu_custom_call" | custom-call | flops 125829120 | bytes 221184 | tf_op jit(solution)/shard_map/experts_back/pallas_call | solution.py:769
  325.1 25.3 %collective-permute-done.23 = bf16[800,256]{1,0:T(8,128)(2,1)S(1)} collective-permute-done((bf16[800,256]{1,0:T(8,128)(2,1)S(1)}, bf16[800,256]{1,0:T(8,128)(2,1)S(1)}, u32[]{:S(2)}, u32[]{:S(2)}) %collective-permute-start.23) | collective-permute-done | bytes 409632 | tf_op jit(solution)/shard_map/ppermute | solution.py:68
  352.4 12.4 %collective-permute-done.28 = bf16[2,768,256]{2,1,0:T(8,128)(2,1)S(1)} collective-permute-done((bf16[2,768,256]{2,1,0:T(8,128)(2,1)S(1)}, bf16[2,768,256]{2,1,0:T(8,128)(2,1)S(1)}, u32[]{:S(2)}, u32[]{:S(2)}) %collective-permute-start.28) | collective-permute-done | bytes 786464 | tf_op jit(solution)/shard_map/ppermute | solution.py:68
  373.9 5.1 collective-permute-done.29
  396.7 11.4 %all-to-all-start = ((bf16[4,2,256,256]{3,2,1,0:T(8,128)(2,1)}), bf16[4,2,256,256]{3,2,1,0:T(8,128)(2,1)}, u32[]{:S(2)}, u32[]{:S(2)}) async-start(bf16[4,2,256,256]{3,2,1,0:T(8,128)(2,1)} %copy-done.8), calls=%async_computation | async-start | bytes 2097152 | tf_op jit(solution)/shard_map/all_to_all | solution.py:1000
  424.4 4.8 collective-permute-start.36
  431.6 4.9 fusion.87
  437.6 7.4 %all-to-all-done = bf16[4,2,256,256]{3,2,1,0:T(8,128)(2,1)} async-done(((bf16[4,2,256,256]{3,2,1,0:T(8,128)(2,1)}), bf16[4,2,256,256]{3,2,1,0:T(8,128)(2,1)}, u32[]{:S(2)}, u32[]{:S(2)}) %all-to-all-start) | async-done | bytes 1048608 | tf_op jit(solution)/shard_map/all_to_all | solution.py:1000
  446.4 6.4 %all-to-all-start.1 = ((bf16[4,2,256,256]{3,2,1,0:T(8,128)(2,1)}), bf16[4,2,256,256]{3,2,1,0:T(8,128)(2,1)}, u32[]{:S(2)}, u32[]{:S(2)}) async-start(bf16[4,2,256,256]{3,2,1,0:T(8,128)(2,1)} %get-tuple-element.258), calls=%async_computation.1 | async-start | bytes 2097152 | tf_op jit(solution)/shard_map/all_to_all | solution.py:1000
  465.2 4.8 row_products.3
  476.3 4.9 collective-permute-done.55
  483.9 4.5 row_products.4
  532.1 4.3 collective-permute-done.53
  538.1 6.8 %all-to-all-start.2 = ((bf16[8,48,128]{2,1,0:T(8,128)(2,1)}), bf16[8,48,128]{2,1,0:T(8,128)(2,1)S(1)}, u32[]{:S(2)}, u32[]{:S(2)}) async-start(bf16[8,48,128]{2,1,0:T(8,128)(2,1)} %maximum_maximum_fusion), calls=%async_computation.2 | async-start | bytes 196608 | tf_op jit(solution)/shard_map/all_to_all | solution.py:1077
  547.0 5.0 all-to-all-done.2
  (448 shorter events, 224.4 us)
Async XLA Ops:
  10.9 59.5 %collective-permute-start.2 = (bf16[1024,256]{1,0:T(8,128)(2,1)S(1)}, bf16[1024,256]{1,0:T(8,128)(2,1)S(1)}, u32[]{:S(2)}, u32[]{:S(2)}) collective-permute-start(bf16[1024,256]{1,0:T(8,128)(2,1)S(1)} %pad_maximum_fusion.15.refs_0_.refs_4_), channel_id=1, source_target_pairs={{0,6},{1,7},{8,14},{9,15},{16,22},{17,23},{24,30},{25,31}} | collective-permute-start | bytes 1572872 | tf_op jit(solution)/shard_map/ppermute | solution.py:841
  17.9 52.5 %collective-permute-start.1 = (bf16[1024,256]{1,0:T(8,128)(2,1)S(1)}, bf16[1024,256]{1,0:T(8,128)(2,1)S(1)}, u32[]{:S(2)}, u32[]{:S(2)}) collective-permute-start(bf16[1024,256]{1,0:T(8,128)(2,1)S(1)} %pad_maximum_fusion.15.refs_0_.refs_4_), channel_id=1, source_target_pairs={{0,4},{2,6},{1,5},{3,7},{8,12},{10,14},{9,13},{11,15},{16,20},{18,... | collective-permute-start | bytes 1572872 | tf_op jit(solution)/shard_map/ppermute | solution.py:841
  19.2 51.2 %collective-permute-start = (bf16[1024,256]{1,0:T(8,128)(2,1)S(1)}, bf16[1024,256]{1,0:T(8,128)(2,1)S(1)}, u32[]{:S(2)}, u32[]{:S(2)}) collective-permute-start(bf16[1024,256]{1,0:T(8,128)(2,1)S(1)} %pad_maximum_fusion.15.refs_0_.refs_4_), channel_id=1, source_target_pairs={{0,2},{2,4},{4,6},{1,3},{3,5},{5,7},{8,10},{10,12},{12,14},{9,11},... | collective-permute-start | bytes 1572872 | tf_op jit(solution)/shard_map/ppermute | solution.py:841
  21.9 47.0 %collective-permute-start.4 = (bf16[1568,256]{1,0:T(8,128)(2,1)}, bf16[1568,256]{1,0:T(8,128)(2,1)}, u32[]{:S(2)}, u32[]{:S(2)}) collective-permute-start(bf16[1568,256]{1,0:T(8,128)(2,1)} %pad_maximum_fusion.12.refs_11_), channel_id=1, source_target_pairs={{0,2},{2,0},{4,6},{6,4},{1,3},{3,1},{5,7},{7,5},{8,10},{10,8},{12,... | collective-permute-start | bytes 2408456 | tf_op jit(solution)/shard_map/ppermute | solution.py:68
  21.9 48.4 %collective-permute-start.3 = (bf16[1568,256]{1,0:T(8,128)(2,1)}, bf16[1568,256]{1,0:T(8,128)(2,1)}, u32[]{:S(2)}, u32[]{:S(2)}) collective-permute-start(bf16[1568,256]{1,0:T(8,128)(2,1)} %pad_maximum_fusion.12.refs_11_), channel_id=1, source_target_pairs={{16,0},{24,8},{0,16},{8,24},{17,1},{25,9},{1,17},{9,25},{18,2},{26... | collective-permute-start | bytes 2408456 | tf_op jit(solution)/shard_map/ppermute | solution.py:61
  71.9 44.6 %collective-permute-start.8 = (bf16[3136,256]{1,0:T(8,128)(2,1)S(1)}, bf16[3136,256]{1,0:T(8,128)(2,1)S(1)}, u32[]{:S(2)}, u32[]{:S(2)}) collective-permute-start(bf16[3136,256]{1,0:T(8,128)(2,1)S(1)} %pad_maximum_fusion.6), channel_id=1, source_target_pairs={{8,0},{0,8},{24,16},{16,24},{9,1},{1,9},{25,17},{17,25},{10,2},{2,... | collective-permute-start | bytes 4816904 | tf_op jit(solution)/shard_map/ppermute | solution.py:61
  147.7 37.6 %collective-permute-start.17 = (bf16[2,1,1152,256]{3,2,1,0:T(8,128)(2,1)}, bf16[2,1,1152,256]{3,2,1,0:T(8,128)(2,1)}, u32[]{:S(2)}, u32[]{:S(2)}) collective-permute-start(bf16[2,1,1152,256]{3,2,1,0:T(8,128)(2,1)} %get-tuple-element.198), channel_id=1, source_target_pairs={{0,1},{1,0},{2,3},{3,2},{4,5},{5,4},{6,7},{7,6},{8,9},{9,8},{10,11... | collective-permute-start | bytes 3538952 | tf_op jit(solution)/shard_map/ppermute | solution.py:155
  149.2 70.6 %collective-permute-start.14 = (bf16[768,256]{1,0:T(8,128)(2,1)}, bf16[768,256]{1,0:T(8,128)(2,1)S(1)}, u32[]{:S(2)}, u32[]{:S(2)}) collective-permute-start(bf16[768,256]{1,0:T(8,128)(2,1)} %get-tuple-element.191), channel_id=1, source_target_pairs={{16,0},{24,8},{0,16},{8,24},{17,1},{25,9},{1,17},{9,25},{18,2},{26... | collective-permute-start | bytes 1179656 | tf_op jit(solution)/shard_map/ppermute | solution.py:61
  149.8 70.1 %collective-permute-start.15 = (bf16[768,256]{1,0:T(8,128)(2,1)}, bf16[768,256]{1,0:T(8,128)(2,1)}, u32[]{:S(2)}, u32[]{:S(2)}) collective-permute-start(bf16[768,256]{1,0:T(8,128)(2,1)} %get-tuple-element.192), channel_id=1, source_target_pairs={{8,0},{0,8},{24,16},{16,24},{9,1},{1,9},{25,17},{17,25},{10,2},{2,... | collective-permute-start | bytes 1179656 | tf_op jit(solution)/shard_map/ppermute | solution.py:61
  149.8 70.1 %collective-permute-start.16 = (bf16[768,256]{1,0:T(8,128)(2,1)}, bf16[768,256]{1,0:T(8,128)(2,1)S(1)}, u32[]{:S(2)}, u32[]{:S(2)}) collective-permute-start(bf16[768,256]{1,0:T(8,128)(2,1)} %get-tuple-element.193), channel_id=1, source_target_pairs={{24,0},{16,8},{8,16},{0,24},{25,1},{17,9},{9,17},{1,25},{26,2},{18... | collective-permute-start | bytes 1179656 | tf_op jit(solution)/shard_map/ppermute | solution.py:61
  229.1 36.9 %collective-permute-start.18 = (bf16[4,1600,256]{2,1,0:T(8,128)(2,1)}, bf16[4,1600,256]{2,1,0:T(8,128)(2,1)}, u32[]{:S(2)}, u32[]{:S(2)}) collective-permute-start(bf16[4,1600,256]{2,1,0:T(8,128)(2,1)} %experts_out.3), channel_id=1, source_target_pairs={{0,8},{8,0},{16,24},{24,16},{1,9},{9,1},{17,25},{25,17},{2,10},{10... | collective-permute-start | bytes 9830408 | tf_op jit(solution)/shard_map/ppermute | solution.py:65
  229.2 54.2 %collective-permute-start.21 = (bf16[2,2,1152,256]{3,2,1,0:T(8,128)(2,1)}, bf16[2,2,1152,256]{3,2,1,0:T(8,128)(2,1)}, u32[]{:S(2)}, u32[]{:S(2)}) collective-permute-start(bf16[2,2,1152,256]{3,2,1,0:T(8,128)(2,1)} %get-tuple-element.214), channel_id=1, source_target_pairs={{0,1},{1,0},{2,3},{3,2},{4,5},{5,4},{6,7},{7,6},{8,9},{9,8},{10,11... | collective-permute-start | bytes 7077896 | tf_op jit(solution)/shard_map/ppermute | solution.py:155
  243.6 65.6 %collective-permute-start.26 = (bf16[4,1536,256]{2,1,0:T(8,128)(2,1)}, bf16[4,1536,256]{2,1,0:T(8,128)(2,1)}, u32[]{:S(2)}, u32[]{:S(2)}) collective-permute-start(bf16[4,1536,256]{2,1,0:T(8,128)(2,1)} %experts_back.3), channel_id=1, source_target_pairs={{0,8},{8,0},{16,24},{24,16},{1,9},{9,1},{17,25},{25,17},{2,10},{10... | collective-permute-start | bytes 9437192 | tf_op jit(solution)/shard_map/ppermute | solution.py:65
  247.3 32.9 %collective-permute-start.22 = (bf16[1,1152,256]{2,1,0:T(8,128)(2,1)}, bf16[1,1152,256]{2,1,0:T(8,128)(2,1)}, u32[]{:S(2)}, u32[]{:S(2)}) collective-permute-start(bf16[1,1152,256]{2,1,0:T(8,128)(2,1)} %get-tuple-element.366), channel_id=1, source_target_pairs={{0,4},{2,6},{4,0},{6,2},{1,5},{3,7},{5,1},{7,3},{8,12},{10,14},{12... | collective-permute-start | bytes 1769480 | tf_op jit(solution)/shard_map/ppermute | solution.py:167
  269.9 37.1 %collective-permute-start.20 = (bf16[2,800,256]{2,1,0:T(8,128)(2,1)}, bf16[2,800,256]{2,1,0:T(8,128)(2,1)}, u32[]{:S(2)}, u32[]{:S(2)}) collective-permute-start(bf16[2,800,256]{2,1,0:T(8,128)(2,1)} %get-tuple-element.354), channel_id=1, source_target_pairs={{0,2},{2,0},{4,6},{6,4},{1,3},{3,1},{5,7},{7,5},{8,10},{10,8},{12,... | collective-permute-start | bytes 2457608 | tf_op jit(solution)/shard_map/ppermute | solution.py:68
  274.6 32.4 %collective-permute-start.19 = (bf16[2,800,256]{2,1,0:T(8,128)(2,1)}, bf16[2,800,256]{2,1,0:T(8,128)(2,1)}, u32[]{:S(2)}, u32[]{:S(2)}) collective-permute-start(bf16[2,800,256]{2,1,0:T(8,128)(2,1)} %get-tuple-element.356), channel_id=1, source_target_pairs={{0,16},{8,24},{16,0},{24,8},{1,17},{9,25},{17,1},{25,9},{2,18},{10... | collective-permute-start | bytes 2457608 | tf_op jit(solution)/shard_map/ppermute | solution.py:65
  280.3 72.2 %collective-permute-start.25 = (bf16[2,2,1152,256]{3,2,1,0:T(8,128)(2,1)}, bf16[2,2,1152,256]{3,2,1,0:T(8,128)(2,1)}, u32[]{:S(2)}, u32[]{:S(2)}) collective-permute-start(bf16[2,2,1152,256]{3,2,1,0:T(8,128)(2,1)} %get-tuple-element.230), channel_id=1, source_target_pairs={{0,1},{1,0},{2,3},{3,2},{4,5},{5,4},{6,7},{7,6},{8,9},{9,8},{10,11... | collective-permute-start | bytes 7077896 | tf_op jit(solution)/shard_map/ppermute | solution.py:155
  287.0 104.5 %collective-permute-start.31 = (bf16[2,1152,256]{2,1,0:T(8,128)(2,1)}, bf16[2,1152,256]{2,1,0:T(8,128)(2,1)}, u32[]{:S(2)}, u32[]{:S(2)}) collective-permute-start(bf16[2,1152,256]{2,1,0:T(8,128)(2,1)} %get-tuple-element.362), channel_id=1, source_target_pairs={{0,4},{2,6},{4,0},{6,2},{1,5},{3,7},{5,1},{7,3},{8,12},{10,14},{12... | collective-permute-start | bytes 3538952 | tf_op jit(solution)/shard_map/ppermute | solution.py:167
  313.5 36.9 %collective-permute-start.23 = (bf16[800,256]{1,0:T(8,128)(2,1)S(1)}, bf16[800,256]{1,0:T(8,128)(2,1)S(1)}, u32[]{:S(2)}, u32[]{:S(2)}) collective-permute-start(bf16[800,256]{1,0:T(8,128)(2,1)S(1)} %fusion.33), channel_id=1, source_target_pairs={{0,2},{2,0},{4,6},{6,4},{1,3},{3,1},{5,7},{7,5},{8,10},{10,8},{12,... | collective-permute-start | bytes 1228808 | tf_op jit(solution)/shard_map/ppermute | solution.py:68
  314.9 37.5 %collective-permute-start.27 = (bf16[2,768,256]{2,1,0:T(8,128)(2,1)S(1)}, bf16[2,768,256]{2,1,0:T(8,128)(2,1)S(1)}, u32[]{:S(2)}, u32[]{:S(2)}) collective-permute-start(bf16[2,768,256]{2,1,0:T(8,128)(2,1)S(1)} %fusion.26), channel_id=1, source_target_pairs={{0,16},{8,24},{16,0},{24,8},{1,17},{9,25},{17,1},{25,9},{2,18},{10... | collective-permute-start | bytes 2359304 | tf_op jit(solution)/shard_map/ppermute | solution.py:65
  321.0 43.9 %collective-permute-start.28 = (bf16[2,768,256]{2,1,0:T(8,128)(2,1)S(1)}, bf16[2,768,256]{2,1,0:T(8,128)(2,1)S(1)}, u32[]{:S(2)}, u32[]{:S(2)}) collective-permute-start(bf16[2,768,256]{2,1,0:T(8,128)(2,1)S(1)} %get-tuple-element.358), channel_id=1, source_target_pairs={{0,2},{2,0},{4,6},{6,4},{1,3},{3,1},{5,7},{7,5},{8,10},{10,8},{12,... | collective-permute-start | bytes 2359304 | tf_op jit(solution)/shard_map/ppermute | solution.py:68
  370.4 66.1 %collective-permute-start.35 = (bf16[2,1152,256]{2,1,0:T(8,128)(2,1)}, bf16[2,1152,256]{2,1,0:T(8,128)(2,1)}, u32[]{:S(2)}, u32[]{:S(2)}) collective-permute-start(bf16[2,1152,256]{2,1,0:T(8,128)(2,1)} %get-tuple-element.360), channel_id=1, source_target_pairs={{0,4},{2,6},{4,0},{6,2},{1,5},{3,7},{5,1},{7,3},{8,12},{10,14},{12... | collective-permute-start | bytes 3538952 | tf_op jit(solution)/shard_map/ppermute | solution.py:167
  396.7 48.3 %all-to-all-start = ((bf16[4,2,256,256]{3,2,1,0:T(8,128)(2,1)}), bf16[4,2,256,256]{3,2,1,0:T(8,128)(2,1)}, u32[]{:S(2)}, u32[]{:S(2)}) async-start(bf16[4,2,256,256]{3,2,1,0:T(8,128)(2,1)} %copy-done.8), calls=%async_computation | async-start | bytes 2097152 | tf_op jit(solution)/shard_map/all_to_all | solution.py:1000
  412.9 32.1 %collective-permute-start.33 = (bf16[1584,256]{1,0:T(8,128)(2,1)}, bf16[1584,256]{1,0:T(8,128)(2,1)}, u32[]{:S(2)}, u32[]{:S(2)}) collective-permute-start(bf16[1584,256]{1,0:T(8,128)(2,1)} %pad_maximum_fusion.11.refs_4_), channel_id=1, source_target_pairs={{8,0},{0,8},{24,16},{16,24},{9,1},{1,9},{25,17},{17,25},{10,2},{2,... | collective-permute-start | bytes 2433032 | tf_op jit(solution)/shard_map/ppermute | solution.py:61
  412.9 32.1 %collective-permute-start.34 = (bf16[1584,256]{1,0:T(8,128)(2,1)}, bf16[1584,256]{1,0:T(8,128)(2,1)}, u32[]{:S(2)}, u32[]{:S(2)}) collective-permute-start(bf16[1584,256]{1,0:T(8,128)(2,1)} %collective-permute-done.32.refs_5_), channel_id=1, source_target_pairs={{8,0},{0,8},{24,16},{16,24},{9,1},{1,9},{25,17},{17,25},{10,2},{2,... | collective-permute-start | bytes 2433032 | tf_op jit(solution)/shard_map/ppermute | solution.py:61
  424.4 65.7 %collective-permute-start.36 = (bf16[3,2,192,256]{3,2,0,1:T(8,128)(2,1)}, bf16[3,2,192,256]{3,2,0,1:T(8,128)(2,1)}, u32[]{:S(2)}, u32[]{:S(2)}) collective-permute-start(bf16[3,2,192,256]{3,2,0,1:T(8,128)(2,1)} %fusion.32), channel_id=1, source_target_pairs={{0,2},{2,0},{4,6},{6,4},{1,3},{3,1},{5,7},{7,5},{8,10},{10,8},{12,... | collective-permute-start | bytes 1769480 | tf_op jit(solution)/shard_map/ppermute | solution.py:68
  436.5 47.4 %collective-permute-start.40 = (bf16[1536,256]{1,0:T(8,128)(2,1)S(1)}, bf16[1536,256]{1,0:T(8,128)(2,1)}, u32[]{:S(2)}, u32[]{:S(2)}) collective-permute-start(bf16[1536,256]{1,0:T(8,128)(2,1)S(1)} %pad_maximum_fusion.14.refs_4_), channel_id=1, source_target_pairs={{8,0},{0,8},{24,16},{16,24},{9,1},{1,9},{25,17},{17,25},{10,2},{2,... | collective-permute-start | bytes 2359304 | tf_op jit(solution)/shard_map/ppermute | solution.py:61
  437.6 46.3 %collective-permute-start.41 = (bf16[1536,256]{1,0:T(8,128)(2,1)}, bf16[1536,256]{1,0:T(8,128)(2,1)}, u32[]{:S(2)}, u32[]{:S(2)}) collective-permute-start(bf16[1536,256]{1,0:T(8,128)(2,1)} %collective-permute-done.39.refs_5_), channel_id=1, source_target_pairs={{8,0},{0,8},{24,16},{16,24},{9,1},{1,9},{25,17},{17,25},{10,2},{2,... | collective-permute-start | bytes 2359304 | tf_op jit(solution)/shard_map/ppermute | solution.py:61
  446.4 43.6 %all-to-all-start.1 = ((bf16[4,2,256,256]{3,2,1,0:T(8,128)(2,1)}), bf16[4,2,256,256]{3,2,1,0:T(8,128)(2,1)}, u32[]{:S(2)}, u32[]{:S(2)}) async-start(bf16[4,2,256,256]{3,2,1,0:T(8,128)(2,1)} %get-tuple-element.258), calls=%async_computation.1 | async-start | bytes 2097152 | tf_op jit(solution)/shard_map/all_to_all | solution.py:1000
  470.0 40.7 %collective-permute-start.38 = (bf16[4,48,1536]{2,1,0:T(8,128)(2,1)}, bf16[4,48,1536]{2,1,0:T(8,128)(2,1)}, u32[]{:S(2)}, u32[]{:S(2)}) collective-permute-start(bf16[4,48,1536]{2,1,0:T(8,128)(2,1)} %get-tuple-element.269), channel_id=1, source_target_pairs={{0,1},{1,0},{2,3},{3,2},{4,5},{5,4},{6,7},{7,6},{8,9},{9,8},{10,11... | collective-permute-start | bytes 1769480 | tf_op jit(solution)/shard_map/ppermute | solution.py:155
  521.5 23.4 %collective-permute-start.43 = (bf16[48,1536]{1,0:T(8,128)(2,1)}, bf16[48,1536]{1,0:T(8,128)(2,1)S(1)}, u32[]{:S(2)}, u32[]{:S(2)}) collective-permute-start(bf16[48,1536]{1,0:T(8,128)(2,1)} %get-tuple-element.373), channel_id=1, source_target_pairs={{0,2},{2,4},{4,6},{6,0},{1,3},{3,5},{5,7},{7,1},{8,10},{10,12},{12... | collective-permute-start | bytes 442376 | tf_op jit(solution)/shard_map/ppermute | solution.py:167
  522.4 22.5 %collective-permute-start.45 = (bf16[48,1536]{1,0:T(8,128)(2,1)}, bf16[48,1536]{1,0:T(8,128)(2,1)}, u32[]{:S(2)}, u32[]{:S(2)}) collective-permute-start(bf16[48,1536]{1,0:T(8,128)(2,1)} %get-tuple-element.374), channel_id=1, source_target_pairs={{0,6},{2,0},{4,2},{6,4},{1,7},{3,1},{5,3},{7,5},{8,14},{10,8},{12,... | collective-permute-start | bytes 442376 | tf_op jit(solution)/shard_map/ppermute | solution.py:167
  (118 other events, 918.4 us)
